TPU v7x, 128 devices: a whole 4x4x4 slice. The times are simulated.
128 devices in a mesh: tm: 64 (over x_hi, z, y, core), row: 2 (over x_lo).
Axes of the slice: x: 4 (x_hi: 2, x_lo: 2; x = x_hi * 2 + x_lo), y: 4, z: 4, core: 2. Of those that a mesh axis runs over, the one named last changes fastest.
Arguments:
- wavefront: float32 [512, 2, 256, 256], P('tm', None, 'row'), may hold values from -6 to 6
- particle_phase: float32 [512, 4096], P('tm', 'row'), may hold values from -3.140625 to 3.140625
- particle_energy: float32 [512, 4096], P('tm', 'row'), may hold values from -6 to 6
- row_offset: float32 [512, 4096], P('tm', 'row'), may hold values from -0.5 to 0.5
- row_cell: int32 [512, 4096], P('tm', 'row'), may hold values from 0 to 255, as said below
- col_cell: int32 [512, 4096], P('tm', 'row'), may hold values from 0 to 255
Outputs:
- wavefront_out: float32 [512, 2, 256, 256], P('tm', None, 'row')
- phase_out: float32 [512, 4096], P('tm', 'row')
- energy_out: float32 [512, 4096], P('tm', 'row')
Inputs may be any that keep to these rules, and one draw needn't show every extreme that they name: `row_cell`: the particle at position p of a slice lies in rows 128 * (p // 2048) to 128 * (p // 2048) + 127.
All inputs are finite; a program needn't handle non-finite values.
Results may differ from a plain program's by a relative error of at most 0.0003.
Values sent between devices are 32-bit elements; how exact they have to be, the bound alone decides.
No kernel may reach another device: no remote copies, remote signals or barrier semaphores. Data moves between devices by JAX's collectives and lax.ppermute only.
A program may use at most 64 MiB of HBM per device.

v0:
```python
import math
import numpy as np
import ml_dtypes
import jax, jax.numpy as jnp
from jax import lax
from jax.experimental import pallas as pl
from jax.experimental.pallas import tpu as pltpu

BF = jnp.bfloat16
F32 = jnp.float32
N = 256
WIN = 144

def split_np(m):
    hi = m.astype(ml_dtypes.bfloat16)
    lo = (m - hi.astype(np.float64)).astype(ml_dtypes.bfloat16)
    return hi, lo

def tables():
    k = np.arange(N)
    m = np.where(k < N // 2, k, k - N).astype(np.float64)
    h = np.exp(-1j * np.pi / N * m * m)
    dft = np.exp(-2j * np.pi / N * (k[:, None] * k[None, :] % N))
    a = (np.conj(dft) / N) @ (h[:, None] * dft)
    ar, ai = a.real, a.imag
    right = np.block([[ar, ai], [-ai, ar]])
    left = np.block([[ar, -ai], [ai, ar]])
    rh, rl = split_np(right)
    lh, ll = split_np(left)
    return np.concatenate([rh, rh, rl], 0), np.concatenate([lh, lh, ll], 1)

def sincos(x):
    n = jnp.round(x * (1.0 / math.pi))
    r = x - n * 3.140625
    r = r - n * 9.670257568359375e-4
    r = r - n * 6.277114152908325e-07
    half = n * 0.5
    odd = half - jnp.floor(half)
    sign = 1.0 - 4.0 * odd
    y = r * r
    s = -2.3889859e-08
    s = s * y + 2.7525562e-06
    s = s * y - 1.98408740e-04
    s = s * y + 8.33333310e-03
    s = s * y - 1.66666667e-01
    s = r + r * y * s
    c = 2.08767570e-09 - 1.1470746e-11 * y
    c = c * y - 2.75573192e-07
    c = c * y + 2.48015873e-05
    c = c * y - 1.38888889e-03
    c = c * y + 4.16666667e-02
    c = c * y - 0.5
    c = c * y + 1.0
    return s * sign, c * sign

def hilo(x):
    hi = x.astype(BF)
    lo = (x - hi.astype(F32)).astype(BF)
    return hi, lo

def body(f_ref, ph_ref, en_ref, off_ref, row_ref, col_ref, r_ref, l_ref,
         fo_ref, pho_ref, eno_ref,
         c_ref, samp_ref, w_ref, s_ref, sr_ref, x_ref):
    off = off_ref[0]
    lg = 0.5 - off
    ug = 0.5 + off
    w_ref[0] = 0.5 * lg * lg
    w_ref[1] = 0.75 - off * off
    w_ref[2] = 0.5 * ug * ug
    iota_c = lax.broadcasted_iota(jnp.int32, (16, 16, 128), 0) * 16 + lax.broadcasted_iota(jnp.int32, (16, 16, 128), 1)
    iota_c = iota_c.astype(F32).astype(BF)
    one = jnp.ones((16, 128), BF)
    zero = jnp.zeros((16, 128), BF)
    iota_r = lax.broadcasted_iota(jnp.int32, (WIN, 128), 0).astype(F32)
    for h in range(2):
        win0 = 0 if h == 0 else N - WIN
        fw = f_ref[0, :, win0:win0 + WIN, :].reshape(2 * WIN, N)
        hi, lo = hilo(fw)
        for k in range(16):
            j = 16 * h + k
            c = jnp.broadcast_to(col_ref[0, j:j + 1, :], (16, 128)).astype(BF)
            c_ref[h, :, 128 * k:128 * k + 128] = jnp.where(iota_c == c[None], one[None], zero[None]).reshape(N, 128)
        for k2 in range(8):
            cc = c_ref[h, :, 256 * k2:256 * k2 + 256]
            g2 = jnp.dot(hi, cc, preferred_element_type=F32) + jnp.dot(lo, cc, preferred_element_type=F32)
            for kk in range(2):
                j = 16 * h + 2 * k2 + kk
                g = g2[:, 128 * kk:128 * kk + 128]
                rr = row_ref[0, j:j + 1, :] - float(win0)
                w = jnp.where(iota_r == rr, w_ref[1, j:j + 1, :],
                    jnp.where(iota_r == rr - 1.0, w_ref[0, j:j + 1, :],
                    jnp.where(iota_r == rr + 1.0, w_ref[2, j:j + 1, :], 0.0)))
                samp_ref[0, j:j + 1, :] = jnp.sum(w * g[:WIN], 0, keepdims=True)
                samp_ref[1, j:j + 1, :] = jnp.sum(w * g[WIN:], 0, keepdims=True)
    ph = ph_ref[0]
    s0, c0 = sincos(ph)
    en = en_ref[0] - 0.5 * (samp_ref[0] * c0 - samp_ref[1] * s0)
    ph = ph + en
    pho_ref[0] = ph
    eno_ref[0] = en
    s1, c1 = sincos(ph)
    s1 = -s1
    for z, v in ((0, c1), (1, s1)):
        vh = v.astype(BF).astype(F32)
        s_ref[2 * z] = vh
        s_ref[2 * z + 1] = v - vh
    iota_d = iota_c[:8]
    for h in range(2):
        for k in range(16):
            j = 16 * h + k
            rr = jnp.broadcast_to(row_ref[0, j:j + 1, :] - float(128 * h), (16, 128)).astype(BF)
            m = iota_d == rr[None]
            for q in range(4):
                sv = jnp.broadcast_to(s_ref[q, j:j + 1, :], (16, 128)).astype(BF)
                sr_ref[128 * q:128 * q + 128, 128 * k:128 * k + 128] = jnp.where(m, sv[None], zero[None]).reshape(128, 128)
        d = lax.dot_general(sr_ref[...], c_ref[h], (((1,), (1,)), ((), ())), preferred_element_type=F32)
        for z in range(2):
            x_ref[128 * h:128 * h + 128, N * z:N * z + N] = (
                f_ref[0, z, 128 * h:128 * h + 128, :] + d[256 * z:256 * z + 128] + d[256 * z + 128:256 * z + 256])
    xh, xl = hilo(x_ref[...])
    y = jnp.dot(jnp.concatenate([xh, xl, xh], 1), r_ref[...], preferred_element_type=F32)
    y2 = jnp.concatenate([y[:, :N], y[:, N:]], 0)
    yh, yl = hilo(y2)
    z = jnp.dot(l_ref[...], jnp.concatenate([yh, yl, yh], 0), preferred_element_type=F32)
    fo_ref[0] = z.reshape(2, N, N)

def slots(field, ph, en, off, row, col, right, left):
    n = field.shape[0]
    fs = pl.BlockSpec((1, 2, N, N), lambda i: (i, 0, 0, 0))
    ps = pl.BlockSpec((1, 32, 128), lambda i: (i, 0, 0))
    full = lambda a: pl.BlockSpec(a.shape, lambda i: (0,) * a.ndim)
    return pl.pallas_call(
        body, grid=(n,),
        in_specs=[fs, ps, ps, ps, ps, ps, full(right), full(left)],
        out_specs=[fs, ps, ps],
        out_shape=[jax.ShapeDtypeStruct(field.shape, F32), jax.ShapeDtypeStruct(ph.shape, F32), jax.ShapeDtypeStruct(ph.shape, F32)],
        scratch_shapes=[pltpu.VMEM((2, N, 2048), BF), pltpu.VMEM((2, 32, 128), F32), pltpu.VMEM((3, 32, 128), F32),
                        pltpu.VMEM((4, 32, 128), F32), pltpu.VMEM((512, 2048), BF), pltpu.VMEM((N, 512), F32)],
        compiler_params=pltpu.CompilerParams(vmem_limit_bytes=48 << 20),
    )(field, ph, en, off, row, col, right, left)


def other_half(value, start, count):
    return lax.dynamic_slice_in_dim(value, start, count, 0)


def run(field, zero_slot, particles, right, left):
    phase, energy, offset, row, col = particles
    device = lax.axis_index(("tm", "row"))
    scale = jnp.where((jnp.arange(4) == zero_slot) & (device == 0), 0.0, 1.0).astype(F32)
    field = field * scale[:, None, None, None]
    return slots(field, phase, energy, offset, row, col, right, left)


def body_all(wavefront, particle_phase, particle_energy, row_offset, row_cell, col_cell):
    right, left = (jnp.asarray(a) for a in tables())
    r = lax.axis_index("row")
    first = r == 0
    nt = lax.axis_size("tm")
    both = ("tm", "row")
    swap = [(2 * t + s, 2 * t + 1 - s) for t in range(nt) for s in range(2)]
    chain = [(i, (i + 1) % (2 * nt)) for i in range(2 * nt)]
    ahead = [(2 * t, (2 * t + 2) % (2 * nt)) for t in range(nt)]
    back = [(j, i) for i, j in chain]

    parts = jnp.stack([particle_phase, particle_energy, row_offset,
                       row_cell.astype(F32), col_cell.astype(F32)], 1).reshape(8, 5, 16, 128)
    p_swap = lax.ppermute(other_half(parts, 4 - 4 * r, 4), both, swap)
    p_chain = lax.ppermute(other_half(parts, 3 + 4 * r, 1), both, chain)
    p_ahead = lax.ppermute(parts[7:8], both, ahead)
    f_chain = lax.ppermute(other_half(wavefront, 2 + 4 * r, 2), both, chain)
    f_ahead = lax.ppermute(wavefront[6:8], both, ahead)
    f_swap = lax.ppermute(other_half(wavefront, 4 - 4 * r, 2), both, swap)

    def joined(own, other, axis):
        return jnp.concatenate([jnp.where(first, own, other), jnp.where(first, other, own)], axis)

    p_own = jnp.where(first, jnp.concatenate([p_ahead, parts[:4]], 0), parts[3:])
    p_all = joined(p_own, jnp.concatenate([p_chain, p_swap], 0), 2)
    f_own = jnp.where(first, jnp.concatenate([f_ahead, wavefront[:2]], 0), wavefront[2:6])
    field = joined(f_own, jnp.concatenate([f_chain, f_swap], 0), 2)
    p_first = [p_all[:4, i] for i in range(5)]
    field, phase, energy = run(field, 1, p_first, right, left)
    pushed = jnp.stack([phase, energy], 1)
    p_last = lax.ppermute(pushed[:1], both, back)
    pushed = jnp.concatenate([pushed[1:], p_last], 0)
    field, phase, energy = run(field, 0, [pushed[:, 0], pushed[:, 1]] + [p_all[1:, i] for i in range(2, 5)], right, left)

    def home(value, axis):
        count = value.shape[axis] // 2
        own = lax.dynamic_slice_in_dim(value, r * count, count, axis)
        away = lax.dynamic_slice_in_dim(value, (1 - r) * count, count, axis)
        return joined(own, lax.ppermute(away, both, swap), 0)

    field = home(field, 2)
    pushed = home(jnp.stack([phase, energy], 1), 2)
    return field, pushed[:, 0].reshape(8, 2048), pushed[:, 1].reshape(8, 2048)


def solution(mesh):
    P = jax.sharding.PartitionSpec
    wide, flat = P("tm", None, "row", None), P("tm", "row")
    return jax.shard_map(body_all, mesh=mesh, in_specs=(wide,) + (flat,) * 5,
                         out_specs=(wide, flat, flat), check_vma=False)
```

profile of v0, /device:TPU:123, one launch (start us, length us, event | category | flops | bytes accessed | tf_op | source)
XLA Modules:
  0.0 129.6 jit_solution(8348690493406566457)
XLA Ops:
  0.6 1.0 convert_bitcast_fusion.1
  1.6 0.8 convert_bitcast_fusion
  2.5 0.9 bitcast_dynamic-update-slice_fusion.4
  3.3 0.9 bitcast_dynamic-update-slice_fusion.3
  4.2 0.9 bitcast_dynamic-update-slice_fusion.2
  5.1 0.6 constant_dynamic-slice_fusion.2
  5.7 0.1 collective-permute-start.4
  5.8 0.7 constant_dynamic-slice_fusion.1
  6.5 1.4 %collective-permute-start.5 = (f32[4,5,16,128]{3,2,0,1:T(8,128)}, f32[4,5,16,128]{3,2,0,1:T(8,128)}, u32[]{:S(2)}, u32[]{:S(2)}) collective-permute-start(f32[4,5,16,128]{3,2,0,1:T(8,128)} %constant_dynamic-slice_fusion.1), channel_id=1, source_target_pairs={{0,1},{1,0},{2,3},{3,2},{4,5},{5,4},{6,7},{7,6},{8,9},{9,8},{10,11... | collective-permute-start | bytes 491528 | tf_op jit(solution)/shard_map/ppermute | solution.py:168
  7.9 0.8 bitcast_dynamic-update-slice_fusion.9
  8.7 0.8 bitcast_dynamic-update-slice_fusion.8
  9.6 0.8 bitcast_dynamic-update-slice_fusion.7
  10.4 0.8 bitcast_dynamic-update-slice_fusion.6
  11.3 0.8 bitcast_dynamic-update-slice_fusion.5
  12.1 0.7 slice.92
  12.8 0.7 collective-permute-start.3
  13.4 1.2 fusion.24
  14.6 1.5 %collective-permute-start = (f32[2,2,128,256]{3,2,1,0:T(8,128)}, f32[2,2,128,256]{3,2,1,0:T(8,128)}, u32[]{:S(2)}, u32[]{:S(2)}) collective-permute-start(f32[2,2,128,256]{3,2,1,0:T(8,128)} %get-tuple-element.19), channel_id=1, source_target_pairs={{0,2},{2,4},{4,6},{6,8},{8,10},{10,12},{12,14},{14,16},{16,18},{18... | collective-permute-start | bytes 1572872 | tf_op jit(solution)/shard_map/ppermute | solution.py:172
  16.1 5.0 %collective-permute-start.2 = (f32[2,2,128,256]{3,2,1,0:T(8,128)}, f32[2,2,128,256]{3,2,1,0:T(8,128)}, u32[]{:S(2)}, u32[]{:S(2)}) collective-permute-start(f32[2,2,128,256]{3,2,1,0:T(8,128)} %get-tuple-element.21), channel_id=1, source_target_pairs={{0,1},{1,0},{2,3},{3,2},{4,5},{5,4},{6,7},{7,6},{8,9},{9,8},{10,11... | collective-permute-start | bytes 1572872 | tf_op jit(solution)/shard_map/ppermute | solution.py:173
  21.2 0.1 slice.77
  21.3 0.1 slice.75
  21.4 0.0 collective-permute-done.4
  21.4 0.1 collective-permute-start.1
  21.5 0.8 constant_dynamic-update-slice_fusion.3
  22.3 0.9 constant_dynamic-update-slice_fusion.2
  23.2 0.0 collective-permute-done.3
  23.2 0.1 broadcast_select_fusion.2
  23.3 0.1 fusion.22
  23.3 26.3 %collective-permute-done.1 = f32[2,2,128,256]{3,2,1,0:T(8,128)S(1)} collective-permute-done((f32[2,2,128,256]{3,2,1,0:T(8,128)}, f32[2,2,128,256]{3,2,1,0:T(8,128)S(1)}, u32[]{:S(2)}, u32[]{:S(2)}) %collective-permute-start.1) | collective-permute-done | bytes 524320 | tf_op jit(solution)/shard_map/ppermute | solution.py:171
  49.7 0.0 collective-permute-done.2
  49.7 1.1 constant_dynamic-update-slice_fusion
  50.8 1.3 broadcast_select_fusion.1
  52.1 0.0 copy-start
  52.1 0.0 copy-start.1
  52.1 1.6 %maximum_multiply_fusion.f_ref = f32[4,2,256,256]{3,2,1,0:T(8,128)} fusion(f32[4,2,128,256]{3,2,1,0:T(8,128)S(1)} %get-tuple-element.16, f32[4,2,128,256]{3,2,1,0:T(8,128)S(1)} %get-tuple-element.15, f32[4]{0:T(128)S(1)} %and_select_fusion.1), kind=kLoop, calls=%fused_computation | loop fusion | flops 1048576 | bytes 4194320 | tf_op jit(solution)/shard_map/mul | solution.py:151
  53.7 0.2 copy-done
  53.8 0.9 copy-done.1
  54.7 21.3 %shard_map.103 = (f32[4,2,256,256]{3,2,1,0:T(8,128)S(1)}, f32[4,32,128]{2,1,0:T(8,128)S(1)}, f32[4,32,128]{2,1,0:T(8,128)S(1)}) custom-call(f32[4,2,256,256]{3,2,1,0:T(8,128)} %maximum_multiply_fusion.f_ref, f32[4,32,128]{2,1,0:T(8,128)S(1)} %get-tuple-element.26.ph_ref, f32[4,32,128]{2,1,0:T(8,128)S(1)} %get-tuple-element.27.en_ref, ...), custom_call_target="tpu_custom_call" | custom-call | tf_op jit(solution)/shard_map/pallas_call | solution.py:132
  76.0 0.1 collective-permute-start.6
  76.1 1.6 %broadcast_multiply_fusion.f_ref = f32[4,2,256,256]{3,2,1,0:T(8,128)} fusion(f32[4,2,256,256]{3,2,1,0:T(8,128)S(1)} %get-tuple-element.9, f32[4]{0:T(128)S(1)} %and_select_fusion), kind=kLoop, calls=%fused_computation.3 | loop fusion | flops 524288 | bytes 4194320 | tf_op jit(solution)/shard_map/mul | solution.py:151
  77.7 5.9 %collective-permute-done.6 = f32[1,2,32,128]{3,2,0,1:T(8,128)S(1)} collective-permute-done((f32[1,2,32,128]{3,2,0,1:T(8,128)S(1)}, f32[1,2,32,128]{3,2,0,1:T(8,128)S(1)}, u32[]{:S(2)}, u32[]{:S(2)}) %collective-permute-start.6) | collective-permute-done | bytes 32800 | tf_op jit(solution)/shard_map/ppermute | solution.py:185
  83.6 21.3 %shard_map.104 = (f32[4,2,256,256]{3,2,1,0:T(8,128)S(1)}, f32[4,32,128]{2,1,0:T(8,128)S(1)}, f32[4,32,128]{2,1,0:T(8,128)S(1)}) custom-call(f32[4,2,256,256]{3,2,1,0:T(8,128)} %broadcast_multiply_fusion.f_ref, f32[4,32,128]{2,1,0:T(8,128)S(1)} %get-tuple-element.38.ph_ref, f32[4,32,128]{2,1,0:T(8,128)S(1)} %get-tuple-element.37.en_ref, ...), custom_call_target="tpu_custom_call" | custom-call | tf_op jit(solution)/shard_map/pallas_call | solution.py:132
  104.9 1.1 constant_dynamic-slice_fusion
  106.0 1.5 %collective-permute-start.8 = (f32[4,2,16,128]{3,2,0,1:T(8,128)S(1)}, f32[4,2,16,128]{3,2,0,1:T(8,128)S(1)}, u32[]{:S(2)}, u32[]{:S(2)}) collective-permute-start(f32[4,2,16,128]{3,2,0,1:T(8,128)S(1)} %fusion.5), channel_id=1, source_target_pairs={{0,1},{1,0},{2,3},{3,2},{4,5},{5,4},{6,7},{7,6},{8,9},{9,8},{10,11... | collective-permute-start | bytes 196616 | tf_op jit(solution)/shard_map/ppermute | solution.py:193
  107.5 19.6 %collective-permute-done.8 = f32[4,2,16,128]{3,2,0,1:T(8,128)S(1)} collective-permute-done((f32[4,2,16,128]{3,2,0,1:T(8,128)S(1)}, f32[4,2,16,128]{3,2,0,1:T(8,128)S(1)}, u32[]{:S(2)}, u32[]{:S(2)}) %collective-permute-start.8) | collective-permute-done | bytes 65568 | tf_op jit(solution)/shard_map/ppermute | solution.py:193
  127.1 0.7 copy_bitcast_fusion
  127.8 0.2 dynamic-slice_select_fusion.1
  128.1 1.6 %pad_maximum_fusion = f32[8,2,128,256]{3,2,1,0:T(8,128)} fusion(f32[4,2,128,256]{3,2,1,0:T(8,128)S(1)} %get-tuple-element.18, f32[4,2,128,256]{3,2,1,0:T(8,128)S(1)} %get-tuple-element.17), kind=kLoop, calls=%fused_computation.1 | loop fusion | flops 524288 | bytes 4194304 | tf_op jit(solution)/shard_map/concatenate | solution.py:176
  (19 shorter events, 0.2 us)
Async XLA Ops:
  0.6 12.8 %copy-start.2 = (f32[8,2,128,256]{3,2,1,0:T(8,128)S(1)}, f32[8,2,128,256]{3,2,1,0:T(8,128)}, u32[]{:S(2)}) copy-start(f32[8,2,128,256]{3,2,1,0:T(8,128)} %param.8) | copy-start | bytes 6291460
  5.7 15.7 %collective-permute-start.4 = (f32[1,5,16,128]{3,2,0,1:T(8,128)}, f32[1,5,16,128]{3,2,0,1:T(8,128)}, u32[]{:S(2)}, u32[]{:S(2)}) collective-permute-start(f32[1,5,16,128]{3,2,0,1:T(8,128)} %constant_dynamic-slice_fusion.2), channel_id=1, source_target_pairs={{0,1},{1,2},{2,3},{3,4},{4,5},{5,6},{6,7},{7,8},{8,9},{9,10},{10,1... | collective-permute-start | bytes 122888 | tf_op jit(solution)/shard_map/ppermute | solution.py:169
  6.5 15.8 %collective-permute-start.5 = (f32[4,5,16,128]{3,2,0,1:T(8,128)}, f32[4,5,16,128]{3,2,0,1:T(8,128)}, u32[]{:S(2)}, u32[]{:S(2)}) collective-permute-start(f32[4,5,16,128]{3,2,0,1:T(8,128)} %constant_dynamic-slice_fusion.1), channel_id=1, source_target_pairs={{0,1},{1,0},{2,3},{3,2},{4,5},{5,4},{6,7},{7,6},{8,9},{9,8},{10,11... | collective-permute-start | bytes 491528 | tf_op jit(solution)/shard_map/ppermute | solution.py:168
  12.8 10.4 %collective-permute-start.3 = (f32[1,5,16,128]{3,2,0,1:T(8,128)}, f32[1,5,16,128]{3,2,0,1:T(8,128)S(1)}, u32[]{:S(2)}, u32[]{:S(2)}) collective-permute-start(f32[1,5,16,128]{3,2,0,1:T(8,128)} %bitcast.5), channel_id=1, source_target_pairs={{0,2},{2,4},{4,6},{6,8},{8,10},{10,12},{12,14},{14,16},{16,18},{18... | collective-permute-start | bytes 122888 | tf_op jit(solution)/shard_map/ppermute | solution.py:170
  14.6 36.2 %collective-permute-start = (f32[2,2,128,256]{3,2,1,0:T(8,128)}, f32[2,2,128,256]{3,2,1,0:T(8,128)}, u32[]{:S(2)}, u32[]{:S(2)}) collective-permute-start(f32[2,2,128,256]{3,2,1,0:T(8,128)} %get-tuple-element.19), channel_id=1, source_target_pairs={{0,2},{2,4},{4,6},{6,8},{8,10},{10,12},{12,14},{14,16},{16,18},{18... | collective-permute-start | bytes 1572872 | tf_op jit(solution)/shard_map/ppermute | solution.py:172
  16.1 33.6 %collective-permute-start.2 = (f32[2,2,128,256]{3,2,1,0:T(8,128)}, f32[2,2,128,256]{3,2,1,0:T(8,128)}, u32[]{:S(2)}, u32[]{:S(2)}) collective-permute-start(f32[2,2,128,256]{3,2,1,0:T(8,128)} %get-tuple-element.21), channel_id=1, source_target_pairs={{0,1},{1,0},{2,3},{3,2},{4,5},{5,4},{6,7},{7,6},{8,9},{9,8},{10,11... | collective-permute-start | bytes 1572872 | tf_op jit(solution)/shard_map/ppermute | solution.py:173
  21.4 28.3 %collective-permute-start.1 = (f32[2,2,128,256]{3,2,1,0:T(8,128)}, f32[2,2,128,256]{3,2,1,0:T(8,128)S(1)}, u32[]{:S(2)}, u32[]{:S(2)}) collective-permute-start(f32[2,2,128,256]{3,2,1,0:T(8,128)} %get-tuple-element.22), channel_id=1, source_target_pairs={{0,1},{1,2},{2,3},{3,4},{4,5},{5,6},{6,7},{7,8},{8,9},{9,10},{10,1... | collective-permute-start | bytes 1572872 | tf_op jit(solution)/shard_map/ppermute | solution.py:171
  52.1 1.8 %copy-start = (bf16[512,1536]{1,0:T(8,128)(2,1)S(1)}, bf16[512,1536]{1,0:T(8,128)(2,1)}, u32[]{:S(2)}) copy-start(bf16[512,1536]{1,0:T(8,128)(2,1)} %constant.44.clone.l_ref) | copy-start | bytes 4718596
  52.1 2.6 %copy-start.1 = (bf16[1536,512]{1,0:T(8,128)(2,1)S(1)}, bf16[1536,512]{1,0:T(8,128)(2,1)}, u32[]{:S(2)}) copy-start(bf16[1536,512]{1,0:T(8,128)(2,1)} %constant.43.clone.r_ref) | copy-start | bytes 4718596
  76.0 7.6 %collective-permute-start.6 = (f32[1,2,32,128]{3,2,0,1:T(8,128)S(1)}, f32[1,2,32,128]{3,2,0,1:T(8,128)S(1)}, u32[]{:S(2)}, u32[]{:S(2)}) collective-permute-start(f32[1,2,32,128]{3,2,0,1:T(8,128)S(1)} %pad_maximum_fusion.4), channel_id=1, source_target_pairs={{1,0},{2,1},{3,2},{4,3},{5,4},{6,5},{7,6},{8,7},{9,8},{10,9},{11,1... | collective-permute-start | bytes 98312 | tf_op jit(solution)/shard_map/ppermute | solution.py:185
  106.0 21.8 %collective-permute-start.7 = (f32[4,2,128,256]{3,2,1,0:T(8,128)}, f32[4,2,128,256]{3,2,1,0:T(8,128)S(1)}, u32[]{:S(2)}, u32[]{:S(2)}) collective-permute-start(f32[4,2,128,256]{3,2,1,0:T(8,128)} %constant_dynamic-slice_fusion), channel_id=1, source_target_pairs={{0,1},{1,0},{2,3},{3,2},{4,5},{5,4},{6,7},{7,6},{8,9},{9,8},{10,11... | collective-permute-start | bytes 3145736 | tf_op jit(solution)/shard_map/ppermute | solution.py:193
  106.0 21.1 %collective-permute-start.8 = (f32[4,2,16,128]{3,2,0,1:T(8,128)S(1)}, f32[4,2,16,128]{3,2,0,1:T(8,128)S(1)}, u32[]{:S(2)}, u32[]{:S(2)}) collective-permute-start(f32[4,2,16,128]{3,2,0,1:T(8,128)S(1)} %fusion.5), channel_id=1, source_target_pairs={{0,1},{1,0},{2,3},{3,2},{4,5},{5,4},{6,7},{7,6},{8,9},{9,8},{10,11... | collective-permute-start | bytes 196616 | tf_op jit(solution)/shard_map/ppermute | solution.py:193
where the time goes:
time: 130 us
  waiting for transfers between devices  51.9 us (40%)
  Pallas kernels  42.5 us (33%)
  local copies, waits for them, and re-layouts  14.1 us (11%)
  starting transfers between devices  10.2 us (8%)
  other arithmetic  9.96 us (8%)
    pallas_call x2, Pallas kernels, slots(): pl.pallas_call(body, grid=(n,), in_specs=[fs, ps, ps, ps, ps, ps, full(ri...  42.5 us
    ppermute x1, waiting for transfers between devices, body_all(): f_chain = lax.ppermute(other_half(wavefront, 2 + 4 * r, 2), both, chain)  26.3 us
    ppermute x2, waiting for transfers between devices, home(): return joined(own, lax.ppermute(away, both, swap), 0)  19.6 us
    unnamed x15, local copies, waits for them, and re-layouts  6.95 us
    ppermute x1, waiting for transfers between devices, body_all(): p_last = lax.ppermute(pushed[:1], both, back)  5.94 us
    ppermute x1, starting transfers between devices, body_all(): f_swap = lax.ppermute(other_half(wavefront, 4 - 4 * r, 2), both, swap)  5.03 us
    mul x2, other arithmetic, run(): field = field * scale[:, None, None, None]  3.2 us
    unnamed x4, other arithmetic  2.7 us
  transfers between devices with their start and end apart: 9, of which 3 were waited for; matrix products, arithmetic and copies ran while one was open for 9% of the time, Pallas kernels for 0%

commit v1 on v0

v1 whole, which is shorter than its diff:
```python
import math

import jax
import jax.numpy as jnp
import ml_dtypes
import numpy as np
from jax import lax
from jax.experimental import pallas as pl
from jax.experimental.pallas import tpu as pltpu

BF = jnp.bfloat16
F32 = jnp.float32
N = 256
HALF = 128
PART = 2048
ROWS = PART // N
WIN = 144
FIELDS = 5 * ROWS
PUSHED = 2 * ROWS
PIECE = 2 * HALF + PUSHED


def split_np(m):
    hi = m.astype(ml_dtypes.bfloat16)
    return hi, (m - hi.astype(np.float64)).astype(ml_dtypes.bfloat16)


def tables():
    k = np.arange(N)
    m = np.where(k < N // 2, k, k - N).astype(np.float64)
    h = np.exp(-1j * np.pi / N * m * m)
    dft = np.exp(-2j * np.pi / N * (k[:, None] * k[None, :] % N))
    a = (np.conj(dft) / N) @ (h[:, None] * dft)
    right = np.block([[a.real, a.imag], [-a.imag, a.real]])
    left = np.block([[a.real, -a.imag], [a.imag, a.real]])
    return np.stack(split_np(right)), np.stack(split_np(left))


def sincos(x):
    n = jnp.round(x * (1.0 / math.pi))
    r = x - n * 3.140625
    r = r - n * 9.670257568359375e-4
    r = r - n * 6.277114152908325e-07
    half = n * 0.5
    sign = 1.0 - 4.0 * (half - jnp.floor(half))
    y = r * r
    s = -2.3889859e-08
    for c in (2.7525562e-06, -1.98408740e-04, 8.33333310e-03, -1.66666667e-01):
        s = s * y + c
    s = r + r * y * s
    c = 2.08767570e-09 - 1.1470746e-11 * y
    for d in (-2.75573192e-07, 2.48015873e-05, -1.38888889e-03, 4.16666667e-02, -0.5, 1.0):
        c = c * y + d
    return s * sign, c * sign


def hilo(x):
    hi = x.astype(BF)
    return hi, (x - hi.astype(F32)).astype(BF)


def mm(a, b):
    return jnp.dot(a, b, preferred_element_type=F32)


def step(f_ref, p_ref, tab_r, tab_l, out_ref, c_ref, w_ref, s_ref, sr_ref, x_ref, samp_ref):
    iota_c = (lax.broadcasted_iota(jnp.int32, (16, 16, N), 0) * 16
              + lax.broadcasted_iota(jnp.int32, (16, 16, N), 1)).astype(F32).astype(BF)
    one = jnp.ones((16, N), BF)
    zero = jnp.zeros((16, N), BF)
    iota_r = lax.broadcasted_iota(jnp.int32, (WIN, N), 0).astype(F32)
    for h in range(2):
        off = p_ref[h, 2 * ROWS:3 * ROWS]
        lower = 0.5 - off
        upper = 0.5 + off
        w_ref[0] = 0.5 * lower * lower
        w_ref[1] = 0.75 - off * off
        w_ref[2] = 0.5 * upper * upper
        win0 = 0 if h == 0 else N - WIN
        hi, lo = hilo(f_ref[:, win0:win0 + WIN, :].reshape(2 * WIN, N))
        for k in range(ROWS):
            col = jnp.broadcast_to(p_ref[h, 4 * ROWS + k:4 * ROWS + k + 1, :], (16, N)).astype(BF)
            hot = jnp.where(iota_c == col[None], one[None], zero[None]).reshape(N, N)
            c_ref[h, :, N * k:N * k + N] = hot
            g = mm(hi, hot) + mm(lo, hot)
            at = p_ref[h, 3 * ROWS + k:3 * ROWS + k + 1, :] - float(win0)
            w = jnp.where(iota_r == at, w_ref[1, k:k + 1, :],
                          jnp.where(iota_r == at - 1.0, w_ref[0, k:k + 1, :],
                                    jnp.where(iota_r == at + 1.0, w_ref[2, k:k + 1, :], 0.0)))
            samp_ref[0, k:k + 1, :] = jnp.sum(w * g[:WIN], 0, keepdims=True)
            samp_ref[1, k:k + 1, :] = jnp.sum(w * g[WIN:], 0, keepdims=True)
        phase = p_ref[h, :ROWS]
        sine, cosine = sincos(phase)
        energy = p_ref[h, ROWS:2 * ROWS] - 0.5 * (samp_ref[0] * cosine - samp_ref[1] * sine)
        phase = phase + energy
        p_ref[h, :ROWS] = phase
        p_ref[h, ROWS:2 * ROWS] = energy
        sine, cosine = sincos(phase)
        for z, v in ((0, cosine), (1, -sine)):
            vh = v.astype(BF).astype(F32)
            s_ref[2 * z] = vh
            s_ref[2 * z + 1] = v - vh
        for k in range(ROWS):
            at = jnp.broadcast_to(p_ref[h, 3 * ROWS + k:3 * ROWS + k + 1, :] - float(HALF * h), (16, N)).astype(BF)
            here = iota_c[:8] == at[None]
            for q in range(4):
                value = jnp.broadcast_to(s_ref[q, k:k + 1, :], (16, N)).astype(BF)
                sr_ref[HALF * q:HALF * q + HALF, N * k:N * k + N] = jnp.where(here, value[None], zero[None]).reshape(HALF, N)
        d = lax.dot_general(sr_ref[...], c_ref[h], (((1,), (1,)), ((), ())), preferred_element_type=F32)
        for z in range(2):
            x_ref[HALF * h:HALF * h + HALF, N * z:N * z + N] = (
                f_ref[z, HALF * h:HALF * h + HALF, :]
                + d[2 * HALF * z:2 * HALF * z + HALF] + d[2 * HALF * z + HALF:2 * HALF * z + 2 * HALF])
    xh, xl = hilo(x_ref[...])
    y = mm(xh, tab_r[0]) + mm(xl, tab_r[0]) + mm(xh, tab_r[1])
    yh, yl = hilo(jnp.concatenate([y[:, :N], y[:, N:]], 0))
    out = mm(tab_l[0], yh) + mm(tab_l[0], yl) + mm(tab_l[1], yh)
    out_ref[...] = out.reshape(2, N, N)


WORK = [pltpu.VMEM((2, N, PART), BF), pltpu.VMEM((3, ROWS, N), F32), pltpu.VMEM((4, ROWS, N), F32),
        pltpu.VMEM((4 * HALF, PART), BF), pltpu.VMEM((N, 2 * N), F32), pltpu.VMEM((2, ROWS, N), F32)]
FIELD = pltpu.VMEM((2, N, N), F32)
PARTS = pltpu.VMEM((2, FIELDS, N), F32)
ANY = pl.BlockSpec(memory_space=pl.ANY)
VM = pl.BlockSpec(memory_space=pltpu.VMEM)
SM = pl.BlockSpec(memory_space=pltpu.SMEM)


class Copies:
    def __init__(self, sems):
        self.sems = sems
        self.used = 0
        self.open = []

    def start(self, src, dst):
        copy = pltpu.make_async_copy(src, dst, self.sems.at[self.used])
        self.used += 1
        copy.start()
        self.open.append(copy)

    def wait(self):
        for copy in self.open:
            copy.wait()
        self.open = []


def call(kernel, outs, out_specs, scratch, copies, in_specs, flops):
    return pl.pallas_call(
        kernel, out_shape=[jax.ShapeDtypeStruct(s, F32) for s in outs], in_specs=in_specs, out_specs=out_specs,
        scratch_shapes=scratch + [pltpu.SemaphoreType.DMA((copies,))],
        cost_estimate=pl.CostEstimate(flops=flops, bytes_accessed=4 << 20, transcendentals=0),
        compiler_params=pltpu.CompilerParams(vmem_limit_bytes=40 << 20))


def pack_kernel(meta, wave, *refs):
    sources, (all_ref, swap_ref, chain_ref, ahead_ref), (packed, sems) = refs[:5], refs[5:9], refs[9:]
    r = meta[0]
    rows = 2 * N
    copies = Copies(sems)
    copies.start(wave.at[pl.ds(N * (4 - 4 * r), rows)], swap_ref.at[pl.ds(0, rows)])
    copies.start(wave.at[pl.ds(N * (2 + 4 * r), rows)], chain_ref.at[pl.ds(0, rows)])
    copies.start(wave.at[pl.ds(N * (6 - 4 * r), rows)], ahead_ref.at[pl.ds(0, rows)])
    for a, src in enumerate(sources):
        for s in range(8):
            for k in range(ROWS):
                packed[s, a * ROWS + k:a * ROWS + k + 1, :] = src[s:s + 1, N * k:N * k + N].astype(F32)
    copies.start(packed, all_ref)
    for i in range(4):
        copies.start(packed.at[4 - 4 * r + i], swap_ref.at[pl.ds(rows + FIELDS * i, FIELDS)])
    copies.start(packed.at[3 + 4 * r], chain_ref.at[pl.ds(rows, FIELDS)])
    copies.start(packed.at[7 - 4 * r], ahead_ref.at[pl.ds(rows, FIELDS)])
    copies.wait()


def field_in(copies, r, f_ref, own, own_row, other, other_row):
    for z in range(2):
        copies.start(own.at[pl.ds(own_row + HALF * z, HALF)], f_ref.at[z, pl.ds(pl.multiple_of(HALF * r, HALF), HALF)])
        copies.start(other.at[pl.ds(other_row + HALF * z, HALF)],
                     f_ref.at[z, pl.ds(pl.multiple_of(HALF - HALF * r, HALF), HALF)])


def piece_out(copies, r, z_ref, p_ref, own, away, i):
    for half, dst in ((r, own), (1 - r, away)):
        for z in range(2):
            copies.start(z_ref.at[z, pl.ds(pl.multiple_of(HALF * half, HALF), HALF)], dst.at[i, pl.ds(HALF * z, HALF)])
        copies.start(p_ref.at[half, pl.ds(0, PUSHED)], dst.at[i, pl.ds(2 * HALF, PUSHED)])


def first_kernel(meta, wave, parts, swap, tab_r, tab_l, d_ref, q_ref, own, away, f2, f3, p1, p2, z, *rest):
    work, sems = rest[:-1], rest[-1]
    r = meta[0]
    copies = Copies(sems)
    field_in(copies, r, f2, wave, N * 4 * r, swap, 0)
    field_in(copies, r, f3, wave, N * (4 * r + 1), swap, N)
    for p, i in ((p1, 1), (p2, 2)):
        copies.start(parts.at[4 * r + i], p.at[r])
        copies.start(swap.at[pl.ds(2 * N + FIELDS * i, FIELDS)], p.at[1 - r])
    copies.wait()
    step(f3, p2, tab_r, tab_l, d_ref, *work)
    step(f2, p1, tab_r, tab_l, f3, *work)
    copies.start(p1, q_ref)
    step(f3, p2, tab_r, tab_l, z, *work)
    piece_out(copies, r, z, p2, own, away, 0)
    copies.wait()


def second_kernel(meta, parts, swap, chain, ahead, tab_r, tab_l, d_ref, q_ref, pushed, f0, f1, p0, pm, *rest):
    work, sems = rest[:-1], rest[-1]
    r = meta[0]
    copies = Copies(sems)
    field_in(copies, r, f0, ahead, 0, chain, 0)
    field_in(copies, r, f1, ahead, N, chain, N)
    copies.start(ahead.at[pl.ds(2 * N, FIELDS)], pm.at[r])
    copies.start(chain.at[pl.ds(2 * N, FIELDS)], pm.at[1 - r])
    copies.start(parts.at[4 * r], p0.at[r])
    copies.start(swap.at[pl.ds(2 * N, FIELDS)], p0.at[1 - r])
    copies.wait()

    @pl.when(meta[1] == 1)
    def _():
        f1[...] = jnp.zeros_like(f1)

    step(f0, pm, tab_r, tab_l, d_ref.at[0], *work)
    copies.start(pm.at[:, pl.ds(0, PUSHED)], pushed)
    step(f1, p0, tab_r, tab_l, d_ref.at[1], *work)
    copies.start(p0, q_ref)
    copies.wait()


def third_kernel(meta, d_ref, q0, q1, tab_r, tab_l, own, away, f0, p0, p1, z0, z1, *rest):
    work, sems = rest[:-1], rest[-1]
    r = meta[0]
    copies = Copies(sems)
    copies.start(d_ref.at[0], f0)
    copies.start(q0, p0)
    copies.start(q1, p1)
    copies.wait()

    @pl.when(meta[1] == 1)
    def _():
        f0[...] = jnp.zeros_like(f0)

    step(f0, p0, tab_r, tab_l, z0, *work)
    piece_out(copies, r, z0, p0, own, away, 0)
    step(d_ref.at[1], p1, tab_r, tab_l, z1, *work)
    piece_out(copies, r, z1, p1, own, away, 1)
    copies.wait()


def fourth_kernel(meta, d_ref, parts, swap, pushed, tab_r, tab_l, own, away, p3, z, *rest):
    work, sems = rest[:-1], rest[-1]
    r = meta[0]
    copies = Copies(sems)
    copies.start(parts.at[4 * r + 3], p3.at[r])
    copies.start(swap.at[pl.ds(2 * N + FIELDS * 3, FIELDS)], p3.at[1 - r])
    copies.wait()
    copies.start(pushed, p3.at[:, pl.ds(0, PUSHED)])
    copies.wait()
    step(d_ref, p3, tab_r, tab_l, z, *work)
    piece_out(copies, r, z, p3, own, away, 0)
    copies.wait()


def final_kernel(meta, *refs):
    pieces, (wave, phase, energy), (packed, sems) = refs[:6], refs[6:9], refs[9:]
    r = meta[0]
    copies = Copies(sems)
    for half in range(2):
        base = 4 * r if half == 0 else 4 - 4 * r
        for ref, slots in zip(pieces[3 * half:3 * half + 3], ((2,), (0, 1), (3,))):
            for i, slot in enumerate(slots):
                copies.start(ref.at[i, pl.ds(0, N)], wave.at[pl.ds((base + slot) * N, N)])
                copies.start(ref.at[i, pl.ds(N, PUSHED)], packed.at[base + slot])
    copies.wait()
    for s in range(8):
        for k in range(ROWS):
            phase[s:s + 1, N * k:N * k + N] = packed[s, k:k + 1, :]
            energy[s:s + 1, N * k:N * k + N] = packed[s, ROWS + k:ROWS + k + 1, :]


def body(wavefront, particle_phase, particle_energy, row_offset, row_cell, col_cell):
    tab_r, tab_l = (jnp.asarray(a) for a in tables())
    r = lax.axis_index("row")
    nt = lax.axis_size("tm")
    both = ("tm", "row")
    swap = [(i, i ^ 1) for i in range(2 * nt)]
    chain = [(i, (i + 1) % (2 * nt)) for i in range(2 * nt)]
    ahead = [(i, (i + 2) % (2 * nt) if i % 2 == 0 else i) for i in range(2 * nt)]
    back = [(j, i) for i, j in chain]
    meta = jnp.stack([r, (lax.axis_index(both) == 0).astype(jnp.int32)]).astype(jnp.int32)
    wave = wavefront.reshape(8 * N, N)
    unit = 1 << 31

    parts, to_swap, to_chain, to_ahead = call(
        pack_kernel, [(8, FIELDS, N), (2 * N + 4 * FIELDS, N), (2 * N + FIELDS, N), (2 * N + FIELDS, N)],
        [ANY] * 4, [pltpu.VMEM((8, FIELDS, N), F32)], 10, [SM, ANY] + [VM] * 5, 1 << 20,
    )(meta, wave, particle_phase, particle_energy, row_offset, row_cell, col_cell)
    f_swap = lax.ppermute(to_swap, both, swap)
    f_chain = lax.ppermute(to_chain, both, chain)
    f_ahead = lax.ppermute(to_ahead, both, ahead)

    d3, q1, own_a, away_a = call(
        first_kernel, [(2, N, N), (2, FIELDS, N), (1, PIECE, N), (1, PIECE, N)], [VM, ANY, ANY, ANY],
        [FIELD, FIELD, PARTS, PARTS, FIELD] + WORK, 24, [SM, ANY, ANY, ANY, VM, VM], 3 * unit,
    )(meta, wave, parts, f_swap, tab_r, tab_l)
    back_a = lax.ppermute(away_a, both, swap)
    d01, q0, pushed = call(
        second_kernel, [(2, 2, N, N), (2, FIELDS, N), (2, PUSHED, N)], [VM, ANY, ANY],
        [FIELD, FIELD, PARTS, PARTS] + WORK, 24, [SM, ANY, ANY, ANY, ANY, VM, VM], 2 * unit,
    )(meta, parts, f_swap, f_chain, f_ahead, tab_r, tab_l)
    pushed = lax.ppermute(pushed, both, back)
    own_b, away_b = call(
        third_kernel, [(2, PIECE, N), (2, PIECE, N)], [ANY, ANY],
        [FIELD, PARTS, PARTS, FIELD, FIELD] + WORK, 24, [SM, VM, ANY, ANY, VM, VM], 2 * unit,
    )(meta, d01, q0, q1, tab_r, tab_l)
    back_b = lax.ppermute(away_b, both, swap)
    own_c, away_c = call(
        fourth_kernel, [(1, PIECE, N), (1, PIECE, N)], [ANY, ANY],
        [PARTS, FIELD] + WORK, 24, [SM, VM, ANY, ANY, ANY, VM, VM], unit,
    )(meta, d3, parts, f_swap, pushed, tab_r, tab_l)
    back_c = lax.ppermute(away_c, both, swap)
    wave, phase, energy = call(
        final_kernel, [(8 * N, N), (8, PART), (8, PART)], [ANY, VM, VM],
        [pltpu.VMEM((8, PUSHED, N), F32)], 16, [SM] + [ANY] * 6, 1 << 20,
    )(meta, own_a, own_b, own_c, back_a, back_b, back_c)
    return wave.reshape(8, 2, HALF, N), phase, energy


def solution(mesh):
    P = jax.sharding.PartitionSpec
    wide, flat = P("tm", None, "row", None), P("tm", "row")
    return jax.shard_map(body, mesh=mesh, in_specs=(wide,) + (flat,) * 5,
                         out_specs=(wide, flat, flat), check_vma=False)
```

time: 130 us -> 108 us (0.83)
  the two profiles are of different devices: /device:TPU:123 before, /device:TPU:4 now
where the time goes in v1:
time: 108 us; the launch traced here: 106 us
  Pallas kernels  55.5 us (51%)
  waiting for transfers between devices  37.1 us (34%)
  starting transfers between devices  6.28 us (6%)
  local copies, waits for them, and re-layouts  5.79 us (5%)
    pallas_call x1, Pallas kernels, body(): call(first_kernel, [(2, N, N), (2, FIELDS, N), (1, PIECE, N), (1, PIECE,...  18.2 us
    ppermute x1, waiting for transfers between devices, body(): f_swap = lax.ppermute(to_swap, both, swap)  14.4 us
    pallas_call x1, Pallas kernels, body(): call(third_kernel, [(2, PIECE, N), (2, PIECE, N)], [ANY, ANY], [FIELD, PA...  13.5 us
    pallas_call x1, Pallas kernels, body(): call(second_kernel, [(2, 2, N, N), (2, FIELDS, N), (2, PUSHED, N)], [VM,...  13.5 us
    ppermute x1, waiting for transfers between devices, body(): pushed = lax.ppermute(pushed, both, back)  10.7 us
    ppermute x1, waiting for transfers between devices, body(): back_c = lax.ppermute(away_c, both, swap)  7.26 us
    pallas_call x1, Pallas kernels, body(): call(fourth_kernel, [(1, PIECE, N), (1, PIECE, N)], [ANY, ANY], [PARTS, F...  6.29 us
    unnamed x16, local copies, waits for them, and re-layouts  5.79 us
  transfers between devices with their start and end apart: 7, of which 4 were waited for; matrix products, arithmetic and copies ran while one was open for 0% of the time, Pallas kernels for 23%

profile of v1, /device:TPU:4, one launch (start us, length us, event | category | flops | bytes accessed | tf_op | source)
XLA Modules:
  0.0 105.7 jit_solution(22151190834687157)
XLA Ops:
  0.6 0.1 pad_add_fusion.meta
  0.7 0.0 copy-start
  0.7 1.6 %copy-done = f32[8,2,128,256]{3,2,1,0:T(8,128)S(1)} copy-done((f32[8,2,128,256]{3,2,1,0:T(8,128)S(1)}, f32[8,2,128,256]{3,2,1,0:T(8,128)}, u32[]{:S(2)}) %copy-start) | copy-done | bytes 2097176
  2.3 0.0 copy-start.1
  2.3 0.8 copy-done.1
  3.1 0.0 copy-start.2
  3.1 0.8 copy-done.2
  4.0 0.0 copy-start.3
  4.0 0.8 copy-done.3
  4.8 0.0 copy-start.4
  4.8 0.8 copy-done.4
  5.7 0.0 copy-start.5
  5.7 0.8 copy-done.5
  6.5 0.0 copy-start.6
  6.5 0.0 copy-start.7
  6.5 1.4 %shard_map.103 = (f32[8,40,256]{2,1,0:T(8,128)S(1)}, f32[672,256]{1,0:T(8,128)S(1)}, f32[552,256]{1,0:T(8,128)S(1)}, f32[552,256]{1,0:T(8,128)S(1)}) custom-call(s32[2]{0:T(128)S(1)} %pad_add_fusion.meta, f32[2048,256]{1,0:T(8,128)S(1)} %bitcast.4, f32[8,2048]{1,0:T(8,128)S(1)} %copy-done.1, f32[8,2048]{1,0:T(8,128)S(1)} %copy-done.2, ...), custom_call_target="tpu_custom_call" | custom-call | flops 1048576 | bytes 4194304 | tf_op jit(solution)/shard_map/pallas_call | solution.py:295
  7.9 1.3 %collective-permute-start = (f32[672,256]{1,0:T(8,128)S(1)}, f32[672,256]{1,0:T(8,128)S(1)}, u32[]{:S(2)}, u32[]{:S(2)}) collective-permute-start(f32[672,256]{1,0:T(8,128)S(1)} %get-tuple-element.22), channel_id=1, source_target_pairs={{0,1},{1,0},{2,3},{3,2},{4,5},{5,4},{6,7},{7,6},{8,9},{9,8},{10,11... | collective-permute-start | bytes 2064392 | tf_op jit(solution)/shard_map/ppermute | solution.py:299
  9.2 0.8 collective-permute-start.1
  10.0 1.9 %collective-permute-start.2 = (f32[552,256]{1,0:T(8,128)S(1)}, f32[552,256]{1,0:T(8,128)S(1)}, u32[]{:S(2)}, u32[]{:S(2)}) collective-permute-start(f32[552,256]{1,0:T(8,128)S(1)} %get-tuple-element.25), channel_id=1, source_target_pairs={{0,2},{1,1},{2,4},{3,3},{4,6},{5,5},{6,8},{7,7},{8,10},{9,9},{10,1... | collective-permute-start | bytes 1695752 | tf_op jit(solution)/shard_map/ppermute | solution.py:301
  11.9 14.4 %collective-permute-done.swap = f32[672,256]{1,0:T(8,128)S(1)} collective-permute-done((f32[672,256]{1,0:T(8,128)S(1)}, f32[672,256]{1,0:T(8,128)S(1)}, u32[]{:S(2)}, u32[]{:S(2)}) %collective-permute-start) | collective-permute-done | bytes 688160 | tf_op jit(solution)/shard_map/ppermute | solution.py:299
  26.3 0.0 copy-done.6
  26.3 0.0 copy-done.7
  26.3 18.2 %shard_map.104 = (f32[2,256,256]{2,1,0:T(8,128)S(1)}, f32[2,40,256]{2,1,0:T(8,128)S(1)}, f32[1,272,256]{2,1,0:T(8,128)S(1)}, f32[1,272,256]{2,1,0:T(8,128)S(1)}) custom-call(s32[2]{0:T(128)S(1)} %pad_add_fusion.meta, f32[2048,256]{1,0:T(8,128)S(1)} %bitcast.5, f32[8,40,256]{2,1,0:T(8,128)S(1)} %get-tuple-element.21.parts, ...), custom_call_target="tpu_custom_call" | custom-call | flops 6442450944 | bytes 4194304 | tf_op jit(solution)/shard_map/pallas_call | solution.py:303
  44.5 0.0 collective-permute-done.1.chain
  44.5 4.7 %collective-permute-done.2.ahead = f32[552,256]{1,0:T(8,128)S(1)} collective-permute-done((f32[552,256]{1,0:T(8,128)S(1)}, f32[552,256]{1,0:T(8,128)S(1)}, u32[]{:S(2)}, u32[]{:S(2)}) %collective-permute-start.2) | collective-permute-done | bytes 565280 | tf_op jit(solution)/shard_map/ppermute | solution.py:301
  49.2 13.5 %shard_map.105 = (f32[2,2,256,256]{3,2,1,0:T(8,128)S(1)}, f32[2,40,256]{2,1,0:T(8,128)S(1)}, f32[2,16,256]{2,1,0:T(8,128)S(1)}) custom-call(s32[2]{0:T(128)S(1)} %pad_add_fusion.meta, f32[8,40,256]{2,1,0:T(8,128)S(1)} %get-tuple-element.21.parts, f32[672,256]{1,0:T(8,128)S(1)} %collective-permute-done.swap, f32[552,256]{1,0:T(8,128)S(1)} %collective-permute-done.1.chain, ...), custom_call_target="tpu_custom_call" | custom-call | flops 4294967296 | bytes 4194304 | tf_op jit(solution)/shard_map/pallas_call | solution.py:308
  62.7 13.5 %shard_map.106 = (f32[2,272,256]{2,1,0:T(8,128)S(1)}, f32[2,272,256]{2,1,0:T(8,128)S(1)}) custom-call(s32[2]{0:T(128)S(1)} %pad_add_fusion.meta, f32[2,2,256,256]{3,2,1,0:T(8,128)S(1)} %get-tuple-element.26.d_ref, f32[2,40,256]{2,1,0:T(8,128)S(1)} %get-tuple-element.27.q0, f32[2,40,256]{2,1,0:T(8,128)S(1)} %get-tuple-element.28.q1, ...), custom_call_target="tpu_custom_call" | custom-call | flops 4294967296 | bytes 4194304 | tf_op jit(solution)/shard_map/pallas_call | solution.py:313
  76.2 0.1 collective-permute-start.5
  76.3 0.1 collective-permute-start.3
  76.4 2.0 %collective-permute-start.4 = (f32[1,272,256]{2,1,0:T(8,128)S(1)}, f32[1,272,256]{2,1,0:T(8,128)S(1)}, u32[]{:S(2)}, u32[]{:S(2)}) collective-permute-start(f32[1,272,256]{2,1,0:T(8,128)S(1)} %get-tuple-element.33), channel_id=1, source_target_pairs={{0,1},{1,0},{2,3},{3,2},{4,5},{5,4},{6,7},{7,6},{8,9},{9,8},{10,11... | collective-permute-start | bytes 835592 | tf_op jit(solution)/shard_map/ppermute | solution.py:307
  78.4 10.7 %collective-permute-done.3.pushed = f32[2,16,256]{2,1,0:T(8,128)S(1)} collective-permute-done((f32[2,16,256]{2,1,0:T(8,128)S(1)}, f32[2,16,256]{2,1,0:T(8,128)S(1)}, u32[]{:S(2)}, u32[]{:S(2)}) %collective-permute-start.3) | collective-permute-done | bytes 32800 | tf_op jit(solution)/shard_map/ppermute | solution.py:312
  89.2 6.3 %shard_map.107 = (f32[1,272,256]{2,1,0:T(8,128)S(1)}, f32[1,272,256]{2,1,0:T(8,128)S(1)}) custom-call(s32[2]{0:T(128)S(1)} %pad_add_fusion.meta, f32[2,256,256]{2,1,0:T(8,128)S(1)} %get-tuple-element.30.d_ref, f32[8,40,256]{2,1,0:T(8,128)S(1)} %get-tuple-element.21.parts, f32[672,256]{1,0:T(8,128)S(1)} %collective-permute-done.swap, ...), custom_call_target="tpu_custom_call" | custom-call | flops 2147483648 | bytes 4194304 | tf_op jit(solution)/shard_map/pallas_call | solution.py:318
  95.5 0.1 collective-permute-start.6
  95.6 0.0 collective-permute-done.4.refs_3_
  95.6 7.3 %collective-permute-done.6.refs_5_ = f32[1,272,256]{2,1,0:T(8,128)S(1)} collective-permute-done((f32[1,272,256]{2,1,0:T(8,128)S(1)}, f32[1,272,256]{2,1,0:T(8,128)S(1)}, u32[]{:S(2)}, u32[]{:S(2)}) %collective-permute-start.6) | collective-permute-done | bytes 278560 | tf_op jit(solution)/shard_map/ppermute | solution.py:322
  102.8 0.0 collective-permute-done.5.refs_4_
  102.8 2.7 %shard_map.108 = (f32[2048,256]{1,0:T(8,128)}, f32[8,2048]{1,0:T(8,128)}, f32[8,2048]{1,0:T(8,128)}) custom-call(s32[2]{0:T(128)S(1)} %pad_add_fusion.meta, f32[1,272,256]{2,1,0:T(8,128)S(1)} %get-tuple-element.23.refs_0_, f32[2,272,256]{2,1,0:T(8,128)S(1)} %get-tuple-element.29.refs_1_, f32[1,272,256]{2,1,0:T(8,128)S(1)} %get-tuple-element.32.refs_2_, ...), custom_call_target="tpu_custom_call" | custom-call | flops 1048576 | bytes 4194304 | tf_op jit(solution)/shard_map/pallas_call | solution.py:323
Async XLA Ops:
  0.7 1.6 %copy-start = (f32[8,2,128,256]{3,2,1,0:T(8,128)S(1)}, f32[8,2,128,256]{3,2,1,0:T(8,128)}, u32[]{:S(2)}) copy-start(f32[8,2,128,256]{3,2,1,0:T(8,128)} %param.8) | copy-start | bytes 6291460
  2.3 0.8 copy-start.1
  3.1 0.8 copy-start.2
  4.0 0.8 copy-start.3
  4.8 0.8 copy-start.4
  5.7 0.8 copy-start.5
  6.5 19.8 %copy-start.6 = (bf16[2,512,512]{2,1,0:T(8,128)(2,1)S(1)}, bf16[2,512,512]{2,1,0:T(8,128)(2,1)}, u32[]{:S(2)}) copy-start(bf16[2,512,512]{2,1,0:T(8,128)(2,1)} %constant.17.clone.tab_l) | copy-start | bytes 3145732
  6.5 19.8 %copy-start.7 = (bf16[2,512,512]{2,1,0:T(8,128)(2,1)S(1)}, bf16[2,512,512]{2,1,0:T(8,128)(2,1)}, u32[]{:S(2)}) copy-start(bf16[2,512,512]{2,1,0:T(8,128)(2,1)} %constant.16.clone.tab_r) | copy-start | bytes 3145732
  7.9 18.4 %collective-permute-start = (f32[672,256]{1,0:T(8,128)S(1)}, f32[672,256]{1,0:T(8,128)S(1)}, u32[]{:S(2)}, u32[]{:S(2)}) collective-permute-start(f32[672,256]{1,0:T(8,128)S(1)} %get-tuple-element.22), channel_id=1, source_target_pairs={{0,1},{1,0},{2,3},{3,2},{4,5},{5,4},{6,7},{7,6},{8,9},{9,8},{10,11... | collective-permute-start | bytes 2064392 | tf_op jit(solution)/shard_map/ppermute | solution.py:299
  9.2 35.3 %collective-permute-start.1 = (f32[552,256]{1,0:T(8,128)S(1)}, f32[552,256]{1,0:T(8,128)S(1)}, u32[]{:S(2)}, u32[]{:S(2)}) collective-permute-start(f32[552,256]{1,0:T(8,128)S(1)} %get-tuple-element.24), channel_id=1, source_target_pairs={{0,1},{1,2},{2,3},{3,4},{4,5},{5,6},{6,7},{7,8},{8,9},{9,10},{10,1... | collective-permute-start | bytes 1695752 | tf_op jit(solution)/shard_map/ppermute | solution.py:300
  10.0 39.2 %collective-permute-start.2 = (f32[552,256]{1,0:T(8,128)S(1)}, f32[552,256]{1,0:T(8,128)S(1)}, u32[]{:S(2)}, u32[]{:S(2)}) collective-permute-start(f32[552,256]{1,0:T(8,128)S(1)} %get-tuple-element.25), channel_id=1, source_target_pairs={{0,2},{1,1},{2,4},{3,3},{4,6},{5,5},{6,8},{7,7},{8,10},{9,9},{10,1... | collective-permute-start | bytes 1695752 | tf_op jit(solution)/shard_map/ppermute | solution.py:301
  76.2 26.6 %collective-permute-start.5 = (f32[2,272,256]{2,1,0:T(8,128)S(1)}, f32[2,272,256]{2,1,0:T(8,128)S(1)}, u32[]{:S(2)}, u32[]{:S(2)}) collective-permute-start(f32[2,272,256]{2,1,0:T(8,128)S(1)} %get-tuple-element.34), channel_id=1, source_target_pairs={{0,1},{1,0},{2,3},{3,2},{4,5},{5,4},{6,7},{7,6},{8,9},{9,8},{10,11... | collective-permute-start | bytes 1671176 | tf_op jit(solution)/shard_map/ppermute | solution.py:317
  76.3 12.9 %collective-permute-start.3 = (f32[2,16,256]{2,1,0:T(8,128)S(1)}, f32[2,16,256]{2,1,0:T(8,128)S(1)}, u32[]{:S(2)}, u32[]{:S(2)}) collective-permute-start(f32[2,16,256]{2,1,0:T(8,128)S(1)} %get-tuple-element.31), channel_id=1, source_target_pairs={{1,0},{2,1},{3,2},{4,3},{5,4},{6,5},{7,6},{8,7},{9,8},{10,9},{11,1... | collective-permute-start | bytes 98312 | tf_op jit(solution)/shard_map/ppermute | solution.py:312
  76.4 19.2 %collective-permute-start.4 = (f32[1,272,256]{2,1,0:T(8,128)S(1)}, f32[1,272,256]{2,1,0:T(8,128)S(1)}, u32[]{:S(2)}, u32[]{:S(2)}) collective-permute-start(f32[1,272,256]{2,1,0:T(8,128)S(1)} %get-tuple-element.33), channel_id=1, source_target_pairs={{0,1},{1,0},{2,3},{3,2},{4,5},{5,4},{6,7},{7,6},{8,9},{9,8},{10,11... | collective-permute-start | bytes 835592 | tf_op jit(solution)/shard_map/ppermute | solution.py:307
  95.5 7.4 %collective-permute-start.6 = (f32[1,272,256]{2,1,0:T(8,128)S(1)}, f32[1,272,256]{2,1,0:T(8,128)S(1)}, u32[]{:S(2)}, u32[]{:S(2)}) collective-permute-start(f32[1,272,256]{2,1,0:T(8,128)S(1)} %get-tuple-element.35), channel_id=1, source_target_pairs={{0,1},{1,0},{2,3},{3,2},{4,5},{5,4},{6,7},{7,6},{8,9},{9,8},{10,11... | collective-permute-start | bytes 835592 | tf_op jit(solution)/shard_map/ppermute | solution.py:322

commit v2 on v1

v2 whole, which is shorter than its diff:
```python
import math

import jax
import jax.numpy as jnp
import ml_dtypes
import numpy as np
from jax import lax
from jax.experimental import pallas as pl
from jax.experimental.pallas import tpu as pltpu

BF = jnp.bfloat16
F32 = jnp.float32
F8 = jnp.float8_e5m2
UP = 1024.0
DOWN = 1.0 / UP
N = 256
HALF = 128
PART = 2048
ROWS = PART // N
WIN = 144
FIELDS = 5 * ROWS
PUSHED = 2 * ROWS
PIECE = 2 * HALF + PUSHED


def split_np(m):
    hi = m.astype(ml_dtypes.bfloat16)
    return hi, (m - hi.astype(np.float64)).astype(ml_dtypes.bfloat16)


def tables():
    k = np.arange(N)
    m = np.where(k < N // 2, k, k - N).astype(np.float64)
    h = np.exp(-1j * np.pi / N * m * m)
    dft = np.exp(-2j * np.pi / N * (k[:, None] * k[None, :] % N))
    a = (np.conj(dft) / N) @ (h[:, None] * dft)
    c0, c1 = a[:HALF, :HALF], a[:HALF, HALF:]
    both = [0.5 * (c0 + c1), 0.5 * (c0 - c1)]
    right = np.stack([np.block([[b.real, b.imag], [-b.imag, b.real]]) for b in both])
    left = np.stack([np.block([[b.real, -b.imag], [b.imag, b.real]]) for b in both])
    return np.stack(split_np(right)), np.stack(split_np(left))


def sincos(x):
    n = jnp.round(x * (1.0 / math.pi))
    r = x - n * 3.140625
    r = r - n * 9.670257568359375e-4
    r = r - n * 6.277114152908325e-07
    half = n * 0.5
    sign = 1.0 - 4.0 * (half - jnp.floor(half))
    y = r * r
    s = -2.3889859e-08
    for c in (2.7525562e-06, -1.98408740e-04, 8.33333310e-03, -1.66666667e-01):
        s = s * y + c
    s = r + r * y * s
    c = 2.08767570e-09 - 1.1470746e-11 * y
    for d in (-2.75573192e-07, 2.48015873e-05, -1.38888889e-03, 4.16666667e-02, -0.5, 1.0):
        c = c * y + d
    return s * sign, c * sign


def hilo(x):
    hi = x.astype(BF)
    return hi, (x - hi.astype(F32)).astype(BF)


def mm(a, b):
    return jnp.dot(a, b, preferred_element_type=F32)


def step(f_ref, p_ref, tab_r, tab_l, out_ref, c_ref, w_ref, s_ref, sr_ref, x_ref, samp_ref, c8_ref, sr8_ref):
    iota_c = (lax.broadcasted_iota(jnp.int32, (16, 16, N), 0) * 16
              + lax.broadcasted_iota(jnp.int32, (16, 16, N), 1)).astype(F32).astype(BF)
    one = jnp.ones((16, N), BF)
    zero = jnp.zeros((16, N), BF)
    down = jnp.full((16, N), DOWN, BF)
    iota_r = lax.broadcasted_iota(jnp.int32, (WIN, N), 0).astype(F32)
    for h in range(2):
        off = p_ref[h, 2 * ROWS:3 * ROWS]
        lower = 0.5 - off
        upper = 0.5 + off
        w_ref[0] = 0.5 * lower * lower
        w_ref[1] = 0.75 - off * off
        w_ref[2] = 0.5 * upper * upper
        win0 = 0 if h == 0 else N - WIN
        field = f_ref[:, win0:win0 + WIN, :].reshape(2 * WIN, N)
        hi = field.astype(BF)
        lo = ((field - hi.astype(F32)) * UP).astype(F8)
        for k in range(ROWS):
            col = jnp.broadcast_to(p_ref[h, 4 * ROWS + k:4 * ROWS + k + 1, :], (16, N)).astype(BF)
            hot = jnp.where(iota_c == col[None], one[None], zero[None]).reshape(N, N)
            c_ref[h, :, N * k:N * k + N] = hot
            hot8 = jnp.where(iota_c == col[None], down[None], zero[None]).reshape(N, N).astype(F8)
            c8_ref[h, :, N * k:N * k + N] = hot8
            g = mm(hi, hot) + mm(lo, hot8)
            at = p_ref[h, 3 * ROWS + k:3 * ROWS + k + 1, :] - float(win0)
            w = jnp.where(iota_r == at, w_ref[1, k:k + 1, :],
                          jnp.where(iota_r == at - 1.0, w_ref[0, k:k + 1, :],
                                    jnp.where(iota_r == at + 1.0, w_ref[2, k:k + 1, :], 0.0)))
            samp_ref[0, k:k + 1, :] = jnp.sum(w * g[:WIN], 0, keepdims=True)
            samp_ref[1, k:k + 1, :] = jnp.sum(w * g[WIN:], 0, keepdims=True)
        phase = p_ref[h, :ROWS]
        sine, cosine = sincos(phase)
        energy = p_ref[h, ROWS:2 * ROWS] - 0.5 * (samp_ref[0] * cosine - samp_ref[1] * sine)
        phase = phase + energy
        p_ref[h, :ROWS] = phase
        p_ref[h, ROWS:2 * ROWS] = energy
        sine, cosine = sincos(phase)
        for z, v in ((0, cosine), (1, -sine)):
            vh = v.astype(BF).astype(F32)
            s_ref[2 * z] = vh
            s_ref[2 * z + 1] = v - vh
        for k in range(ROWS):
            at = jnp.broadcast_to(p_ref[h, 3 * ROWS + k:3 * ROWS + k + 1, :] - float(HALF * h), (16, N)).astype(BF)
            here = iota_c[:8] == at[None]
            for z in range(2):
                value = jnp.broadcast_to(s_ref[2 * z, k:k + 1, :], (16, N)).astype(BF)
                sr_ref[HALF * z:HALF * z + HALF, N * k:N * k + N] = jnp.where(here, value[None], zero[None]).reshape(HALF, N)
                value = jnp.broadcast_to(s_ref[2 * z + 1, k:k + 1, :] * UP, (16, N)).astype(BF)
                sr8_ref[HALF * z:HALF * z + HALF, N * k:N * k + N] = jnp.where(here, value[None], zero[None]).reshape(HALF, N).astype(F8)
        d = lax.dot_general(sr_ref[...], c_ref[h], (((1,), (1,)), ((), ())), preferred_element_type=F32)
        d = d + lax.dot_general(sr8_ref[...], c8_ref[h], (((1,), (1,)), ((), ())), preferred_element_type=F32)
        for z in range(2):
            x_ref[HALF * h:HALF * h + HALF, N * z:N * z + N] = (
                f_ref[z, HALF * h:HALF * h + HALF, :]
                + d[HALF * z:HALF * z + HALF])
    quads = [[], []]
    for z in range(2):
        top = x_ref[:HALF, N * z:N * z + N]
        low = x_ref[HALF:, N * z:N * z + N]
        rows = jnp.concatenate([top + low, top - low], 0)
        quads[0].append(rows[:, :HALF] + rows[:, HALF:])
        quads[1].append(rows[:, :HALF] - rows[:, HALF:])
    turned = []
    for e in range(2):
        xh, xl = hilo(jnp.concatenate(quads[e], 1))
        turned.append(mm(xh, tab_r[0, e]) + mm(xl, tab_r[0, e]) + mm(xh, tab_r[1, e]))
    halves = []
    for e in range(2):
        rows = slice(HALF * e, HALF * e + HALF)
        y = jnp.concatenate([jnp.concatenate([turned[0][rows, :HALF], turned[1][rows, :HALF]], 1),
                             jnp.concatenate([turned[0][rows, HALF:], turned[1][rows, HALF:]], 1)], 0)
        yh, yl = hilo(y)
        halves.append(mm(tab_l[0, e], yh) + mm(tab_l[0, e], yl) + mm(tab_l[1, e], yh))
    for e, rows in enumerate((halves[0] + halves[1], halves[0] - halves[1])):
        left, right = rows[:, :HALF], rows[:, HALF:]
        out = jnp.concatenate([left + right, left - right], 1)
        out_ref[0, HALF * e:HALF * e + HALF] = out[:HALF]
        out_ref[1, HALF * e:HALF * e + HALF] = out[HALF:]


WORK = [pltpu.VMEM((2, N, PART), BF), pltpu.VMEM((3, ROWS, N), F32), pltpu.VMEM((4, ROWS, N), F32),
        pltpu.VMEM((N, PART), BF), pltpu.VMEM((N, 2 * N), F32), pltpu.VMEM((2, ROWS, N), F32),
        pltpu.VMEM((2, N, PART), F8), pltpu.VMEM((N, PART), F8)]
FIELD = pltpu.VMEM((2, N, N), F32)
PARTS = pltpu.VMEM((2, FIELDS, N), F32)
TABLE = pltpu.VMEM((2, 2, N, N), BF)
ANY = pl.BlockSpec(memory_space=pl.ANY)
VM = pl.BlockSpec(memory_space=pltpu.VMEM)
SM = pl.BlockSpec(memory_space=pltpu.SMEM)
HB = pl.BlockSpec(memory_space=pltpu.HBM)


class Copies:
    def __init__(self, sems):
        self.sems = sems
        self.used = 0
        self.open = []

    def start(self, src, dst):
        copy = pltpu.make_async_copy(src, dst, self.sems.at[self.used])
        self.used += 1
        copy.start()
        self.open.append(copy)

    def wait(self):
        for copy in self.open:
            copy.wait()
        self.open = []


def call(kernel, outs, out_specs, scratch, copies, in_specs, flops, aliases={}, vmem=40960):
    return pl.pallas_call(
        kernel, out_shape=[jax.ShapeDtypeStruct(s, F32) for s in outs], in_specs=in_specs, out_specs=out_specs,
        scratch_shapes=scratch + [pltpu.SemaphoreType.DMA((copies,))],
        input_output_aliases=aliases, cost_estimate=pl.CostEstimate(flops=flops, bytes_accessed=4 << 20, transcendentals=0),
        compiler_params=pltpu.CompilerParams(vmem_limit_bytes=vmem << 10))


def pack_kernel(meta, wave, *refs):
    sources, (all_ref, swap_ref, chain_ref, ahead_ref), rest = refs[:5], refs[5:9], refs[9:]
    floats, ints, packed, sems = rest
    r = meta[0]
    rows = 2 * N
    loads, copies = Copies(sems), Copies(sems)
    copies.used = 5
    for a, src in enumerate(sources):
        loads.start(src, floats.at[a] if a < 3 else ints.at[a - 3])
    copies.start(wave.at[pl.ds(N * (4 - 4 * r), rows)], swap_ref.at[pl.ds(0, rows)])
    copies.start(wave.at[pl.ds(N * (2 + 4 * r), rows)], chain_ref.at[pl.ds(0, rows)])
    copies.start(wave.at[pl.ds(N * (6 - 4 * r), rows)], ahead_ref.at[pl.ds(0, rows)])
    loads.wait()
    for a in range(5):
        src = floats.at[a] if a < 3 else ints.at[a - 3]
        for s in range(8):
            for k in range(ROWS):
                packed[s, a * ROWS + k:a * ROWS + k + 1, :] = src[s:s + 1, N * k:N * k + N].astype(F32)
    copies.start(packed, all_ref)
    for i in range(4):
        copies.start(packed.at[4 - 4 * r + i], swap_ref.at[pl.ds(rows + FIELDS * i, FIELDS)])
    copies.start(packed.at[3 + 4 * r], chain_ref.at[pl.ds(rows, FIELDS)])
    copies.start(packed.at[7 - 4 * r], ahead_ref.at[pl.ds(rows, FIELDS)])
    copies.wait()


def field_in(copies, r, f_ref, own, own_row, other, other_row):
    for z in range(2):
        copies.start(own.at[pl.ds(own_row + HALF * z, HALF)], f_ref.at[z, pl.ds(pl.multiple_of(HALF * r, HALF), HALF)])
        copies.start(other.at[pl.ds(other_row + HALF * z, HALF)],
                     f_ref.at[z, pl.ds(pl.multiple_of(HALF - HALF * r, HALF), HALF)])


def piece_out(copies, r, z_ref, p_ref, own, away, i):
    for half, dst in ((r, own), (1 - r, away)):
        for z in range(2):
            copies.start(z_ref.at[z, pl.ds(pl.multiple_of(HALF * half, HALF), HALF)], dst.at[i, pl.ds(HALF * z, HALF)])
        copies.start(p_ref.at[half, pl.ds(0, PUSHED)], dst.at[i, pl.ds(2 * HALF, PUSHED)])


def first_kernel(meta, wave, parts, swap, tab_r, tab_l, d_ref, q_ref, own, away, f2, f3, p1, p2, z, z3, tr, tl, *rest):
    work, sems = rest[:-1], rest[-1]
    r = meta[0]
    copies = Copies(sems)
    field_in(copies, r, f3, wave, N * (4 * r + 1), swap, N)
    for p, i in ((p2, 2), (p1, 1)):
        copies.start(parts.at[4 * r + i], p.at[r])
        copies.start(swap.at[pl.ds(2 * N + FIELDS * i, FIELDS)], p.at[1 - r])
    copies.start(tab_r, tr)
    copies.start(tab_l, tl)
    field_in(copies, r, f2, wave, N * 4 * r, swap, 0)
    copies.wait()
    step(f3, p2, tr, tl, z3, *work)
    copies.start(z3, d_ref)
    step(f2, p1, tr, tl, f3, *work)
    copies.start(p1, q_ref)
    step(f3, p2, tr, tl, z, *work)
    piece_out(copies, r, z, p2, own, away, 0)
    copies.wait()


def second_kernel(meta, after, parts, swap, chain, ahead, tab_r, tab_l, d_ref, q_ref, pushed,
                  f0, f1, p0, pm, z0, z1, tr, tl, *rest):
    work, sems = rest[:-1], rest[-1]
    r = meta[0]
    copies = Copies(sems)
    field_in(copies, r, f0, ahead, 0, chain, 0)
    copies.start(ahead.at[pl.ds(2 * N, FIELDS)], pm.at[r])
    copies.start(chain.at[pl.ds(2 * N, FIELDS)], pm.at[1 - r])
    copies.start(tab_r, tr)
    copies.start(tab_l, tl)
    field_in(copies, r, f1, ahead, N, chain, N)
    copies.start(parts.at[4 * r], p0.at[r])
    copies.start(swap.at[pl.ds(2 * N, FIELDS)], p0.at[1 - r])
    copies.wait()

    @pl.when(meta[1] == 1)
    def _():
        f1[...] = jnp.zeros_like(f1)

    step(f0, pm, tr, tl, z0, *work)
    copies.start(pm.at[:, pl.ds(0, PUSHED)], pushed)
    copies.start(z0, d_ref.at[0])
    step(f1, p0, tr, tl, z1, *work)
    copies.start(p0, q_ref)
    copies.start(z1, d_ref.at[1])
    copies.wait()


def own_out(copies, r, z_ref, wave, slot):
    for z in range(2):
        copies.start(z_ref.at[z, pl.ds(pl.multiple_of(HALF * r, HALF), HALF)],
                     wave.at[pl.ds((4 * r + slot) * N + HALF * z, HALF)])


def third_kernel(meta, d_ref, q0, q1, own_a, back_a, tab_r, tab_l, own, away, wave,
                 f0, f1, p0, p1, z0, z1, tr, tl, *rest):
    work, sems = rest[:-1], rest[-1]
    r = meta[0]
    copies, moves = Copies(sems), Copies(sems)
    moves.used = 24
    copies.start(d_ref.at[0], f0)
    copies.start(q0, p0)
    copies.start(tab_r, tr)
    copies.start(tab_l, tl)
    copies.start(d_ref.at[1], f1)
    copies.start(q1, p1)
    copies.wait()
    for ref, slot in ((own_a, 4 * r + 2), (back_a, 6 - 4 * r)):
        moves.start(ref.at[0, pl.ds(0, N)], wave.at[pl.ds(slot * N, N)])

    @pl.when(meta[1] == 1)
    def _():
        f0[...] = jnp.zeros_like(f0)

    step(f0, p0, tr, tl, z0, *work)
    piece_out(copies, r, z0, p0, own, away, 0)
    own_out(moves, r, z0, wave, 0)
    step(f1, p1, tr, tl, z1, *work)
    piece_out(copies, r, z1, p1, own, away, 1)
    own_out(moves, r, z1, wave, 1)
    copies.wait()
    moves.wait()


def fourth_kernel(meta, d_ref, parts, swap, pushed, tab_r, tab_l, wave_in, own, away, wave, f3, p3, z, tr, tl, *rest):
    work, sems = rest[:-1], rest[-1]
    r = meta[0]
    copies = Copies(sems)
    copies.start(parts.at[4 * r + 3], p3.at[r])
    copies.start(swap.at[pl.ds(2 * N + FIELDS * 3, FIELDS)], p3.at[1 - r])
    copies.start(d_ref, f3)
    copies.start(tab_r, tr)
    copies.start(tab_l, tl)
    copies.wait()
    copies.start(pushed, p3.at[:, pl.ds(0, PUSHED)])
    copies.wait()
    step(f3, p3, tr, tl, z, *work)
    piece_out(copies, r, z, p3, own, away, 0)
    own_out(copies, r, z, wave, 3)
    copies.wait()


def final_kernel(meta, *refs):
    pieces, (wave, phase, energy), (packed, sems) = refs[:6], refs[7:10], refs[10:]
    r = meta[0]
    moves, copies = Copies(sems), Copies(sems)
    copies.used = 4
    for half in range(2):
        base = 4 * r if half == 0 else 4 - 4 * r
        for n, (ref, slots) in enumerate(zip(pieces[3 * half:3 * half + 3], ((2,), (0, 1), (3,)))):
            for i, slot in enumerate(slots):
                if half == 1 and n > 0:
                    moves.start(ref.at[i, pl.ds(0, N)], wave.at[pl.ds((base + slot) * N, N)])
                copies.start(ref.at[i, pl.ds(N, PUSHED)], packed.at[base + slot])
    copies.wait()
    for s in range(8):
        for k in range(ROWS):
            phase[s:s + 1, N * k:N * k + N] = packed[s, k:k + 1, :]
            energy[s:s + 1, N * k:N * k + N] = packed[s, ROWS + k:ROWS + k + 1, :]
    moves.wait()


def body(wavefront, particle_phase, particle_energy, row_offset, row_cell, col_cell):
    tab_r, tab_l = (jnp.asarray(a) for a in tables())
    r = lax.axis_index("row")
    nt = lax.axis_size("tm")
    both = ("tm", "row")
    swap = [(i, i ^ 1) for i in range(2 * nt)]
    chain = [(i, (i + 1) % (2 * nt)) for i in range(2 * nt)]
    ahead = [(i, (i + 2) % (2 * nt) if i % 2 == 0 else i) for i in range(2 * nt)]
    back = [(j, i) for i, j in chain]
    meta = jnp.stack([r, (lax.axis_index(both) == 0).astype(jnp.int32)]).astype(jnp.int32)
    wave = wavefront.reshape(8 * N, N)
    unit = 1 << 33

    parts, to_swap, to_chain, to_ahead = call(
        pack_kernel, [(8, FIELDS, N), (2 * N + 4 * FIELDS, N), (2 * N + FIELDS, N), (2 * N + FIELDS, N)],
        [ANY] * 4, [pltpu.VMEM((3, 8, PART), F32), pltpu.VMEM((2, 8, PART), jnp.int32), pltpu.VMEM((8, FIELDS, N), F32)],
        16, [SM] + [HB] * 6, 1 << 20, vmem=60 << 10,
    )(meta, wave, particle_phase, particle_energy, row_offset, row_cell, col_cell)
    f_swap = lax.ppermute(to_swap, both, swap)
    f_chain = lax.ppermute(to_chain, both, chain)
    f_ahead = lax.ppermute(to_ahead, both, ahead)

    d3, q1, own_a, away_a = call(
        first_kernel, [(2, N, N), (2, FIELDS, N), (1, PIECE, N), (1, PIECE, N)], [ANY] * 4,
        [FIELD, FIELD, PARTS, PARTS, FIELD, FIELD, TABLE, TABLE] + WORK, 32, [SM] + [ANY] * 5, 3 * unit,
    )(meta, wave, parts, f_swap, tab_r, tab_l)
    back_a = lax.ppermute(away_a, both, swap)
    d01, q0, pushed = call(
        second_kernel, [(2, 2, N, N), (2, FIELDS, N), (2, PUSHED, N)], [ANY] * 3,
        [FIELD, FIELD, PARTS, PARTS, FIELD, FIELD, TABLE, TABLE] + WORK, 32, [SM] + [ANY] * 7, 2 * unit,
    )(meta, q1, parts, f_swap, f_chain, f_ahead, tab_r, tab_l)
    pushed = lax.ppermute(pushed, both, back)
    own_b, away_b, wave = call(
        third_kernel, [(2, PIECE, N), (2, PIECE, N), (8 * N, N)], [ANY] * 3,
        [FIELD, FIELD, PARTS, PARTS, FIELD, FIELD, TABLE, TABLE] + WORK, 32, [SM] + [ANY] * 7, 2 * unit,
    )(meta, d01, q0, q1, own_a, back_a, tab_r, tab_l)
    back_b = lax.ppermute(away_b, both, swap)
    own_c, away_c, wave = call(
        fourth_kernel, [(1, PIECE, N), (1, PIECE, N), (8 * N, N)], [ANY] * 3,
        [FIELD, PARTS, FIELD, TABLE, TABLE] + WORK, 32, [SM] + [ANY] * 7, 2 * unit, {7: 2},
    )(meta, d3, parts, f_swap, pushed, tab_r, tab_l, wave)
    back_c = lax.ppermute(away_c, both, swap)
    wave, phase, energy = call(
        final_kernel, [(8 * N, N), (8, PART), (8, PART)], [HB, VM, VM],
        [pltpu.VMEM((8, PUSHED, N), F32)], 16, [SM] + [ANY] * 6 + [HB], 1 << 20, {7: 0},
    )(meta, own_a, own_b, own_c, back_a, back_b, back_c, wave)
    return wave.reshape(8, 2, HALF, N), phase, energy


def solution(mesh):
    P = jax.sharding.PartitionSpec
    wide, flat = P("tm", None, "row", None), P("tm", "row")
    return jax.shard_map(body, mesh=mesh, in_specs=(wide,) + (flat,) * 5,
                         out_specs=(wide, flat, flat), check_vma=False)
```

time: 108 us -> 134 us (1.24); the launches traced: 106 us -> 134 us
  Pallas kernels: 55.5 us -> 93.7 us
  waiting for transfers between devices: 37.1 us -> 27.7 us
  local copies, waits for them, and re-layouts: 5.79 us -> 3.08 us
    pallas_call x1, Pallas kernels: 1.36 us -> 49.7 us  [body(): call(pack_kernel, [(8, FIELDS, N), (2 * N + 4 * FIELDS, N), (2 * N + FIEL...]
    ppermute x1, waiting for transfers between devices: 10.7 us -> 0.01 us  [body(): pushed = lax.ppermute(pushed, both, back)]
    pallas_call x4, Pallas kernels: 36 us -> 29.6 us  [the longest x1 10.9 us: body(): call(third_kernel, [(2, PIECE, N), (2, PIECE, N), (8 * N, N)], [ANY] * 3,...]
    pallas_call x1, Pallas kernels: 18.2 us -> 14.4 us  [body(): call(first_kernel, [(2, N, N), (2, FIELDS, N), (1, PIECE, N), (1, PIECE,...]
    unnamed x16, local copies, waits for them, and re-layouts: 5.79 us -> 3.08 us
    ppermute x1, starting transfers between devices: 0.09 us -> 2.07 us  [body(): back_b = lax.ppermute(away_b, both, swap)]
    ppermute x1, waiting for transfers between devices: 7.26 us -> 9 us  [body(): back_c = lax.ppermute(away_c, both, swap)]
  transfers between devices with their start and end apart: 7 -> 7, of which waited for: 4 -> 3; matrix products, arithmetic and copies ran while one was open for 0% -> 0% of each run, Pallas kernels for 23% -> 31%
where the time goes in v2:
time: 134 us
  Pallas kernels  93.7 us (70%)
  waiting for transfers between devices  27.7 us (21%)
  starting transfers between devices  7.61 us (6%)
  local copies, waits for them, and re-layouts  3.08 us (2%)
    pallas_call x1, Pallas kernels, body(): call(pack_kernel, [(8, FIELDS, N), (2 * N + 4 * FIELDS, N), (2 * N + FIEL...  49.7 us
    ppermute x1, waiting for transfers between devices, body(): f_swap = lax.ppermute(to_swap, both, swap)  14.6 us
    pallas_call x1, Pallas kernels, body(): call(first_kernel, [(2, N, N), (2, FIELDS, N), (1, PIECE, N), (1, PIECE,...  14.4 us
    pallas_call x1, Pallas kernels, body(): call(third_kernel, [(2, PIECE, N), (2, PIECE, N), (8 * N, N)], [ANY] * 3,...  10.9 us
    pallas_call x1, Pallas kernels, body(): call(second_kernel, [(2, 2, N, N), (2, FIELDS, N), (2, PUSHED, N)], [ANY]...  10.2 us
    ppermute x1, waiting for transfers between devices, body(): back_c = lax.ppermute(away_c, both, swap)  9 us
    pallas_call x1, Pallas kernels, body(): call(fourth_kernel, [(1, PIECE, N), (1, PIECE, N), (8 * N, N)], [ANY] * 3...  6.15 us
    ppermute x1, waiting for transfers between devices, body(): f_ahead = lax.ppermute(to_ahead, both, ahead)  4.12 us
  transfers between devices with their start and end apart: 7, of which 3 were waited for; matrix products, arithmetic and copies ran while one was open for 0% of the time, Pallas kernels for 31%

profile of v2, /device:TPU:4, one launch (start us, length us, event | category | flops | bytes accessed | tf_op | source)
XLA Modules:
  0.0 133.7 jit_solution(14989943018101249027)
XLA Ops:
  0.6 0.0 copy-start
  0.6 0.6 pad_add_fusion.meta
  1.2 0.0 copy-start.1
  1.2 49.7 %shard_map.103 = (f32[8,40,256]{2,1,0:T(8,128)}, f32[672,256]{1,0:T(8,128)}, f32[552,256]{1,0:T(8,128)}, f32[552,256]{1,0:T(8,128)}) custom-call(s32[2]{0:T(128)} %pad_add_fusion.meta, f32[2048,256]{1,0:T(8,128)} %bitcast.4, f32[8,2048]{1,0:T(8,128)} %refs_0_.1, f32[8,2048]{1,0:T(8,128)} %refs_1_.1, f32[8,2048]{1,0:T(8,128)} %refs_2_.1, s32[8,2048]{1,0:T(8,128)} %refs_3_.1, ...), custom_call_target="tpu_custom_call" | custom-call | flops 1048576 | bytes 4194304 | tf_op jit(solution)/shard_map/pallas_call | solution.py:366
  51.0 1.3 collective-permute-start
  52.2 0.8 collective-permute-start.1
  53.1 1.9 %collective-permute-start.2 = (f32[552,256]{1,0:T(8,128)}, f32[552,256]{1,0:T(8,128)S(1)}, u32[]{:S(2)}, u32[]{:S(2)}) collective-permute-start(f32[552,256]{1,0:T(8,128)} %get-tuple-element.28), channel_id=1, source_target_pairs={{0,2},{1,1},{2,4},{3,3},{4,6},{5,5},{6,8},{7,7},{8,10},{9,9},{10,1... | collective-permute-start | bytes 1695752 | tf_op jit(solution)/shard_map/ppermute | solution.py:373
  55.0 14.6 %collective-permute-done.swap = f32[672,256]{1,0:T(8,128)S(1)} collective-permute-done((f32[672,256]{1,0:T(8,128)}, f32[672,256]{1,0:T(8,128)S(1)}, u32[]{:S(2)}, u32[]{:S(2)}) %collective-permute-start) | collective-permute-done | bytes 688160 | tf_op jit(solution)/shard_map/ppermute | solution.py:371
  69.6 0.0 copy-done
  69.6 0.0 copy-done.1
  69.6 0.0 copy-start.2
  69.6 1.0 copy-done.2
  70.5 0.0 copy-start.4
  70.5 1.0 copy-done.4
  71.6 0.0 copy-start.6
  71.6 1.0 copy-done.6
  72.6 0.0 copy-start.5
  72.6 14.4 %shard_map.104 = (f32[2,256,256]{2,1,0:T(8,128)S(1)}, f32[2,40,256]{2,1,0:T(8,128)S(1)}, f32[1,272,256]{2,1,0:T(8,128)S(1)}, f32[1,272,256]{2,1,0:T(8,128)S(1)}) custom-call(s32[2]{0:T(128)S(1)} %copy-done.1, f32[2048,256]{1,0:T(8,128)S(1)} %bitcast.5, f32[8,40,256]{2,1,0:T(8,128)S(1)} %copy-done.2, f32[672,256]{1,0:T(8,128)S(1)} %collective-permute-done.swap, ...), custom_call_target="tpu_custom_call" | custom-call | flops 25769803776 | bytes 4194304 | tf_op jit(solution)/shard_map/pallas_call | solution.py:375
  87.0 1.3 collective-permute-start.3
  88.4 0.0 collective-permute-done.1.chain
  88.4 4.1 %collective-permute-done.2.ahead = f32[552,256]{1,0:T(8,128)S(1)} collective-permute-done((f32[552,256]{1,0:T(8,128)}, f32[552,256]{1,0:T(8,128)S(1)}, u32[]{:S(2)}, u32[]{:S(2)}) %collective-permute-start.2) | collective-permute-done | bytes 565280 | tf_op jit(solution)/shard_map/ppermute | solution.py:373
  92.5 0.0 copy-done.5
  92.5 0.0 copy-start.7
  92.5 10.2 %shard_map.105 = (f32[2,2,256,256]{3,2,1,0:T(8,128)S(1)}, f32[2,40,256]{2,1,0:T(8,128)S(1)}, f32[2,16,256]{2,1,0:T(8,128)S(1)}) custom-call(s32[2]{0:T(128)S(1)} %copy-done.1, f32[2,40,256]{2,1,0:T(8,128)S(1)} %get-tuple-element.26.after.q1, f32[8,40,256]{2,1,0:T(8,128)S(1)} %copy-done.2, f32[672,256]{1,0:T(8,128)S(1)} %collective-permute-done.swap, ...), custom_call_target="tpu_custom_call" | custom-call | flops 17179869184 | bytes 4194304 | tf_op jit(solution)/shard_map/pallas_call | solution.py:380
  102.7 0.1 collective-permute-start.4
  102.8 0.0 collective-permute-done.3.back_a.refs_3_
  102.8 0.0 copy-done.7
  102.9 0.0 copy-start.3
  102.9 10.9 %shard_map.106 = (f32[2,272,256]{2,1,0:T(8,128)S(1)}, f32[2,272,256]{2,1,0:T(8,128)S(1)}, f32[2048,256]{1,0:T(8,128)}) custom-call(s32[2]{0:T(128)S(1)} %copy-done.1, f32[2,2,256,256]{3,2,1,0:T(8,128)S(1)} %get-tuple-element.29.d_ref, f32[2,40,256]{2,1,0:T(8,128)S(1)} %get-tuple-element.30.q0, f32[2,40,256]{2,1,0:T(8,128)S(1)} %get-tuple-element.26.after.q1, ...), custom_call_target="tpu_custom_call" | custom-call | flops 17179869184 | bytes 4194304 | tf_op jit(solution)/shard_map/pallas_call | solution.py:385
  113.8 2.1 %collective-permute-start.5 = (f32[2,272,256]{2,1,0:T(8,128)S(1)}, f32[2,272,256]{2,1,0:T(8,128)S(1)}, u32[]{:S(2)}, u32[]{:S(2)}) collective-permute-start(f32[2,272,256]{2,1,0:T(8,128)S(1)} %get-tuple-element.37), channel_id=1, source_target_pairs={{0,1},{1,0},{2,3},{3,2},{4,5},{5,4},{6,7},{7,6},{8,9},{9,8},{10,11... | collective-permute-start | bytes 1671176 | tf_op jit(solution)/shard_map/ppermute | solution.py:389
  115.9 0.0 collective-permute-done.4.pushed
  115.9 0.0 copy-done.3
  115.9 6.1 %shard_map.107 = (f32[1,272,256]{2,1,0:T(8,128)S(1)}, f32[1,272,256]{2,1,0:T(8,128)S(1)}, f32[2048,256]{1,0:T(8,128)}) custom-call(s32[2]{0:T(128)S(1)} %copy-done.1, f32[2,256,256]{2,1,0:T(8,128)S(1)} %get-tuple-element.33.d_ref, f32[8,40,256]{2,1,0:T(8,128)S(1)} %copy-done.3, ...), custom_call_target="tpu_custom_call", output_to_operand_aliasing={{2}: (7, {})} | custom-call | flops 17179869184 | bytes 4194304 | tf_op jit(solution)/shard_map/pallas_call | solution.py:390
  122.0 0.1 collective-permute-start.6
  122.1 9.0 %collective-permute-done.6.refs_5_ = f32[1,272,256]{2,1,0:T(8,128)S(1)} collective-permute-done((f32[1,272,256]{2,1,0:T(8,128)S(1)}, f32[1,272,256]{2,1,0:T(8,128)S(1)}, u32[]{:S(2)}, u32[]{:S(2)}) %collective-permute-start.6) | collective-permute-done | bytes 278560 | tf_op jit(solution)/shard_map/ppermute | solution.py:394
  131.1 0.0 collective-permute-done.5.refs_4_
  131.2 2.3 %shard_map.108 = (f32[2048,256]{1,0:T(8,128)}, f32[8,2048]{1,0:T(8,128)}, f32[8,2048]{1,0:T(8,128)}) custom-call(s32[2]{0:T(128)S(1)} %copy-done.1, f32[1,272,256]{2,1,0:T(8,128)S(1)} %get-tuple-element.25.own_a.refs_0_, f32[2,272,256]{2,1,0:T(8,128)S(1)} %get-tuple-element.32.refs_1_, ...), custom_call_target="tpu_custom_call", output_to_operand_aliasing={{0}: (7, {})} | custom-call | flops 1048576 | bytes 4194304 | tf_op jit(solution)/shard_map/pallas_call | solution.py:395
Async XLA Ops:
  0.6 68.9 %copy-start = (f32[8,2,128,256]{3,2,1,0:T(8,128)S(1)}, f32[8,2,128,256]{3,2,1,0:T(8,128)}, u32[]{:S(2)}) copy-start(f32[8,2,128,256]{3,2,1,0:T(8,128)} %param.8) | copy-start | bytes 6291460
  1.2 68.3 %copy-start.1 = (s32[2]{0:T(128)S(1)}, s32[2]{0:T(128)}, u32[]{:S(2)}) copy-start(s32[2]{0:T(128)} %pad_add_fusion.meta) | copy-start | bytes 28
  51.0 18.6 %collective-permute-start = (f32[672,256]{1,0:T(8,128)}, f32[672,256]{1,0:T(8,128)S(1)}, u32[]{:S(2)}, u32[]{:S(2)}) collective-permute-start(f32[672,256]{1,0:T(8,128)} %get-tuple-element.24), channel_id=1, source_target_pairs={{0,1},{1,0},{2,3},{3,2},{4,5},{5,4},{6,7},{7,6},{8,9},{9,8},{10,11... | collective-permute-start | bytes 2064392 | tf_op jit(solution)/shard_map/ppermute | solution.py:371
  52.2 36.1 %collective-permute-start.1 = (f32[552,256]{1,0:T(8,128)}, f32[552,256]{1,0:T(8,128)S(1)}, u32[]{:S(2)}, u32[]{:S(2)}) collective-permute-start(f32[552,256]{1,0:T(8,128)} %get-tuple-element.27), channel_id=1, source_target_pairs={{0,1},{1,2},{2,3},{3,4},{4,5},{5,6},{6,7},{7,8},{8,9},{9,10},{10,1... | collective-permute-start | bytes 1695752 | tf_op jit(solution)/shard_map/ppermute | solution.py:372
  53.1 39.4 %collective-permute-start.2 = (f32[552,256]{1,0:T(8,128)}, f32[552,256]{1,0:T(8,128)S(1)}, u32[]{:S(2)}, u32[]{:S(2)}) collective-permute-start(f32[552,256]{1,0:T(8,128)} %get-tuple-element.28), channel_id=1, source_target_pairs={{0,2},{1,1},{2,4},{3,3},{4,6},{5,5},{6,8},{7,7},{8,10},{9,9},{10,1... | collective-permute-start | bytes 1695752 | tf_op jit(solution)/shard_map/ppermute | solution.py:373
  69.6 1.0 copy-start.2
  70.5 1.0 copy-start.4
  71.6 1.0 copy-start.6
  72.6 19.9 %copy-start.5 = (bf16[2,2,256,256]{3,2,1,0:T(8,128)(2,1)S(1)}, bf16[2,2,256,256]{3,2,1,0:T(8,128)(2,1)}, u32[]{:S(2)}) copy-start(bf16[2,2,256,256]{3,2,1,0:T(8,128)(2,1)} %constant.17.clone.tab_l) | copy-start | bytes 1572868
  87.0 15.8 %collective-permute-start.3 = (f32[1,272,256]{2,1,0:T(8,128)S(1)}, f32[1,272,256]{2,1,0:T(8,128)S(1)}, u32[]{:S(2)}, u32[]{:S(2)}) collective-permute-start(f32[1,272,256]{2,1,0:T(8,128)S(1)} %get-tuple-element.31), channel_id=1, source_target_pairs={{0,1},{1,0},{2,3},{3,2},{4,5},{5,4},{6,7},{7,6},{8,9},{9,8},{10,11... | collective-permute-start | bytes 835592 | tf_op jit(solution)/shard_map/ppermute | solution.py:379
  92.5 10.4 %copy-start.7 = (bf16[2,2,256,256]{3,2,1,0:T(8,128)(2,1)S(1)}, bf16[2,2,256,256]{3,2,1,0:T(8,128)(2,1)}, u32[]{:S(2)}) copy-start(bf16[2,2,256,256]{3,2,1,0:T(8,128)(2,1)} %constant.16.clone.tab_r) | copy-start | bytes 1572868
  102.7 13.1 %collective-permute-start.4 = (f32[2,16,256]{2,1,0:T(8,128)S(1)}, f32[2,16,256]{2,1,0:T(8,128)S(1)}, u32[]{:S(2)}, u32[]{:S(2)}) collective-permute-start(f32[2,16,256]{2,1,0:T(8,128)S(1)} %get-tuple-element.34), channel_id=1, source_target_pairs={{1,0},{2,1},{3,2},{4,3},{5,4},{6,5},{7,6},{8,7},{9,8},{10,9},{11,1... | collective-permute-start | bytes 98312 | tf_op jit(solution)/shard_map/ppermute | solution.py:384
  102.9 13.0 %copy-start.3 = (f32[8,40,256]{2,1,0:T(8,128)S(1)}, f32[8,40,256]{2,1,0:T(8,128)}, u32[]{:S(2)}) copy-start(f32[8,40,256]{2,1,0:T(8,128)} %get-tuple-element.23.parts) | copy-start | bytes 983044
  113.8 17.4 %collective-permute-start.5 = (f32[2,272,256]{2,1,0:T(8,128)S(1)}, f32[2,272,256]{2,1,0:T(8,128)S(1)}, u32[]{:S(2)}, u32[]{:S(2)}) collective-permute-start(f32[2,272,256]{2,1,0:T(8,128)S(1)} %get-tuple-element.37), channel_id=1, source_target_pairs={{0,1},{1,0},{2,3},{3,2},{4,5},{5,4},{6,7},{7,6},{8,9},{9,8},{10,11... | collective-permute-start | bytes 1671176 | tf_op jit(solution)/shard_map/ppermute | solution.py:389
  122.0 9.1 %collective-permute-start.6 = (f32[1,272,256]{2,1,0:T(8,128)S(1)}, f32[1,272,256]{2,1,0:T(8,128)S(1)}, u32[]{:S(2)}, u32[]{:S(2)}) collective-permute-start(f32[1,272,256]{2,1,0:T(8,128)S(1)} %get-tuple-element.38), channel_id=1, source_target_pairs={{0,1},{1,0},{2,3},{3,2},{4,5},{5,4},{6,7},{7,6},{8,9},{9,8},{10,11... | collective-permute-start | bytes 835592 | tf_op jit(solution)/shard_map/ppermute | solution.py:394

commit v3 on v2

--- a/solution.py
+++ b/solution.py
@@ -38,7 +38,7 @@
     both = [0.5 * (c0 + c1), 0.5 * (c0 - c1)]
     right = np.stack([np.block([[b.real, b.imag], [-b.imag, b.real]]) for b in both])
     left = np.stack([np.block([[b.real, -b.imag], [b.imag, b.real]]) for b in both])
-    return np.stack(split_np(right)), np.stack(split_np(left))
+    return np.stack(split_np(np.stack([right, left])))
 
 
 def sincos(x):
@@ -68,7 +68,7 @@
     return jnp.dot(a, b, preferred_element_type=F32)
 
 
-def step(f_ref, p_ref, tab_r, tab_l, out_ref, c_ref, w_ref, s_ref, sr_ref, x_ref, samp_ref, c8_ref, sr8_ref):
+def step(f_ref, p_ref, tab, out_ref, c_ref, w_ref, s_ref, sr_ref, x_ref, samp_ref, c8_ref, sr8_ref):
     iota_c = (lax.broadcasted_iota(jnp.int32, (16, 16, N), 0) * 16
               + lax.broadcasted_iota(jnp.int32, (16, 16, N), 1)).astype(F32).astype(BF)
     one = jnp.ones((16, N), BF)
@@ -134,14 +134,14 @@
     turned = []
     for e in range(2):
         xh, xl = hilo(jnp.concatenate(quads[e], 1))
-        turned.append(mm(xh, tab_r[0, e]) + mm(xl, tab_r[0, e]) + mm(xh, tab_r[1, e]))
+        turned.append(mm(xh, tab[0, 0, e]) + mm(xl, tab[0, 0, e]) + mm(xh, tab[1, 0, e]))
     halves = []
     for e in range(2):
         rows = slice(HALF * e, HALF * e + HALF)
         y = jnp.concatenate([jnp.concatenate([turned[0][rows, :HALF], turned[1][rows, :HALF]], 1),
                              jnp.concatenate([turned[0][rows, HALF:], turned[1][rows, HALF:]], 1)], 0)
         yh, yl = hilo(y)
-        halves.append(mm(tab_l[0, e], yh) + mm(tab_l[0, e], yl) + mm(tab_l[1, e], yh))
+        halves.append(mm(tab[0, 1, e], yh) + mm(tab[0, 1, e], yl) + mm(tab[1, 1, e], yh))
     for e, rows in enumerate((halves[0] + halves[1], halves[0] - halves[1])):
         left, right = rows[:, :HALF], rows[:, HALF:]
         out = jnp.concatenate([left + right, left - right], 1)
@@ -154,7 +154,7 @@
         pltpu.VMEM((2, N, PART), F8), pltpu.VMEM((N, PART), F8)]
 FIELD = pltpu.VMEM((2, N, N), F32)
 PARTS = pltpu.VMEM((2, FIELDS, N), F32)
-TABLE = pltpu.VMEM((2, 2, N, N), BF)
+TABLE = pltpu.VMEM((2, 2, 2, N, N), BF)
 ANY = pl.BlockSpec(memory_space=pl.ANY)
 VM = pl.BlockSpec(memory_space=pltpu.VMEM)
 SM = pl.BlockSpec(memory_space=pltpu.SMEM)
@@ -179,17 +179,16 @@
         self.open = []
 
 
-def call(kernel, outs, out_specs, scratch, copies, in_specs, flops, aliases={}, vmem=40960):
+def call(kernel, outs, out_specs, scratch, copies, in_specs, flops, aliases={}, vmem=40 << 20):
     return pl.pallas_call(
         kernel, out_shape=[jax.ShapeDtypeStruct(s, F32) for s in outs], in_specs=in_specs, out_specs=out_specs,
         scratch_shapes=scratch + [pltpu.SemaphoreType.DMA((copies,))],
         input_output_aliases=aliases, cost_estimate=pl.CostEstimate(flops=flops, bytes_accessed=4 << 20, transcendentals=0),
-        compiler_params=pltpu.CompilerParams(vmem_limit_bytes=vmem << 10))
+        compiler_params=pltpu.CompilerParams(vmem_limit_bytes=vmem))
 
 
 def pack_kernel(meta, wave, *refs):
-    sources, (all_ref, swap_ref, chain_ref, ahead_ref), rest = refs[:5], refs[5:9], refs[9:]
-    floats, ints, packed, sems = rest
+    sources, (all_ref, swap_ref, chain_ref, ahead_ref), (floats, ints, sems) = refs[:5], refs[5:9], refs[9:]
     r = meta[0]
     rows = 2 * N
     loads, copies = Copies(sems), Copies(sems)
@@ -204,12 +203,11 @@
         src = floats.at[a] if a < 3 else ints.at[a - 3]
         for s in range(8):
             for k in range(ROWS):
-                packed[s, a * ROWS + k:a * ROWS + k + 1, :] = src[s:s + 1, N * k:N * k + N].astype(F32)
-    copies.start(packed, all_ref)
+                all_ref[s, a * ROWS + k:a * ROWS + k + 1, :] = src[s:s + 1, N * k:N * k + N].astype(F32)
     for i in range(4):
-        copies.start(packed.at[4 - 4 * r + i], swap_ref.at[pl.ds(rows + FIELDS * i, FIELDS)])
-    copies.start(packed.at[3 + 4 * r], chain_ref.at[pl.ds(rows, FIELDS)])
-    copies.start(packed.at[7 - 4 * r], ahead_ref.at[pl.ds(rows, FIELDS)])
+        swap_ref[rows + FIELDS * i:rows + FIELDS * i + FIELDS, :] = all_ref[4 - 4 * r + i]
+    chain_ref[rows:, :] = all_ref[3 + 4 * r]
+    ahead_ref[rows:, :] = all_ref[7 - 4 * r]
     copies.wait()
 
 
@@ -227,7 +225,7 @@
         copies.start(p_ref.at[half, pl.ds(0, PUSHED)], dst.at[i, pl.ds(2 * HALF, PUSHED)])
 
 
-def first_kernel(meta, wave, parts, swap, tab_r, tab_l, d_ref, q_ref, own, away, f2, f3, p1, p2, z, z3, tr, tl, *rest):
+def first_kernel(meta, wave, parts, swap, table, d_ref, q_ref, own, away, f2, f3, p1, p2, z, z3, tab, *rest):
     work, sems = rest[:-1], rest[-1]
     r = meta[0]
     copies = Copies(sems)
@@ -235,44 +233,44 @@
     for p, i in ((p2, 2), (p1, 1)):
         copies.start(parts.at[4 * r + i], p.at[r])
         copies.start(swap.at[pl.ds(2 * N + FIELDS * i, FIELDS)], p.at[1 - r])
-    copies.start(tab_r, tr)
-    copies.start(tab_l, tl)
+    copies.start(table, tab)
     field_in(copies, r, f2, wave, N * 4 * r, swap, 0)
     copies.wait()
-    step(f3, p2, tr, tl, z3, *work)
+    step(f3, p2, tab, z3, *work)
     copies.start(z3, d_ref)
-    step(f2, p1, tr, tl, f3, *work)
+    step(f2, p1, tab, f3, *work)
     copies.start(p1, q_ref)
-    step(f3, p2, tr, tl, z, *work)
+    step(f3, p2, tab, z, *work)
     piece_out(copies, r, z, p2, own, away, 0)
     copies.wait()
 
 
-def second_kernel(meta, after, parts, swap, chain, ahead, tab_r, tab_l, d_ref, q_ref, pushed,
-                  f0, f1, p0, pm, z0, z1, tr, tl, *rest):
+def second_kernel(meta, q1, parts, swap, chain, ahead, table, d_ref, q_ref, pushed, own, away,
+                  f0, f1, p0, p1, pm, z0, z1, tab, *rest):
     work, sems = rest[:-1], rest[-1]
     r = meta[0]
     copies = Copies(sems)
     field_in(copies, r, f0, ahead, 0, chain, 0)
     copies.start(ahead.at[pl.ds(2 * N, FIELDS)], pm.at[r])
     copies.start(chain.at[pl.ds(2 * N, FIELDS)], pm.at[1 - r])
-    copies.start(tab_r, tr)
-    copies.start(tab_l, tl)
+    copies.start(table, tab)
     field_in(copies, r, f1, ahead, N, chain, N)
     copies.start(parts.at[4 * r], p0.at[r])
     copies.start(swap.at[pl.ds(2 * N, FIELDS)], p0.at[1 - r])
+    copies.start(q1, p1)
     copies.wait()
 
     @pl.when(meta[1] == 1)
     def _():
         f1[...] = jnp.zeros_like(f1)
 
-    step(f0, pm, tr, tl, z0, *work)
+    step(f0, pm, tab, z0, *work)
     copies.start(pm.at[:, pl.ds(0, PUSHED)], pushed)
-    copies.start(z0, d_ref.at[0])
-    step(f1, p0, tr, tl, z1, *work)
+    copies.start(z0, d_ref)
+    step(f1, p0, tab, z1, *work)
     copies.start(p0, q_ref)
-    copies.start(z1, d_ref.at[1])
+    step(z1, p1, tab, f1, *work)
+    piece_out(copies, r, f1, p1, own, away, 0)
     copies.wait()
 
 
@@ -282,66 +280,57 @@
                      wave.at[pl.ds((4 * r + slot) * N + HALF * z, HALF)])
 
 
-def third_kernel(meta, d_ref, q0, q1, own_a, back_a, tab_r, tab_l, own, away, wave,
-                 f0, f1, p0, p1, z0, z1, tr, tl, *rest):
+def third_kernel(meta, d_ref, q0, own_a, own_b, back_a, table, own, away, wave, f0, p0, z0, tab, *rest):
     work, sems = rest[:-1], rest[-1]
     r = meta[0]
     copies, moves = Copies(sems), Copies(sems)
-    moves.used = 24
-    copies.start(d_ref.at[0], f0)
+    moves.used = 16
+    copies.start(d_ref, f0)
     copies.start(q0, p0)
-    copies.start(tab_r, tr)
-    copies.start(tab_l, tl)
-    copies.start(d_ref.at[1], f1)
-    copies.start(q1, p1)
-    copies.wait()
-    for ref, slot in ((own_a, 4 * r + 2), (back_a, 6 - 4 * r)):
+    copies.start(table, tab)
+    copies.wait()
+    for ref, slot in ((own_a, 4 * r + 2), (own_b, 4 * r + 1), (back_a, 6 - 4 * r)):
         moves.start(ref.at[0, pl.ds(0, N)], wave.at[pl.ds(slot * N, N)])
 
     @pl.when(meta[1] == 1)
     def _():
         f0[...] = jnp.zeros_like(f0)
 
-    step(f0, p0, tr, tl, z0, *work)
+    step(f0, p0, tab, z0, *work)
     piece_out(copies, r, z0, p0, own, away, 0)
     own_out(moves, r, z0, wave, 0)
-    step(f1, p1, tr, tl, z1, *work)
-    piece_out(copies, r, z1, p1, own, away, 1)
-    own_out(moves, r, z1, wave, 1)
     copies.wait()
     moves.wait()
 
 
-def fourth_kernel(meta, d_ref, parts, swap, pushed, tab_r, tab_l, wave_in, own, away, wave, f3, p3, z, tr, tl, *rest):
+def fourth_kernel(meta, d_ref, parts, swap, pushed, table, wave_in, own, away, wave, f3, p3, z, tab, *rest):
     work, sems = rest[:-1], rest[-1]
     r = meta[0]
     copies = Copies(sems)
     copies.start(parts.at[4 * r + 3], p3.at[r])
     copies.start(swap.at[pl.ds(2 * N + FIELDS * 3, FIELDS)], p3.at[1 - r])
     copies.start(d_ref, f3)
-    copies.start(tab_r, tr)
-    copies.start(tab_l, tl)
+    copies.start(table, tab)
     copies.wait()
     copies.start(pushed, p3.at[:, pl.ds(0, PUSHED)])
     copies.wait()
-    step(f3, p3, tr, tl, z, *work)
+    step(f3, p3, tab, z, *work)
     piece_out(copies, r, z, p3, own, away, 0)
     own_out(copies, r, z, wave, 3)
     copies.wait()
 
 
 def final_kernel(meta, *refs):
-    pieces, (wave, phase, energy), (packed, sems) = refs[:6], refs[7:10], refs[10:]
+    pieces, (wave, phase, energy), (packed, sems) = refs[:8], refs[9:12], refs[12:]
     r = meta[0]
     moves, copies = Copies(sems), Copies(sems)
     copies.used = 4
     for half in range(2):
         base = 4 * r if half == 0 else 4 - 4 * r
-        for n, (ref, slots) in enumerate(zip(pieces[3 * half:3 * half + 3], ((2,), (0, 1), (3,)))):
-            for i, slot in enumerate(slots):
-                if half == 1 and n > 0:
-                    moves.start(ref.at[i, pl.ds(0, N)], wave.at[pl.ds((base + slot) * N, N)])
-                copies.start(ref.at[i, pl.ds(N, PUSHED)], packed.at[base + slot])
+        for n, (ref, slot) in enumerate(zip(pieces[4 * half:4 * half + 4], (2, 1, 0, 3))):
+            if half == 1 and n > 0:
+                moves.start(ref.at[0, pl.ds(0, N)], wave.at[pl.ds((base + slot) * N, N)])
+            copies.start(ref.at[0, pl.ds(N, PUSHED)], packed.at[base + slot])
     copies.wait()
     for s in range(8):
         for k in range(ROWS):
@@ -351,7 +340,7 @@
 
 
 def body(wavefront, particle_phase, particle_energy, row_offset, row_cell, col_cell):
-    tab_r, tab_l = (jnp.asarray(a) for a in tables())
+    table = jnp.asarray(tables())
     r = lax.axis_index("row")
     nt = lax.axis_size("tm")
     both = ("tm", "row")
@@ -365,8 +354,8 @@
 
     parts, to_swap, to_chain, to_ahead = call(
         pack_kernel, [(8, FIELDS, N), (2 * N + 4 * FIELDS, N), (2 * N + FIELDS, N), (2 * N + FIELDS, N)],
-        [ANY] * 4, [pltpu.VMEM((3, 8, PART), F32), pltpu.VMEM((2, 8, PART), jnp.int32), pltpu.VMEM((8, FIELDS, N), F32)],
-        16, [SM] + [HB] * 6, 1 << 20, vmem=60 << 10,
+        [VM] * 4, [pltpu.VMEM((3, 8, PART), F32), pltpu.VMEM((2, 8, PART), jnp.int32)],
+        16, [SM] + [HB] * 6, 1 << 20, vmem=61000 << 10,
     )(meta, wave, particle_phase, particle_energy, row_offset, row_cell, col_cell)
     f_swap = lax.ppermute(to_swap, both, swap)
     f_chain = lax.ppermute(to_chain, both, chain)
@@ -374,28 +363,29 @@
 
     d3, q1, own_a, away_a = call(
         first_kernel, [(2, N, N), (2, FIELDS, N), (1, PIECE, N), (1, PIECE, N)], [ANY] * 4,
-        [FIELD, FIELD, PARTS, PARTS, FIELD, FIELD, TABLE, TABLE] + WORK, 32, [SM] + [ANY] * 5, 3 * unit,
-    )(meta, wave, parts, f_swap, tab_r, tab_l)
+        [FIELD, FIELD, PARTS, PARTS, FIELD, FIELD, TABLE] + WORK, 32, [SM] + [ANY] * 4, 3 * unit,
+    )(meta, wave, parts, f_swap, table)
     back_a = lax.ppermute(away_a, both, swap)
-    d01, q0, pushed = call(
-        second_kernel, [(2, 2, N, N), (2, FIELDS, N), (2, PUSHED, N)], [ANY] * 3,
-        [FIELD, FIELD, PARTS, PARTS, FIELD, FIELD, TABLE, TABLE] + WORK, 32, [SM] + [ANY] * 7, 2 * unit,
-    )(meta, q1, parts, f_swap, f_chain, f_ahead, tab_r, tab_l)
+    d0, q0, pushed, own_b, away_b = call(
+        second_kernel, [(2, N, N), (2, FIELDS, N), (2, PUSHED, N), (1, PIECE, N), (1, PIECE, N)], [ANY] * 5,
+        [FIELD, FIELD, PARTS, PARTS, PARTS, FIELD, FIELD, TABLE] + WORK, 32, [SM] + [ANY] * 6, 3 * unit,
+    )(meta, q1, parts, f_swap, f_chain, f_ahead, table)
     pushed = lax.ppermute(pushed, both, back)
-    own_b, away_b, wave = call(
-        third_kernel, [(2, PIECE, N), (2, PIECE, N), (8 * N, N)], [ANY] * 3,
-        [FIELD, FIELD, PARTS, PARTS, FIELD, FIELD, TABLE, TABLE] + WORK, 32, [SM] + [ANY] * 7, 2 * unit,
-    )(meta, d01, q0, q1, own_a, back_a, tab_r, tab_l)
     back_b = lax.ppermute(away_b, both, swap)
     own_c, away_c, wave = call(
+        third_kernel, [(1, PIECE, N), (1, PIECE, N), (8 * N, N)], [ANY] * 3,
+        [FIELD, PARTS, FIELD, TABLE] + WORK, 32, [SM] + [ANY] * 6, unit,
+    )(meta, d0, q0, own_a, own_b, back_a, table)
+    back_c = lax.ppermute(away_c, both, swap)
+    own_d, away_d, wave = call(
         fourth_kernel, [(1, PIECE, N), (1, PIECE, N), (8 * N, N)], [ANY] * 3,
-        [FIELD, PARTS, FIELD, TABLE, TABLE] + WORK, 32, [SM] + [ANY] * 7, 2 * unit, {7: 2},
-    )(meta, d3, parts, f_swap, pushed, tab_r, tab_l, wave)
-    back_c = lax.ppermute(away_c, both, swap)
+        [FIELD, PARTS, FIELD, TABLE] + WORK, 32, [SM] + [ANY] * 6, 2 * unit, {6: 2},
+    )(meta, d3, parts, f_swap, pushed, table, wave)
+    back_d = lax.ppermute(away_d, both, swap)
     wave, phase, energy = call(
         final_kernel, [(8 * N, N), (8, PART), (8, PART)], [HB, VM, VM],
-        [pltpu.VMEM((8, PUSHED, N), F32)], 16, [SM] + [ANY] * 6 + [HB], 1 << 20, {7: 0},
-    )(meta, own_a, own_b, own_c, back_a, back_b, back_c, wave)
+        [pltpu.VMEM((8, PUSHED, N), F32)], 16, [SM] + [ANY] * 8 + [HB], 1 << 20, {9: 0},
+    )(meta, own_a, own_b, own_c, own_d, back_a, back_b, back_c, back_d, wave)
     return wave.reshape(8, 2, HALF, N), phase, energy
 
 

time: 134 us -> 88.3 us (0.66)
  the two profiles are of different devices: /device:TPU:4 before, /device:TPU:2 now
where the time goes in v3:
time: 88.3 us; the launch traced here: 88 us
  Pallas kernels  47.7 us (54%)
  waiting for transfers between devices  22.1 us (25%)
  starting transfers between devices  14.4 us (16%)
  local copies, waits for them, and re-layouts  2.22 us (3%)
    ppermute x1, waiting for transfers between devices, body(): f_swap = lax.ppermute(to_swap, both, swap)  15.6 us
    pallas_call x1, Pallas kernels, body(): call(second_kernel, [(2, N, N), (2, FIELDS, N), (2, PUSHED, N), (1, PIECE...  14.7 us
    pallas_call x1, Pallas kernels, body(): call(first_kernel, [(2, N, N), (2, FIELDS, N), (1, PIECE, N), (1, PIECE,...  14.4 us
    ppermute x1, starting transfers between devices, body(): pushed = lax.ppermute(pushed, both, back)  8.59 us
    ppermute x1, waiting for transfers between devices, body(): back_d = lax.ppermute(away_d, both, swap)  6.48 us
    pallas_call x1, Pallas kernels, body(): call(third_kernel, [(1, PIECE, N), (1, PIECE, N), (8 * N, N)], [ANY] * 3,...  6.36 us
    pallas_call x1, Pallas kernels, body(): call(fourth_kernel, [(1, PIECE, N), (1, PIECE, N), (8 * N, N)], [ANY] * 3...  6.15 us
    pallas_call x1, Pallas kernels, body(): call(pack_kernel, [(8, FIELDS, N), (2 * N + 4 * FIELDS, N), (2 * N + FIEL...  3.74 us
  transfers between devices with their start and end apart: 8, of which 2 were waited for; matrix products, arithmetic and copies ran while one was open for 0% of the time, Pallas kernels for 47%

profile of v3, /device:TPU:2, one launch (start us, length us, event | category | flops | bytes accessed | tf_op | source)
XLA Modules:
  0.0 88.0 jit_solution(12219752626985584195)
XLA Ops:
  0.6 0.0 copy-start
  0.6 0.7 pad_add_fusion.meta
  1.3 0.0 copy-start.1
  1.3 3.7 %shard_map.94 = (f32[8,40,256]{2,1,0:T(8,128)}, f32[672,256]{1,0:T(8,128)}, f32[552,256]{1,0:T(8,128)}, f32[552,256]{1,0:T(8,128)}) custom-call(s32[2]{0:T(128)} %pad_add_fusion.meta, f32[2048,256]{1,0:T(8,128)} %bitcast.4, f32[8,2048]{1,0:T(8,128)} %refs_0_.1, f32[8,2048]{1,0:T(8,128)} %refs_1_.1, f32[8,2048]{1,0:T(8,128)} %refs_2_.1, s32[8,2048]{1,0:T(8,128)} %refs_3_.1, ...), custom_call_target="tpu_custom_call" | custom-call | flops 1048576 | bytes 4194304 | tf_op jit(solution)/shard_map/pallas_call | solution.py:355
  5.1 0.5 collective-permute-start
  5.6 0.7 collective-permute-start.1
  6.3 1.7 %collective-permute-start.2 = (f32[552,256]{1,0:T(8,128)}, f32[552,256]{1,0:T(8,128)S(1)}, u32[]{:S(2)}, u32[]{:S(2)}) collective-permute-start(f32[552,256]{1,0:T(8,128)} %get-tuple-element.30), channel_id=1, source_target_pairs={{0,2},{1,1},{2,4},{3,3},{4,6},{5,5},{6,8},{7,7},{8,10},{9,9},{10,1... | collective-permute-start | bytes 1695752 | tf_op jit(solution)/shard_map/ppermute | solution.py:362
  8.0 15.6 %collective-permute-done.swap = f32[672,256]{1,0:T(8,128)S(1)} collective-permute-done((f32[672,256]{1,0:T(8,128)}, f32[672,256]{1,0:T(8,128)S(1)}, u32[]{:S(2)}, u32[]{:S(2)}) %collective-permute-start) | collective-permute-done | bytes 688160 | tf_op jit(solution)/shard_map/ppermute | solution.py:360
  23.7 0.0 copy-done
  23.7 0.0 copy-done.1
  23.7 0.0 copy-start.2
  23.7 1.0 %copy-done.2 = f32[8,40,256]{2,1,0:T(8,128)S(1)} copy-done((f32[8,40,256]{2,1,0:T(8,128)S(1)}, f32[8,40,256]{2,1,0:T(8,128)}, u32[]{:S(2)}) %copy-start.2) | copy-done | bytes 327704
  24.7 0.0 copy-start.4
  24.7 1.2 %copy-done.4 = bf16[2,2,2,256,256]{4,3,2,1,0:T(8,128)(2,1)S(1)} copy-done((bf16[2,2,2,256,256]{4,3,2,1,0:T(8,128)(2,1)S(1)}, bf16[2,2,2,256,256]{4,3,2,1,0:T(8,128)(2,1)}, u32[]{:S(2)}) %copy-start.4) | copy-done | bytes 1048600
  25.9 14.4 %shard_map.95 = (f32[2,256,256]{2,1,0:T(8,128)S(1)}, f32[2,40,256]{2,1,0:T(8,128)S(1)}, f32[1,272,256]{2,1,0:T(8,128)S(1)}, f32[1,272,256]{2,1,0:T(8,128)S(1)}) custom-call(s32[2]{0:T(128)S(1)} %copy-done.1, f32[2048,256]{1,0:T(8,128)S(1)} %bitcast.5, f32[8,40,256]{2,1,0:T(8,128)S(1)} %copy-done.2, f32[672,256]{1,0:T(8,128)S(1)} %collective-permute-done.swap, ...), custom_call_target="tpu_custom_call" | custom-call | flops 25769803776 | bytes 4194304 | tf_op jit(solution)/shard_map/pallas_call | solution.py:364
  40.3 0.6 collective-permute-start.3
  40.9 0.0 collective-permute-done.1.chain
  40.9 0.0 collective-permute-done.2.ahead
  40.9 0.0 copy-start.5
  40.9 14.7 %shard_map.96 = (f32[2,256,256]{2,1,0:T(8,128)S(1)}, f32[2,40,256]{2,1,0:T(8,128)S(1)}, f32[2,16,256]{2,1,0:T(8,128)S(1)}, f32[1,272,256]{2,1,0:T(8,128)S(1)}, f32[1,272,256]{2,1,0:T(8,128)S(1)}) custom-call(s32[2]{0:T(128)S(1)} %copy-done.1, f32[2,40,256]{2,1,0:T(8,128)S(1)} %get-tuple-element.28.q1, f32[8,40,256]{2,1,0:T(8,128)S(1)} %copy-done.2, ...), custom_call_target="tpu_custom_call" | custom-call | flops 25769803776 | bytes 4194304 | tf_op jit(solution)/shard_map/pallas_call | solution.py:369
  55.6 8.6 %collective-permute-start.4 = (f32[2,16,256]{2,1,0:T(8,128)S(1)}, f32[2,16,256]{2,1,0:T(8,128)S(1)}, u32[]{:S(2)}, u32[]{:S(2)}) collective-permute-start(f32[2,16,256]{2,1,0:T(8,128)S(1)} %get-tuple-element.37), channel_id=1, source_target_pairs={{1,0},{2,1},{3,2},{4,3},{5,4},{6,5},{7,6},{8,7},{9,8},{10,9},{11,1... | collective-permute-start | bytes 98312 | tf_op jit(solution)/shard_map/ppermute | solution.py:373
  64.2 0.1 collective-permute-start.5
  64.3 0.0 collective-permute-done.3.back_a.refs_4_
  64.3 0.0 copy-done.5
  64.3 0.0 copy-start.3
  64.3 6.4 %shard_map.97 = (f32[1,272,256]{2,1,0:T(8,128)S(1)}, f32[1,272,256]{2,1,0:T(8,128)S(1)}, f32[2048,256]{1,0:T(8,128)}) custom-call(s32[2]{0:T(128)S(1)} %copy-done.1, f32[2,256,256]{2,1,0:T(8,128)S(1)} %get-tuple-element.32.d_ref, f32[2,40,256]{2,1,0:T(8,128)S(1)} %get-tuple-element.33.q0, f32[1,272,256]{2,1,0:T(8,128)S(1)} %get-tuple-element.27.own_a.refs_0_, ...), custom_call_target="tpu_custom_call" | custom-call | flops 8589934592 | bytes 4194304 | tf_op jit(solution)/shard_map/pallas_call | solution.py:375
  70.7 2.0 %collective-permute-start.6 = (f32[1,272,256]{2,1,0:T(8,128)S(1)}, f32[1,272,256]{2,1,0:T(8,128)S(1)}, u32[]{:S(2)}, u32[]{:S(2)}) collective-permute-start(f32[1,272,256]{2,1,0:T(8,128)S(1)} %get-tuple-element.41), channel_id=1, source_target_pairs={{0,1},{1,0},{2,3},{3,2},{4,5},{5,4},{6,7},{7,6},{8,9},{9,8},{10,11... | collective-permute-start | bytes 835592 | tf_op jit(solution)/shard_map/ppermute | solution.py:379
  72.7 0.0 collective-permute-done.4.pushed
  72.7 0.0 copy-done.3
  72.7 6.1 %shard_map.98 = (f32[1,272,256]{2,1,0:T(8,128)S(1)}, f32[1,272,256]{2,1,0:T(8,128)S(1)}, f32[2048,256]{1,0:T(8,128)}) custom-call(s32[2]{0:T(128)S(1)} %copy-done.1, f32[2,256,256]{2,1,0:T(8,128)S(1)} %get-tuple-element.36.d_ref, f32[8,40,256]{2,1,0:T(8,128)S(1)} %copy-done.3, ...), custom_call_target="tpu_custom_call", output_to_operand_aliasing={{2}: (6, {})} | custom-call | flops 17179869184 | bytes 4194304 | tf_op jit(solution)/shard_map/pallas_call | solution.py:380
  78.9 0.1 collective-permute-start.7
  79.0 0.0 collective-permute-done.5.refs_5_
  79.0 0.0 collective-permute-done.6.refs_6_
  79.0 6.5 %collective-permute-done.7.refs_7_ = f32[1,272,256]{2,1,0:T(8,128)S(1)} collective-permute-done((f32[1,272,256]{2,1,0:T(8,128)S(1)}, f32[1,272,256]{2,1,0:T(8,128)S(1)}, u32[]{:S(2)}, u32[]{:S(2)}) %collective-permute-start.7) | collective-permute-done | bytes 278560 | tf_op jit(solution)/shard_map/ppermute | solution.py:384
  85.5 2.3 %shard_map.99 = (f32[2048,256]{1,0:T(8,128)}, f32[8,2048]{1,0:T(8,128)}, f32[8,2048]{1,0:T(8,128)}) custom-call(s32[2]{0:T(128)S(1)} %copy-done.1, f32[1,272,256]{2,1,0:T(8,128)S(1)} %get-tuple-element.27.own_a.refs_0_, f32[1,272,256]{2,1,0:T(8,128)S(1)} %get-tuple-element.31.own_b.refs_1_, ...), custom_call_target="tpu_custom_call", output_to_operand_aliasing={{0}: (9, {})} | custom-call | flops 1048576 | bytes 4194304 | tf_op jit(solution)/shard_map/pallas_call | solution.py:385
Async XLA Ops:
  0.6 23.1 %copy-start = (f32[8,2,128,256]{3,2,1,0:T(8,128)S(1)}, f32[8,2,128,256]{3,2,1,0:T(8,128)}, u32[]{:S(2)}) copy-start(f32[8,2,128,256]{3,2,1,0:T(8,128)} %param.7) | copy-start | bytes 6291460
  1.3 22.4 %copy-start.1 = (s32[2]{0:T(128)S(1)}, s32[2]{0:T(128)}, u32[]{:S(2)}) copy-start(s32[2]{0:T(128)} %pad_add_fusion.meta) | copy-start | bytes 28
  5.1 18.6 %collective-permute-start = (f32[672,256]{1,0:T(8,128)}, f32[672,256]{1,0:T(8,128)S(1)}, u32[]{:S(2)}, u32[]{:S(2)}) collective-permute-start(f32[672,256]{1,0:T(8,128)} %get-tuple-element.26), channel_id=1, source_target_pairs={{0,1},{1,0},{2,3},{3,2},{4,5},{5,4},{6,7},{7,6},{8,9},{9,8},{10,11... | collective-permute-start | bytes 2064392 | tf_op jit(solution)/shard_map/ppermute | solution.py:360
  5.6 35.3 %collective-permute-start.1 = (f32[552,256]{1,0:T(8,128)}, f32[552,256]{1,0:T(8,128)S(1)}, u32[]{:S(2)}, u32[]{:S(2)}) collective-permute-start(f32[552,256]{1,0:T(8,128)} %get-tuple-element.29), channel_id=1, source_target_pairs={{0,1},{1,2},{2,3},{3,4},{4,5},{5,6},{6,7},{7,8},{8,9},{9,10},{10,1... | collective-permute-start | bytes 1695752 | tf_op jit(solution)/shard_map/ppermute | solution.py:361
  6.3 34.5 %collective-permute-start.2 = (f32[552,256]{1,0:T(8,128)}, f32[552,256]{1,0:T(8,128)S(1)}, u32[]{:S(2)}, u32[]{:S(2)}) collective-permute-start(f32[552,256]{1,0:T(8,128)} %get-tuple-element.30), channel_id=1, source_target_pairs={{0,2},{1,1},{2,4},{3,3},{4,6},{5,5},{6,8},{7,7},{8,10},{9,9},{10,1... | collective-permute-start | bytes 1695752 | tf_op jit(solution)/shard_map/ppermute | solution.py:362
  23.7 1.0 %copy-start.2 = (f32[8,40,256]{2,1,0:T(8,128)S(1)}, f32[8,40,256]{2,1,0:T(8,128)}, u32[]{:S(2)}) copy-start(f32[8,40,256]{2,1,0:T(8,128)} %get-tuple-element.25.parts) | copy-start | bytes 983044
  24.7 1.2 %copy-start.4 = (bf16[2,2,2,256,256]{4,3,2,1,0:T(8,128)(2,1)S(1)}, bf16[2,2,2,256,256]{4,3,2,1,0:T(8,128)(2,1)}, u32[]{:S(2)}) copy-start(bf16[2,2,2,256,256]{4,3,2,1,0:T(8,128)(2,1)} %constant.14.clone.table) | copy-start | bytes 3145732
  40.3 24.0 %collective-permute-start.3 = (f32[1,272,256]{2,1,0:T(8,128)S(1)}, f32[1,272,256]{2,1,0:T(8,128)S(1)}, u32[]{:S(2)}, u32[]{:S(2)}) collective-permute-start(f32[1,272,256]{2,1,0:T(8,128)S(1)} %get-tuple-element.34), channel_id=1, source_target_pairs={{0,1},{1,0},{2,3},{3,2},{4,5},{5,4},{6,7},{7,6},{8,9},{9,8},{10,11... | collective-permute-start | bytes 835592 | tf_op jit(solution)/shard_map/ppermute | solution.py:368
  40.9 23.4 %copy-start.5 = (bf16[2,2,2,256,256]{4,3,2,1,0:T(8,128)(2,1)S(1)}, bf16[2,2,2,256,256]{4,3,2,1,0:T(8,128)(2,1)}, u32[]{:S(2)}) copy-start(bf16[2,2,2,256,256]{4,3,2,1,0:T(8,128)(2,1)} %constant.14.clone.table) | copy-start | bytes 3145732
  55.6 17.1 %collective-permute-start.4 = (f32[2,16,256]{2,1,0:T(8,128)S(1)}, f32[2,16,256]{2,1,0:T(8,128)S(1)}, u32[]{:S(2)}, u32[]{:S(2)}) collective-permute-start(f32[2,16,256]{2,1,0:T(8,128)S(1)} %get-tuple-element.37), channel_id=1, source_target_pairs={{1,0},{2,1},{3,2},{4,3},{5,4},{6,5},{7,6},{8,7},{9,8},{10,9},{11,1... | collective-permute-start | bytes 98312 | tf_op jit(solution)/shard_map/ppermute | solution.py:373
  64.2 14.8 %collective-permute-start.5 = (f32[1,272,256]{2,1,0:T(8,128)S(1)}, f32[1,272,256]{2,1,0:T(8,128)S(1)}, u32[]{:S(2)}, u32[]{:S(2)}) collective-permute-start(f32[1,272,256]{2,1,0:T(8,128)S(1)} %get-tuple-element.40), channel_id=1, source_target_pairs={{0,1},{1,0},{2,3},{3,2},{4,5},{5,4},{6,7},{7,6},{8,9},{9,8},{10,11... | collective-permute-start | bytes 835592 | tf_op jit(solution)/shard_map/ppermute | solution.py:374
  64.3 8.4 %copy-start.3 = (f32[8,40,256]{2,1,0:T(8,128)S(1)}, f32[8,40,256]{2,1,0:T(8,128)}, u32[]{:S(2)}) copy-start(f32[8,40,256]{2,1,0:T(8,128)} %get-tuple-element.25.parts) | copy-start | bytes 983044
  70.7 8.4 %collective-permute-start.6 = (f32[1,272,256]{2,1,0:T(8,128)S(1)}, f32[1,272,256]{2,1,0:T(8,128)S(1)}, u32[]{:S(2)}, u32[]{:S(2)}) collective-permute-start(f32[1,272,256]{2,1,0:T(8,128)S(1)} %get-tuple-element.41), channel_id=1, source_target_pairs={{0,1},{1,0},{2,3},{3,2},{4,5},{5,4},{6,7},{7,6},{8,9},{9,8},{10,11... | collective-permute-start | bytes 835592 | tf_op jit(solution)/shard_map/ppermute | solution.py:379
  78.9 6.6 %collective-permute-start.7 = (f32[1,272,256]{2,1,0:T(8,128)S(1)}, f32[1,272,256]{2,1,0:T(8,128)S(1)}, u32[]{:S(2)}, u32[]{:S(2)}) collective-permute-start(f32[1,272,256]{2,1,0:T(8,128)S(1)} %get-tuple-element.42), channel_id=1, source_target_pairs={{0,1},{1,0},{2,3},{3,2},{4,5},{5,4},{6,7},{7,6},{8,9},{9,8},{10,11... | collective-permute-start | bytes 835592 | tf_op jit(solution)/shard_map/ppermute | solution.py:384

commit v4 on v3

--- a/solution.py
+++ b/solution.py
@@ -68,7 +68,7 @@
     return jnp.dot(a, b, preferred_element_type=F32)
 
 
-def step(f_ref, p_ref, tab, out_ref, c_ref, w_ref, s_ref, sr_ref, x_ref, samp_ref, c8_ref, sr8_ref):
+def step(f_ref, p_ref, q_ref, tab, out_ref, c_ref, w_ref, s_ref, sr_ref, x_ref, samp_ref, c8_ref, sr8_ref):
     iota_c = (lax.broadcasted_iota(jnp.int32, (16, 16, N), 0) * 16
               + lax.broadcasted_iota(jnp.int32, (16, 16, N), 1)).astype(F32).astype(BF)
     one = jnp.ones((16, N), BF)
@@ -103,8 +103,8 @@
         sine, cosine = sincos(phase)
         energy = p_ref[h, ROWS:2 * ROWS] - 0.5 * (samp_ref[0] * cosine - samp_ref[1] * sine)
         phase = phase + energy
-        p_ref[h, :ROWS] = phase
-        p_ref[h, ROWS:2 * ROWS] = energy
+        q_ref[h, :ROWS] = phase
+        q_ref[h, ROWS:2 * ROWS] = energy
         sine, cosine = sincos(phase)
         for z, v in ((0, cosine), (1, -sine)):
             vh = v.astype(BF).astype(F32)
@@ -155,6 +155,7 @@
 FIELD = pltpu.VMEM((2, N, N), F32)
 PARTS = pltpu.VMEM((2, FIELDS, N), F32)
 TABLE = pltpu.VMEM((2, 2, 2, N, N), BF)
+PUSH = pltpu.VMEM((2, PUSHED, N), F32)
 ANY = pl.BlockSpec(memory_space=pl.ANY)
 VM = pl.BlockSpec(memory_space=pltpu.VMEM)
 SM = pl.BlockSpec(memory_space=pltpu.SMEM)
@@ -188,26 +189,27 @@
 
 
 def pack_kernel(meta, wave, *refs):
-    sources, (all_ref, swap_ref, chain_ref, ahead_ref), (floats, ints, sems) = refs[:5], refs[5:9], refs[9:]
-    r = meta[0]
-    rows = 2 * N
+    sources, (all_ref, near_ref, swap_ref, chain_ref, ahead_ref), (floats, ints, sems) = refs[:5], refs[5:10], refs[10:]
+    r = meta[0]
     loads, copies = Copies(sems), Copies(sems)
     copies.used = 5
     for a, src in enumerate(sources):
         loads.start(src, floats.at[a] if a < 3 else ints.at[a - 3])
-    copies.start(wave.at[pl.ds(N * (4 - 4 * r), rows)], swap_ref.at[pl.ds(0, rows)])
-    copies.start(wave.at[pl.ds(N * (2 + 4 * r), rows)], chain_ref.at[pl.ds(0, rows)])
-    copies.start(wave.at[pl.ds(N * (6 - 4 * r), rows)], ahead_ref.at[pl.ds(0, rows)])
+    copies.start(wave.at[pl.ds(N * (6 - 4 * r), 2 * N)], ahead_ref.at[pl.ds(0, 2 * N)])
+    copies.start(wave.at[pl.ds(N * (5 - 4 * r), N)], near_ref.at[pl.ds(0, N)])
+    copies.start(wave.at[pl.ds(N * (4 - 4 * r), N)], swap_ref.at[pl.ds(0, N)])
+    copies.start(wave.at[pl.ds(N * (2 + 4 * r), 2 * N)], chain_ref.at[pl.ds(0, 2 * N)])
     loads.wait()
     for a in range(5):
         src = floats.at[a] if a < 3 else ints.at[a - 3]
         for s in range(8):
             for k in range(ROWS):
                 all_ref[s, a * ROWS + k:a * ROWS + k + 1, :] = src[s:s + 1, N * k:N * k + N].astype(F32)
-    for i in range(4):
-        swap_ref[rows + FIELDS * i:rows + FIELDS * i + FIELDS, :] = all_ref[4 - 4 * r + i]
-    chain_ref[rows:, :] = all_ref[3 + 4 * r]
-    ahead_ref[rows:, :] = all_ref[7 - 4 * r]
+    near_ref[N:, :] = all_ref[6 - 4 * r]
+    for i, rel in enumerate((0, 1, 3)):
+        swap_ref[N + FIELDS * i:N + FIELDS * i + FIELDS, :] = all_ref[4 - 4 * r + rel]
+    chain_ref[2 * N:, :] = all_ref[3 + 4 * r]
+    ahead_ref[2 * N:, :] = all_ref[7 - 4 * r]
     copies.wait()
 
 
@@ -218,35 +220,52 @@
                      f_ref.at[z, pl.ds(pl.multiple_of(HALF - HALF * r, HALF), HALF)])
 
 
-def piece_out(copies, r, z_ref, p_ref, own, away, i):
+def parts_in(copies, r, p_ref, parts, rel, other, row, first=0):
+    count = FIELDS - first
+    copies.start(parts.at[4 * r + rel, pl.ds(first, count)], p_ref.at[r, pl.ds(first, count)])
+    copies.start(other.at[pl.ds(row + first, count)], p_ref.at[1 - r, pl.ds(first, count)])
+
+
+def piece_out(r, z_ref, q_ref, own, away):
     for half, dst in ((r, own), (1 - r, away)):
         for z in range(2):
-            copies.start(z_ref.at[z, pl.ds(pl.multiple_of(HALF * half, HALF), HALF)], dst.at[i, pl.ds(HALF * z, HALF)])
-        copies.start(p_ref.at[half, pl.ds(0, PUSHED)], dst.at[i, pl.ds(2 * HALF, PUSHED)])
-
-
-def first_kernel(meta, wave, parts, swap, table, d_ref, q_ref, own, away, f2, f3, p1, p2, z, z3, tab, *rest):
+            dst[HALF * z:HALF * z + HALF, :] = z_ref[z, pl.ds(pl.multiple_of(HALF * half, HALF), HALF), :]
+        dst[2 * HALF:, :] = q_ref[half, :PUSHED, :]
+
+
+def moves_out(moves, wave, *items):
+    for ref, slot in items:
+        moves.start(ref.at[pl.ds(0, N)], wave.at[pl.ds(slot * N, N)])
+
+
+def near_kernel(meta, wave, parts, near, table, d_ref, q_ref, f3, p2, tab, *rest):
     work, sems = rest[:-1], rest[-1]
     r = meta[0]
     copies = Copies(sems)
-    field_in(copies, r, f3, wave, N * (4 * r + 1), swap, N)
-    for p, i in ((p2, 2), (p1, 1)):
-        copies.start(parts.at[4 * r + i], p.at[r])
-        copies.start(swap.at[pl.ds(2 * N + FIELDS * i, FIELDS)], p.at[1 - r])
+    field_in(copies, r, f3, wave, N * (4 * r + 1), near, 0)
+    parts_in(copies, r, p2, parts, 2, near, N)
     copies.start(table, tab)
+    copies.wait()
+    step(f3, p2, p2, tab, d_ref, *work)
+    q_ref[...] = p2[...]
+
+
+def first_kernel(meta, q2, wave, parts, swap, table, q_ref, own, away, f2, p1, pushed, z, tab, *rest):
+    work, sems = rest[:-1], rest[-1]
+    r = meta[0]
+    copies = Copies(sems)
     field_in(copies, r, f2, wave, N * 4 * r, swap, 0)
-    copies.wait()
-    step(f3, p2, tab, z3, *work)
-    copies.start(z3, d_ref)
-    step(f2, p1, tab, f3, *work)
-    copies.start(p1, q_ref)
-    step(f3, p2, tab, z, *work)
-    piece_out(copies, r, z, p2, own, away, 0)
-    copies.wait()
-
-
-def second_kernel(meta, q1, parts, swap, chain, ahead, table, d_ref, q_ref, pushed, own, away,
-                  f0, f1, p0, p1, pm, z0, z1, tab, *rest):
+    parts_in(copies, r, p1, parts, 1, swap, N + FIELDS)
+    copies.start(table, tab)
+    copies.wait()
+    step(f2, p1, p1, tab, z, *work)
+    q_ref[...] = p1[...]
+    step(z, q2, pushed, tab, f2, *work)
+    piece_out(r, f2, pushed, own, away)
+
+
+def second_kernel(meta, q1, parts, swap, chain, ahead, table, d_ref, q_ref, to_back, own, away,
+                  f0, f1, p0, pm, pushed, z, tab, *rest):
     work, sems = rest[:-1], rest[-1]
     r = meta[0]
     copies = Copies(sems)
@@ -255,69 +274,60 @@
     copies.start(chain.at[pl.ds(2 * N, FIELDS)], pm.at[1 - r])
     copies.start(table, tab)
     field_in(copies, r, f1, ahead, N, chain, N)
-    copies.start(parts.at[4 * r], p0.at[r])
-    copies.start(swap.at[pl.ds(2 * N, FIELDS)], p0.at[1 - r])
-    copies.start(q1, p1)
+    parts_in(copies, r, p0, parts, 0, swap, N)
     copies.wait()
 
     @pl.when(meta[1] == 1)
     def _():
         f1[...] = jnp.zeros_like(f1)
 
-    step(f0, pm, tab, z0, *work)
-    copies.start(pm.at[:, pl.ds(0, PUSHED)], pushed)
-    copies.start(z0, d_ref)
-    step(f1, p0, tab, z1, *work)
-    copies.start(p0, q_ref)
-    step(z1, p1, tab, f1, *work)
-    piece_out(copies, r, f1, p1, own, away, 0)
-    copies.wait()
-
-
-def own_out(copies, r, z_ref, wave, slot):
-    for z in range(2):
-        copies.start(z_ref.at[z, pl.ds(pl.multiple_of(HALF * r, HALF), HALF)],
-                     wave.at[pl.ds((4 * r + slot) * N + HALF * z, HALF)])
-
-
-def third_kernel(meta, d_ref, q0, own_a, own_b, back_a, table, own, away, wave, f0, p0, z0, tab, *rest):
+    step(f0, pm, to_back, tab, d_ref, *work)
+    step(f1, p0, p0, tab, z, *work)
+    q_ref[...] = p0[...]
+    step(z, q1, pushed, tab, f1, *work)
+    piece_out(r, f1, pushed, own, away)
+
+
+def third_kernel(meta, d_ref, q0, own_a, own_b, back_a, table, own, away, wave, f0, pushed, z, tab, *rest):
     work, sems = rest[:-1], rest[-1]
     r = meta[0]
     copies, moves = Copies(sems), Copies(sems)
-    moves.used = 16
+    moves.used = 2
     copies.start(d_ref, f0)
-    copies.start(q0, p0)
     copies.start(table, tab)
-    copies.wait()
-    for ref, slot in ((own_a, 4 * r + 2), (own_b, 4 * r + 1), (back_a, 6 - 4 * r)):
-        moves.start(ref.at[0, pl.ds(0, N)], wave.at[pl.ds(slot * N, N)])
+    moves_out(moves, wave, (own_a, 4 * r + 2), (own_b, 4 * r + 1), (back_a, 6 - 4 * r))
+    copies.wait()
 
     @pl.when(meta[1] == 1)
     def _():
         f0[...] = jnp.zeros_like(f0)
 
-    step(f0, p0, tab, z0, *work)
-    piece_out(copies, r, z0, p0, own, away, 0)
-    own_out(moves, r, z0, wave, 0)
-    copies.wait()
+    step(f0, q0, pushed, tab, z, *work)
+    piece_out(r, z, pushed, own, away)
     moves.wait()
 
 
-def fourth_kernel(meta, d_ref, parts, swap, pushed, table, wave_in, own, away, wave, f3, p3, z, tab, *rest):
+def fourth_kernel(meta, d_ref, parts, swap, from_back, own_c, table, wave_in, own, away, wave,
+                  p3, pushed, z, tab, *rest):
     work, sems = rest[:-1], rest[-1]
     r = meta[0]
-    copies = Copies(sems)
-    copies.start(parts.at[4 * r + 3], p3.at[r])
-    copies.start(swap.at[pl.ds(2 * N + FIELDS * 3, FIELDS)], p3.at[1 - r])
-    copies.start(d_ref, f3)
+    copies, moves = Copies(sems), Copies(sems)
+    moves.used = 8
+    parts_in(copies, r, p3, parts, 3, swap, N + 2 * FIELDS, PUSHED)
+    copies.start(from_back, p3.at[:, pl.ds(0, PUSHED)])
     copies.start(table, tab)
-    copies.wait()
-    copies.start(pushed, p3.at[:, pl.ds(0, PUSHED)])
-    copies.wait()
-    step(f3, p3, tab, z, *work)
-    piece_out(copies, r, z, p3, own, away, 0)
-    own_out(copies, r, z, wave, 3)
-    copies.wait()
+    moves_out(moves, wave, (own_c, 4 * r))
+    copies.wait()
+    step(d_ref, p3, pushed, tab, z, *work)
+    piece_out(r, z, pushed, own, away)
+    moves.wait()
+
+
+def late_kernel(meta, back_b, back_c, own_d, wave_in, wave, sems):
+    r = meta[0]
+    moves = Copies(sems)
+    moves_out(moves, wave, (back_b, 5 - 4 * r), (back_c, 4 - 4 * r), (own_d, 4 * r + 3))
+    moves.wait()
 
 
 def final_kernel(meta, *refs):
@@ -325,12 +335,11 @@
     r = meta[0]
     moves, copies = Copies(sems), Copies(sems)
     copies.used = 4
-    for half in range(2):
-        base = 4 * r if half == 0 else 4 - 4 * r
-        for n, (ref, slot) in enumerate(zip(pieces[4 * half:4 * half + 4], (2, 1, 0, 3))):
-            if half == 1 and n > 0:
-                moves.start(ref.at[0, pl.ds(0, N)], wave.at[pl.ds((base + slot) * N, N)])
-            copies.start(ref.at[0, pl.ds(N, PUSHED)], packed.at[base + slot])
+    own, other = 4 * r, 4 - 4 * r
+    for base, group in ((own, pieces[:4]), (other, pieces[4:])):
+        for ref, slot in zip(group, (2, 1, 0, 3)):
+            copies.start(ref.at[pl.ds(N, PUSHED)], packed.at[base + slot])
+    moves_out(moves, wave, (pieces[7], other + 3))
     copies.wait()
     for s in range(8):
         for k in range(ROWS):
@@ -352,36 +361,45 @@
     wave = wavefront.reshape(8 * N, N)
     unit = 1 << 33
 
-    parts, to_swap, to_chain, to_ahead = call(
-        pack_kernel, [(8, FIELDS, N), (2 * N + 4 * FIELDS, N), (2 * N + FIELDS, N), (2 * N + FIELDS, N)],
-        [VM] * 4, [pltpu.VMEM((3, 8, PART), F32), pltpu.VMEM((2, 8, PART), jnp.int32)],
+    full, field = (2, FIELDS, N), (2, N, N)
+    pieces = [(PIECE, N), (PIECE, N)]
+    parts, to_near, to_swap, to_chain, to_ahead = call(
+        pack_kernel, [(8, FIELDS, N), (N + FIELDS, N), (N + 3 * FIELDS, N), (2 * N + FIELDS, N), (2 * N + FIELDS, N)],
+        [VM] * 5, [pltpu.VMEM((3, 8, PART), F32), pltpu.VMEM((2, 8, PART), jnp.int32)],
         16, [SM] + [HB] * 6, 1 << 20, vmem=61000 << 10,
     )(meta, wave, particle_phase, particle_energy, row_offset, row_cell, col_cell)
+    f_ahead = lax.ppermute(to_ahead, both, ahead)
+    f_near = lax.ppermute(to_near, both, swap)
     f_swap = lax.ppermute(to_swap, both, swap)
     f_chain = lax.ppermute(to_chain, both, chain)
-    f_ahead = lax.ppermute(to_ahead, both, ahead)
-
-    d3, q1, own_a, away_a = call(
-        first_kernel, [(2, N, N), (2, FIELDS, N), (1, PIECE, N), (1, PIECE, N)], [ANY] * 4,
-        [FIELD, FIELD, PARTS, PARTS, FIELD, FIELD, TABLE] + WORK, 32, [SM] + [ANY] * 4, 3 * unit,
-    )(meta, wave, parts, f_swap, table)
+
+    d3, q2 = call(
+        near_kernel, [field, full], [VM, VM], [FIELD, PARTS, TABLE] + WORK, 8, [SM] + [ANY] * 4, unit, vmem=59000 << 10,
+    )(meta, wave, parts, f_near, table)
+    q1, own_a, away_a = call(
+        first_kernel, [full] + pieces, [VM] * 3, [FIELD, PARTS, PUSH, FIELD, TABLE] + WORK, 8,
+        [SM, VM] + [ANY] * 4, 2 * unit,
+    )(meta, q2, wave, parts, f_swap, table)
     back_a = lax.ppermute(away_a, both, swap)
-    d0, q0, pushed, own_b, away_b = call(
-        second_kernel, [(2, N, N), (2, FIELDS, N), (2, PUSHED, N), (1, PIECE, N), (1, PIECE, N)], [ANY] * 5,
-        [FIELD, FIELD, PARTS, PARTS, PARTS, FIELD, FIELD, TABLE] + WORK, 32, [SM] + [ANY] * 6, 3 * unit,
+    d0, q0, to_back, own_b, away_b = call(
+        second_kernel, [field, full, (2, PUSHED, N)] + pieces, [VM] * 5,
+        [FIELD, FIELD, PARTS, PARTS, PUSH, FIELD, TABLE] + WORK, 16, [SM, VM] + [ANY] * 5, 3 * unit,
     )(meta, q1, parts, f_swap, f_chain, f_ahead, table)
-    pushed = lax.ppermute(pushed, both, back)
+    from_back = lax.ppermute(to_back, both, back)
     back_b = lax.ppermute(away_b, both, swap)
     own_c, away_c, wave = call(
-        third_kernel, [(1, PIECE, N), (1, PIECE, N), (8 * N, N)], [ANY] * 3,
-        [FIELD, PARTS, FIELD, TABLE] + WORK, 32, [SM] + [ANY] * 6, unit,
+        third_kernel, pieces + [(8 * N, N)], [VM, VM, ANY],
+        [FIELD, PUSH, FIELD, TABLE] + WORK, 8, [SM, ANY, VM] + [ANY] * 4, unit,
     )(meta, d0, q0, own_a, own_b, back_a, table)
     back_c = lax.ppermute(away_c, both, swap)
     own_d, away_d, wave = call(
-        fourth_kernel, [(1, PIECE, N), (1, PIECE, N), (8 * N, N)], [ANY] * 3,
-        [FIELD, PARTS, FIELD, TABLE] + WORK, 32, [SM] + [ANY] * 6, 2 * unit, {6: 2},
-    )(meta, d3, parts, f_swap, pushed, table, wave)
+        fourth_kernel, pieces + [(8 * N, N)], [VM, VM, ANY],
+        [PARTS, PUSH, FIELD, TABLE] + WORK, 12, [SM, VM] + [ANY] * 6, 2 * unit, {7: 2},
+    )(meta, d3, parts, f_swap, from_back, own_c, table, wave)
     back_d = lax.ppermute(away_d, both, swap)
+    wave, = call(
+        late_kernel, [(8 * N, N)], [ANY], [], 4, [SM] + [ANY] * 4, 1 << 20, {4: 0},
+    )(meta, back_b, back_c, own_d, wave)
     wave, phase, energy = call(
         final_kernel, [(8 * N, N), (8, PART), (8, PART)], [HB, VM, VM],
         [pltpu.VMEM((8, PUSHED, N), F32)], 16, [SM] + [ANY] * 8 + [HB], 1 << 20, {9: 0},

time: 88.3 us -> 86.3 us (0.977)
  starting transfers between devices: 14.4 us -> 23.8 us
  waiting for transfers between devices: 22.1 us -> 13.2 us
  Pallas kernels: 47.7 us -> 46 us
    ppermute x1, waiting for transfers between devices: 15.6 us -> 0.44 us  [body(): f_swap = lax.ppermute(to_swap, both, swap)]
    ppermute x1 -> x2, starting transfers between devices: 8.59 us -> 17.7 us  [the longest x1 17.2 us: body(): from_back = lax.ppermute(to_back, both, back)]
    ppermute x1 -> x2, waiting for transfers between devices: 0.01 us -> 6.55 us  [the longest x1 6.55 us: body(): f_near = lax.ppermute(to_near, both, swap)]
    pallas_call x5 -> x7, Pallas kernels: 45.4 us -> 43.7 us  [the longest x1 13.4 us: body(): call(second_kernel, [field, full, (2, PUSHED, N)] + pieces, [VM] * 5, [FI...]
    ppermute x1, waiting for transfers between devices: 6.48 us -> 5.01 us  [body(): back_d = lax.ppermute(away_d, both, swap)]
    ppermute x1, waiting for transfers between devices: 0.01 us -> 1.16 us  [body(): f_chain = lax.ppermute(to_chain, both, chain)]
    ppermute x1, starting transfers between devices: 0.53 us -> 1.57 us  [body(): f_swap = lax.ppermute(to_swap, both, swap)]
    unnamed x12 -> x14, local copies, waits for them, and re-layouts: 2.22 us -> 1.61 us
  transfers between devices with their start and end apart: 8 -> 9, of which waited for: 2 -> 4; matrix products, arithmetic and copies ran while one was open for 0% -> 0% of each run, Pallas kernels for 47% -> 47%
where the time goes in v4:
time: 86.3 us; the launch traced here: 86.1 us
  Pallas kernels  46 us (53%)
  starting transfers between devices  23.8 us (28%)
  waiting for transfers between devices  13.2 us (15%)
  local copies, waits for them, and re-layouts  1.61 us (2%)
  between operations  0.91 us (1%)
    ppermute x1, starting transfers between devices, body(): from_back = lax.ppermute(to_back, both, back)  17.2 us
    pallas_call x1, Pallas kernels, body(): call(second_kernel, [field, full, (2, PUSHED, N)] + pieces, [VM] * 5, [FI...  13.4 us
    pallas_call x1, Pallas kernels, body(): call(first_kernel, [full] + pieces, [VM] * 3, [FIELD, PARTS, PUSH, FIELD,...  8.92 us
    pallas_call x1, Pallas kernels, body(): call(near_kernel, [field, full], [VM, VM], [FIELD, PARTS, TABLE] + WORK,...  7.08 us
    ppermute x1, waiting for transfers between devices, body(): f_near = lax.ppermute(to_near, both, swap)  6.55 us
    ppermute x1, waiting for transfers between devices, body(): back_d = lax.ppermute(away_d, both, swap)  5.01 us
    pallas_call x1, Pallas kernels, body(): call(third_kernel, pieces + [(8 * N, N)], [VM, VM, ANY], [FIELD, PUSH, FI...  4.65 us
    pallas_call x1, Pallas kernels, body(): call(fourth_kernel, pieces + [(8 * N, N)], [VM, VM, ANY], [PARTS, PUSH, F...  4.53 us
  transfers between devices with their start and end apart: 9, of which 4 were waited for; matrix products, arithmetic and copies ran while one was open for 0% of the time, Pallas kernels for 47%

profile of v4, /device:TPU:2, one launch (start us, length us, event | category | flops | bytes accessed | tf_op | source)
XLA Modules:
  0.0 86.1 jit_solution(7165286599560970093)
XLA Ops:
  0.6 0.6 pad_add_fusion.meta
  1.2 3.7 %shard_map.94 = (f32[8,40,256]{2,1,0:T(8,128)}, f32[296,256]{1,0:T(8,128)}, f32[376,256]{1,0:T(8,128)}, f32[552,256]{1,0:T(8,128)}, f32[552,256]{1,0:T(8,128)}) custom-call(s32[2]{0:T(128)} %pad_add_fusion.meta, f32[2048,256]{1,0:T(8,128)} %bitcast.4, f32[8,2048]{1,0:T(8,128)} %refs_0_.1, f32[8,2048]{1,0:T(8,128)} %refs_1_.1, f32[8,2048]{1,0:T(8,128)} %refs_2_.1, ...), custom_call_target="tpu_custom_call" | custom-call | flops 1048576 | bytes 4194304 | tf_op jit(solution)/shard_map/pallas_call | solution.py:366
  4.9 0.5 collective-permute-start
  5.4 1.6 %collective-permute-start.1 = (f32[376,256]{1,0:T(8,128)}, f32[376,256]{1,0:T(8,128)S(1)}, u32[]{:S(2)}, u32[]{:S(2)}) collective-permute-start(f32[376,256]{1,0:T(8,128)} %get-tuple-element.30), channel_id=1, source_target_pairs={{0,1},{1,0},{2,3},{3,2},{4,5},{5,4},{6,7},{7,6},{8,9},{9,8},{10,11... | collective-permute-start | bytes 1155080 | tf_op jit(solution)/shard_map/ppermute | solution.py:373
  7.0 0.0 collective-permute-start.2
  7.0 1.7 %collective-permute-start.3 = (f32[552,256]{1,0:T(8,128)}, f32[552,256]{1,0:T(8,128)S(1)}, u32[]{:S(2)}, u32[]{:S(2)}) collective-permute-start(f32[552,256]{1,0:T(8,128)} %get-tuple-element.34), channel_id=1, source_target_pairs={{0,2},{1,1},{2,4},{3,3},{4,6},{5,5},{6,8},{7,7},{8,10},{9,9},{10,1... | collective-permute-start | bytes 1695752 | tf_op jit(solution)/shard_map/ppermute | solution.py:371
  8.7 6.5 %collective-permute-done.near = f32[296,256]{1,0:T(8,128)S(1)} collective-permute-done((f32[296,256]{1,0:T(8,128)}, f32[296,256]{1,0:T(8,128)S(1)}, u32[]{:S(2)}, u32[]{:S(2)}) %collective-permute-start) | collective-permute-done | bytes 303136 | tf_op jit(solution)/shard_map/ppermute | solution.py:372
  15.3 0.0 copy-start.6
  15.3 0.7 copy-done.6
  16.0 0.0 copy-start
  16.0 0.0 copy-start.1
  16.0 0.0 copy-start.2
  16.0 0.0 copy-start.3
  16.0 7.1 %shard_map.95 = (f32[2,256,256]{2,1,0:T(8,128)}, f32[2,40,256]{2,1,0:T(8,128)}) custom-call(s32[2]{0:T(128)} %pad_add_fusion.meta, f32[2048,256]{1,0:T(8,128)} %bitcast.5, f32[8,40,256]{2,1,0:T(8,128)} %get-tuple-element.27.parts, f32[296,256]{1,0:T(8,128)} %copy-done.6, bf16[2,2,2,256,256]{4,3,2,1,0:T(8,128)(2,1)} %constant.14.clone.table), custom_call_target="tpu_custom_call" | custom-call | flops 8589934592 | bytes 4194304 | tf_op jit(solution)/shard_map/pallas_call | solution.py:376
  23.1 0.4 collective-permute-done.1.swap
  23.5 0.0 copy-done
  23.5 0.0 copy-done.1
  23.5 0.0 copy-done.2
  23.5 0.0 copy-done.3
  23.5 0.0 copy-start.5
  23.5 0.9 %copy-done.5 = f32[2,40,256]{2,1,0:T(8,128)S(1)} copy-done((f32[2,40,256]{2,1,0:T(8,128)S(1)}, f32[2,40,256]{2,1,0:T(8,128)}, u32[]{:S(2)}) %copy-start.5) | copy-done | bytes 81944
  24.4 8.9 %shard_map.96 = (f32[2,40,256]{2,1,0:T(8,128)S(1)}, f32[272,256]{1,0:T(8,128)S(1)}, f32[272,256]{1,0:T(8,128)S(1)}) custom-call(s32[2]{0:T(128)S(1)} %copy-done.1, f32[2,40,256]{2,1,0:T(8,128)S(1)} %copy-done.5, f32[2048,256]{1,0:T(8,128)S(1)} %bitcast.6, f32[8,40,256]{2,1,0:T(8,128)S(1)} %copy-done.2, f32[376,256]{1,0:T(8,128)S(1)} %collective-permute-done.1.swap, ...), custom_call_target="tpu_custom_call" | custom-call | flops 17179869184 | bytes 4194304 | tf_op jit(solution)/shard_map/pallas_call | solution.py:379
  33.3 0.6 collective-permute-start.4
  33.9 1.2 %collective-permute-done.2.chain = f32[552,256]{1,0:T(8,128)S(1)} collective-permute-done((f32[552,256]{1,0:T(8,128)}, f32[552,256]{1,0:T(8,128)S(1)}, u32[]{:S(2)}, u32[]{:S(2)}) %collective-permute-start.2) | collective-permute-done | bytes 565280 | tf_op jit(solution)/shard_map/ppermute | solution.py:374
  35.1 0.0 collective-permute-done.3.ahead
  35.1 13.4 %shard_map.97 = (f32[2,256,256]{2,1,0:T(8,128)S(1)}, f32[2,40,256]{2,1,0:T(8,128)S(1)}, f32[2,16,256]{2,1,0:T(8,128)S(1)}, f32[272,256]{1,0:T(8,128)S(1)}, f32[272,256]{1,0:T(8,128)S(1)}) custom-call(s32[2]{0:T(128)S(1)} %copy-done.1, f32[2,40,256]{2,1,0:T(8,128)S(1)} %get-tuple-element.32.q1, f32[8,40,256]{2,1,0:T(8,128)S(1)} %copy-done.2, ...), custom_call_target="tpu_custom_call" | custom-call | flops 25769803776 | bytes 4194304 | tf_op jit(solution)/shard_map/pallas_call | solution.py:384
  48.5 17.2 %collective-permute-start.5 = (f32[2,16,256]{2,1,0:T(8,128)S(1)}, f32[2,16,256]{2,1,0:T(8,128)S(1)}, u32[]{:S(2)}, u32[]{:S(2)}) collective-permute-start(f32[2,16,256]{2,1,0:T(8,128)S(1)} %get-tuple-element.41), channel_id=1, source_target_pairs={{1,0},{2,1},{3,2},{4,3},{5,4},{6,5},{7,6},{8,7},{9,8},{10,9},{11,1... | collective-permute-start | bytes 98312 | tf_op jit(solution)/shard_map/ppermute | solution.py:388
  65.7 0.1 collective-permute-start.6
  65.8 0.0 collective-permute-done.4.back_a.refs_4_
  65.8 0.0 copy-start.4
  65.8 4.7 %shard_map.98 = (f32[272,256]{1,0:T(8,128)S(1)}, f32[272,256]{1,0:T(8,128)S(1)}, f32[2048,256]{1,0:T(8,128)}) custom-call(s32[2]{0:T(128)S(1)} %copy-done.1, f32[2,256,256]{2,1,0:T(8,128)S(1)} %get-tuple-element.36.d_ref, f32[2,40,256]{2,1,0:T(8,128)S(1)} %get-tuple-element.37.q0, f32[272,256]{1,0:T(8,128)S(1)} %get-tuple-element.31.own_a.refs_0_, ...), custom_call_target="tpu_custom_call" | custom-call | flops 8589934592 | bytes 4194304 | tf_op jit(solution)/shard_map/pallas_call | solution.py:390
  70.5 2.0 %collective-permute-start.7 = (f32[272,256]{1,0:T(8,128)S(1)}, f32[272,256]{1,0:T(8,128)S(1)}, u32[]{:S(2)}, u32[]{:S(2)}) collective-permute-start(f32[272,256]{1,0:T(8,128)S(1)} %get-tuple-element.45), channel_id=1, source_target_pairs={{0,1},{1,0},{2,3},{3,2},{4,5},{5,4},{6,7},{7,6},{8,9},{9,8},{10,11... | collective-permute-start | bytes 835592 | tf_op jit(solution)/shard_map/ppermute | solution.py:394
  72.5 0.0 collective-permute-done.5.from_back
  72.5 0.0 copy-done.4
  72.5 4.5 %shard_map.99 = (f32[272,256]{1,0:T(8,128)S(1)}, f32[272,256]{1,0:T(8,128)S(1)}, f32[2048,256]{1,0:T(8,128)}) custom-call(s32[2]{0:T(128)S(1)} %copy-done.1, f32[2,256,256]{2,1,0:T(8,128)S(1)} %copy-done.4, f32[8,40,256]{2,1,0:T(8,128)S(1)} %copy-done.2, f32[376,256]{1,0:T(8,128)S(1)} %collective-permute-done.1.swap, ...), custom_call_target="tpu_custom_call", output_to_operand_aliasing={{2}: (7, {})} | custom-call | flops 17179869184 | bytes 4194304 | tf_op jit(solution)/shard_map/pallas_call | solution.py:395
  77.1 0.1 collective-permute-start.8
  77.2 0.0 collective-permute-done.6.back_b.refs_5_
  77.2 0.0 collective-permute-done.7.back_c.refs_6_
  77.2 1.5 %shard_map.100.refs_8_ = f32[2048,256]{1,0:T(8,128)} custom-call(s32[2]{0:T(128)S(1)} %copy-done.1, f32[272,256]{1,0:T(8,128)S(1)} %collective-permute-done.6.back_b.refs_5_, f32[272,256]{1,0:T(8,128)S(1)} %collective-permute-done.7.back_c.refs_6_, f32[272,256]{1,0:T(8,128)S(1)} %get-tuple-element.43.own_d.refs_3_, ...), custom_call_target="tpu_custom_call", output_to_operand_aliasing={{}: (4, {})} | custom-call | flops 1048576 | bytes 4194304 | tf_op jit(solution)/shard_map/pallas_call | solution.py:400
  78.7 5.0 %collective-permute-done.8.refs_7_ = f32[272,256]{1,0:T(8,128)S(1)} collective-permute-done((f32[272,256]{1,0:T(8,128)S(1)}, f32[272,256]{1,0:T(8,128)S(1)}, u32[]{:S(2)}, u32[]{:S(2)}) %collective-permute-start.8) | collective-permute-done | bytes 278560 | tf_op jit(solution)/shard_map/ppermute | solution.py:399
  83.7 2.2 %shard_map.101 = (f32[2048,256]{1,0:T(8,128)}, f32[8,2048]{1,0:T(8,128)}, f32[8,2048]{1,0:T(8,128)}) custom-call(s32[2]{0:T(128)S(1)} %copy-done.1, f32[272,256]{1,0:T(8,128)S(1)} %get-tuple-element.31.own_a.refs_0_, f32[272,256]{1,0:T(8,128)S(1)} %get-tuple-element.35.own_b.refs_1_, ...), custom_call_target="tpu_custom_call", output_to_operand_aliasing={{0}: (9, {})} | custom-call | flops 1048576 | bytes 4194304 | tf_op jit(solution)/shard_map/pallas_call | solution.py:403
Async XLA Ops:
  4.9 10.4 %collective-permute-start = (f32[296,256]{1,0:T(8,128)}, f32[296,256]{1,0:T(8,128)S(1)}, u32[]{:S(2)}, u32[]{:S(2)}) collective-permute-start(f32[296,256]{1,0:T(8,128)} %get-tuple-element.28), channel_id=1, source_target_pairs={{0,1},{1,0},{2,3},{3,2},{4,5},{5,4},{6,7},{7,6},{8,9},{9,8},{10,11... | collective-permute-start | bytes 909320 | tf_op jit(solution)/shard_map/ppermute | solution.py:372
  5.4 18.1 %collective-permute-start.1 = (f32[376,256]{1,0:T(8,128)}, f32[376,256]{1,0:T(8,128)S(1)}, u32[]{:S(2)}, u32[]{:S(2)}) collective-permute-start(f32[376,256]{1,0:T(8,128)} %get-tuple-element.30), channel_id=1, source_target_pairs={{0,1},{1,0},{2,3},{3,2},{4,5},{5,4},{6,7},{7,6},{8,9},{9,8},{10,11... | collective-permute-start | bytes 1155080 | tf_op jit(solution)/shard_map/ppermute | solution.py:373
  7.0 28.0 %collective-permute-start.2 = (f32[552,256]{1,0:T(8,128)}, f32[552,256]{1,0:T(8,128)S(1)}, u32[]{:S(2)}, u32[]{:S(2)}) collective-permute-start(f32[552,256]{1,0:T(8,128)} %get-tuple-element.33), channel_id=1, source_target_pairs={{0,1},{1,2},{2,3},{3,4},{4,5},{5,6},{6,7},{7,8},{8,9},{9,10},{10,1... | collective-permute-start | bytes 1695752 | tf_op jit(solution)/shard_map/ppermute | solution.py:374
  7.0 28.0 %collective-permute-start.3 = (f32[552,256]{1,0:T(8,128)}, f32[552,256]{1,0:T(8,128)S(1)}, u32[]{:S(2)}, u32[]{:S(2)}) collective-permute-start(f32[552,256]{1,0:T(8,128)} %get-tuple-element.34), channel_id=1, source_target_pairs={{0,2},{1,1},{2,4},{3,3},{4,6},{5,5},{6,8},{7,7},{8,10},{9,9},{10,1... | collective-permute-start | bytes 1695752 | tf_op jit(solution)/shard_map/ppermute | solution.py:371
  15.3 0.7 copy-start.6
  16.0 7.5 %copy-start = (f32[8,2,128,256]{3,2,1,0:T(8,128)S(1)}, f32[8,2,128,256]{3,2,1,0:T(8,128)}, u32[]{:S(2)}) copy-start(f32[8,2,128,256]{3,2,1,0:T(8,128)} %param.7) | copy-start | bytes 6291460
  16.0 7.5 %copy-start.1 = (s32[2]{0:T(128)S(1)}, s32[2]{0:T(128)}, u32[]{:S(2)}) copy-start(s32[2]{0:T(128)} %pad_add_fusion.meta) | copy-start | bytes 28
  16.0 7.5 %copy-start.2 = (f32[8,40,256]{2,1,0:T(8,128)S(1)}, f32[8,40,256]{2,1,0:T(8,128)}, u32[]{:S(2)}) copy-start(f32[8,40,256]{2,1,0:T(8,128)} %get-tuple-element.27.parts) | copy-start | bytes 983044
  16.0 7.5 %copy-start.3 = (bf16[2,2,2,256,256]{4,3,2,1,0:T(8,128)(2,1)S(1)}, bf16[2,2,2,256,256]{4,3,2,1,0:T(8,128)(2,1)}, u32[]{:S(2)}) copy-start(bf16[2,2,2,256,256]{4,3,2,1,0:T(8,128)(2,1)} %constant.14.clone.table) | copy-start | bytes 3145732
  23.5 0.9 %copy-start.5 = (f32[2,40,256]{2,1,0:T(8,128)S(1)}, f32[2,40,256]{2,1,0:T(8,128)}, u32[]{:S(2)}) copy-start(f32[2,40,256]{2,1,0:T(8,128)} %get-tuple-element.29.q2) | copy-start | bytes 245764
  33.3 32.5 %collective-permute-start.4 = (f32[272,256]{1,0:T(8,128)S(1)}, f32[272,256]{1,0:T(8,128)S(1)}, u32[]{:S(2)}, u32[]{:S(2)}) collective-permute-start(f32[272,256]{1,0:T(8,128)S(1)} %get-tuple-element.38), channel_id=1, source_target_pairs={{0,1},{1,0},{2,3},{3,2},{4,5},{5,4},{6,7},{7,6},{8,9},{9,8},{10,11... | collective-permute-start | bytes 835592 | tf_op jit(solution)/shard_map/ppermute | solution.py:383
  48.5 24.0 %collective-permute-start.5 = (f32[2,16,256]{2,1,0:T(8,128)S(1)}, f32[2,16,256]{2,1,0:T(8,128)S(1)}, u32[]{:S(2)}, u32[]{:S(2)}) collective-permute-start(f32[2,16,256]{2,1,0:T(8,128)S(1)} %get-tuple-element.41), channel_id=1, source_target_pairs={{1,0},{2,1},{3,2},{4,3},{5,4},{6,5},{7,6},{8,7},{9,8},{10,9},{11,1... | collective-permute-start | bytes 98312 | tf_op jit(solution)/shard_map/ppermute | solution.py:388
  65.7 11.5 %collective-permute-start.6 = (f32[272,256]{1,0:T(8,128)S(1)}, f32[272,256]{1,0:T(8,128)S(1)}, u32[]{:S(2)}, u32[]{:S(2)}) collective-permute-start(f32[272,256]{1,0:T(8,128)S(1)} %get-tuple-element.44), channel_id=1, source_target_pairs={{0,1},{1,0},{2,3},{3,2},{4,5},{5,4},{6,7},{7,6},{8,9},{9,8},{10,11... | collective-permute-start | bytes 835592 | tf_op jit(solution)/shard_map/ppermute | solution.py:389
  65.8 6.7 %copy-start.4 = (f32[2,256,256]{2,1,0:T(8,128)S(1)}, f32[2,256,256]{2,1,0:T(8,128)}, u32[]{:S(2)}) copy-start(f32[2,256,256]{2,1,0:T(8,128)} %get-tuple-element.40.d_ref) | copy-start | bytes 1572868
  70.5 6.7 %collective-permute-start.7 = (f32[272,256]{1,0:T(8,128)S(1)}, f32[272,256]{1,0:T(8,128)S(1)}, u32[]{:S(2)}, u32[]{:S(2)}) collective-permute-start(f32[272,256]{1,0:T(8,128)S(1)} %get-tuple-element.45), channel_id=1, source_target_pairs={{0,1},{1,0},{2,3},{3,2},{4,5},{5,4},{6,7},{7,6},{8,9},{9,8},{10,11... | collective-permute-start | bytes 835592 | tf_op jit(solution)/shard_map/ppermute | solution.py:394
  77.1 6.6 %collective-permute-start.8 = (f32[272,256]{1,0:T(8,128)S(1)}, f32[272,256]{1,0:T(8,128)S(1)}, u32[]{:S(2)}, u32[]{:S(2)}) collective-permute-start(f32[272,256]{1,0:T(8,128)S(1)} %get-tuple-element.46), channel_id=1, source_target_pairs={{0,1},{1,0},{2,3},{3,2},{4,5},{5,4},{6,7},{7,6},{8,9},{9,8},{10,11... | collective-permute-start | bytes 835592 | tf_op jit(solution)/shard_map/ppermute | solution.py:399

commit v5 on v4

--- a/solution.py
+++ b/solution.py
@@ -68,7 +68,7 @@
     return jnp.dot(a, b, preferred_element_type=F32)
 
 
-def step(f_ref, p_ref, q_ref, tab, out_ref, c_ref, w_ref, s_ref, sr_ref, x_ref, samp_ref, c8_ref, sr8_ref):
+def step(f_ref, p_ref, q_ref, tab, out_ref, c_ref, w_ref, s_ref, sr_ref, x_ref, samp_ref, c8_ref, sr8_ref, ready=None):
     iota_c = (lax.broadcasted_iota(jnp.int32, (16, 16, N), 0) * 16
               + lax.broadcasted_iota(jnp.int32, (16, 16, N), 1)).astype(F32).astype(BF)
     one = jnp.ones((16, N), BF)
@@ -124,6 +124,8 @@
             x_ref[HALF * h:HALF * h + HALF, N * z:N * z + N] = (
                 f_ref[z, HALF * h:HALF * h + HALF, :]
                 + d[HALF * z:HALF * z + HALF])
+    if ready is not None:
+        ready.wait()
     quads = [[], []]
     for z in range(2):
         top = x_ref[:HALF, N * z:N * z + N]
@@ -241,47 +243,61 @@
 def near_kernel(meta, wave, parts, near, table, d_ref, q_ref, f3, p2, tab, *rest):
     work, sems = rest[:-1], rest[-1]
     r = meta[0]
-    copies = Copies(sems)
+    copies, later = Copies(sems), Copies(sems)
+    later.used = 7
     field_in(copies, r, f3, wave, N * (4 * r + 1), near, 0)
     parts_in(copies, r, p2, parts, 2, near, N)
-    copies.start(table, tab)
-    copies.wait()
-    step(f3, p2, p2, tab, d_ref, *work)
+    later.start(table, tab)
+    copies.wait()
+    step(f3, p2, p2, tab, d_ref, *work, ready=later)
     q_ref[...] = p2[...]
 
 
 def first_kernel(meta, q2, wave, parts, swap, table, q_ref, own, away, f2, p1, pushed, z, tab, *rest):
     work, sems = rest[:-1], rest[-1]
     r = meta[0]
-    copies = Copies(sems)
+    copies, later = Copies(sems), Copies(sems)
+    later.used = 7
     field_in(copies, r, f2, wave, N * 4 * r, swap, 0)
     parts_in(copies, r, p1, parts, 1, swap, N + FIELDS)
-    copies.start(table, tab)
-    copies.wait()
-    step(f2, p1, p1, tab, z, *work)
+    later.start(table, tab)
+    copies.wait()
+    step(f2, p1, p1, tab, z, *work, ready=later)
     q_ref[...] = p1[...]
     step(z, q2, pushed, tab, f2, *work)
     piece_out(r, f2, pushed, own, away)
 
 
-def second_kernel(meta, q1, parts, swap, chain, ahead, table, d_ref, q_ref, to_back, own, away,
+def second_kernel(meta, q1, parts, swap, chain, ahead, relay, table, d_ref, q_ref, to_back, own, away,
                   f0, f1, p0, pm, pushed, z, tab, *rest):
     work, sems = rest[:-1], rest[-1]
     r = meta[0]
-    copies = Copies(sems)
+    copies, later = Copies(sems), Copies(sems)
+    later.used = 23
     field_in(copies, r, f0, ahead, 0, chain, 0)
     copies.start(ahead.at[pl.ds(2 * N, FIELDS)], pm.at[r])
     copies.start(chain.at[pl.ds(2 * N, FIELDS)], pm.at[1 - r])
-    copies.start(table, tab)
+    later.start(table, tab)
     field_in(copies, r, f1, ahead, N, chain, N)
     parts_in(copies, r, p0, parts, 0, swap, N)
     copies.wait()
+
+    @pl.when(meta[2] == 1)
+    def _():
+        again = Copies(sems)
+        again.used = 15
+        for i, f in enumerate((f0, f1)):
+            for z in range(2):
+                again.start(relay.at[pl.ds(N * i + HALF * z, HALF)],
+                            f.at[z, pl.ds(pl.multiple_of(HALF * r, HALF), HALF)])
+        again.start(relay.at[pl.ds(2 * N, FIELDS)], pm.at[r])
+        again.wait()
 
     @pl.when(meta[1] == 1)
     def _():
         f1[...] = jnp.zeros_like(f1)
 
-    step(f0, pm, to_back, tab, d_ref, *work)
+    step(f0, pm, to_back, tab, d_ref, *work, ready=later)
     step(f1, p0, p0, tab, z, *work)
     q_ref[...] = p0[...]
     step(z, q1, pushed, tab, f1, *work)
@@ -291,10 +307,11 @@
 def third_kernel(meta, d_ref, q0, own_a, own_b, back_a, table, own, away, wave, f0, pushed, z, tab, *rest):
     work, sems = rest[:-1], rest[-1]
     r = meta[0]
-    copies, moves = Copies(sems), Copies(sems)
+    copies, moves, later = Copies(sems), Copies(sems), Copies(sems)
+    later.used = 11
     moves.used = 2
     copies.start(d_ref, f0)
-    copies.start(table, tab)
+    later.start(table, tab)
     moves_out(moves, wave, (own_a, 4 * r + 2), (own_b, 4 * r + 1), (back_a, 6 - 4 * r))
     copies.wait()
 
@@ -302,7 +319,7 @@
     def _():
         f0[...] = jnp.zeros_like(f0)
 
-    step(f0, q0, pushed, tab, z, *work)
+    step(f0, q0, pushed, tab, z, *work, ready=later)
     piece_out(r, z, pushed, own, away)
     moves.wait()
 
@@ -311,14 +328,15 @@
                   p3, pushed, z, tab, *rest):
     work, sems = rest[:-1], rest[-1]
     r = meta[0]
-    copies, moves = Copies(sems), Copies(sems)
+    copies, moves, later = Copies(sems), Copies(sems), Copies(sems)
+    later.used = 11
     moves.used = 8
     parts_in(copies, r, p3, parts, 3, swap, N + 2 * FIELDS, PUSHED)
     copies.start(from_back, p3.at[:, pl.ds(0, PUSHED)])
-    copies.start(table, tab)
+    later.start(table, tab)
     moves_out(moves, wave, (own_c, 4 * r))
     copies.wait()
-    step(d_ref, p3, pushed, tab, z, *work)
+    step(d_ref, p3, pushed, tab, z, *work, ready=later)
     piece_out(r, z, pushed, own, away)
     moves.wait()
 
@@ -355,9 +373,13 @@
     both = ("tm", "row")
     swap = [(i, i ^ 1) for i in range(2 * nt)]
     chain = [(i, (i + 1) % (2 * nt)) for i in range(2 * nt)]
-    ahead = [(i, (i + 2) % (2 * nt) if i % 2 == 0 else i) for i in range(2 * nt)]
+    far = [2 * t for t in range(nt) if (t + 1) % (nt // 2) == 0]
+    ahead = [(i, i + 2 if i % 2 == 0 else i) for i in range(2 * nt) if i not in far]
+    around = [(i, (i + 3) % (2 * nt)) for i in far]
+    onward = [(j, j - 1) for i, j in around]
     back = [(j, i) for i, j in chain]
-    meta = jnp.stack([r, (lax.axis_index(both) == 0).astype(jnp.int32)]).astype(jnp.int32)
+    index = lax.axis_index(both)
+    meta = jnp.stack([r, (index == 0).astype(jnp.int32), (index % nt == 0).astype(jnp.int32)]).astype(jnp.int32)
     wave = wavefront.reshape(8 * N, N)
     unit = 1 << 33
 
@@ -369,6 +391,7 @@
         16, [SM] + [HB] * 6, 1 << 20, vmem=61000 << 10,
     )(meta, wave, particle_phase, particle_energy, row_offset, row_cell, col_cell)
     f_ahead = lax.ppermute(to_ahead, both, ahead)
+    f_around = lax.ppermute(to_ahead, both, around)
     f_near = lax.ppermute(to_near, both, swap)
     f_swap = lax.ppermute(to_swap, both, swap)
     f_chain = lax.ppermute(to_chain, both, chain)
@@ -376,6 +399,8 @@
     d3, q2 = call(
         near_kernel, [field, full], [VM, VM], [FIELD, PARTS, TABLE] + WORK, 8, [SM] + [ANY] * 4, unit, vmem=59000 << 10,
     )(meta, wave, parts, f_near, table)
+    q2, f_around = lax.optimization_barrier((q2, f_around))
+    f_relay = lax.ppermute(f_around, both, onward)
     q1, own_a, away_a = call(
         first_kernel, [full] + pieces, [VM] * 3, [FIELD, PARTS, PUSH, FIELD, TABLE] + WORK, 8,
         [SM, VM] + [ANY] * 4, 2 * unit,
@@ -383,13 +408,13 @@
     back_a = lax.ppermute(away_a, both, swap)
     d0, q0, to_back, own_b, away_b = call(
         second_kernel, [field, full, (2, PUSHED, N)] + pieces, [VM] * 5,
-        [FIELD, FIELD, PARTS, PARTS, PUSH, FIELD, TABLE] + WORK, 16, [SM, VM] + [ANY] * 5, 3 * unit,
-    )(meta, q1, parts, f_swap, f_chain, f_ahead, table)
+        [FIELD, FIELD, PARTS, PARTS, PUSH, FIELD, TABLE] + WORK, 24, [SM, VM] + [ANY] * 6, 3 * unit,
+    )(meta, q1, parts, f_swap, f_chain, f_ahead, f_relay, table)
     from_back = lax.ppermute(to_back, both, back)
     back_b = lax.ppermute(away_b, both, swap)
     own_c, away_c, wave = call(
         third_kernel, pieces + [(8 * N, N)], [VM, VM, ANY],
-        [FIELD, PUSH, FIELD, TABLE] + WORK, 8, [SM, ANY, VM] + [ANY] * 4, unit,
+        [FIELD, PUSH, FIELD, TABLE] + WORK, 12, [SM, ANY, VM] + [ANY] * 4, unit,
     )(meta, d0, q0, own_a, own_b, back_a, table)
     back_c = lax.ppermute(away_c, both, swap)
     own_d, away_d, wave = call(

time: 86.3 us -> 80.4 us (0.932)
  the two profiles are of different devices: /device:TPU:2 before, /device:TPU:4 now
where the time goes in v5:
time: 80.4 us; the launch traced here: 80.1 us
  Pallas kernels  46.7 us (58%)
  waiting for transfers between devices  16 us (20%)
  starting transfers between devices  14.2 us (18%)
  local copies, waits for them, and re-layouts  1.61 us (2%)
  between operations  0.99 us (1%)
    pallas_call x1, Pallas kernels, body(): call(second_kernel, [field, full, (2, PUSHED, N)] + pieces, [VM] * 5, [FI...  14.3 us
    pallas_call x1, Pallas kernels, body(): call(first_kernel, [full] + pieces, [VM] * 3, [FIELD, PARTS, PUSH, FIELD,...  8.96 us
    ppermute x1, waiting for transfers between devices, body(): f_relay = lax.ppermute(f_around, both, onward)  6.93 us
    pallas_call x1, Pallas kernels, body(): call(near_kernel, [field, full], [VM, VM], [FIELD, PARTS, TABLE] + WORK,...  6.74 us
    pallas_call x1, Pallas kernels, body(): call(third_kernel, pieces + [(8 * N, N)], [VM, VM, ANY], [FIELD, PUSH, FI...  4.74 us
    pallas_call x1, Pallas kernels, body(): call(fourth_kernel, pieces + [(8 * N, N)], [VM, VM, ANY], [PARTS, PUSH, F...  4.58 us
    ppermute x1, waiting for transfers between devices, body(): f_near = lax.ppermute(to_near, both, swap)  4.32 us
    pallas_call x1, Pallas kernels, body(): call(pack_kernel, [(8, FIELDS, N), (N + FIELDS, N), (N + 3 * FIELDS, N),...  3.68 us
  transfers between devices with their start and end apart: 11, of which 4 were waited for; matrix products, arithmetic and copies ran while one was open for 0% of the time, Pallas kernels for 51%

profile of v5, /device:TPU:4, one launch (start us, length us, event | category | flops | bytes accessed | tf_op | source)
XLA Modules:
  0.0 80.1 jit_solution(7558261698559661220)
XLA Ops:
  0.6 0.6 pad_add_fusion.meta
  1.2 3.7 %shard_map.94 = (f32[8,40,256]{2,1,0:T(8,128)}, f32[296,256]{1,0:T(8,128)}, f32[376,256]{1,0:T(8,128)}, f32[552,256]{1,0:T(8,128)}, f32[552,256]{1,0:T(8,128)}) custom-call(s32[3]{0:T(128)} %pad_add_fusion.meta, f32[2048,256]{1,0:T(8,128)} %bitcast.5, f32[8,2048]{1,0:T(8,128)} %refs_0_.1, f32[8,2048]{1,0:T(8,128)} %refs_1_.1, f32[8,2048]{1,0:T(8,128)} %refs_2_.1, ...), custom_call_target="tpu_custom_call" | custom-call | flops 1048576 | bytes 4194304 | tf_op jit(solution)/shard_map/pallas_call | solution.py:388
  4.9 1.3 %collective-permute-start = (f32[296,256]{1,0:T(8,128)}, f32[296,256]{1,0:T(8,128)S(1)}, u32[]{:S(2)}, u32[]{:S(2)}) collective-permute-start(f32[296,256]{1,0:T(8,128)} %get-tuple-element.30), channel_id=1, source_target_pairs={{0,1},{1,0},{2,3},{3,2},{4,5},{5,4},{6,7},{7,6},{8,9},{9,8},{10,11... | collective-permute-start | bytes 909320 | tf_op jit(solution)/shard_map/ppermute | solution.py:395
  6.2 1.5 %collective-permute-start.4 = (f32[552,256]{1,0:T(8,128)}, f32[552,256]{1,0:T(8,128)S(1)}, u32[]{:S(2)}, u32[]{:S(2)}) collective-permute-start(f32[552,256]{1,0:T(8,128)} %get-tuple-element.32), channel_id=1, source_target_pairs={{0,2},{1,1},{2,4},{3,3},{4,6},{5,5},{6,8},{7,7},{8,10},{9,9},{10,1... | collective-permute-start | bytes 1695752 | tf_op jit(solution)/shard_map/ppermute | solution.py:393
  7.7 0.7 collective-permute-start.1
  8.4 1.7 %collective-permute-start.2 = (f32[376,256]{1,0:T(8,128)}, f32[376,256]{1,0:T(8,128)S(1)}, u32[]{:S(2)}, u32[]{:S(2)}) collective-permute-start(f32[376,256]{1,0:T(8,128)} %get-tuple-element.34), channel_id=1, source_target_pairs={{0,1},{1,0},{2,3},{3,2},{4,5},{5,4},{6,7},{7,6},{8,9},{9,8},{10,11... | collective-permute-start | bytes 1155080 | tf_op jit(solution)/shard_map/ppermute | solution.py:396
  10.1 0.4 collective-permute-start.3
  10.5 4.3 %collective-permute-done.near = f32[296,256]{1,0:T(8,128)S(1)} collective-permute-done((f32[296,256]{1,0:T(8,128)}, f32[296,256]{1,0:T(8,128)S(1)}, u32[]{:S(2)}, u32[]{:S(2)}) %collective-permute-start) | collective-permute-done | bytes 303136 | tf_op jit(solution)/shard_map/ppermute | solution.py:395
  14.8 0.0 copy-start.6
  14.8 0.7 copy-done.6
  15.6 0.0 copy-start
  15.6 0.0 copy-start.1
  15.6 0.0 copy-start.2
  15.6 0.0 copy-start.3
  15.6 6.7 %shard_map.95 = (f32[2,256,256]{2,1,0:T(8,128)}, f32[2,40,256]{2,1,0:T(8,128)}) custom-call(s32[3]{0:T(128)} %pad_add_fusion.meta, f32[2048,256]{1,0:T(8,128)} %bitcast.6, f32[8,40,256]{2,1,0:T(8,128)} %get-tuple-element.29.parts, f32[296,256]{1,0:T(8,128)} %copy-done.6, bf16[2,2,2,256,256]{4,3,2,1,0:T(8,128)(2,1)} %constant.26.clone.table), custom_call_target="tpu_custom_call" | custom-call | flops 8589934592 | bytes 4194304 | tf_op jit(solution)/shard_map/pallas_call | solution.py:399
  22.3 0.0 collective-permute-done.1
  22.3 1.3 %collective-permute-start.5 = (f32[552,256]{1,0:T(8,128)S(1)}, f32[552,256]{1,0:T(8,128)S(1)}, u32[]{:S(2)}, u32[]{:S(2)}) collective-permute-start(f32[552,256]{1,0:T(8,128)S(1)} %collective-permute-done.1), channel_id=1, source_target_pairs={{65,64},{1,0}} | collective-permute-start | bytes 1695752 | tf_op jit(solution)/shard_map/ppermute | solution.py:403
  23.6 0.0 collective-permute-done.2.swap
  23.6 0.0 copy-done
  23.6 0.0 copy-done.1
  23.6 0.0 copy-done.2
  23.7 0.0 copy-done.3
  23.7 0.0 copy-start.5
  23.7 0.9 %copy-done.5 = f32[2,40,256]{2,1,0:T(8,128)S(1)} copy-done((f32[2,40,256]{2,1,0:T(8,128)S(1)}, f32[2,40,256]{2,1,0:T(8,128)}, u32[]{:S(2)}) %copy-start.5) | copy-done | bytes 81944
  24.6 9.0 %shard_map.96 = (f32[2,40,256]{2,1,0:T(8,128)S(1)}, f32[272,256]{1,0:T(8,128)S(1)}, f32[272,256]{1,0:T(8,128)S(1)}) custom-call(s32[3]{0:T(128)S(1)} %copy-done.1, f32[2,40,256]{2,1,0:T(8,128)S(1)} %copy-done.5, f32[2048,256]{1,0:T(8,128)S(1)} %bitcast.7, f32[8,40,256]{2,1,0:T(8,128)S(1)} %copy-done.2, f32[376,256]{1,0:T(8,128)S(1)} %collective-permute-done.2.swap, ...), custom_call_target="tpu_custom_call" | custom-call | flops 17179869184 | bytes 4194304 | tf_op jit(solution)/shard_map/pallas_call | solution.py:404
  33.5 3.1 %collective-permute-start.6 = (f32[272,256]{1,0:T(8,128)S(1)}, f32[272,256]{1,0:T(8,128)S(1)}, u32[]{:S(2)}, u32[]{:S(2)}) collective-permute-start(f32[272,256]{1,0:T(8,128)S(1)} %get-tuple-element.42), channel_id=1, source_target_pairs={{0,1},{1,0},{2,3},{3,2},{4,5},{5,4},{6,7},{7,6},{8,9},{9,8},{10,11... | collective-permute-start | bytes 835592 | tf_op jit(solution)/shard_map/ppermute | solution.py:408
  36.6 0.0 collective-permute-done.3.chain
  36.6 0.0 collective-permute-done.4.ahead
  36.6 6.9 %collective-permute-done.5.relay = f32[552,256]{1,0:T(8,128)S(1)} collective-permute-done((f32[552,256]{1,0:T(8,128)S(1)}, f32[552,256]{1,0:T(8,128)S(1)}, u32[]{:S(2)}, u32[]{:S(2)}) %collective-permute-start.5) | collective-permute-done | bytes 565280 | tf_op jit(solution)/shard_map/ppermute | solution.py:403
  43.6 14.3 %shard_map.97 = (f32[2,256,256]{2,1,0:T(8,128)S(1)}, f32[2,40,256]{2,1,0:T(8,128)S(1)}, f32[2,16,256]{2,1,0:T(8,128)S(1)}, f32[272,256]{1,0:T(8,128)S(1)}, f32[272,256]{1,0:T(8,128)S(1)}) custom-call(s32[3]{0:T(128)S(1)} %copy-done.1, f32[2,40,256]{2,1,0:T(8,128)S(1)} %get-tuple-element.36.q1, f32[8,40,256]{2,1,0:T(8,128)S(1)} %copy-done.2, ...), custom_call_target="tpu_custom_call" | custom-call | flops 25769803776 | bytes 4194304 | tf_op jit(solution)/shard_map/pallas_call | solution.py:409
  57.9 0.1 collective-permute-start.7
  58.0 2.0 %collective-permute-start.8 = (f32[272,256]{1,0:T(8,128)S(1)}, f32[272,256]{1,0:T(8,128)S(1)}, u32[]{:S(2)}, u32[]{:S(2)}) collective-permute-start(f32[272,256]{1,0:T(8,128)S(1)} %get-tuple-element.48), channel_id=1, source_target_pairs={{0,1},{1,0},{2,3},{3,2},{4,5},{5,4},{6,7},{7,6},{8,9},{9,8},{10,11... | collective-permute-start | bytes 835592 | tf_op jit(solution)/shard_map/ppermute | solution.py:414
  60.0 0.0 collective-permute-done.6.back_a.refs_4_
  60.0 0.0 copy-start.4
  60.0 4.7 %shard_map.98 = (f32[272,256]{1,0:T(8,128)S(1)}, f32[272,256]{1,0:T(8,128)S(1)}, f32[2048,256]{1,0:T(8,128)}) custom-call(s32[3]{0:T(128)S(1)} %copy-done.1, f32[2,256,256]{2,1,0:T(8,128)S(1)} %get-tuple-element.40.d_ref, f32[2,40,256]{2,1,0:T(8,128)S(1)} %get-tuple-element.41.q0, f32[272,256]{1,0:T(8,128)S(1)} %get-tuple-element.35.own_a.refs_0_, ...), custom_call_target="tpu_custom_call" | custom-call | flops 8589934592 | bytes 4194304 | tf_op jit(solution)/shard_map/pallas_call | solution.py:415
  64.7 0.2 collective-permute-start.9
  64.9 0.0 collective-permute-done.7.from_back
  64.9 0.0 copy-done.4
  64.9 4.6 %shard_map.99 = (f32[272,256]{1,0:T(8,128)S(1)}, f32[272,256]{1,0:T(8,128)S(1)}, f32[2048,256]{1,0:T(8,128)}) custom-call(s32[3]{0:T(128)S(1)} %copy-done.1, f32[2,256,256]{2,1,0:T(8,128)S(1)} %copy-done.4, f32[8,40,256]{2,1,0:T(8,128)S(1)} %copy-done.2, f32[376,256]{1,0:T(8,128)S(1)} %collective-permute-done.2.swap, ...), custom_call_target="tpu_custom_call", output_to_operand_aliasing={{2}: (7, {})} | custom-call | flops 17179869184 | bytes 4194304 | tf_op jit(solution)/shard_map/pallas_call | solution.py:420
  69.5 2.0 %collective-permute-start.10 = (f32[272,256]{1,0:T(8,128)S(1)}, f32[272,256]{1,0:T(8,128)S(1)}, u32[]{:S(2)}, u32[]{:S(2)}) collective-permute-start(f32[272,256]{1,0:T(8,128)S(1)} %get-tuple-element.50), channel_id=1, source_target_pairs={{0,1},{1,0},{2,3},{3,2},{4,5},{5,4},{6,7},{7,6},{8,9},{9,8},{10,11... | collective-permute-start | bytes 835592 | tf_op jit(solution)/shard_map/ppermute | solution.py:424
  71.5 0.0 collective-permute-done.8.back_b.refs_5_
  71.5 1.5 %collective-permute-done.9.back_c.refs_6_ = f32[272,256]{1,0:T(8,128)S(1)} collective-permute-done((f32[272,256]{1,0:T(8,128)S(1)}, f32[272,256]{1,0:T(8,128)S(1)}, u32[]{:S(2)}, u32[]{:S(2)}) %collective-permute-start.9) | collective-permute-done | bytes 278560 | tf_op jit(solution)/shard_map/ppermute | solution.py:419
  73.0 1.5 %shard_map.100.refs_8_ = f32[2048,256]{1,0:T(8,128)} custom-call(s32[3]{0:T(128)S(1)} %copy-done.1, f32[272,256]{1,0:T(8,128)S(1)} %collective-permute-done.8.back_b.refs_5_, f32[272,256]{1,0:T(8,128)S(1)} %collective-permute-done.9.back_c.refs_6_, f32[272,256]{1,0:T(8,128)S(1)} %get-tuple-element.47.own_d.refs_3_, ...), custom_call_target="tpu_custom_call", output_to_operand_aliasing={{}: (4, {})} | custom-call | flops 1048576 | bytes 4194304 | tf_op jit(solution)/shard_map/pallas_call | solution.py:425
  74.5 3.3 %collective-permute-done.10.refs_7_ = f32[272,256]{1,0:T(8,128)S(1)} collective-permute-done((f32[272,256]{1,0:T(8,128)S(1)}, f32[272,256]{1,0:T(8,128)S(1)}, u32[]{:S(2)}, u32[]{:S(2)}) %collective-permute-start.10) | collective-permute-done | bytes 278560 | tf_op jit(solution)/shard_map/ppermute | solution.py:424
  77.7 2.2 %shard_map.101 = (f32[2048,256]{1,0:T(8,128)}, f32[8,2048]{1,0:T(8,128)}, f32[8,2048]{1,0:T(8,128)}) custom-call(s32[3]{0:T(128)S(1)} %copy-done.1, f32[272,256]{1,0:T(8,128)S(1)} %get-tuple-element.35.own_a.refs_0_, f32[272,256]{1,0:T(8,128)S(1)} %get-tuple-element.39.own_b.refs_1_, ...), custom_call_target="tpu_custom_call", output_to_operand_aliasing={{0}: (9, {})} | custom-call | flops 1048576 | bytes 4194304 | tf_op jit(solution)/shard_map/pallas_call | solution.py:428
Async XLA Ops:
  4.9 9.9 %collective-permute-start = (f32[296,256]{1,0:T(8,128)}, f32[296,256]{1,0:T(8,128)S(1)}, u32[]{:S(2)}, u32[]{:S(2)}) collective-permute-start(f32[296,256]{1,0:T(8,128)} %get-tuple-element.30), channel_id=1, source_target_pairs={{0,1},{1,0},{2,3},{3,2},{4,5},{5,4},{6,7},{7,6},{8,9},{9,8},{10,11... | collective-permute-start | bytes 909320 | tf_op jit(solution)/shard_map/ppermute | solution.py:395
  6.2 30.4 %collective-permute-start.4 = (f32[552,256]{1,0:T(8,128)}, f32[552,256]{1,0:T(8,128)S(1)}, u32[]{:S(2)}, u32[]{:S(2)}) collective-permute-start(f32[552,256]{1,0:T(8,128)} %get-tuple-element.32), channel_id=1, source_target_pairs={{0,2},{1,1},{2,4},{3,3},{4,6},{5,5},{6,8},{7,7},{8,10},{9,9},{10,1... | collective-permute-start | bytes 1695752 | tf_op jit(solution)/shard_map/ppermute | solution.py:393
  7.7 14.6 %collective-permute-start.1 = (f32[552,256]{1,0:T(8,128)}, f32[552,256]{1,0:T(8,128)S(1)}, u32[]{:S(2)}, u32[]{:S(2)}) collective-permute-start(f32[552,256]{1,0:T(8,128)} %get-tuple-element.32), channel_id=1, source_target_pairs={{62,65},{126,1}} | collective-permute-start | bytes 1695752 | tf_op jit(solution)/shard_map/ppermute | solution.py:394
  8.4 15.2 %collective-permute-start.2 = (f32[376,256]{1,0:T(8,128)}, f32[376,256]{1,0:T(8,128)S(1)}, u32[]{:S(2)}, u32[]{:S(2)}) collective-permute-start(f32[376,256]{1,0:T(8,128)} %get-tuple-element.34), channel_id=1, source_target_pairs={{0,1},{1,0},{2,3},{3,2},{4,5},{5,4},{6,7},{7,6},{8,9},{9,8},{10,11... | collective-permute-start | bytes 1155080 | tf_op jit(solution)/shard_map/ppermute | solution.py:396
  10.1 26.5 %collective-permute-start.3 = (f32[552,256]{1,0:T(8,128)}, f32[552,256]{1,0:T(8,128)S(1)}, u32[]{:S(2)}, u32[]{:S(2)}) collective-permute-start(f32[552,256]{1,0:T(8,128)} %get-tuple-element.37), channel_id=1, source_target_pairs={{0,1},{1,2},{2,3},{3,4},{4,5},{5,6},{6,7},{7,8},{8,9},{9,10},{10,1... | collective-permute-start | bytes 1695752 | tf_op jit(solution)/shard_map/ppermute | solution.py:397
  14.8 0.7 copy-start.6
  15.6 8.1 %copy-start = (f32[8,2,128,256]{3,2,1,0:T(8,128)S(1)}, f32[8,2,128,256]{3,2,1,0:T(8,128)}, u32[]{:S(2)}) copy-start(f32[8,2,128,256]{3,2,1,0:T(8,128)} %param.7) | copy-start | bytes 6291460
  15.6 8.1 %copy-start.1 = (s32[3]{0:T(128)S(1)}, s32[3]{0:T(128)}, u32[]{:S(2)}) copy-start(s32[3]{0:T(128)} %pad_add_fusion.meta) | copy-start | bytes 40
  15.6 8.1 %copy-start.2 = (f32[8,40,256]{2,1,0:T(8,128)S(1)}, f32[8,40,256]{2,1,0:T(8,128)}, u32[]{:S(2)}) copy-start(f32[8,40,256]{2,1,0:T(8,128)} %get-tuple-element.29.parts) | copy-start | bytes 983044
  15.6 8.1 %copy-start.3 = (bf16[2,2,2,256,256]{4,3,2,1,0:T(8,128)(2,1)S(1)}, bf16[2,2,2,256,256]{4,3,2,1,0:T(8,128)(2,1)}, u32[]{:S(2)}) copy-start(bf16[2,2,2,256,256]{4,3,2,1,0:T(8,128)(2,1)} %constant.26.clone.table) | copy-start | bytes 3145732
  22.3 21.2 %collective-permute-start.5 = (f32[552,256]{1,0:T(8,128)S(1)}, f32[552,256]{1,0:T(8,128)S(1)}, u32[]{:S(2)}, u32[]{:S(2)}) collective-permute-start(f32[552,256]{1,0:T(8,128)S(1)} %collective-permute-done.1), channel_id=1, source_target_pairs={{65,64},{1,0}} | collective-permute-start | bytes 1695752 | tf_op jit(solution)/shard_map/ppermute | solution.py:403
  23.7 0.9 %copy-start.5 = (f32[2,40,256]{2,1,0:T(8,128)S(1)}, f32[2,40,256]{2,1,0:T(8,128)}, u32[]{:S(2)}) copy-start(f32[2,40,256]{2,1,0:T(8,128)} %get-tuple-element.33.q2) | copy-start | bytes 245764
  33.5 26.4 %collective-permute-start.6 = (f32[272,256]{1,0:T(8,128)S(1)}, f32[272,256]{1,0:T(8,128)S(1)}, u32[]{:S(2)}, u32[]{:S(2)}) collective-permute-start(f32[272,256]{1,0:T(8,128)S(1)} %get-tuple-element.42), channel_id=1, source_target_pairs={{0,1},{1,0},{2,3},{3,2},{4,5},{5,4},{6,7},{7,6},{8,9},{9,8},{10,11... | collective-permute-start | bytes 835592 | tf_op jit(solution)/shard_map/ppermute | solution.py:408
  57.9 7.0 %collective-permute-start.7 = (f32[2,16,256]{2,1,0:T(8,128)S(1)}, f32[2,16,256]{2,1,0:T(8,128)S(1)}, u32[]{:S(2)}, u32[]{:S(2)}) collective-permute-start(f32[2,16,256]{2,1,0:T(8,128)S(1)} %get-tuple-element.45), channel_id=1, source_target_pairs={{1,0},{2,1},{3,2},{4,3},{5,4},{6,5},{7,6},{8,7},{9,8},{10,9},{11,1... | collective-permute-start | bytes 98312 | tf_op jit(solution)/shard_map/ppermute | solution.py:413
  58.0 13.5 %collective-permute-start.8 = (f32[272,256]{1,0:T(8,128)S(1)}, f32[272,256]{1,0:T(8,128)S(1)}, u32[]{:S(2)}, u32[]{:S(2)}) collective-permute-start(f32[272,256]{1,0:T(8,128)S(1)} %get-tuple-element.48), channel_id=1, source_target_pairs={{0,1},{1,0},{2,3},{3,2},{4,5},{5,4},{6,7},{7,6},{8,9},{9,8},{10,11... | collective-permute-start | bytes 835592 | tf_op jit(solution)/shard_map/ppermute | solution.py:414
  60.0 4.9 %copy-start.4 = (f32[2,256,256]{2,1,0:T(8,128)S(1)}, f32[2,256,256]{2,1,0:T(8,128)}, u32[]{:S(2)}) copy-start(f32[2,256,256]{2,1,0:T(8,128)} %get-tuple-element.44.d_ref) | copy-start | bytes 1572868
  64.7 8.3 %collective-permute-start.9 = (f32[272,256]{1,0:T(8,128)S(1)}, f32[272,256]{1,0:T(8,128)S(1)}, u32[]{:S(2)}, u32[]{:S(2)}) collective-permute-start(f32[272,256]{1,0:T(8,128)S(1)} %get-tuple-element.49), channel_id=1, source_target_pairs={{0,1},{1,0},{2,3},{3,2},{4,5},{5,4},{6,7},{7,6},{8,9},{9,8},{10,11... | collective-permute-start | bytes 835592 | tf_op jit(solution)/shard_map/ppermute | solution.py:419
  69.5 8.2 %collective-permute-start.10 = (f32[272,256]{1,0:T(8,128)S(1)}, f32[272,256]{1,0:T(8,128)S(1)}, u32[]{:S(2)}, u32[]{:S(2)}) collective-permute-start(f32[272,256]{1,0:T(8,128)S(1)} %get-tuple-element.50), channel_id=1, source_target_pairs={{0,1},{1,0},{2,3},{3,2},{4,5},{5,4},{6,7},{7,6},{8,9},{9,8},{10,11... | collective-permute-start | bytes 835592 | tf_op jit(solution)/shard_map/ppermute | solution.py:424

commit v6 on v5

--- a/solution.py
+++ b/solution.py
@@ -21,6 +21,7 @@
 FIELDS = 5 * ROWS
 PUSHED = 2 * ROWS
 PIECE = 2 * HALF + PUSHED
+BOTH = ("tm", "row")
 
 
 def split_np(m):
@@ -136,14 +137,16 @@
     turned = []
     for e in range(2):
         xh, xl = hilo(jnp.concatenate(quads[e], 1))
-        turned.append(mm(xh, tab[0, 0, e]) + mm(xl, tab[0, 0, e]) + mm(xh, tab[1, 0, e]))
+        t = mm(jnp.concatenate([xh, xl], 0), tab[0, 0, e])
+        turned.append(t[:N] + t[N:] + mm(xh, tab[1, 0, e]))
     halves = []
     for e in range(2):
         rows = slice(HALF * e, HALF * e + HALF)
         y = jnp.concatenate([jnp.concatenate([turned[0][rows, :HALF], turned[1][rows, :HALF]], 1),
                              jnp.concatenate([turned[0][rows, HALF:], turned[1][rows, HALF:]], 1)], 0)
         yh, yl = hilo(y)
-        halves.append(mm(tab[0, 1, e], yh) + mm(tab[0, 1, e], yl) + mm(tab[1, 1, e], yh))
+        t = mm(jnp.concatenate([tab[0, 1, e], tab[1, 1, e]], 0), yh)
+        halves.append(t[:N] + t[N:] + mm(tab[0, 1, e], yl))
     for e, rows in enumerate((halves[0] + halves[1], halves[0] - halves[1])):
         left, right = rows[:, :HALF], rows[:, HALF:]
         out = jnp.concatenate([left + right, left - right], 1)
@@ -160,7 +163,6 @@
 PUSH = pltpu.VMEM((2, PUSHED, N), F32)
 ANY = pl.BlockSpec(memory_space=pl.ANY)
 VM = pl.BlockSpec(memory_space=pltpu.VMEM)
-SM = pl.BlockSpec(memory_space=pltpu.SMEM)
 HB = pl.BlockSpec(memory_space=pltpu.HBM)
 
 
@@ -190,28 +192,47 @@
         compiler_params=pltpu.CompilerParams(vmem_limit_bytes=vmem))
 
 
-def pack_kernel(meta, wave, *refs):
-    sources, (all_ref, near_ref, swap_ref, chain_ref, ahead_ref), (floats, ints, sems) = refs[:5], refs[5:10], refs[10:]
-    r = meta[0]
+def load_all(copies, sources, floats, ints):
+    for a, src in enumerate(sources):
+        copies.start(src, floats.at[a] if a < 3 else ints.at[a - 3])
+
+
+def pack_slice(floats, ints, index, dst, row):
+    for a in range(5):
+        src = floats.at[a] if a < 3 else ints.at[a - 3]
+        for k in range(ROWS):
+            at = row + a * ROWS + k
+            dst[at:at + 1, :] = src[pl.ds(index, 1), N * k:N * k + N].astype(F32)
+
+
+def early_pack_kernel(wave, *refs):
+    sources, (near_ref, ahead_ref), (floats, ints, sems) = refs[:5], refs[5:7], refs[7:]
+    r = lax.axis_index("row")
     loads, copies = Copies(sems), Copies(sems)
     copies.used = 5
-    for a, src in enumerate(sources):
-        loads.start(src, floats.at[a] if a < 3 else ints.at[a - 3])
+    load_all(loads, sources, floats, ints)
+    copies.start(wave.at[pl.ds(N * (5 - 4 * r), N)], near_ref.at[pl.ds(0, N)])
     copies.start(wave.at[pl.ds(N * (6 - 4 * r), 2 * N)], ahead_ref.at[pl.ds(0, 2 * N)])
-    copies.start(wave.at[pl.ds(N * (5 - 4 * r), N)], near_ref.at[pl.ds(0, N)])
+    loads.wait()
+    pack_slice(floats, ints, 6 - 4 * r, near_ref, N)
+    pack_slice(floats, ints, 7 - 4 * r, ahead_ref, 2 * N)
+    copies.wait()
+
+
+def pack_kernel(near, wave, *refs):
+    sources, (all_ref, swap_ref, chain_ref), (floats, ints, sems) = refs[:5], refs[5:8], refs[8:]
+    r = lax.axis_index("row")
+    loads, copies = Copies(sems), Copies(sems)
+    copies.used = 5
+    load_all(loads, sources, floats, ints)
     copies.start(wave.at[pl.ds(N * (4 - 4 * r), N)], swap_ref.at[pl.ds(0, N)])
     copies.start(wave.at[pl.ds(N * (2 + 4 * r), 2 * N)], chain_ref.at[pl.ds(0, 2 * N)])
     loads.wait()
-    for a in range(5):
-        src = floats.at[a] if a < 3 else ints.at[a - 3]
-        for s in range(8):
-            for k in range(ROWS):
-                all_ref[s, a * ROWS + k:a * ROWS + k + 1, :] = src[s:s + 1, N * k:N * k + N].astype(F32)
-    near_ref[N:, :] = all_ref[6 - 4 * r]
+    for s in range(8):
+        pack_slice(floats, ints, s, all_ref.at[s], 0)
     for i, rel in enumerate((0, 1, 3)):
         swap_ref[N + FIELDS * i:N + FIELDS * i + FIELDS, :] = all_ref[4 - 4 * r + rel]
     chain_ref[2 * N:, :] = all_ref[3 + 4 * r]
-    ahead_ref[2 * N:, :] = all_ref[7 - 4 * r]
     copies.wait()
 
 
@@ -240,9 +261,9 @@
         moves.start(ref.at[pl.ds(0, N)], wave.at[pl.ds(slot * N, N)])
 
 
-def near_kernel(meta, wave, parts, near, table, d_ref, q_ref, f3, p2, tab, *rest):
+def near_kernel(wave, parts, near, table, d_ref, q_ref, f3, p2, tab, *rest):
     work, sems = rest[:-1], rest[-1]
-    r = meta[0]
+    r = lax.axis_index("row")
     copies, later = Copies(sems), Copies(sems)
     later.used = 7
     field_in(copies, r, f3, wave, N * (4 * r + 1), near, 0)
@@ -253,9 +274,9 @@
     q_ref[...] = p2[...]
 
 
-def first_kernel(meta, q2, wave, parts, swap, table, q_ref, own, away, f2, p1, pushed, z, tab, *rest):
+def first_kernel(q2, wave, parts, swap, table, q_ref, own, away, f2, p1, pushed, z, tab, *rest):
     work, sems = rest[:-1], rest[-1]
-    r = meta[0]
+    r = lax.axis_index("row")
     copies, later = Copies(sems), Copies(sems)
     later.used = 7
     field_in(copies, r, f2, wave, N * 4 * r, swap, 0)
@@ -268,10 +289,10 @@
     piece_out(r, f2, pushed, own, away)
 
 
-def second_kernel(meta, q1, parts, swap, chain, ahead, relay, table, d_ref, q_ref, to_back, own, away,
+def second_kernel(q1, parts, swap, chain, ahead, relay, table, d_ref, q_ref, to_back, own, away,
                   f0, f1, p0, pm, pushed, z, tab, *rest):
     work, sems = rest[:-1], rest[-1]
-    r = meta[0]
+    r = lax.axis_index("row")
     copies, later = Copies(sems), Copies(sems)
     later.used = 23
     field_in(copies, r, f0, ahead, 0, chain, 0)
@@ -282,7 +303,7 @@
     parts_in(copies, r, p0, parts, 0, swap, N)
     copies.wait()
 
-    @pl.when(meta[2] == 1)
+    @pl.when((r == 0) & (lax.rem(lax.axis_index("tm"), lax.axis_size("tm") // 2) == 0))
     def _():
         again = Copies(sems)
         again.used = 15
@@ -293,7 +314,7 @@
         again.start(relay.at[pl.ds(2 * N, FIELDS)], pm.at[r])
         again.wait()
 
-    @pl.when(meta[1] == 1)
+    @pl.when((r == 0) & (lax.axis_index("tm") == 0))
     def _():
         f1[...] = jnp.zeros_like(f1)
 
@@ -304,9 +325,9 @@
     piece_out(r, f1, pushed, own, away)
 
 
-def third_kernel(meta, d_ref, q0, own_a, own_b, back_a, table, own, away, wave, f0, pushed, z, tab, *rest):
+def third_kernel(d_ref, q0, own_a, own_b, back_a, table, own, away, wave, f0, pushed, z, tab, *rest):
     work, sems = rest[:-1], rest[-1]
-    r = meta[0]
+    r = lax.axis_index("row")
     copies, moves, later = Copies(sems), Copies(sems), Copies(sems)
     later.used = 11
     moves.used = 2
@@ -315,7 +336,7 @@
     moves_out(moves, wave, (own_a, 4 * r + 2), (own_b, 4 * r + 1), (back_a, 6 - 4 * r))
     copies.wait()
 
-    @pl.when(meta[1] == 1)
+    @pl.when((r == 0) & (lax.axis_index("tm") == 0))
     def _():
         f0[...] = jnp.zeros_like(f0)
 
@@ -324,10 +345,10 @@
     moves.wait()
 
 
-def fourth_kernel(meta, d_ref, parts, swap, from_back, own_c, table, wave_in, own, away, wave,
+def fourth_kernel(d_ref, parts, swap, from_back, own_c, table, wave_in, own, away, wave,
                   p3, pushed, z, tab, *rest):
     work, sems = rest[:-1], rest[-1]
-    r = meta[0]
+    r = lax.axis_index("row")
     copies, moves, later = Copies(sems), Copies(sems), Copies(sems)
     later.used = 11
     moves.used = 8
@@ -341,23 +362,15 @@
     moves.wait()
 
 
-def late_kernel(meta, back_b, back_c, own_d, wave_in, wave, sems):
-    r = meta[0]
-    moves = Copies(sems)
-    moves_out(moves, wave, (back_b, 5 - 4 * r), (back_c, 4 - 4 * r), (own_d, 4 * r + 3))
-    moves.wait()
-
-
-def final_kernel(meta, *refs):
-    pieces, (wave, phase, energy), (packed, sems) = refs[:8], refs[9:12], refs[12:]
-    r = meta[0]
+def late_kernel(own_a, own_b, own_c, own_d, back_a, back_b, back_c, wave_in, wave, phase, energy, packed, sems):
+    r = lax.axis_index("row")
+    own, other = 4 * r, 4 - 4 * r
     moves, copies = Copies(sems), Copies(sems)
     copies.used = 4
-    own, other = 4 * r, 4 - 4 * r
-    for base, group in ((own, pieces[:4]), (other, pieces[4:])):
+    for base, group in ((own, (own_a, own_b, own_c, own_d)), (other, (back_a, back_b, back_c, back_c))):
         for ref, slot in zip(group, (2, 1, 0, 3)):
             copies.start(ref.at[pl.ds(N, PUSHED)], packed.at[base + slot])
-    moves_out(moves, wave, (pieces[7], other + 3))
+    moves_out(moves, wave, (back_b, other + 1), (back_c, other), (own_d, own + 3))
     copies.wait()
     for s in range(8):
         for k in range(ROWS):
@@ -366,11 +379,24 @@
     moves.wait()
 
 
+def final_kernel(back_d, wave_in, phase_in, energy_in, wave, phase, energy, sems):
+    r = lax.axis_index("row")
+    last = 7 - 4 * r
+    moves = Copies(sems)
+    moves_out(moves, wave, (back_d, last))
+    phase[...] = phase_in[...]
+    energy[...] = energy_in[...]
+    for k in range(ROWS):
+        phase[pl.ds(last, 1), N * k:N * k + N] = back_d[N + k:N + k + 1, :]
+        energy[pl.ds(last, 1), N * k:N * k + N] = back_d[N + ROWS + k:N + ROWS + k + 1, :]
+    moves.wait()
+
+
 def body(wavefront, particle_phase, particle_energy, row_offset, row_cell, col_cell):
     table = jnp.asarray(tables())
     r = lax.axis_index("row")
     nt = lax.axis_size("tm")
-    both = ("tm", "row")
+    both = BOTH
     swap = [(i, i ^ 1) for i in range(2 * nt)]
     chain = [(i, (i + 1) % (2 * nt)) for i in range(2 * nt)]
     far = [2 * t for t in range(nt) if (t + 1) % (nt // 2) == 0]
@@ -378,57 +404,62 @@
     around = [(i, (i + 3) % (2 * nt)) for i in far]
     onward = [(j, j - 1) for i, j in around]
     back = [(j, i) for i, j in chain]
-    index = lax.axis_index(both)
-    meta = jnp.stack([r, (index == 0).astype(jnp.int32), (index % nt == 0).astype(jnp.int32)]).astype(jnp.int32)
     wave = wavefront.reshape(8 * N, N)
     unit = 1 << 33
 
     full, field = (2, FIELDS, N), (2, N, N)
     pieces = [(PIECE, N), (PIECE, N)]
-    parts, to_near, to_swap, to_chain, to_ahead = call(
-        pack_kernel, [(8, FIELDS, N), (N + FIELDS, N), (N + 3 * FIELDS, N), (2 * N + FIELDS, N), (2 * N + FIELDS, N)],
-        [VM] * 5, [pltpu.VMEM((3, 8, PART), F32), pltpu.VMEM((2, 8, PART), jnp.int32)],
-        16, [SM] + [HB] * 6, 1 << 20, vmem=61000 << 10,
-    )(meta, wave, particle_phase, particle_energy, row_offset, row_cell, col_cell)
+    raw = (wave, particle_phase, particle_energy, row_offset, row_cell, col_cell)
+    stage = [pltpu.VMEM((3, 8, PART), F32), pltpu.VMEM((2, 8, PART), jnp.int32)]
+    to_near, to_ahead = call(
+        early_pack_kernel, [(N + FIELDS, N), (2 * N + FIELDS, N)], [VM, VM], stage, 8, [HB] * 6, 1 << 20,
+        vmem=61000 << 10,
+    )(*raw)
+    f_near = lax.ppermute(to_near, both, swap)
+    f_around = lax.ppermute(to_ahead, both, around)
+    parts, to_swap, to_chain = call(
+        pack_kernel, [(8, FIELDS, N), (N + 3 * FIELDS, N), (2 * N + FIELDS, N)],
+        [VM] * 3, stage, 8, [ANY] + [HB] * 6, 4 * unit, vmem=61000 << 10,
+    )(to_near, *raw)
+    f_swap = lax.ppermute(to_swap, both, swap)
+    to_ahead, to_chain = lax.optimization_barrier((to_ahead, to_chain))
     f_ahead = lax.ppermute(to_ahead, both, ahead)
-    f_around = lax.ppermute(to_ahead, both, around)
-    f_near = lax.ppermute(to_near, both, swap)
-    f_swap = lax.ppermute(to_swap, both, swap)
     f_chain = lax.ppermute(to_chain, both, chain)
+    f_near, f_around = lax.optimization_barrier((f_near, f_around))
+    f_relay = lax.ppermute(f_around, both, onward)
 
     d3, q2 = call(
-        near_kernel, [field, full], [VM, VM], [FIELD, PARTS, TABLE] + WORK, 8, [SM] + [ANY] * 4, unit, vmem=59000 << 10,
-    )(meta, wave, parts, f_near, table)
-    q2, f_around = lax.optimization_barrier((q2, f_around))
-    f_relay = lax.ppermute(f_around, both, onward)
+        near_kernel, [field, full], [VM, VM], [FIELD, PARTS, TABLE] + WORK, 8, [ANY] * 4, unit, vmem=50000 << 10,
+    )(wave, parts, f_near, table)
     q1, own_a, away_a = call(
         first_kernel, [full] + pieces, [VM] * 3, [FIELD, PARTS, PUSH, FIELD, TABLE] + WORK, 8,
-        [SM, VM] + [ANY] * 4, 2 * unit,
-    )(meta, q2, wave, parts, f_swap, table)
+        [VM] + [ANY] * 4, 2 * unit,
+    )(q2, wave, parts, f_swap, table)
     back_a = lax.ppermute(away_a, both, swap)
     d0, q0, to_back, own_b, away_b = call(
         second_kernel, [field, full, (2, PUSHED, N)] + pieces, [VM] * 5,
-        [FIELD, FIELD, PARTS, PARTS, PUSH, FIELD, TABLE] + WORK, 24, [SM, VM] + [ANY] * 6, 3 * unit,
-    )(meta, q1, parts, f_swap, f_chain, f_ahead, f_relay, table)
+        [FIELD, FIELD, PARTS, PARTS, PUSH, FIELD, TABLE] + WORK, 24, [VM] + [ANY] * 6, 3 * unit,
+    )(q1, parts, f_swap, f_chain, f_ahead, f_relay, table)
     from_back = lax.ppermute(to_back, both, back)
     back_b = lax.ppermute(away_b, both, swap)
     own_c, away_c, wave = call(
         third_kernel, pieces + [(8 * N, N)], [VM, VM, ANY],
-        [FIELD, PUSH, FIELD, TABLE] + WORK, 12, [SM, ANY, VM] + [ANY] * 4, unit,
-    )(meta, d0, q0, own_a, own_b, back_a, table)
+        [FIELD, PUSH, FIELD, TABLE] + WORK, 12, [ANY, VM] + [ANY] * 4, unit,
+    )(d0, q0, own_a, own_b, back_a, table)
     back_c = lax.ppermute(away_c, both, swap)
     own_d, away_d, wave = call(
         fourth_kernel, pieces + [(8 * N, N)], [VM, VM, ANY],
-        [PARTS, PUSH, FIELD, TABLE] + WORK, 12, [SM, VM] + [ANY] * 6, 2 * unit, {7: 2},
-    )(meta, d3, parts, f_swap, from_back, own_c, table, wave)
+        [PARTS, PUSH, FIELD, TABLE] + WORK, 12, [VM] + [ANY] * 6, 2 * unit, {6: 2},
+    )(d3, parts, f_swap, from_back, own_c, table, wave)
     back_d = lax.ppermute(away_d, both, swap)
-    wave, = call(
-        late_kernel, [(8 * N, N)], [ANY], [], 4, [SM] + [ANY] * 4, 1 << 20, {4: 0},
-    )(meta, back_b, back_c, own_d, wave)
+    particles = [(8, PART), (8, PART)]
     wave, phase, energy = call(
-        final_kernel, [(8 * N, N), (8, PART), (8, PART)], [HB, VM, VM],
-        [pltpu.VMEM((8, PUSHED, N), F32)], 16, [SM] + [ANY] * 8 + [HB], 1 << 20, {9: 0},
-    )(meta, own_a, own_b, own_c, own_d, back_a, back_b, back_c, back_d, wave)
+        late_kernel, [(8 * N, N)] + particles, [ANY, VM, VM], [pltpu.VMEM((8, PUSHED, N), F32)], 16,
+        [ANY] * 8, 1 << 20, {7: 0},
+    )(own_a, own_b, own_c, own_d, back_a, back_b, back_c, wave)
+    wave, phase, energy = call(
+        final_kernel, [(8 * N, N)] + particles, [HB, VM, VM], [], 4, [VM, HB, VM, VM], 1 << 20, {1: 0},
+    )(back_d, wave, phase, energy)
     return wave.reshape(8, 2, HALF, N), phase, energy
 
 

time: 80.4 us -> 76.9 us (0.956)
  starting transfers between devices: 14.2 us -> 18.5 us
  Pallas kernels: 46.7 us -> 42.5 us
  waiting for transfers between devices: 16 us -> 13.8 us
    ppermute x1, starting transfers between devices: 3.09 us -> 7.42 us  [body(): back_a = lax.ppermute(away_a, both, swap)]
    ppermute x1, waiting for transfers between devices: 6.93 us -> 4.2 us  [body(): f_relay = lax.ppermute(f_around, both, onward)]
    ppermute x1, waiting for transfers between devices: 4.32 us -> 2.11 us  [body(): f_near = lax.ppermute(to_near, both, swap)]
    pallas_call x1, Pallas kernels: 6.74 us -> 4.62 us  [body(): call(near_kernel, [field, full], [VM, VM], [FIELD, PARTS, TABLE] + WORK,...]
    ppermute x1, waiting for transfers between devices: 1.49 us -> 3.42 us  [body(): back_c = lax.ppermute(away_c, both, swap)]
    ppermute x1, waiting for transfers between devices: 0.01 us -> 1.33 us  [body(): f_swap = lax.ppermute(to_swap, both, swap)]
    unnamed x14 -> x8, local copies, waits for them, and re-layouts: 1.61 us -> 0.98 us
    pallas_call x3 -> x4, Pallas kernels: 7.35 us -> 7.54 us  [the longest x1 2.7 us: body(): call(pack_kernel, [(8, FIELDS, N), (N + 3 * FIELDS, N), (2 * N + FIELDS,...]
  transfers between devices with their start and end apart: 11 -> 11, of which waited for: 4 -> 5; matrix products, arithmetic and copies ran while one was open for 0% -> 0% of each run, Pallas kernels for 51% -> 51%
where the time goes in v6:
time: 76.9 us; the launch traced here: 76.7 us
  Pallas kernels  42.5 us (55%)
  starting transfers between devices  18.5 us (24%)
  waiting for transfers between devices  13.8 us (18%)
  local copies, waits for them, and re-layouts  0.98 us (1%)
  between operations  0.94 us (1%)
    pallas_call x1, Pallas kernels, body(): call(second_kernel, [field, full, (2, PUSHED, N)] + pieces, [VM] * 5, [FI...  13.7 us
    pallas_call x1, Pallas kernels, body(): call(first_kernel, [full] + pieces, [VM] * 3, [FIELD, PARTS, PUSH, FIELD,...  8.38 us
    ppermute x1, starting transfers between devices, body(): back_a = lax.ppermute(away_a, both, swap)  7.42 us
    pallas_call x1, Pallas kernels, body(): call(near_kernel, [field, full], [VM, VM], [FIELD, PARTS, TABLE] + WORK,...  4.62 us
    pallas_call x1, Pallas kernels, body(): call(third_kernel, pieces + [(8 * N, N)], [VM, VM, ANY], [FIELD, PUSH, FI...  4.21 us
    ppermute x1, waiting for transfers between devices, body(): f_relay = lax.ppermute(f_around, both, onward)  4.2 us
    pallas_call x1, Pallas kernels, body(): call(fourth_kernel, pieces + [(8 * N, N)], [VM, VM, ANY], [PARTS, PUSH, F...  4.05 us
    ppermute x1, waiting for transfers between devices, body(): back_c = lax.ppermute(away_c, both, swap)  3.42 us
  transfers between devices with their start and end apart: 11, of which 5 were waited for; matrix products, arithmetic and copies ran while one was open for 0% of the time, Pallas kernels for 51%

profile of v6, /device:TPU:4, one launch (start us, length us, event | category | flops | bytes accessed | tf_op | source)
XLA Modules:
  0.0 76.7 jit_solution(15327707951890158913)
XLA Ops:
  0.6 2.3 %shard_map.94 = (f32[296,256]{1,0:T(8,128)}, f32[552,256]{1,0:T(8,128)}) custom-call(f32[2048,256]{1,0:T(8,128)} %bitcast.2, f32[8,2048]{1,0:T(8,128)} %refs_0_.3, f32[8,2048]{1,0:T(8,128)} %refs_1_.3, f32[8,2048]{1,0:T(8,128)} %refs_2_.3, s32[8,2048]{1,0:T(8,128)} %refs_3_.3, s32[8,2048]{1,0:T(8,128)} %refs_4_.3), custom_call_target="tpu_custom_call" | custom-call | flops 1048576 | bytes 4194304 | tf_op jit(solution)/shard_map/pallas_call | solution.py:414
  2.9 1.3 %collective-permute-start = (f32[296,256]{1,0:T(8,128)}, f32[296,256]{1,0:T(8,128)S(1)}, u32[]{:S(2)}, u32[]{:S(2)}) collective-permute-start(f32[296,256]{1,0:T(8,128)} %get-tuple-element.34.near), channel_id=1, source_target_pairs={{0,1},{1,0},{2,3},{3,2},{4,5},{5,4},{6,7},{7,6},{8,9},{9,8},{10,11... | collective-permute-start | bytes 909320 | tf_op jit(solution)/shard_map/ppermute | solution.py:418
  4.2 0.0 copy-start.3
  4.2 0.0 copy-start
  4.2 0.0 copy-start.1
  4.2 0.8 %collective-permute-start.1 = (f32[552,256]{1,0:T(8,128)}, f32[552,256]{1,0:T(8,128)S(1)}, u32[]{:S(2)}, u32[]{:S(2)}) collective-permute-start(f32[552,256]{1,0:T(8,128)} %get-tuple-element.44), channel_id=1, source_target_pairs={{62,65},{126,1}} | collective-permute-start | bytes 1695752 | tf_op jit(solution)/shard_map/ppermute | solution.py:419
  5.0 2.7 %shard_map.95 = (f32[8,40,256]{2,1,0:T(8,128)}, f32[376,256]{1,0:T(8,128)}, f32[552,256]{1,0:T(8,128)}) custom-call(f32[296,256]{1,0:T(8,128)} %get-tuple-element.34.near, f32[2048,256]{1,0:T(8,128)} %bitcast.3, f32[8,2048]{1,0:T(8,128)} %refs_0_.3, f32[8,2048]{1,0:T(8,128)} %refs_1_.3, f32[8,2048]{1,0:T(8,128)} %refs_2_.3, s32[8,2048]{1,0:T(8,128)} %refs_3_.3, ...), custom_call_target="tpu_custom_call" | custom-call | flops 34359738368 | bytes 4194304 | tf_op jit(solution)/shard_map/pallas_call | solution.py:420
  7.7 1.4 %collective-permute-start.2 = (f32[376,256]{1,0:T(8,128)}, f32[376,256]{1,0:T(8,128)S(1)}, u32[]{:S(2)}, u32[]{:S(2)}) collective-permute-start(f32[376,256]{1,0:T(8,128)} %get-tuple-element.39), channel_id=1, source_target_pairs={{0,1},{1,0},{2,3},{3,2},{4,5},{5,4},{6,7},{7,6},{8,9},{9,8},{10,11... | collective-permute-start | bytes 1155080 | tf_op jit(solution)/shard_map/ppermute | solution.py:424
  9.1 0.7 collective-permute-start.3
  9.8 0.0 copy-done.3
  9.8 1.3 %collective-permute-start.4 = (f32[552,256]{1,0:T(8,128)S(1)}, f32[552,256]{1,0:T(8,128)S(1)}, u32[]{:S(2)}, u32[]{:S(2)}) collective-permute-start(f32[552,256]{1,0:T(8,128)S(1)} %copy-done.3), channel_id=1, source_target_pairs={{0,2},{1,1},{2,4},{3,3},{4,6},{5,5},{6,8},{7,7},{8,10},{9,9},{10,1... | collective-permute-start | bytes 1695752 | tf_op jit(solution)/shard_map/ppermute | solution.py:426
  11.2 2.1 %collective-permute-done.near = f32[296,256]{1,0:T(8,128)S(1)} collective-permute-done((f32[296,256]{1,0:T(8,128)}, f32[296,256]{1,0:T(8,128)S(1)}, u32[]{:S(2)}, u32[]{:S(2)}) %collective-permute-start) | collective-permute-done | bytes 303136 | tf_op jit(solution)/shard_map/ppermute | solution.py:418
  13.3 0.0 collective-permute-done.1
  13.3 1.3 %collective-permute-start.5 = (f32[552,256]{1,0:T(8,128)S(1)}, f32[552,256]{1,0:T(8,128)S(1)}, u32[]{:S(2)}, u32[]{:S(2)}) collective-permute-start(f32[552,256]{1,0:T(8,128)S(1)} %collective-permute-done.1), channel_id=1, source_target_pairs={{65,64},{1,0}} | collective-permute-start | bytes 1695752 | tf_op jit(solution)/shard_map/ppermute | solution.py:429
  14.6 0.0 copy-done
  14.6 0.0 copy-done.1
  14.6 0.0 copy-start.2
  14.6 1.0 %copy-done.2 = f32[8,40,256]{2,1,0:T(8,128)S(1)} copy-done((f32[8,40,256]{2,1,0:T(8,128)S(1)}, f32[8,40,256]{2,1,0:T(8,128)}, u32[]{:S(2)}) %copy-start.2) | copy-done | bytes 327704
  15.6 4.6 %shard_map.96 = (f32[2,256,256]{2,1,0:T(8,128)S(1)}, f32[2,40,256]{2,1,0:T(8,128)S(1)}) custom-call(f32[2048,256]{1,0:T(8,128)S(1)} %bitcast.4, f32[8,40,256]{2,1,0:T(8,128)S(1)} %copy-done.2, f32[296,256]{1,0:T(8,128)S(1)} %collective-permute-done.near, bf16[2,2,2,256,256]{4,3,2,1,0:T(8,128)(2,1)S(1)} %copy-done.1), custom_call_target="tpu_custom_call" | custom-call | flops 8589934592 | bytes 4194304 | tf_op jit(solution)/shard_map/pallas_call | solution.py:431
  20.2 1.3 %collective-permute-done.2.swap = f32[376,256]{1,0:T(8,128)S(1)} collective-permute-done((f32[376,256]{1,0:T(8,128)}, f32[376,256]{1,0:T(8,128)S(1)}, u32[]{:S(2)}, u32[]{:S(2)}) %collective-permute-start.2) | collective-permute-done | bytes 385056 | tf_op jit(solution)/shard_map/ppermute | solution.py:424
  21.5 8.4 %shard_map.97 = (f32[2,40,256]{2,1,0:T(8,128)S(1)}, f32[272,256]{1,0:T(8,128)S(1)}, f32[272,256]{1,0:T(8,128)S(1)}) custom-call(f32[2,40,256]{2,1,0:T(8,128)S(1)} %get-tuple-element.40.q2, f32[2048,256]{1,0:T(8,128)S(1)} %bitcast.5, f32[8,40,256]{2,1,0:T(8,128)S(1)} %copy-done.2, f32[376,256]{1,0:T(8,128)S(1)} %collective-permute-done.2.swap, ...), custom_call_target="tpu_custom_call" | custom-call | flops 17179869184 | bytes 4194304 | tf_op jit(solution)/shard_map/pallas_call | solution.py:434
  29.9 7.4 %collective-permute-start.7 = (f32[272,256]{1,0:T(8,128)S(1)}, f32[272,256]{1,0:T(8,128)S(1)}, u32[]{:S(2)}, u32[]{:S(2)}) collective-permute-start(f32[272,256]{1,0:T(8,128)S(1)} %get-tuple-element.51), channel_id=1, source_target_pairs={{0,1},{1,0},{2,3},{3,2},{4,5},{5,4},{6,7},{7,6},{8,9},{9,8},{10,11... | collective-permute-start | bytes 835592 | tf_op jit(solution)/shard_map/ppermute | solution.py:438
  37.3 0.0 collective-permute-done.3.chain
  37.3 0.0 collective-permute-done.4.ahead
  37.3 4.2 %collective-permute-done.5.relay = f32[552,256]{1,0:T(8,128)S(1)} collective-permute-done((f32[552,256]{1,0:T(8,128)S(1)}, f32[552,256]{1,0:T(8,128)S(1)}, u32[]{:S(2)}, u32[]{:S(2)}) %collective-permute-start.5) | collective-permute-done | bytes 565280 | tf_op jit(solution)/shard_map/ppermute | solution.py:429
  41.5 13.7 %shard_map.98 = (f32[2,256,256]{2,1,0:T(8,128)S(1)}, f32[2,40,256]{2,1,0:T(8,128)S(1)}, f32[2,16,256]{2,1,0:T(8,128)S(1)}, f32[272,256]{1,0:T(8,128)S(1)}, f32[272,256]{1,0:T(8,128)S(1)}) custom-call(f32[2,40,256]{2,1,0:T(8,128)S(1)} %get-tuple-element.41.q1, f32[8,40,256]{2,1,0:T(8,128)S(1)} %copy-done.2, f32[376,256]{1,0:T(8,128)S(1)} %collective-permute-done.2.swap, ...), custom_call_target="tpu_custom_call" | custom-call | flops 25769803776 | bytes 4194304 | tf_op jit(solution)/shard_map/pallas_call | solution.py:439
  55.3 0.1 collective-permute-start.6
  55.4 2.0 %collective-permute-start.9 = (f32[272,256]{1,0:T(8,128)S(1)}, f32[272,256]{1,0:T(8,128)S(1)}, u32[]{:S(2)}, u32[]{:S(2)}) collective-permute-start(f32[272,256]{1,0:T(8,128)S(1)} %get-tuple-element.56), channel_id=1, source_target_pairs={{0,1},{1,0},{2,3},{3,2},{4,5},{5,4},{6,7},{7,6},{8,9},{9,8},{10,11... | collective-permute-start | bytes 835592 | tf_op jit(solution)/shard_map/ppermute | solution.py:444
  57.4 0.0 collective-permute-done.7.back_a
  57.4 4.2 %shard_map.99 = (f32[272,256]{1,0:T(8,128)S(1)}, f32[272,256]{1,0:T(8,128)S(1)}, f32[2048,256]{1,0:T(8,128)}) custom-call(f32[2,256,256]{2,1,0:T(8,128)S(1)} %get-tuple-element.47.d_ref, f32[2,40,256]{2,1,0:T(8,128)S(1)} %get-tuple-element.48.q0, f32[272,256]{1,0:T(8,128)S(1)} %get-tuple-element.49.own_a, f32[272,256]{1,0:T(8,128)S(1)} %get-tuple-element.50.own_b, ...), custom_call_target="tpu_custom_call" | custom-call | flops 8589934592 | bytes 4194304 | tf_op jit(solution)/shard_map/pallas_call | solution.py:445
  61.6 0.2 collective-permute-start.10
  61.8 0.0 collective-permute-done.6.from_back
  61.8 4.1 %shard_map.100 = (f32[272,256]{1,0:T(8,128)S(1)}, f32[272,256]{1,0:T(8,128)S(1)}, f32[2048,256]{1,0:T(8,128)}) custom-call(f32[2,256,256]{2,1,0:T(8,128)S(1)} %get-tuple-element.38.d_ref, f32[8,40,256]{2,1,0:T(8,128)S(1)} %copy-done.2, f32[376,256]{1,0:T(8,128)S(1)} %collective-permute-done.2.swap, ...), custom_call_target="tpu_custom_call", output_to_operand_aliasing={{2}: (6, {})} | custom-call | flops 17179869184 | bytes 4194304 | tf_op jit(solution)/shard_map/pallas_call | solution.py:450
  65.8 2.0 %collective-permute-start.8 = (f32[272,256]{1,0:T(8,128)S(1)}, f32[272,256]{1,0:T(8,128)S(1)}, u32[]{:S(2)}, u32[]{:S(2)}) collective-permute-start(f32[272,256]{1,0:T(8,128)S(1)} %get-tuple-element.54), channel_id=1, source_target_pairs={{0,1},{1,0},{2,3},{3,2},{4,5},{5,4},{6,7},{7,6},{8,9},{9,8},{10,11... | collective-permute-start | bytes 835592 | tf_op jit(solution)/shard_map/ppermute | solution.py:454
  67.8 0.0 collective-permute-done.9.back_b
  67.8 3.4 %collective-permute-done.10.back_c = f32[272,256]{1,0:T(8,128)S(1)} collective-permute-done((f32[272,256]{1,0:T(8,128)S(1)}, f32[272,256]{1,0:T(8,128)S(1)}, u32[]{:S(2)}, u32[]{:S(2)}) %collective-permute-start.10) | collective-permute-done | bytes 278560 | tf_op jit(solution)/shard_map/ppermute | solution.py:449
  71.3 1.2 %shard_map.101 = (f32[2048,256]{1,0:T(8,128)}, f32[8,2048]{1,0:T(8,128)S(1)}, f32[8,2048]{1,0:T(8,128)S(1)}) custom-call(f32[272,256]{1,0:T(8,128)S(1)} %get-tuple-element.49.own_a, f32[272,256]{1,0:T(8,128)S(1)} %get-tuple-element.50.own_b, f32[272,256]{1,0:T(8,128)S(1)} %get-tuple-element.52.own_c, ...), custom_call_target="tpu_custom_call", output_to_operand_aliasing={{0}: (7, {})} | custom-call | flops 1048576 | bytes 4194304 | tf_op jit(solution)/shard_map/pallas_call | solution.py:456
  72.4 2.7 %collective-permute-done.8.back_d = f32[272,256]{1,0:T(8,128)S(1)} collective-permute-done((f32[272,256]{1,0:T(8,128)S(1)}, f32[272,256]{1,0:T(8,128)S(1)}, u32[]{:S(2)}, u32[]{:S(2)}) %collective-permute-start.8) | collective-permute-done | bytes 278560 | tf_op jit(solution)/shard_map/ppermute | solution.py:454
  75.1 1.4 %shard_map.102 = (f32[2048,256]{1,0:T(8,128)}, f32[8,2048]{1,0:T(8,128)}, f32[8,2048]{1,0:T(8,128)}) custom-call(f32[272,256]{1,0:T(8,128)S(1)} %collective-permute-done.8.back_d, f32[2048,256]{1,0:T(8,128)} %get-tuple-element.59.wave_in, f32[8,2048]{1,0:T(8,128)S(1)} %get-tuple-element.60.phase_in, ...), custom_call_target="tpu_custom_call", output_to_operand_aliasing={{0}: (1, {})} | custom-call | flops 1048576 | bytes 4194304 | tf_op jit(solution)/shard_map/pallas_call | solution.py:460
Async XLA Ops:
  2.9 10.4 %collective-permute-start = (f32[296,256]{1,0:T(8,128)}, f32[296,256]{1,0:T(8,128)S(1)}, u32[]{:S(2)}, u32[]{:S(2)}) collective-permute-start(f32[296,256]{1,0:T(8,128)} %get-tuple-element.34.near), channel_id=1, source_target_pairs={{0,1},{1,0},{2,3},{3,2},{4,5},{5,4},{6,7},{7,6},{8,9},{9,8},{10,11... | collective-permute-start | bytes 909320 | tf_op jit(solution)/shard_map/ppermute | solution.py:418
  4.2 5.6 %copy-start.3 = (f32[552,256]{1,0:T(8,128)S(1)}, f32[552,256]{1,0:T(8,128)}, u32[]{:S(2)}) copy-start(f32[552,256]{1,0:T(8,128)} %get-tuple-element.44) | copy-start | bytes 1695748
  4.2 10.4 %copy-start = (f32[8,2,128,256]{3,2,1,0:T(8,128)S(1)}, f32[8,2,128,256]{3,2,1,0:T(8,128)}, u32[]{:S(2)}) copy-start(f32[8,2,128,256]{3,2,1,0:T(8,128)} %param.7) | copy-start | bytes 6291460
  4.2 10.4 %copy-start.1 = (bf16[2,2,2,256,256]{4,3,2,1,0:T(8,128)(2,1)S(1)}, bf16[2,2,2,256,256]{4,3,2,1,0:T(8,128)(2,1)}, u32[]{:S(2)}) copy-start(bf16[2,2,2,256,256]{4,3,2,1,0:T(8,128)(2,1)} %constant.2.clone.table) | copy-start | bytes 3145732
  4.2 9.1 %collective-permute-start.1 = (f32[552,256]{1,0:T(8,128)}, f32[552,256]{1,0:T(8,128)S(1)}, u32[]{:S(2)}, u32[]{:S(2)}) collective-permute-start(f32[552,256]{1,0:T(8,128)} %get-tuple-element.44), channel_id=1, source_target_pairs={{62,65},{126,1}} | collective-permute-start | bytes 1695752 | tf_op jit(solution)/shard_map/ppermute | solution.py:419
  7.7 13.8 %collective-permute-start.2 = (f32[376,256]{1,0:T(8,128)}, f32[376,256]{1,0:T(8,128)S(1)}, u32[]{:S(2)}, u32[]{:S(2)}) collective-permute-start(f32[376,256]{1,0:T(8,128)} %get-tuple-element.39), channel_id=1, source_target_pairs={{0,1},{1,0},{2,3},{3,2},{4,5},{5,4},{6,7},{7,6},{8,9},{9,8},{10,11... | collective-permute-start | bytes 1155080 | tf_op jit(solution)/shard_map/ppermute | solution.py:424
  9.1 28.2 %collective-permute-start.3 = (f32[552,256]{1,0:T(8,128)}, f32[552,256]{1,0:T(8,128)S(1)}, u32[]{:S(2)}, u32[]{:S(2)}) collective-permute-start(f32[552,256]{1,0:T(8,128)} %get-tuple-element.43), channel_id=1, source_target_pairs={{0,1},{1,2},{2,3},{3,4},{4,5},{5,6},{6,7},{7,8},{8,9},{9,10},{10,1... | collective-permute-start | bytes 1695752 | tf_op jit(solution)/shard_map/ppermute | solution.py:427
  9.8 27.5 %collective-permute-start.4 = (f32[552,256]{1,0:T(8,128)S(1)}, f32[552,256]{1,0:T(8,128)S(1)}, u32[]{:S(2)}, u32[]{:S(2)}) collective-permute-start(f32[552,256]{1,0:T(8,128)S(1)} %copy-done.3), channel_id=1, source_target_pairs={{0,2},{1,1},{2,4},{3,3},{4,6},{5,5},{6,8},{7,7},{8,10},{9,9},{10,1... | collective-permute-start | bytes 1695752 | tf_op jit(solution)/shard_map/ppermute | solution.py:426
  13.3 28.3 %collective-permute-start.5 = (f32[552,256]{1,0:T(8,128)S(1)}, f32[552,256]{1,0:T(8,128)S(1)}, u32[]{:S(2)}, u32[]{:S(2)}) collective-permute-start(f32[552,256]{1,0:T(8,128)S(1)} %collective-permute-done.1), channel_id=1, source_target_pairs={{65,64},{1,0}} | collective-permute-start | bytes 1695752 | tf_op jit(solution)/shard_map/ppermute | solution.py:429
  14.6 1.0 %copy-start.2 = (f32[8,40,256]{2,1,0:T(8,128)S(1)}, f32[8,40,256]{2,1,0:T(8,128)}, u32[]{:S(2)}) copy-start(f32[8,40,256]{2,1,0:T(8,128)} %get-tuple-element.35.parts) | copy-start | bytes 983044
  29.9 27.5 %collective-permute-start.7 = (f32[272,256]{1,0:T(8,128)S(1)}, f32[272,256]{1,0:T(8,128)S(1)}, u32[]{:S(2)}, u32[]{:S(2)}) collective-permute-start(f32[272,256]{1,0:T(8,128)S(1)} %get-tuple-element.51), channel_id=1, source_target_pairs={{0,1},{1,0},{2,3},{3,2},{4,5},{5,4},{6,7},{7,6},{8,9},{9,8},{10,11... | collective-permute-start | bytes 835592 | tf_op jit(solution)/shard_map/ppermute | solution.py:438
  55.3 6.5 %collective-permute-start.6 = (f32[2,16,256]{2,1,0:T(8,128)S(1)}, f32[2,16,256]{2,1,0:T(8,128)S(1)}, u32[]{:S(2)}, u32[]{:S(2)}) collective-permute-start(f32[2,16,256]{2,1,0:T(8,128)S(1)} %get-tuple-element.46), channel_id=1, source_target_pairs={{1,0},{2,1},{3,2},{4,3},{5,4},{6,5},{7,6},{8,7},{9,8},{10,9},{11,1... | collective-permute-start | bytes 98312 | tf_op jit(solution)/shard_map/ppermute | solution.py:443
  55.4 12.5 %collective-permute-start.9 = (f32[272,256]{1,0:T(8,128)S(1)}, f32[272,256]{1,0:T(8,128)S(1)}, u32[]{:S(2)}, u32[]{:S(2)}) collective-permute-start(f32[272,256]{1,0:T(8,128)S(1)} %get-tuple-element.56), channel_id=1, source_target_pairs={{0,1},{1,0},{2,3},{3,2},{4,5},{5,4},{6,7},{7,6},{8,9},{9,8},{10,11... | collective-permute-start | bytes 835592 | tf_op jit(solution)/shard_map/ppermute | solution.py:444
  61.6 9.7 %collective-permute-start.10 = (f32[272,256]{1,0:T(8,128)S(1)}, f32[272,256]{1,0:T(8,128)S(1)}, u32[]{:S(2)}, u32[]{:S(2)}) collective-permute-start(f32[272,256]{1,0:T(8,128)S(1)} %get-tuple-element.57), channel_id=1, source_target_pairs={{0,1},{1,0},{2,3},{3,2},{4,5},{5,4},{6,7},{7,6},{8,9},{9,8},{10,11... | collective-permute-start | bytes 835592 | tf_op jit(solution)/shard_map/ppermute | solution.py:449
  65.8 9.3 %collective-permute-start.8 = (f32[272,256]{1,0:T(8,128)S(1)}, f32[272,256]{1,0:T(8,128)S(1)}, u32[]{:S(2)}, u32[]{:S(2)}) collective-permute-start(f32[272,256]{1,0:T(8,128)S(1)} %get-tuple-element.54), channel_id=1, source_target_pairs={{0,1},{1,0},{2,3},{3,2},{4,5},{5,4},{6,7},{7,6},{8,9},{9,8},{10,11... | collective-permute-start | bytes 835592 | tf_op jit(solution)/shard_map/ppermute | solution.py:454

commit v7 on v6

--- a/solution.py
+++ b/solution.py
@@ -206,7 +206,7 @@
 
 
 def early_pack_kernel(wave, *refs):
-    sources, (near_ref, ahead_ref), (floats, ints, sems) = refs[:5], refs[5:7], refs[7:]
+    sources, (near_ref, ahead_ref, mine_ref), (floats, ints, sems) = refs[:5], refs[5:8], refs[8:]
     r = lax.axis_index("row")
     loads, copies = Copies(sems), Copies(sems)
     copies.used = 5
@@ -215,6 +215,7 @@
     copies.start(wave.at[pl.ds(N * (6 - 4 * r), 2 * N)], ahead_ref.at[pl.ds(0, 2 * N)])
     loads.wait()
     pack_slice(floats, ints, 6 - 4 * r, near_ref, N)
+    pack_slice(floats, ints, 2 + 4 * r, mine_ref, 0)
     pack_slice(floats, ints, 7 - 4 * r, ahead_ref, 2 * N)
     copies.wait()
 
@@ -261,13 +262,14 @@
         moves.start(ref.at[pl.ds(0, N)], wave.at[pl.ds(slot * N, N)])
 
 
-def near_kernel(wave, parts, near, table, d_ref, q_ref, f3, p2, tab, *rest):
+def near_kernel(wave, mine, near, table, d_ref, q_ref, f3, p2, tab, *rest):
     work, sems = rest[:-1], rest[-1]
     r = lax.axis_index("row")
     copies, later = Copies(sems), Copies(sems)
     later.used = 7
     field_in(copies, r, f3, wave, N * (4 * r + 1), near, 0)
-    parts_in(copies, r, p2, parts, 2, near, N)
+    copies.start(mine, p2.at[r])
+    copies.start(near.at[pl.ds(N, FIELDS)], p2.at[1 - r])
     later.start(table, tab)
     copies.wait()
     step(f3, p2, p2, tab, d_ref, *work, ready=later)
@@ -411,8 +413,8 @@
     pieces = [(PIECE, N), (PIECE, N)]
     raw = (wave, particle_phase, particle_energy, row_offset, row_cell, col_cell)
     stage = [pltpu.VMEM((3, 8, PART), F32), pltpu.VMEM((2, 8, PART), jnp.int32)]
-    to_near, to_ahead = call(
-        early_pack_kernel, [(N + FIELDS, N), (2 * N + FIELDS, N)], [VM, VM], stage, 8, [HB] * 6, 1 << 20,
+    to_near, to_ahead, mine = call(
+        early_pack_kernel, [(N + FIELDS, N), (2 * N + FIELDS, N), (FIELDS, N)], [VM] * 3, stage, 8, [HB] * 6, 1 << 20,
         vmem=61000 << 10,
     )(*raw)
     f_near = lax.ppermute(to_near, both, swap)
@@ -424,13 +426,13 @@
     f_swap = lax.ppermute(to_swap, both, swap)
     to_ahead, to_chain = lax.optimization_barrier((to_ahead, to_chain))
     f_ahead = lax.ppermute(to_ahead, both, ahead)
-    f_chain = lax.ppermute(to_chain, both, chain)
-    f_near, f_around = lax.optimization_barrier((f_near, f_around))
-    f_relay = lax.ppermute(f_around, both, onward)
 
     d3, q2 = call(
         near_kernel, [field, full], [VM, VM], [FIELD, PARTS, TABLE] + WORK, 8, [ANY] * 4, unit, vmem=50000 << 10,
-    )(wave, parts, f_near, table)
+    )(wave, mine, f_near, table)
+    q2, f_around, to_chain = lax.optimization_barrier((q2, f_around, to_chain))
+    f_relay = lax.ppermute(f_around, both, onward)
+    f_chain = lax.ppermute(to_chain, both, chain)
     q1, own_a, away_a = call(
         first_kernel, [full] + pieces, [VM] * 3, [FIELD, PARTS, PUSH, FIELD, TABLE] + WORK, 8,
         [VM] + [ANY] * 4, 2 * unit,

time: 76.9 us -> 78.7 us (1.023)
  waiting for transfers between devices: 13.8 us -> 17.9 us
  starting transfers between devices: 18.5 us -> 17.4 us
  local copies, waits for them, and re-layouts: 0.98 us -> 0.02 us
    ppermute x1, starting transfers between devices: 7.42 us -> 2.76 us  [body(): back_a = lax.ppermute(away_a, both, swap)]
    ppermute x1, waiting for transfers between devices: 4.2 us -> 8.76 us  [body(): f_relay = lax.ppermute(f_around, both, onward)]
    ppermute x1, starting transfers between devices: 0.73 us -> 3.98 us  [body(): f_chain = lax.ppermute(to_chain, both, chain)]
    ppermute x1, waiting for transfers between devices: 1.33 us -> 0.01 us  [body(): f_swap = lax.ppermute(to_swap, both, swap)]
    unnamed x8 -> x12, local copies, waits for them, and re-layouts: 0.98 us -> 0.02 us
    ppermute x1, starting transfers between devices: 0.82 us -> 1.62 us  [body(): f_around = lax.ppermute(to_ahead, both, around)]
  transfers between devices with their start and end apart: 11 -> 11, of which waited for: 5 -> 4; matrix products, arithmetic and copies ran while one was open for 0% -> 0% of each run, Pallas kernels for 51% -> 49%
where the time goes in v7:
time: 78.7 us; the launch traced here: 78.5 us
  Pallas kernels  42.3 us (54%)
  waiting for transfers between devices  17.9 us (23%)
  starting transfers between devices  17.4 us (22%)
  between operations  0.96 us (1%)
    pallas_call x1, Pallas kernels, body(): call(second_kernel, [field, full, (2, PUSHED, N)] + pieces, [VM] * 5, [FI...  13.7 us
    ppermute x1, waiting for transfers between devices, body(): f_relay = lax.ppermute(f_around, both, onward)  8.76 us
    pallas_call x1, Pallas kernels, body(): call(first_kernel, [full] + pieces, [VM] * 3, [FIELD, PARTS, PUSH, FIELD,...  8.41 us
    pallas_call x1, Pallas kernels, body(): call(near_kernel, [field, full], [VM, VM], [FIELD, PARTS, TABLE] + WORK,...  4.67 us
    pallas_call x1, Pallas kernels, body(): call(third_kernel, pieces + [(8 * N, N)], [VM, VM, ANY], [FIELD, PUSH, FI...  4.21 us
    pallas_call x1, Pallas kernels, body(): call(fourth_kernel, pieces + [(8 * N, N)], [VM, VM, ANY], [PARTS, PUSH, F...  4.03 us
    ppermute x1, starting transfers between devices, body(): f_chain = lax.ppermute(to_chain, both, chain)  3.98 us
    ppermute x1, waiting for transfers between devices, body(): back_c = lax.ppermute(away_c, both, swap)  3.39 us
  transfers between devices with their start and end apart: 11, of which 4 were waited for; matrix products, arithmetic and copies ran while one was open for 0% of the time, Pallas kernels for 49%

profile of v7, /device:TPU:4, one launch (start us, length us, event | category | flops | bytes accessed | tf_op | source)
XLA Modules:
  0.0 78.5 jit_solution(7519357425829401610)
XLA Ops:
  0.6 2.3 %shard_map.94 = (f32[296,256]{1,0:T(8,128)}, f32[552,256]{1,0:T(8,128)}, f32[40,256]{1,0:T(8,128)}) custom-call(f32[2048,256]{1,0:T(8,128)} %bitcast.2, f32[8,2048]{1,0:T(8,128)} %refs_0_.3, f32[8,2048]{1,0:T(8,128)} %refs_1_.3, f32[8,2048]{1,0:T(8,128)} %refs_2_.3, s32[8,2048]{1,0:T(8,128)} %refs_3_.3, s32[8,2048]{1,0:T(8,128)} %refs_4_.3), custom_call_target="tpu_custom_call" | custom-call | flops 1048576 | bytes 4194304 | tf_op jit(solution)/shard_map/pallas_call | solution.py:416
  2.9 1.3 %collective-permute-start = (f32[296,256]{1,0:T(8,128)}, f32[296,256]{1,0:T(8,128)S(1)}, u32[]{:S(2)}, u32[]{:S(2)}) collective-permute-start(f32[296,256]{1,0:T(8,128)} %get-tuple-element.37.near), channel_id=1, source_target_pairs={{0,1},{1,0},{2,3},{3,2},{4,5},{5,4},{6,7},{7,6},{8,9},{9,8},{10,11... | collective-permute-start | bytes 909320 | tf_op jit(solution)/shard_map/ppermute | solution.py:420
  4.2 0.0 copy-start.4
  4.2 0.0 copy-start
  4.2 0.0 copy-start.1
  4.2 0.0 copy-start.2
  4.2 1.6 %collective-permute-start.2 = (f32[552,256]{1,0:T(8,128)}, f32[552,256]{1,0:T(8,128)}, u32[]{:S(2)}, u32[]{:S(2)}) collective-permute-start(f32[552,256]{1,0:T(8,128)} %get-tuple-element.48), channel_id=1, source_target_pairs={{62,65},{126,1}} | collective-permute-start | bytes 1695752 | tf_op jit(solution)/shard_map/ppermute | solution.py:421
  5.8 2.4 %shard_map.96 = (f32[8,40,256]{2,1,0:T(8,128)}, f32[376,256]{1,0:T(8,128)}, f32[552,256]{1,0:T(8,128)}) custom-call(f32[296,256]{1,0:T(8,128)} %get-tuple-element.37.near, f32[2048,256]{1,0:T(8,128)} %bitcast.3, f32[8,2048]{1,0:T(8,128)} %refs_0_.3, f32[8,2048]{1,0:T(8,128)} %refs_1_.3, f32[8,2048]{1,0:T(8,128)} %refs_2_.3, s32[8,2048]{1,0:T(8,128)} %refs_3_.3, ...), custom_call_target="tpu_custom_call" | custom-call | flops 34359738368 | bytes 4194304 | tf_op jit(solution)/shard_map/pallas_call | solution.py:422
  8.3 0.9 %collective-permute-start.1 = (f32[376,256]{1,0:T(8,128)}, f32[376,256]{1,0:T(8,128)S(1)}, u32[]{:S(2)}, u32[]{:S(2)}) collective-permute-start(f32[376,256]{1,0:T(8,128)} %get-tuple-element.40), channel_id=1, source_target_pairs={{0,1},{1,0},{2,3},{3,2},{4,5},{5,4},{6,7},{7,6},{8,9},{9,8},{10,11... | collective-permute-start | bytes 1155080 | tf_op jit(solution)/shard_map/ppermute | solution.py:426
  9.1 0.0 copy-done.4
  9.1 1.3 %collective-permute-start.4 = (f32[552,256]{1,0:T(8,128)S(1)}, f32[552,256]{1,0:T(8,128)S(1)}, u32[]{:S(2)}, u32[]{:S(2)}) collective-permute-start(f32[552,256]{1,0:T(8,128)S(1)} %copy-done.4), channel_id=1, source_target_pairs={{0,2},{1,1},{2,4},{3,3},{4,6},{5,5},{6,8},{7,7},{8,10},{9,9},{10,1... | collective-permute-start | bytes 1695752 | tf_op jit(solution)/shard_map/ppermute | solution.py:428
  10.4 2.8 %collective-permute-done.near = f32[296,256]{1,0:T(8,128)S(1)} collective-permute-done((f32[296,256]{1,0:T(8,128)}, f32[296,256]{1,0:T(8,128)S(1)}, u32[]{:S(2)}, u32[]{:S(2)}) %collective-permute-start) | collective-permute-done | bytes 303136 | tf_op jit(solution)/shard_map/ppermute | solution.py:420
  13.3 0.0 copy-done
  13.3 0.0 copy-done.1
  13.3 0.0 copy-done.2
  13.3 0.0 copy-start.5
  13.3 0.0 copy-start.3
  13.3 4.7 %shard_map.95 = (f32[2,256,256]{2,1,0:T(8,128)S(1)}, f32[2,40,256]{2,1,0:T(8,128)S(1)}) custom-call(f32[2048,256]{1,0:T(8,128)S(1)} %bitcast.4, f32[40,256]{1,0:T(8,128)S(1)} %copy-done.1, f32[296,256]{1,0:T(8,128)S(1)} %collective-permute-done.near, bf16[2,2,2,256,256]{4,3,2,1,0:T(8,128)(2,1)S(1)} %copy-done.2), custom_call_target="tpu_custom_call" | custom-call | flops 8589934592 | bytes 4194304 | tf_op jit(solution)/shard_map/pallas_call | solution.py:430
  18.0 0.0 collective-permute-done.2
  18.0 0.0 copy-done.5
  18.0 4.0 %collective-permute-start.3 = (f32[552,256]{1,0:T(8,128)S(1)}, f32[552,256]{1,0:T(8,128)S(1)}, u32[]{:S(2)}, u32[]{:S(2)}) collective-permute-start(f32[552,256]{1,0:T(8,128)S(1)} %copy-done.5), channel_id=1, source_target_pairs={{0,1},{1,2},{2,3},{3,4},{4,5},{5,6},{6,7},{7,8},{8,9},{9,10},{10,1... | collective-permute-start | bytes 1695752 | tf_op jit(solution)/shard_map/ppermute | solution.py:435
  22.0 1.3 %collective-permute-start.5 = (f32[552,256]{1,0:T(8,128)}, f32[552,256]{1,0:T(8,128)S(1)}, u32[]{:S(2)}, u32[]{:S(2)}) collective-permute-start(f32[552,256]{1,0:T(8,128)} %collective-permute-done.2), channel_id=1, source_target_pairs={{65,64},{1,0}} | collective-permute-start | bytes 1695752 | tf_op jit(solution)/shard_map/ppermute | solution.py:434
  23.3 0.0 collective-permute-done.1.swap
  23.3 0.0 copy-done.3
  23.3 8.4 %shard_map.97 = (f32[2,40,256]{2,1,0:T(8,128)S(1)}, f32[272,256]{1,0:T(8,128)S(1)}, f32[272,256]{1,0:T(8,128)S(1)}) custom-call(f32[2,40,256]{2,1,0:T(8,128)S(1)} %get-tuple-element.45.q2, f32[2048,256]{1,0:T(8,128)S(1)} %bitcast.5, f32[8,40,256]{2,1,0:T(8,128)S(1)} %copy-done.3, f32[376,256]{1,0:T(8,128)S(1)} %collective-permute-done.1.swap, ...), custom_call_target="tpu_custom_call" | custom-call | flops 17179869184 | bytes 4194304 | tf_op jit(solution)/shard_map/pallas_call | solution.py:436
  31.7 2.8 %collective-permute-start.7 = (f32[272,256]{1,0:T(8,128)S(1)}, f32[272,256]{1,0:T(8,128)S(1)}, u32[]{:S(2)}, u32[]{:S(2)}) collective-permute-start(f32[272,256]{1,0:T(8,128)S(1)} %get-tuple-element.55), channel_id=1, source_target_pairs={{0,1},{1,0},{2,3},{3,2},{4,5},{5,4},{6,7},{7,6},{8,9},{9,8},{10,11... | collective-permute-start | bytes 835592 | tf_op jit(solution)/shard_map/ppermute | solution.py:440
  34.5 0.0 collective-permute-done.4.ahead
  34.5 0.0 collective-permute-done.3.chain
  34.5 8.8 %collective-permute-done.5.relay = f32[552,256]{1,0:T(8,128)S(1)} collective-permute-done((f32[552,256]{1,0:T(8,128)}, f32[552,256]{1,0:T(8,128)S(1)}, u32[]{:S(2)}, u32[]{:S(2)}) %collective-permute-start.5) | collective-permute-done | bytes 565280 | tf_op jit(solution)/shard_map/ppermute | solution.py:434
  43.2 13.7 %shard_map.98 = (f32[2,256,256]{2,1,0:T(8,128)S(1)}, f32[2,40,256]{2,1,0:T(8,128)S(1)}, f32[2,16,256]{2,1,0:T(8,128)S(1)}, f32[272,256]{1,0:T(8,128)S(1)}, f32[272,256]{1,0:T(8,128)S(1)}) custom-call(f32[2,40,256]{2,1,0:T(8,128)S(1)} %get-tuple-element.46.q1, f32[8,40,256]{2,1,0:T(8,128)S(1)} %copy-done.3, f32[376,256]{1,0:T(8,128)S(1)} %collective-permute-done.1.swap, ...), custom_call_target="tpu_custom_call" | custom-call | flops 25769803776 | bytes 4194304 | tf_op jit(solution)/shard_map/pallas_call | solution.py:441
  57.0 0.1 collective-permute-start.6
  57.1 2.0 %collective-permute-start.9 = (f32[272,256]{1,0:T(8,128)S(1)}, f32[272,256]{1,0:T(8,128)S(1)}, u32[]{:S(2)}, u32[]{:S(2)}) collective-permute-start(f32[272,256]{1,0:T(8,128)S(1)} %get-tuple-element.60), channel_id=1, source_target_pairs={{0,1},{1,0},{2,3},{3,2},{4,5},{5,4},{6,7},{7,6},{8,9},{9,8},{10,11... | collective-permute-start | bytes 835592 | tf_op jit(solution)/shard_map/ppermute | solution.py:446
  59.1 0.0 collective-permute-done.7.back_a
  59.1 4.2 %shard_map.99 = (f32[272,256]{1,0:T(8,128)S(1)}, f32[272,256]{1,0:T(8,128)S(1)}, f32[2048,256]{1,0:T(8,128)}) custom-call(f32[2,256,256]{2,1,0:T(8,128)S(1)} %get-tuple-element.51.d_ref, f32[2,40,256]{2,1,0:T(8,128)S(1)} %get-tuple-element.52.q0, f32[272,256]{1,0:T(8,128)S(1)} %get-tuple-element.53.own_a, f32[272,256]{1,0:T(8,128)S(1)} %get-tuple-element.54.own_b, ...), custom_call_target="tpu_custom_call" | custom-call | flops 8589934592 | bytes 4194304 | tf_op jit(solution)/shard_map/pallas_call | solution.py:447
  63.3 0.2 collective-permute-start.10
  63.5 0.0 collective-permute-done.6.from_back
  63.5 4.0 %shard_map.100 = (f32[272,256]{1,0:T(8,128)S(1)}, f32[272,256]{1,0:T(8,128)S(1)}, f32[2048,256]{1,0:T(8,128)}) custom-call(f32[2,256,256]{2,1,0:T(8,128)S(1)} %get-tuple-element.38.d_ref, f32[8,40,256]{2,1,0:T(8,128)S(1)} %copy-done.3, f32[376,256]{1,0:T(8,128)S(1)} %collective-permute-done.1.swap, ...), custom_call_target="tpu_custom_call", output_to_operand_aliasing={{2}: (6, {})} | custom-call | flops 17179869184 | bytes 4194304 | tf_op jit(solution)/shard_map/pallas_call | solution.py:452
  67.5 2.0 %collective-permute-start.8 = (f32[272,256]{1,0:T(8,128)S(1)}, f32[272,256]{1,0:T(8,128)S(1)}, u32[]{:S(2)}, u32[]{:S(2)}) collective-permute-start(f32[272,256]{1,0:T(8,128)S(1)} %get-tuple-element.58), channel_id=1, source_target_pairs={{0,1},{1,0},{2,3},{3,2},{4,5},{5,4},{6,7},{7,6},{8,9},{9,8},{10,11... | collective-permute-start | bytes 835592 | tf_op jit(solution)/shard_map/ppermute | solution.py:456
  69.5 0.0 collective-permute-done.9.back_b
  69.5 3.4 %collective-permute-done.10.back_c = f32[272,256]{1,0:T(8,128)S(1)} collective-permute-done((f32[272,256]{1,0:T(8,128)S(1)}, f32[272,256]{1,0:T(8,128)S(1)}, u32[]{:S(2)}, u32[]{:S(2)}) %collective-permute-start.10) | collective-permute-done | bytes 278560 | tf_op jit(solution)/shard_map/ppermute | solution.py:451
  72.9 1.2 %shard_map.101 = (f32[2048,256]{1,0:T(8,128)}, f32[8,2048]{1,0:T(8,128)S(1)}, f32[8,2048]{1,0:T(8,128)S(1)}) custom-call(f32[272,256]{1,0:T(8,128)S(1)} %get-tuple-element.53.own_a, f32[272,256]{1,0:T(8,128)S(1)} %get-tuple-element.54.own_b, f32[272,256]{1,0:T(8,128)S(1)} %get-tuple-element.56.own_c, ...), custom_call_target="tpu_custom_call", output_to_operand_aliasing={{0}: (7, {})} | custom-call | flops 1048576 | bytes 4194304 | tf_op jit(solution)/shard_map/pallas_call | solution.py:458
  74.1 2.9 %collective-permute-done.8.back_d = f32[272,256]{1,0:T(8,128)S(1)} collective-permute-done((f32[272,256]{1,0:T(8,128)S(1)}, f32[272,256]{1,0:T(8,128)S(1)}, u32[]{:S(2)}, u32[]{:S(2)}) %collective-permute-start.8) | collective-permute-done | bytes 278560 | tf_op jit(solution)/shard_map/ppermute | solution.py:456
  76.9 1.4 %shard_map.102 = (f32[2048,256]{1,0:T(8,128)}, f32[8,2048]{1,0:T(8,128)}, f32[8,2048]{1,0:T(8,128)}) custom-call(f32[272,256]{1,0:T(8,128)S(1)} %collective-permute-done.8.back_d, f32[2048,256]{1,0:T(8,128)} %get-tuple-element.63.wave_in, f32[8,2048]{1,0:T(8,128)S(1)} %get-tuple-element.64.phase_in, ...), custom_call_target="tpu_custom_call", output_to_operand_aliasing={{0}: (1, {})} | custom-call | flops 1048576 | bytes 4194304 | tf_op jit(solution)/shard_map/pallas_call | solution.py:462
Async XLA Ops:
  2.9 10.4 %collective-permute-start = (f32[296,256]{1,0:T(8,128)}, f32[296,256]{1,0:T(8,128)S(1)}, u32[]{:S(2)}, u32[]{:S(2)}) collective-permute-start(f32[296,256]{1,0:T(8,128)} %get-tuple-element.37.near), channel_id=1, source_target_pairs={{0,1},{1,0},{2,3},{3,2},{4,5},{5,4},{6,7},{7,6},{8,9},{9,8},{10,11... | collective-permute-start | bytes 909320 | tf_op jit(solution)/shard_map/ppermute | solution.py:420
  4.2 4.9 %copy-start.4 = (f32[552,256]{1,0:T(8,128)S(1)}, f32[552,256]{1,0:T(8,128)}, u32[]{:S(2)}) copy-start(f32[552,256]{1,0:T(8,128)} %get-tuple-element.48) | copy-start | bytes 1695748
  4.2 9.1 %copy-start = (f32[8,2,128,256]{3,2,1,0:T(8,128)S(1)}, f32[8,2,128,256]{3,2,1,0:T(8,128)}, u32[]{:S(2)}) copy-start(f32[8,2,128,256]{3,2,1,0:T(8,128)} %param.7) | copy-start | bytes 6291460
  4.2 9.1 %copy-start.1 = (f32[40,256]{1,0:T(8,128)S(1)}, f32[40,256]{1,0:T(8,128)}, u32[]{:S(2)}) copy-start(f32[40,256]{1,0:T(8,128)} %get-tuple-element.36.mine) | copy-start | bytes 122884
  4.2 9.1 %copy-start.2 = (bf16[2,2,2,256,256]{4,3,2,1,0:T(8,128)(2,1)S(1)}, bf16[2,2,2,256,256]{4,3,2,1,0:T(8,128)(2,1)}, u32[]{:S(2)}) copy-start(bf16[2,2,2,256,256]{4,3,2,1,0:T(8,128)(2,1)} %constant.2.clone.table) | copy-start | bytes 3145732
  4.2 13.8 %collective-permute-start.2 = (f32[552,256]{1,0:T(8,128)}, f32[552,256]{1,0:T(8,128)}, u32[]{:S(2)}, u32[]{:S(2)}) collective-permute-start(f32[552,256]{1,0:T(8,128)} %get-tuple-element.48), channel_id=1, source_target_pairs={{62,65},{126,1}} | collective-permute-start | bytes 1695752 | tf_op jit(solution)/shard_map/ppermute | solution.py:421
  8.3 15.0 %collective-permute-start.1 = (f32[376,256]{1,0:T(8,128)}, f32[376,256]{1,0:T(8,128)S(1)}, u32[]{:S(2)}, u32[]{:S(2)}) collective-permute-start(f32[376,256]{1,0:T(8,128)} %get-tuple-element.40), channel_id=1, source_target_pairs={{0,1},{1,0},{2,3},{3,2},{4,5},{5,4},{6,7},{7,6},{8,9},{9,8},{10,11... | collective-permute-start | bytes 1155080 | tf_op jit(solution)/shard_map/ppermute | solution.py:426
  9.1 25.4 %collective-permute-start.4 = (f32[552,256]{1,0:T(8,128)S(1)}, f32[552,256]{1,0:T(8,128)S(1)}, u32[]{:S(2)}, u32[]{:S(2)}) collective-permute-start(f32[552,256]{1,0:T(8,128)S(1)} %copy-done.4), channel_id=1, source_target_pairs={{0,2},{1,1},{2,4},{3,3},{4,6},{5,5},{6,8},{7,7},{8,10},{9,9},{10,1... | collective-permute-start | bytes 1695752 | tf_op jit(solution)/shard_map/ppermute | solution.py:428
  13.3 4.7 %copy-start.5 = (f32[552,256]{1,0:T(8,128)S(1)}, f32[552,256]{1,0:T(8,128)}, u32[]{:S(2)}) copy-start(f32[552,256]{1,0:T(8,128)} %get-tuple-element.47) | copy-start | bytes 1695748
  13.3 10.0 %copy-start.3 = (f32[8,40,256]{2,1,0:T(8,128)S(1)}, f32[8,40,256]{2,1,0:T(8,128)}, u32[]{:S(2)}) copy-start(f32[8,40,256]{2,1,0:T(8,128)} %get-tuple-element.39.parts) | copy-start | bytes 983044
  18.0 16.5 %collective-permute-start.3 = (f32[552,256]{1,0:T(8,128)S(1)}, f32[552,256]{1,0:T(8,128)S(1)}, u32[]{:S(2)}, u32[]{:S(2)}) collective-permute-start(f32[552,256]{1,0:T(8,128)S(1)} %copy-done.5), channel_id=1, source_target_pairs={{0,1},{1,2},{2,3},{3,4},{4,5},{5,6},{6,7},{7,8},{8,9},{9,10},{10,1... | collective-permute-start | bytes 1695752 | tf_op jit(solution)/shard_map/ppermute | solution.py:435
  22.0 21.3 %collective-permute-start.5 = (f32[552,256]{1,0:T(8,128)}, f32[552,256]{1,0:T(8,128)S(1)}, u32[]{:S(2)}, u32[]{:S(2)}) collective-permute-start(f32[552,256]{1,0:T(8,128)} %collective-permute-done.2), channel_id=1, source_target_pairs={{65,64},{1,0}} | collective-permute-start | bytes 1695752 | tf_op jit(solution)/shard_map/ppermute | solution.py:434
  31.7 27.4 %collective-permute-start.7 = (f32[272,256]{1,0:T(8,128)S(1)}, f32[272,256]{1,0:T(8,128)S(1)}, u32[]{:S(2)}, u32[]{:S(2)}) collective-permute-start(f32[272,256]{1,0:T(8,128)S(1)} %get-tuple-element.55), channel_id=1, source_target_pairs={{0,1},{1,0},{2,3},{3,2},{4,5},{5,4},{6,7},{7,6},{8,9},{9,8},{10,11... | collective-permute-start | bytes 835592 | tf_op jit(solution)/shard_map/ppermute | solution.py:440
  57.0 6.5 %collective-permute-start.6 = (f32[2,16,256]{2,1,0:T(8,128)S(1)}, f32[2,16,256]{2,1,0:T(8,128)S(1)}, u32[]{:S(2)}, u32[]{:S(2)}) collective-permute-start(f32[2,16,256]{2,1,0:T(8,128)S(1)} %get-tuple-element.50), channel_id=1, source_target_pairs={{1,0},{2,1},{3,2},{4,3},{5,4},{6,5},{7,6},{8,7},{9,8},{10,9},{11,1... | collective-permute-start | bytes 98312 | tf_op jit(solution)/shard_map/ppermute | solution.py:445
  57.1 12.5 %collective-permute-start.9 = (f32[272,256]{1,0:T(8,128)S(1)}, f32[272,256]{1,0:T(8,128)S(1)}, u32[]{:S(2)}, u32[]{:S(2)}) collective-permute-start(f32[272,256]{1,0:T(8,128)S(1)} %get-tuple-element.60), channel_id=1, source_target_pairs={{0,1},{1,0},{2,3},{3,2},{4,5},{5,4},{6,7},{7,6},{8,9},{9,8},{10,11... | collective-permute-start | bytes 835592 | tf_op jit(solution)/shard_map/ppermute | solution.py:446
  63.3 9.6 %collective-permute-start.10 = (f32[272,256]{1,0:T(8,128)S(1)}, f32[272,256]{1,0:T(8,128)S(1)}, u32[]{:S(2)}, u32[]{:S(2)}) collective-permute-start(f32[272,256]{1,0:T(8,128)S(1)} %get-tuple-element.61), channel_id=1, source_target_pairs={{0,1},{1,0},{2,3},{3,2},{4,5},{5,4},{6,7},{7,6},{8,9},{9,8},{10,11... | collective-permute-start | bytes 835592 | tf_op jit(solution)/shard_map/ppermute | solution.py:451
  67.5 9.4 %collective-permute-start.8 = (f32[272,256]{1,0:T(8,128)S(1)}, f32[272,256]{1,0:T(8,128)S(1)}, u32[]{:S(2)}, u32[]{:S(2)}) collective-permute-start(f32[272,256]{1,0:T(8,128)S(1)} %get-tuple-element.58), channel_id=1, source_target_pairs={{0,1},{1,0},{2,3},{3,2},{4,5},{5,4},{6,7},{7,6},{8,9},{9,8},{10,11... | collective-permute-start | bytes 835592 | tf_op jit(solution)/shard_map/ppermute | solution.py:456

commit v8 on v7

--- a/solution.py
+++ b/solution.py
@@ -206,17 +206,18 @@
 
 
 def early_pack_kernel(wave, *refs):
-    sources, (near_ref, ahead_ref, mine_ref), (floats, ints, sems) = refs[:5], refs[5:8], refs[8:]
+    sources, (near_ref, ahead_ref, next_ref, mine_ref), (floats, ints, sems) = refs[:5], refs[5:9], refs[9:]
     r = lax.axis_index("row")
     loads, copies = Copies(sems), Copies(sems)
     copies.used = 5
     load_all(loads, sources, floats, ints)
     copies.start(wave.at[pl.ds(N * (5 - 4 * r), N)], near_ref.at[pl.ds(0, N)])
-    copies.start(wave.at[pl.ds(N * (6 - 4 * r), 2 * N)], ahead_ref.at[pl.ds(0, 2 * N)])
+    copies.start(wave.at[pl.ds(N * (6 - 4 * r), N)], ahead_ref.at[pl.ds(0, N)])
+    copies.start(wave.at[pl.ds(N * (7 - 4 * r), N)], next_ref)
     loads.wait()
     pack_slice(floats, ints, 6 - 4 * r, near_ref, N)
     pack_slice(floats, ints, 2 + 4 * r, mine_ref, 0)
-    pack_slice(floats, ints, 7 - 4 * r, ahead_ref, 2 * N)
+    pack_slice(floats, ints, 7 - 4 * r, ahead_ref, N)
     copies.wait()
 
 
@@ -291,17 +292,17 @@
     piece_out(r, f2, pushed, own, away)
 
 
-def second_kernel(q1, parts, swap, chain, ahead, relay, table, d_ref, q_ref, to_back, own, away,
+def second_kernel(q1, parts, swap, chain, ahead, following, relay, table, d_ref, q_ref, to_back, own, away,
                   f0, f1, p0, pm, pushed, z, tab, *rest):
     work, sems = rest[:-1], rest[-1]
     r = lax.axis_index("row")
     copies, later = Copies(sems), Copies(sems)
     later.used = 23
     field_in(copies, r, f0, ahead, 0, chain, 0)
-    copies.start(ahead.at[pl.ds(2 * N, FIELDS)], pm.at[r])
+    copies.start(ahead.at[pl.ds(N, FIELDS)], pm.at[r])
     copies.start(chain.at[pl.ds(2 * N, FIELDS)], pm.at[1 - r])
     later.start(table, tab)
-    field_in(copies, r, f1, ahead, N, chain, N)
+    field_in(copies, r, f1, following, 0, chain, N)
     parts_in(copies, r, p0, parts, 0, swap, N)
     copies.wait()
 
@@ -309,11 +310,9 @@
     def _():
         again = Copies(sems)
         again.used = 15
-        for i, f in enumerate((f0, f1)):
-            for z in range(2):
-                again.start(relay.at[pl.ds(N * i + HALF * z, HALF)],
-                            f.at[z, pl.ds(pl.multiple_of(HALF * r, HALF), HALF)])
-        again.start(relay.at[pl.ds(2 * N, FIELDS)], pm.at[r])
+        for z in range(2):
+            again.start(relay.at[pl.ds(HALF * z, HALF)], f0.at[z, pl.ds(pl.multiple_of(HALF * r, HALF), HALF)])
+        again.start(relay.at[pl.ds(N, FIELDS)], pm.at[r])
         again.wait()
 
     @pl.when((r == 0) & (lax.axis_index("tm") == 0))
@@ -405,6 +404,7 @@
     ahead = [(i, i + 2 if i % 2 == 0 else i) for i in range(2 * nt) if i not in far]
     around = [(i, (i + 3) % (2 * nt)) for i in far]
     onward = [(j, j - 1) for i, j in around]
+    direct = [(i, i + 2) for i in far if i + 2 < 2 * nt]
     back = [(j, i) for i, j in chain]
     wave = wavefront.reshape(8 * N, N)
     unit = 1 << 33
@@ -413,12 +413,13 @@
     pieces = [(PIECE, N), (PIECE, N)]
     raw = (wave, particle_phase, particle_energy, row_offset, row_cell, col_cell)
     stage = [pltpu.VMEM((3, 8, PART), F32), pltpu.VMEM((2, 8, PART), jnp.int32)]
-    to_near, to_ahead, mine = call(
-        early_pack_kernel, [(N + FIELDS, N), (2 * N + FIELDS, N), (FIELDS, N)], [VM] * 3, stage, 8, [HB] * 6, 1 << 20,
+    to_near, to_ahead, to_next, mine = call(
+        early_pack_kernel, [(N + FIELDS, N), (N + FIELDS, N), (N, N), (FIELDS, N)], [VM] * 4, stage, 8, [HB] * 6, 1 << 20,
         vmem=61000 << 10,
     )(*raw)
     f_near = lax.ppermute(to_near, both, swap)
     f_around = lax.ppermute(to_ahead, both, around)
+    f_next = lax.ppermute(to_next, both, ahead + direct)
     parts, to_swap, to_chain = call(
         pack_kernel, [(8, FIELDS, N), (N + 3 * FIELDS, N), (2 * N + FIELDS, N)],
         [VM] * 3, stage, 8, [ANY] + [HB] * 6, 4 * unit, vmem=61000 << 10,
@@ -440,8 +441,8 @@
     back_a = lax.ppermute(away_a, both, swap)
     d0, q0, to_back, own_b, away_b = call(
         second_kernel, [field, full, (2, PUSHED, N)] + pieces, [VM] * 5,
-        [FIELD, FIELD, PARTS, PARTS, PUSH, FIELD, TABLE] + WORK, 24, [VM] + [ANY] * 6, 3 * unit,
-    )(q1, parts, f_swap, f_chain, f_ahead, f_relay, table)
+        [FIELD, FIELD, PARTS, PARTS, PUSH, FIELD, TABLE] + WORK, 24, [VM] + [ANY] * 7, 3 * unit,
+    )(q1, parts, f_swap, f_chain, f_ahead, f_next, f_relay, table)
     from_back = lax.ppermute(to_back, both, back)
     back_b = lax.ppermute(away_b, both, swap)
     own_c, away_c, wave = call(

time: 78.7 us -> 78.3 us (level)
  waiting for transfers between devices: 17.9 us -> 14.5 us
  starting transfers between devices: 17.4 us -> 20.4 us
    ppermute x1, waiting for transfers between devices: 8.76 us -> 0.01 us  [body(): f_relay = lax.ppermute(f_around, both, onward)]
    ppermute x1, starting transfers between devices: 0.08 us -> 7.25 us  [body(): from_back = lax.ppermute(to_back, both, back)]
    ppermute x1, waiting for transfers between devices: 0.01 us -> 4.69 us  [body(): f_chain = lax.ppermute(to_chain, both, chain)]
    ppermute x1, starting transfers between devices: 2.76 us -> 0.34 us  [body(): back_a = lax.ppermute(away_a, both, swap)]
    ppermute x1, starting transfers between devices: 2.01 us -> 0.01 us  [body(): back_b = lax.ppermute(away_b, both, swap)]
    ppermute x1, starting transfers between devices: 0.18 us -> 2.1 us  [body(): back_c = lax.ppermute(away_c, both, swap)]
    ppermute x0 -> x1, starting transfers between devices: none -> 1.92 us  [body(): f_next = lax.ppermute(to_next, both, ahead + direct)]
    ppermute x1, starting transfers between devices: 2.01 us -> 0.14 us  [body(): back_d = lax.ppermute(away_d, both, swap)]
  transfers between devices with their start and end apart: 11 -> 12, of which waited for: 4 -> 5; matrix products, arithmetic and copies ran while one was open for 0% -> 0% of each run, Pallas kernels for 49% -> 49%
where the time goes in v8:
time: 78.3 us; the launch traced here: 78.1 us
  Pallas kernels  42.2 us (54%)
  starting transfers between devices  20.4 us (26%)
  waiting for transfers between devices  14.5 us (19%)
  between operations  0.97 us (1%)
    pallas_call x1, Pallas kernels, body(): call(second_kernel, [field, full, (2, PUSHED, N)] + pieces, [VM] * 5, [FI...  13.4 us
    pallas_call x1, Pallas kernels, body(): call(first_kernel, [full] + pieces, [VM] * 3, [FIELD, PARTS, PUSH, FIELD,...  8.38 us
    ppermute x1, starting transfers between devices, body(): from_back = lax.ppermute(to_back, both, back)  7.25 us
    ppermute x1, waiting for transfers between devices, body(): f_chain = lax.ppermute(to_chain, both, chain)  4.69 us
    pallas_call x1, Pallas kernels, body(): call(near_kernel, [field, full], [VM, VM], [FIELD, PARTS, TABLE] + WORK,...  4.67 us
    pallas_call x1, Pallas kernels, body(): call(third_kernel, pieces + [(8 * N, N)], [VM, VM, ANY], [FIELD, PUSH, FI...  4.22 us
    pallas_call x1, Pallas kernels, body(): call(fourth_kernel, pieces + [(8 * N, N)], [VM, VM, ANY], [PARTS, PUSH, F...  4.03 us
    ppermute x1, waiting for transfers between devices, body(): back_d = lax.ppermute(away_d, both, swap)  3.4 us
  transfers between devices with their start and end apart: 12, of which 5 were waited for; matrix products, arithmetic and copies ran while one was open for 0% of the time, Pallas kernels for 49%

profile of v8, /device:TPU:4, one launch (start us, length us, event | category | flops | bytes accessed | tf_op | source)
XLA Modules:
  0.0 78.1 jit_solution(17237670079614911203)
XLA Ops:
  0.6 2.3 %shard_map.94 = (f32[296,256]{1,0:T(8,128)}, f32[296,256]{1,0:T(8,128)}, f32[256,256]{1,0:T(8,128)}, f32[40,256]{1,0:T(8,128)}) custom-call(f32[2048,256]{1,0:T(8,128)} %bitcast.2, f32[8,2048]{1,0:T(8,128)} %refs_0_.3, f32[8,2048]{1,0:T(8,128)} %refs_1_.3, f32[8,2048]{1,0:T(8,128)} %refs_2_.3, s32[8,2048]{1,0:T(8,128)} %refs_3_.3, s32[8,2048]{1,0:T(8,128)} %refs_4_.3), custom_call_target="tpu_custom_call" | custom-call | flops 1048576 | bytes 4194304 | tf_op jit(solution)/shard_map/pallas_call | solution.py:416
  3.0 1.9 %collective-permute-start.5 = (f32[256,256]{1,0:T(8,128)}, f32[256,256]{1,0:T(8,128)S(1)}, u32[]{:S(2)}, u32[]{:S(2)}) collective-permute-start(f32[256,256]{1,0:T(8,128)} %get-tuple-element.50), channel_id=1, source_target_pairs={{0,2},{1,1},{2,4},{3,3},{4,6},{5,5},{6,8},{7,7},{8,10},{9,9},{10,1... | collective-permute-start | bytes 786440 | tf_op jit(solution)/shard_map/ppermute | solution.py:422
  4.9 0.9 %collective-permute-start = (f32[296,256]{1,0:T(8,128)}, f32[296,256]{1,0:T(8,128)S(1)}, u32[]{:S(2)}, u32[]{:S(2)}) collective-permute-start(f32[296,256]{1,0:T(8,128)} %get-tuple-element.38.near), channel_id=1, source_target_pairs={{0,1},{1,0},{2,3},{3,2},{4,5},{5,4},{6,7},{7,6},{8,9},{9,8},{10,11... | collective-permute-start | bytes 909320 | tf_op jit(solution)/shard_map/ppermute | solution.py:420
  5.8 0.0 copy-start.5
  5.8 0.0 copy-start
  5.8 0.0 copy-start.1
  5.8 0.0 copy-start.2
  5.8 0.8 %collective-permute-start.2 = (f32[296,256]{1,0:T(8,128)}, f32[296,256]{1,0:T(8,128)S(1)}, u32[]{:S(2)}, u32[]{:S(2)}) collective-permute-start(f32[296,256]{1,0:T(8,128)} %get-tuple-element.49), channel_id=1, source_target_pairs={{62,65},{126,1}} | collective-permute-start | bytes 909320 | tf_op jit(solution)/shard_map/ppermute | solution.py:421
  6.6 2.6 %shard_map.96 = (f32[8,40,256]{2,1,0:T(8,128)}, f32[376,256]{1,0:T(8,128)}, f32[552,256]{1,0:T(8,128)}) custom-call(f32[296,256]{1,0:T(8,128)} %get-tuple-element.38.near, f32[2048,256]{1,0:T(8,128)} %bitcast.3, f32[8,2048]{1,0:T(8,128)} %refs_0_.3, f32[8,2048]{1,0:T(8,128)} %refs_1_.3, f32[8,2048]{1,0:T(8,128)} %refs_2_.3, s32[8,2048]{1,0:T(8,128)} %refs_3_.3, ...), custom_call_target="tpu_custom_call" | custom-call | flops 34359738368 | bytes 4194304 | tf_op jit(solution)/shard_map/pallas_call | solution.py:423
  9.2 0.0 copy-done.5
  9.2 2.8 %collective-permute-start.4 = (f32[296,256]{1,0:T(8,128)S(1)}, f32[296,256]{1,0:T(8,128)S(1)}, u32[]{:S(2)}, u32[]{:S(2)}) collective-permute-start(f32[296,256]{1,0:T(8,128)S(1)} %copy-done.5), channel_id=1, source_target_pairs={{0,2},{1,1},{2,4},{3,3},{4,6},{5,5},{6,8},{7,7},{8,10},{9,9},{10,1... | collective-permute-start | bytes 909320 | tf_op jit(solution)/shard_map/ppermute | solution.py:429
  12.1 0.1 collective-permute-start.1
  12.1 2.4 %collective-permute-done.near = f32[296,256]{1,0:T(8,128)S(1)} collective-permute-done((f32[296,256]{1,0:T(8,128)}, f32[296,256]{1,0:T(8,128)S(1)}, u32[]{:S(2)}, u32[]{:S(2)}) %collective-permute-start) | collective-permute-done | bytes 303136 | tf_op jit(solution)/shard_map/ppermute | solution.py:420
  14.6 0.0 copy-done
  14.6 0.0 copy-done.1
  14.6 0.0 copy-done.2
  14.6 0.0 copy-start.4
  14.6 0.0 copy-start.3
  14.6 4.7 %shard_map.95 = (f32[2,256,256]{2,1,0:T(8,128)S(1)}, f32[2,40,256]{2,1,0:T(8,128)S(1)}) custom-call(f32[2048,256]{1,0:T(8,128)S(1)} %bitcast.4, f32[40,256]{1,0:T(8,128)S(1)} %copy-done.1, f32[296,256]{1,0:T(8,128)S(1)} %collective-permute-done.near, bf16[2,2,2,256,256]{4,3,2,1,0:T(8,128)(2,1)S(1)} %copy-done.2), custom_call_target="tpu_custom_call" | custom-call | flops 8589934592 | bytes 4194304 | tf_op jit(solution)/shard_map/pallas_call | solution.py:431
  19.3 0.0 collective-permute-done.2
  19.3 1.3 %collective-permute-start.6 = (f32[296,256]{1,0:T(8,128)S(1)}, f32[296,256]{1,0:T(8,128)S(1)}, u32[]{:S(2)}, u32[]{:S(2)}) collective-permute-start(f32[296,256]{1,0:T(8,128)S(1)} %collective-permute-done.2), channel_id=1, source_target_pairs={{65,64},{1,0}} | collective-permute-start | bytes 909320 | tf_op jit(solution)/shard_map/ppermute | solution.py:435
  20.6 0.0 copy-done.4
  20.6 2.7 %collective-permute-start.3 = (f32[552,256]{1,0:T(8,128)S(1)}, f32[552,256]{1,0:T(8,128)S(1)}, u32[]{:S(2)}, u32[]{:S(2)}) collective-permute-start(f32[552,256]{1,0:T(8,128)S(1)} %copy-done.4), channel_id=1, source_target_pairs={{0,1},{1,2},{2,3},{3,4},{4,5},{5,6},{6,7},{7,8},{8,9},{9,10},{10,1... | collective-permute-start | bytes 1695752 | tf_op jit(solution)/shard_map/ppermute | solution.py:436
  23.3 0.6 collective-permute-done.1.swap
  24.0 0.0 copy-done.3
  24.0 8.4 %shard_map.97 = (f32[2,40,256]{2,1,0:T(8,128)S(1)}, f32[272,256]{1,0:T(8,128)S(1)}, f32[272,256]{1,0:T(8,128)S(1)}) custom-call(f32[2,40,256]{2,1,0:T(8,128)S(1)} %get-tuple-element.46.q2, f32[2048,256]{1,0:T(8,128)S(1)} %bitcast.5, f32[8,40,256]{2,1,0:T(8,128)S(1)} %copy-done.3, f32[376,256]{1,0:T(8,128)S(1)} %collective-permute-done.1.swap, ...), custom_call_target="tpu_custom_call" | custom-call | flops 17179869184 | bytes 4194304 | tf_op jit(solution)/shard_map/pallas_call | solution.py:437
  32.4 0.3 collective-permute-start.8
  32.7 0.0 collective-permute-done.5.following
  32.7 0.0 collective-permute-done.4.ahead
  32.7 0.0 collective-permute-done.6.relay
  32.7 4.7 %collective-permute-done.3.chain = f32[552,256]{1,0:T(8,128)S(1)} collective-permute-done((f32[552,256]{1,0:T(8,128)S(1)}, f32[552,256]{1,0:T(8,128)S(1)}, u32[]{:S(2)}, u32[]{:S(2)}) %collective-permute-start.3) | collective-permute-done | bytes 565280 | tf_op jit(solution)/shard_map/ppermute | solution.py:436
  37.4 13.4 %shard_map.98 = (f32[2,256,256]{2,1,0:T(8,128)S(1)}, f32[2,40,256]{2,1,0:T(8,128)S(1)}, f32[2,16,256]{2,1,0:T(8,128)S(1)}, f32[272,256]{1,0:T(8,128)S(1)}, f32[272,256]{1,0:T(8,128)S(1)}) custom-call(f32[2,40,256]{2,1,0:T(8,128)S(1)} %get-tuple-element.47.q1, f32[8,40,256]{2,1,0:T(8,128)S(1)} %copy-done.3, f32[376,256]{1,0:T(8,128)S(1)} %collective-permute-done.1.swap, ...), custom_call_target="tpu_custom_call" | custom-call | flops 25769803776 | bytes 4194304 | tf_op jit(solution)/shard_map/pallas_call | solution.py:442
  50.8 7.2 %collective-permute-start.7 = (f32[2,16,256]{2,1,0:T(8,128)S(1)}, f32[2,16,256]{2,1,0:T(8,128)S(1)}, u32[]{:S(2)}, u32[]{:S(2)}) collective-permute-start(f32[2,16,256]{2,1,0:T(8,128)S(1)} %get-tuple-element.52), channel_id=1, source_target_pairs={{1,0},{2,1},{3,2},{4,3},{5,4},{6,5},{7,6},{8,7},{9,8},{10,9},{11,1... | collective-permute-start | bytes 98312 | tf_op jit(solution)/shard_map/ppermute | solution.py:446
  58.0 0.0 collective-permute-start.10
  58.0 0.0 collective-permute-done.8.back_a
  58.0 4.2 %shard_map.99 = (f32[272,256]{1,0:T(8,128)S(1)}, f32[272,256]{1,0:T(8,128)S(1)}, f32[2048,256]{1,0:T(8,128)}) custom-call(f32[2,256,256]{2,1,0:T(8,128)S(1)} %get-tuple-element.53.d_ref, f32[2,40,256]{2,1,0:T(8,128)S(1)} %get-tuple-element.54.q0, f32[272,256]{1,0:T(8,128)S(1)} %get-tuple-element.55.own_a, f32[272,256]{1,0:T(8,128)S(1)} %get-tuple-element.56.own_b, ...), custom_call_target="tpu_custom_call" | custom-call | flops 8589934592 | bytes 4194304 | tf_op jit(solution)/shard_map/pallas_call | solution.py:448
  62.3 2.1 %collective-permute-start.11 = (f32[272,256]{1,0:T(8,128)S(1)}, f32[272,256]{1,0:T(8,128)S(1)}, u32[]{:S(2)}, u32[]{:S(2)}) collective-permute-start(f32[272,256]{1,0:T(8,128)S(1)} %get-tuple-element.63), channel_id=1, source_target_pairs={{0,1},{1,0},{2,3},{3,2},{4,5},{5,4},{6,7},{7,6},{8,9},{9,8},{10,11... | collective-permute-start | bytes 835592 | tf_op jit(solution)/shard_map/ppermute | solution.py:452
  64.4 0.0 collective-permute-done.7.from_back
  64.4 4.0 %shard_map.100 = (f32[272,256]{1,0:T(8,128)S(1)}, f32[272,256]{1,0:T(8,128)S(1)}, f32[2048,256]{1,0:T(8,128)}) custom-call(f32[2,256,256]{2,1,0:T(8,128)S(1)} %get-tuple-element.39.d_ref, f32[8,40,256]{2,1,0:T(8,128)S(1)} %copy-done.3, f32[376,256]{1,0:T(8,128)S(1)} %collective-permute-done.1.swap, ...), custom_call_target="tpu_custom_call", output_to_operand_aliasing={{2}: (6, {})} | custom-call | flops 17179869184 | bytes 4194304 | tf_op jit(solution)/shard_map/pallas_call | solution.py:453
  68.4 0.1 collective-permute-start.9
  68.6 0.0 collective-permute-done.10.back_b
  68.6 3.4 %collective-permute-done.11.back_c = f32[272,256]{1,0:T(8,128)S(1)} collective-permute-done((f32[272,256]{1,0:T(8,128)S(1)}, f32[272,256]{1,0:T(8,128)S(1)}, u32[]{:S(2)}, u32[]{:S(2)}) %collective-permute-start.11) | collective-permute-done | bytes 278560 | tf_op jit(solution)/shard_map/ppermute | solution.py:452
  72.0 1.2 %shard_map.101 = (f32[2048,256]{1,0:T(8,128)}, f32[8,2048]{1,0:T(8,128)S(1)}, f32[8,2048]{1,0:T(8,128)S(1)}) custom-call(f32[272,256]{1,0:T(8,128)S(1)} %get-tuple-element.55.own_a, f32[272,256]{1,0:T(8,128)S(1)} %get-tuple-element.56.own_b, f32[272,256]{1,0:T(8,128)S(1)} %get-tuple-element.58.own_c, ...), custom_call_target="tpu_custom_call", output_to_operand_aliasing={{0}: (7, {})} | custom-call | flops 1048576 | bytes 4194304 | tf_op jit(solution)/shard_map/pallas_call | solution.py:459
  73.1 3.4 %collective-permute-done.9.back_d = f32[272,256]{1,0:T(8,128)S(1)} collective-permute-done((f32[272,256]{1,0:T(8,128)S(1)}, f32[272,256]{1,0:T(8,128)S(1)}, u32[]{:S(2)}, u32[]{:S(2)}) %collective-permute-start.9) | collective-permute-done | bytes 278560 | tf_op jit(solution)/shard_map/ppermute | solution.py:457
  76.5 1.4 %shard_map.102 = (f32[2048,256]{1,0:T(8,128)}, f32[8,2048]{1,0:T(8,128)}, f32[8,2048]{1,0:T(8,128)}) custom-call(f32[272,256]{1,0:T(8,128)S(1)} %collective-permute-done.9.back_d, f32[2048,256]{1,0:T(8,128)} %get-tuple-element.65.wave_in, f32[8,2048]{1,0:T(8,128)S(1)} %get-tuple-element.66.phase_in, ...), custom_call_target="tpu_custom_call", output_to_operand_aliasing={{0}: (1, {})} | custom-call | flops 1048576 | bytes 4194304 | tf_op jit(solution)/shard_map/pallas_call | solution.py:463
Async XLA Ops:
  3.0 29.7 %collective-permute-start.5 = (f32[256,256]{1,0:T(8,128)}, f32[256,256]{1,0:T(8,128)S(1)}, u32[]{:S(2)}, u32[]{:S(2)}) collective-permute-start(f32[256,256]{1,0:T(8,128)} %get-tuple-element.50), channel_id=1, source_target_pairs={{0,2},{1,1},{2,4},{3,3},{4,6},{5,5},{6,8},{7,7},{8,10},{9,9},{10,1... | collective-permute-start | bytes 786440 | tf_op jit(solution)/shard_map/ppermute | solution.py:422
  4.9 9.7 %collective-permute-start = (f32[296,256]{1,0:T(8,128)}, f32[296,256]{1,0:T(8,128)S(1)}, u32[]{:S(2)}, u32[]{:S(2)}) collective-permute-start(f32[296,256]{1,0:T(8,128)} %get-tuple-element.38.near), channel_id=1, source_target_pairs={{0,1},{1,0},{2,3},{3,2},{4,5},{5,4},{6,7},{7,6},{8,9},{9,8},{10,11... | collective-permute-start | bytes 909320 | tf_op jit(solution)/shard_map/ppermute | solution.py:420
  5.8 3.4 %copy-start.5 = (f32[296,256]{1,0:T(8,128)S(1)}, f32[296,256]{1,0:T(8,128)}, u32[]{:S(2)}) copy-start(f32[296,256]{1,0:T(8,128)} %get-tuple-element.49) | copy-start | bytes 909316
  5.8 8.8 %copy-start = (f32[8,2,128,256]{3,2,1,0:T(8,128)S(1)}, f32[8,2,128,256]{3,2,1,0:T(8,128)}, u32[]{:S(2)}) copy-start(f32[8,2,128,256]{3,2,1,0:T(8,128)} %param.7) | copy-start | bytes 6291460
  5.8 8.8 %copy-start.1 = (f32[40,256]{1,0:T(8,128)S(1)}, f32[40,256]{1,0:T(8,128)}, u32[]{:S(2)}) copy-start(f32[40,256]{1,0:T(8,128)} %get-tuple-element.37.mine) | copy-start | bytes 122884
  5.8 8.8 %copy-start.2 = (bf16[2,2,2,256,256]{4,3,2,1,0:T(8,128)(2,1)S(1)}, bf16[2,2,2,256,256]{4,3,2,1,0:T(8,128)(2,1)}, u32[]{:S(2)}) copy-start(bf16[2,2,2,256,256]{4,3,2,1,0:T(8,128)(2,1)} %constant.2.clone.table) | copy-start | bytes 3145732
  5.8 13.5 %collective-permute-start.2 = (f32[296,256]{1,0:T(8,128)}, f32[296,256]{1,0:T(8,128)S(1)}, u32[]{:S(2)}, u32[]{:S(2)}) collective-permute-start(f32[296,256]{1,0:T(8,128)} %get-tuple-element.49), channel_id=1, source_target_pairs={{62,65},{126,1}} | collective-permute-start | bytes 909320 | tf_op jit(solution)/shard_map/ppermute | solution.py:421
  9.2 23.5 %collective-permute-start.4 = (f32[296,256]{1,0:T(8,128)S(1)}, f32[296,256]{1,0:T(8,128)S(1)}, u32[]{:S(2)}, u32[]{:S(2)}) collective-permute-start(f32[296,256]{1,0:T(8,128)S(1)} %copy-done.5), channel_id=1, source_target_pairs={{0,2},{1,1},{2,4},{3,3},{4,6},{5,5},{6,8},{7,7},{8,10},{9,9},{10,1... | collective-permute-start | bytes 909320 | tf_op jit(solution)/shard_map/ppermute | solution.py:429
  12.1 11.9 %collective-permute-start.1 = (f32[376,256]{1,0:T(8,128)}, f32[376,256]{1,0:T(8,128)S(1)}, u32[]{:S(2)}, u32[]{:S(2)}) collective-permute-start(f32[376,256]{1,0:T(8,128)} %get-tuple-element.41), channel_id=1, source_target_pairs={{0,1},{1,0},{2,3},{3,2},{4,5},{5,4},{6,7},{7,6},{8,9},{9,8},{10,11... | collective-permute-start | bytes 1155080 | tf_op jit(solution)/shard_map/ppermute | solution.py:427
  14.6 6.0 %copy-start.4 = (f32[552,256]{1,0:T(8,128)S(1)}, f32[552,256]{1,0:T(8,128)}, u32[]{:S(2)}) copy-start(f32[552,256]{1,0:T(8,128)} %get-tuple-element.48) | copy-start | bytes 1695748
  14.6 9.4 %copy-start.3 = (f32[8,40,256]{2,1,0:T(8,128)S(1)}, f32[8,40,256]{2,1,0:T(8,128)}, u32[]{:S(2)}) copy-start(f32[8,40,256]{2,1,0:T(8,128)} %get-tuple-element.40.parts) | copy-start | bytes 983044
  19.3 13.4 %collective-permute-start.6 = (f32[296,256]{1,0:T(8,128)S(1)}, f32[296,256]{1,0:T(8,128)S(1)}, u32[]{:S(2)}, u32[]{:S(2)}) collective-permute-start(f32[296,256]{1,0:T(8,128)S(1)} %collective-permute-done.2), channel_id=1, source_target_pairs={{65,64},{1,0}} | collective-permute-start | bytes 909320 | tf_op jit(solution)/shard_map/ppermute | solution.py:435
  20.6 16.8 %collective-permute-start.3 = (f32[552,256]{1,0:T(8,128)S(1)}, f32[552,256]{1,0:T(8,128)S(1)}, u32[]{:S(2)}, u32[]{:S(2)}) collective-permute-start(f32[552,256]{1,0:T(8,128)S(1)} %copy-done.4), channel_id=1, source_target_pairs={{0,1},{1,2},{2,3},{3,4},{4,5},{5,6},{6,7},{7,8},{8,9},{9,10},{10,1... | collective-permute-start | bytes 1695752 | tf_op jit(solution)/shard_map/ppermute | solution.py:436
  32.4 25.7 %collective-permute-start.8 = (f32[272,256]{1,0:T(8,128)S(1)}, f32[272,256]{1,0:T(8,128)S(1)}, u32[]{:S(2)}, u32[]{:S(2)}) collective-permute-start(f32[272,256]{1,0:T(8,128)S(1)} %get-tuple-element.57), channel_id=1, source_target_pairs={{0,1},{1,0},{2,3},{3,2},{4,5},{5,4},{6,7},{7,6},{8,9},{9,8},{10,11... | collective-permute-start | bytes 835592 | tf_op jit(solution)/shard_map/ppermute | solution.py:441
  50.8 13.6 %collective-permute-start.7 = (f32[2,16,256]{2,1,0:T(8,128)S(1)}, f32[2,16,256]{2,1,0:T(8,128)S(1)}, u32[]{:S(2)}, u32[]{:S(2)}) collective-permute-start(f32[2,16,256]{2,1,0:T(8,128)S(1)} %get-tuple-element.52), channel_id=1, source_target_pairs={{1,0},{2,1},{3,2},{4,3},{5,4},{6,5},{7,6},{8,7},{9,8},{10,9},{11,1... | collective-permute-start | bytes 98312 | tf_op jit(solution)/shard_map/ppermute | solution.py:446
  58.0 10.5 %collective-permute-start.10 = (f32[272,256]{1,0:T(8,128)S(1)}, f32[272,256]{1,0:T(8,128)S(1)}, u32[]{:S(2)}, u32[]{:S(2)}) collective-permute-start(f32[272,256]{1,0:T(8,128)S(1)} %get-tuple-element.62), channel_id=1, source_target_pairs={{0,1},{1,0},{2,3},{3,2},{4,5},{5,4},{6,7},{7,6},{8,9},{9,8},{10,11... | collective-permute-start | bytes 835592 | tf_op jit(solution)/shard_map/ppermute | solution.py:447
  62.3 9.7 %collective-permute-start.11 = (f32[272,256]{1,0:T(8,128)S(1)}, f32[272,256]{1,0:T(8,128)S(1)}, u32[]{:S(2)}, u32[]{:S(2)}) collective-permute-start(f32[272,256]{1,0:T(8,128)S(1)} %get-tuple-element.63), channel_id=1, source_target_pairs={{0,1},{1,0},{2,3},{3,2},{4,5},{5,4},{6,7},{7,6},{8,9},{9,8},{10,11... | collective-permute-start | bytes 835592 | tf_op jit(solution)/shard_map/ppermute | solution.py:452
  68.4 8.1 %collective-permute-start.9 = (f32[272,256]{1,0:T(8,128)S(1)}, f32[272,256]{1,0:T(8,128)S(1)}, u32[]{:S(2)}, u32[]{:S(2)}) collective-permute-start(f32[272,256]{1,0:T(8,128)S(1)} %get-tuple-element.60), channel_id=1, source_target_pairs={{0,1},{1,0},{2,3},{3,2},{4,5},{5,4},{6,7},{7,6},{8,9},{9,8},{10,11... | collective-permute-start | bytes 835592 | tf_op jit(solution)/shard_map/ppermute | solution.py:457

commit v9 on v8

--- a/solution.py
+++ b/solution.py
@@ -222,19 +222,20 @@
 
 
 def pack_kernel(near, wave, *refs):
-    sources, (all_ref, swap_ref, chain_ref), (floats, ints, sems) = refs[:5], refs[5:8], refs[8:]
+    sources, (all_ref, swap_ref, chain_ref, link_ref), (floats, ints, sems) = refs[:5], refs[5:9], refs[9:]
     r = lax.axis_index("row")
     loads, copies = Copies(sems), Copies(sems)
     copies.used = 5
     load_all(loads, sources, floats, ints)
     copies.start(wave.at[pl.ds(N * (4 - 4 * r), N)], swap_ref.at[pl.ds(0, N)])
-    copies.start(wave.at[pl.ds(N * (2 + 4 * r), 2 * N)], chain_ref.at[pl.ds(0, 2 * N)])
+    copies.start(wave.at[pl.ds(N * (2 + 4 * r), N)], chain_ref.at[pl.ds(0, N)])
+    copies.start(wave.at[pl.ds(N * (3 + 4 * r), N)], link_ref)
     loads.wait()
     for s in range(8):
         pack_slice(floats, ints, s, all_ref.at[s], 0)
     for i, rel in enumerate((0, 1, 3)):
         swap_ref[N + FIELDS * i:N + FIELDS * i + FIELDS, :] = all_ref[4 - 4 * r + rel]
-    chain_ref[2 * N:, :] = all_ref[3 + 4 * r]
+    chain_ref[N:, :] = all_ref[3 + 4 * r]
     copies.wait()
 
 
@@ -292,38 +293,47 @@
     piece_out(r, f2, pushed, own, away)
 
 
-def second_kernel(q1, parts, swap, chain, ahead, following, relay, table, d_ref, q_ref, to_back, own, away,
-                  f0, f1, p0, pm, pushed, z, tab, *rest):
+def second_kernel(q1, parts, swap, link, following, table, q_ref, own, away, f1, p0, pushed, z, tab, *rest):
     work, sems = rest[:-1], rest[-1]
     r = lax.axis_index("row")
     copies, later = Copies(sems), Copies(sems)
-    later.used = 23
+    later.used = 7
+    field_in(copies, r, f1, following, 0, link, 0)
+    parts_in(copies, r, p0, parts, 0, swap, N)
+    later.start(table, tab)
+    copies.wait()
+
+    @pl.when((r == 0) & (lax.axis_index("tm") == 0))
+    def _():
+        f1[...] = jnp.zeros_like(f1)
+
+    step(f1, p0, p0, tab, z, *work, ready=later)
+    q_ref[...] = p0[...]
+    step(z, q1, pushed, tab, f1, *work)
+    piece_out(r, f1, pushed, own, away)
+
+
+def edge_kernel(after, chain, ahead, relay, table, d_ref, to_back, f0, pm, tab, *rest):
+    work, sems = rest[:-1], rest[-1]
+    r = lax.axis_index("row")
+    copies, later = Copies(sems), Copies(sems)
+    later.used = 15
     field_in(copies, r, f0, ahead, 0, chain, 0)
     copies.start(ahead.at[pl.ds(N, FIELDS)], pm.at[r])
-    copies.start(chain.at[pl.ds(2 * N, FIELDS)], pm.at[1 - r])
-    later.start(table, tab)
-    field_in(copies, r, f1, following, 0, chain, N)
-    parts_in(copies, r, p0, parts, 0, swap, N)
+    copies.start(chain.at[pl.ds(N, FIELDS)], pm.at[1 - r])
+    later.start(table, tab)
     copies.wait()
 
     @pl.when((r == 0) & (lax.rem(lax.axis_index("tm"), lax.axis_size("tm") // 2) == 0))
     def _():
         again = Copies(sems)
-        again.used = 15
+        again.used = 8
         for z in range(2):
             again.start(relay.at[pl.ds(HALF * z, HALF)], f0.at[z, pl.ds(pl.multiple_of(HALF * r, HALF), HALF)])
         again.start(relay.at[pl.ds(N, FIELDS)], pm.at[r])
         again.wait()
 
-    @pl.when((r == 0) & (lax.axis_index("tm") == 0))
-    def _():
-        f1[...] = jnp.zeros_like(f1)
-
     step(f0, pm, to_back, tab, d_ref, *work, ready=later)
-    step(f1, p0, p0, tab, z, *work)
-    q_ref[...] = p0[...]
-    step(z, q1, pushed, tab, f1, *work)
-    piece_out(r, f1, pushed, own, away)
 
 
 def third_kernel(d_ref, q0, own_a, own_b, back_a, table, own, away, wave, f0, pushed, z, tab, *rest):
@@ -420,9 +430,9 @@
     f_near = lax.ppermute(to_near, both, swap)
     f_around = lax.ppermute(to_ahead, both, around)
     f_next = lax.ppermute(to_next, both, ahead + direct)
-    parts, to_swap, to_chain = call(
-        pack_kernel, [(8, FIELDS, N), (N + 3 * FIELDS, N), (2 * N + FIELDS, N)],
-        [VM] * 3, stage, 8, [ANY] + [HB] * 6, 4 * unit, vmem=61000 << 10,
+    parts, to_swap, to_chain, to_link = call(
+        pack_kernel, [(8, FIELDS, N), (N + 3 * FIELDS, N), (N + FIELDS, N), (N, N)],
+        [VM] * 4, stage, 8, [ANY] + [HB] * 6, 4 * unit, vmem=61000 << 10,
     )(to_near, *raw)
     f_swap = lax.ppermute(to_swap, both, swap)
     to_ahead, to_chain = lax.optimization_barrier((to_ahead, to_chain))
@@ -431,20 +441,25 @@
     d3, q2 = call(
         near_kernel, [field, full], [VM, VM], [FIELD, PARTS, TABLE] + WORK, 8, [ANY] * 4, unit, vmem=50000 << 10,
     )(wave, mine, f_near, table)
-    q2, f_around, to_chain = lax.optimization_barrier((q2, f_around, to_chain))
-    f_relay = lax.ppermute(f_around, both, onward)
+    q2, to_chain, to_link = lax.optimization_barrier((q2, to_chain, to_link))
+    f_link = lax.ppermute(to_link, both, chain)
     f_chain = lax.ppermute(to_chain, both, chain)
     q1, own_a, away_a = call(
         first_kernel, [full] + pieces, [VM] * 3, [FIELD, PARTS, PUSH, FIELD, TABLE] + WORK, 8,
         [VM] + [ANY] * 4, 2 * unit,
     )(q2, wave, parts, f_swap, table)
+    q1, f_around = lax.optimization_barrier((q1, f_around))
+    f_relay = lax.ppermute(f_around, both, onward)
     back_a = lax.ppermute(away_a, both, swap)
-    d0, q0, to_back, own_b, away_b = call(
-        second_kernel, [field, full, (2, PUSHED, N)] + pieces, [VM] * 5,
-        [FIELD, FIELD, PARTS, PARTS, PUSH, FIELD, TABLE] + WORK, 24, [VM] + [ANY] * 7, 3 * unit,
-    )(q1, parts, f_swap, f_chain, f_ahead, f_next, f_relay, table)
+    q0, own_b, away_b = call(
+        second_kernel, [full] + pieces, [VM] * 3, [FIELD, PARTS, PUSH, FIELD, TABLE] + WORK, 8,
+        [VM] + [ANY] * 5, 2 * unit,
+    )(q1, parts, f_swap, f_link, f_next, table)
+    back_b = lax.ppermute(away_b, both, swap)
+    d0, to_back = call(
+        edge_kernel, [field, (2, PUSHED, N)], [VM, VM], [FIELD, PARTS, TABLE] + WORK, 16, [ANY] * 5, unit,
+    )(q0, f_chain, f_ahead, f_relay, table)
     from_back = lax.ppermute(to_back, both, back)
-    back_b = lax.ppermute(away_b, both, swap)
     own_c, away_c, wave = call(
         third_kernel, pieces + [(8 * N, N)], [VM, VM, ANY],
         [FIELD, PUSH, FIELD, TABLE] + WORK, 12, [ANY, VM] + [ANY] * 4, unit,

time: 78.3 us -> 74.6 us (0.953)
  waiting for transfers between devices: 14.5 us -> 9.34 us
    ppermute x1, waiting for transfers between devices: 4.69 us -> 0.01 us  [body(): f_chain = lax.ppermute(to_chain, both, chain)]
    ppermute x1, waiting for transfers between devices: 0.63 us -> 3.49 us  [body(): f_swap = lax.ppermute(to_swap, both, swap)]
    ppermute x1, starting transfers between devices: 0.01 us -> 2.73 us  [body(): back_b = lax.ppermute(away_b, both, swap)]
    ppermute x1, starting transfers between devices: 2.73 us -> 0.07 us  [body(): f_chain = lax.ppermute(to_chain, both, chain)]
    ppermute x1, waiting for transfers between devices: 3.39 us -> 1.17 us  [body(): back_c = lax.ppermute(away_c, both, swap)]
    ppermute x1, starting transfers between devices: 2.1 us -> 0.09 us  [body(): back_c = lax.ppermute(away_c, both, swap)]
    ppermute x1, starting transfers between devices: 7.25 us -> 5.24 us  [body(): from_back = lax.ppermute(to_back, both, back)]
    ppermute x1, starting transfers between devices: 0.14 us -> 2.05 us  [body(): back_d = lax.ppermute(away_d, both, swap)]
  transfers between devices with their start and end apart: 12 -> 13, of which waited for: 5 -> 4; matrix products, arithmetic and copies ran while one was open for 0% -> 0% of each run, Pallas kernels for 49% -> 52%
where the time goes in v9:
time: 74.6 us; the launch traced here: 73.7 us
  Pallas kernels  42.4 us (57%)
  starting transfers between devices  20.9 us (28%)
  waiting for transfers between devices  9.34 us (13%)
  between operations  1.01 us (1%)
    pallas_call x1, Pallas kernels, body(): call(second_kernel, [full] + pieces, [VM] * 3, [FIELD, PARTS, PUSH, FIELD...  8.43 us
    pallas_call x1, Pallas kernels, body(): call(first_kernel, [full] + pieces, [VM] * 3, [FIELD, PARTS, PUSH, FIELD,...  8.39 us
    ppermute x1, starting transfers between devices, body(): from_back = lax.ppermute(to_back, both, back)  5.24 us
    pallas_call x1, Pallas kernels, body(): call(edge_kernel, [field, (2, PUSHED, N)], [VM, VM], [FIELD, PARTS, TABLE...  5.15 us
    pallas_call x1, Pallas kernels, body(): call(near_kernel, [field, full], [VM, VM], [FIELD, PARTS, TABLE] + WORK,...  4.67 us
    pallas_call x1, Pallas kernels, body(): call(third_kernel, pieces + [(8 * N, N)], [VM, VM, ANY], [FIELD, PUSH, FI...  4.21 us
    pallas_call x1, Pallas kernels, body(): call(fourth_kernel, pieces + [(8 * N, N)], [VM, VM, ANY], [PARTS, PUSH, F...  4.07 us
    ppermute x1, waiting for transfers between devices, body(): f_swap = lax.ppermute(to_swap, both, swap)  3.49 us
  transfers between devices with their start and end apart: 13, of which 4 were waited for; matrix products, arithmetic and copies ran while one was open for 0% of the time, Pallas kernels for 52%

profile of v9, /device:TPU:4, one launch (start us, length us, event | category | flops | bytes accessed | tf_op | source)
XLA Modules:
  0.0 73.7 jit_solution(7657036873081987409)
XLA Ops:
  0.6 2.3 %shard_map.94 = (f32[296,256]{1,0:T(8,128)}, f32[296,256]{1,0:T(8,128)}, f32[256,256]{1,0:T(8,128)}, f32[40,256]{1,0:T(8,128)}) custom-call(f32[2048,256]{1,0:T(8,128)} %bitcast.2, f32[8,2048]{1,0:T(8,128)} %refs_0_.3, f32[8,2048]{1,0:T(8,128)} %refs_1_.3, f32[8,2048]{1,0:T(8,128)} %refs_2_.3, s32[8,2048]{1,0:T(8,128)} %refs_3_.3, s32[8,2048]{1,0:T(8,128)} %refs_4_.3), custom_call_target="tpu_custom_call" | custom-call | flops 1048576 | bytes 4194304 | tf_op jit(solution)/shard_map/pallas_call | solution.py:426
  2.9 1.9 %collective-permute-start.4 = (f32[256,256]{1,0:T(8,128)}, f32[256,256]{1,0:T(8,128)S(1)}, u32[]{:S(2)}, u32[]{:S(2)}) collective-permute-start(f32[256,256]{1,0:T(8,128)} %get-tuple-element.54), channel_id=1, source_target_pairs={{0,2},{1,1},{2,4},{3,3},{4,6},{5,5},{6,8},{7,7},{8,10},{9,9},{10,1... | collective-permute-start | bytes 786440 | tf_op jit(solution)/shard_map/ppermute | solution.py:432
  4.9 0.9 %collective-permute-start = (f32[296,256]{1,0:T(8,128)}, f32[296,256]{1,0:T(8,128)S(1)}, u32[]{:S(2)}, u32[]{:S(2)}) collective-permute-start(f32[296,256]{1,0:T(8,128)} %get-tuple-element.41.near), channel_id=1, source_target_pairs={{0,1},{1,0},{2,3},{3,2},{4,5},{5,4},{6,7},{7,6},{8,9},{9,8},{10,11... | collective-permute-start | bytes 909320 | tf_op jit(solution)/shard_map/ppermute | solution.py:430
  5.7 0.0 copy-start.4
  5.7 0.0 copy-start
  5.7 0.8 %collective-permute-start.2 = (f32[296,256]{1,0:T(8,128)}, f32[296,256]{1,0:T(8,128)S(1)}, u32[]{:S(2)}, u32[]{:S(2)}) collective-permute-start(f32[296,256]{1,0:T(8,128)} %get-tuple-element.57), channel_id=1, source_target_pairs={{62,65},{126,1}} | collective-permute-start | bytes 909320 | tf_op jit(solution)/shard_map/ppermute | solution.py:431
  6.6 2.6 %shard_map.96 = (f32[8,40,256]{2,1,0:T(8,128)}, f32[376,256]{1,0:T(8,128)}, f32[296,256]{1,0:T(8,128)}, f32[256,256]{1,0:T(8,128)}) custom-call(f32[296,256]{1,0:T(8,128)} %get-tuple-element.41.near, f32[2048,256]{1,0:T(8,128)} %bitcast.3, f32[8,2048]{1,0:T(8,128)} %refs_0_.3, f32[8,2048]{1,0:T(8,128)} %refs_1_.3, f32[8,2048]{1,0:T(8,128)} %refs_2_.3, ...), custom_call_target="tpu_custom_call" | custom-call | flops 34359738368 | bytes 4194304 | tf_op jit(solution)/shard_map/pallas_call | solution.py:433
  9.2 0.0 copy-done.4
  9.2 2.8 %collective-permute-start.6 = (f32[296,256]{1,0:T(8,128)S(1)}, f32[296,256]{1,0:T(8,128)S(1)}, u32[]{:S(2)}, u32[]{:S(2)}) collective-permute-start(f32[296,256]{1,0:T(8,128)S(1)} %copy-done.4), channel_id=1, source_target_pairs={{0,2},{1,1},{2,4},{3,3},{4,6},{5,5},{6,8},{7,7},{8,10},{9,9},{10,1... | collective-permute-start | bytes 909320 | tf_op jit(solution)/shard_map/ppermute | solution.py:439
  12.0 0.1 collective-permute-start.1
  12.1 2.4 %collective-permute-done.near = f32[296,256]{1,0:T(8,128)S(1)} collective-permute-done((f32[296,256]{1,0:T(8,128)}, f32[296,256]{1,0:T(8,128)S(1)}, u32[]{:S(2)}, u32[]{:S(2)}) %collective-permute-start) | collective-permute-done | bytes 303136 | tf_op jit(solution)/shard_map/ppermute | solution.py:430
  14.5 0.0 copy-done
  14.5 0.0 copy-done.1
  14.5 0.0 copy-done.2
  14.5 0.0 copy-start.6
  14.6 0.0 copy-start.5
  14.6 0.0 copy-start.3
  14.6 4.7 %shard_map.95 = (f32[2,256,256]{2,1,0:T(8,128)S(1)}, f32[2,40,256]{2,1,0:T(8,128)S(1)}) custom-call(f32[2048,256]{1,0:T(8,128)S(1)} %bitcast.4, f32[40,256]{1,0:T(8,128)S(1)} %copy-done.1, f32[296,256]{1,0:T(8,128)S(1)} %collective-permute-done.near, bf16[2,2,2,256,256]{4,3,2,1,0:T(8,128)(2,1)S(1)} %copy-done.2), custom_call_target="tpu_custom_call" | custom-call | flops 8589934592 | bytes 4194304 | tf_op jit(solution)/shard_map/pallas_call | solution.py:441
  19.3 0.0 copy-done.6
  19.3 1.4 %collective-permute-start.3 = (f32[256,256]{1,0:T(8,128)S(1)}, f32[256,256]{1,0:T(8,128)S(1)}, u32[]{:S(2)}, u32[]{:S(2)}) collective-permute-start(f32[256,256]{1,0:T(8,128)S(1)} %copy-done.6), channel_id=1, source_target_pairs={{0,1},{1,2},{2,3},{3,4},{4,5},{5,6},{6,7},{7,8},{8,9},{9,10},{10,1... | collective-permute-start | bytes 786440 | tf_op jit(solution)/shard_map/ppermute | solution.py:445
  20.6 3.5 %collective-permute-done.1.swap = f32[376,256]{1,0:T(8,128)S(1)} collective-permute-done((f32[376,256]{1,0:T(8,128)}, f32[376,256]{1,0:T(8,128)S(1)}, u32[]{:S(2)}, u32[]{:S(2)}) %collective-permute-start.1) | collective-permute-done | bytes 385056 | tf_op jit(solution)/shard_map/ppermute | solution.py:437
  24.1 0.0 copy-done.5
  24.1 0.1 collective-permute-start.5
  24.2 0.0 copy-done.3
  24.2 8.4 %shard_map.97 = (f32[2,40,256]{2,1,0:T(8,128)S(1)}, f32[272,256]{1,0:T(8,128)S(1)}, f32[272,256]{1,0:T(8,128)S(1)}) custom-call(f32[2,40,256]{2,1,0:T(8,128)S(1)} %get-tuple-element.50.q2, f32[2048,256]{1,0:T(8,128)S(1)} %bitcast.5, f32[8,40,256]{2,1,0:T(8,128)S(1)} %copy-done.3, f32[376,256]{1,0:T(8,128)S(1)} %collective-permute-done.1.swap, ...), custom_call_target="tpu_custom_call" | custom-call | flops 17179869184 | bytes 4194304 | tf_op jit(solution)/shard_map/pallas_call | solution.py:447
  32.6 0.0 collective-permute-done.2
  32.6 1.6 %collective-permute-start.9 = (f32[272,256]{1,0:T(8,128)S(1)}, f32[272,256]{1,0:T(8,128)S(1)}, u32[]{:S(2)}, u32[]{:S(2)}) collective-permute-start(f32[272,256]{1,0:T(8,128)S(1)} %get-tuple-element.63), channel_id=1, source_target_pairs={{0,1},{1,0},{2,3},{3,2},{4,5},{5,4},{6,7},{7,6},{8,9},{9,8},{10,11... | collective-permute-start | bytes 835592 | tf_op jit(solution)/shard_map/ppermute | solution.py:453
  34.2 0.0 collective-permute-done.4.following
  34.2 1.3 %collective-permute-start.7 = (f32[296,256]{1,0:T(8,128)S(1)}, f32[296,256]{1,0:T(8,128)S(1)}, u32[]{:S(2)}, u32[]{:S(2)}) collective-permute-start(f32[296,256]{1,0:T(8,128)S(1)} %collective-permute-done.2), channel_id=1, source_target_pairs={{65,64},{1,0}} | collective-permute-start | bytes 909320 | tf_op jit(solution)/shard_map/ppermute | solution.py:452
  35.5 0.0 collective-permute-done.3.link
  35.5 8.4 %shard_map.98 = (f32[2,40,256]{2,1,0:T(8,128)S(1)}, f32[272,256]{1,0:T(8,128)S(1)}, f32[272,256]{1,0:T(8,128)S(1)}) custom-call(f32[2,40,256]{2,1,0:T(8,128)S(1)} %get-tuple-element.52.q1, f32[8,40,256]{2,1,0:T(8,128)S(1)} %copy-done.3, f32[376,256]{1,0:T(8,128)S(1)} %collective-permute-done.1.swap, f32[256,256]{1,0:T(8,128)S(1)} %collective-permute-done.3.link, ...), custom_call_target="tpu_custom_call" | custom-call | flops 17179869184 | bytes 4194304 | tf_op jit(solution)/shard_map/pallas_call | solution.py:454
  43.9 2.7 %collective-permute-start.11 = (f32[272,256]{1,0:T(8,128)S(1)}, f32[272,256]{1,0:T(8,128)S(1)}, u32[]{:S(2)}, u32[]{:S(2)}) collective-permute-start(f32[272,256]{1,0:T(8,128)S(1)} %get-tuple-element.68), channel_id=1, source_target_pairs={{0,1},{1,0},{2,3},{3,2},{4,5},{5,4},{6,7},{7,6},{8,9},{9,8},{10,11... | collective-permute-start | bytes 835592 | tf_op jit(solution)/shard_map/ppermute | solution.py:458
  46.6 0.0 collective-permute-done.6.ahead
  46.6 0.0 collective-permute-done.5.chain
  46.6 0.0 collective-permute-done.7.relay
  46.6 5.1 %shard_map.99 = (f32[2,256,256]{2,1,0:T(8,128)S(1)}, f32[2,16,256]{2,1,0:T(8,128)S(1)}) custom-call(f32[2,40,256]{2,1,0:T(8,128)S(1)} %get-tuple-element.55.after.q0, f32[296,256]{1,0:T(8,128)S(1)} %collective-permute-done.5.chain, f32[296,256]{1,0:T(8,128)S(1)} %collective-permute-done.6.ahead, f32[296,256]{1,0:T(8,128)S(1)} %collective-permute-done.7.relay, ...), custom_call_target="tpu_custom_call" | custom-call | flops 8589934592 | bytes 4194304 | tf_op jit(solution)/shard_map/pallas_call | solution.py:459
  51.8 5.2 %collective-permute-start.8 = (f32[2,16,256]{2,1,0:T(8,128)S(1)}, f32[2,16,256]{2,1,0:T(8,128)S(1)}, u32[]{:S(2)}, u32[]{:S(2)}) collective-permute-start(f32[2,16,256]{2,1,0:T(8,128)S(1)} %get-tuple-element.59), channel_id=1, source_target_pairs={{1,0},{2,1},{3,2},{4,3},{5,4},{6,5},{7,6},{8,7},{9,8},{10,9},{11,1... | collective-permute-start | bytes 98312 | tf_op jit(solution)/shard_map/ppermute | solution.py:462
  57.0 0.0 collective-permute-done.9.back_a
  57.0 4.2 %shard_map.100 = (f32[272,256]{1,0:T(8,128)S(1)}, f32[272,256]{1,0:T(8,128)S(1)}, f32[2048,256]{1,0:T(8,128)}) custom-call(f32[2,256,256]{2,1,0:T(8,128)S(1)} %get-tuple-element.60.d_ref, f32[2,40,256]{2,1,0:T(8,128)S(1)} %get-tuple-element.55.after.q0, f32[272,256]{1,0:T(8,128)S(1)} %get-tuple-element.61.own_a, f32[272,256]{1,0:T(8,128)S(1)} %get-tuple-element.62.own_b, ...), custom_call_target="tpu_custom_call" | custom-call | flops 8589934592 | bytes 4194304 | tf_op jit(solution)/shard_map/pallas_call | solution.py:463
  61.3 0.1 collective-permute-start.12
  61.4 0.0 collective-permute-done.8.from_back
  61.4 4.1 %shard_map.101 = (f32[272,256]{1,0:T(8,128)S(1)}, f32[272,256]{1,0:T(8,128)S(1)}, f32[2048,256]{1,0:T(8,128)}) custom-call(f32[2,256,256]{2,1,0:T(8,128)S(1)} %get-tuple-element.42.d_ref, f32[8,40,256]{2,1,0:T(8,128)S(1)} %copy-done.3, f32[376,256]{1,0:T(8,128)S(1)} %collective-permute-done.1.swap, ...), custom_call_target="tpu_custom_call", output_to_operand_aliasing={{2}: (6, {})} | custom-call | flops 17179869184 | bytes 4194304 | tf_op jit(solution)/shard_map/pallas_call | solution.py:468
  65.4 2.0 %collective-permute-start.10 = (f32[272,256]{1,0:T(8,128)S(1)}, f32[272,256]{1,0:T(8,128)S(1)}, u32[]{:S(2)}, u32[]{:S(2)}) collective-permute-start(f32[272,256]{1,0:T(8,128)S(1)} %get-tuple-element.66), channel_id=1, source_target_pairs={{0,1},{1,0},{2,3},{3,2},{4,5},{5,4},{6,7},{7,6},{8,9},{9,8},{10,11... | collective-permute-start | bytes 835592 | tf_op jit(solution)/shard_map/ppermute | solution.py:472
  67.5 0.0 collective-permute-done.11.back_b
  67.5 1.2 %collective-permute-done.12.back_c = f32[272,256]{1,0:T(8,128)S(1)} collective-permute-done((f32[272,256]{1,0:T(8,128)S(1)}, f32[272,256]{1,0:T(8,128)S(1)}, u32[]{:S(2)}, u32[]{:S(2)}) %collective-permute-start.12) | collective-permute-done | bytes 278560 | tf_op jit(solution)/shard_map/ppermute | solution.py:467
  68.7 1.2 %shard_map.102 = (f32[2048,256]{1,0:T(8,128)}, f32[8,2048]{1,0:T(8,128)S(1)}, f32[8,2048]{1,0:T(8,128)S(1)}) custom-call(f32[272,256]{1,0:T(8,128)S(1)} %get-tuple-element.61.own_a, f32[272,256]{1,0:T(8,128)S(1)} %get-tuple-element.62.own_b, f32[272,256]{1,0:T(8,128)S(1)} %get-tuple-element.64.own_c, ...), custom_call_target="tpu_custom_call", output_to_operand_aliasing={{0}: (7, {})} | custom-call | flops 1048576 | bytes 4194304 | tf_op jit(solution)/shard_map/pallas_call | solution.py:474
  69.8 2.2 %collective-permute-done.10.back_d = f32[272,256]{1,0:T(8,128)S(1)} collective-permute-done((f32[272,256]{1,0:T(8,128)S(1)}, f32[272,256]{1,0:T(8,128)S(1)}, u32[]{:S(2)}, u32[]{:S(2)}) %collective-permute-start.10) | collective-permute-done | bytes 278560 | tf_op jit(solution)/shard_map/ppermute | solution.py:472
  72.1 1.4 %shard_map.103 = (f32[2048,256]{1,0:T(8,128)}, f32[8,2048]{1,0:T(8,128)}, f32[8,2048]{1,0:T(8,128)}) custom-call(f32[272,256]{1,0:T(8,128)S(1)} %collective-permute-done.10.back_d, f32[2048,256]{1,0:T(8,128)} %get-tuple-element.71.wave_in, f32[8,2048]{1,0:T(8,128)S(1)} %get-tuple-element.72.phase_in, ...), custom_call_target="tpu_custom_call", output_to_operand_aliasing={{0}: (1, {})} | custom-call | flops 1048576 | bytes 4194304 | tf_op jit(solution)/shard_map/pallas_call | solution.py:478
  (2 shorter events, 0.0 us)
Async XLA Ops:
  2.9 31.2 %collective-permute-start.4 = (f32[256,256]{1,0:T(8,128)}, f32[256,256]{1,0:T(8,128)S(1)}, u32[]{:S(2)}, u32[]{:S(2)}) collective-permute-start(f32[256,256]{1,0:T(8,128)} %get-tuple-element.54), channel_id=1, source_target_pairs={{0,2},{1,1},{2,4},{3,3},{4,6},{5,5},{6,8},{7,7},{8,10},{9,9},{10,1... | collective-permute-start | bytes 786440 | tf_op jit(solution)/shard_map/ppermute | solution.py:432
  4.9 9.7 %collective-permute-start = (f32[296,256]{1,0:T(8,128)}, f32[296,256]{1,0:T(8,128)S(1)}, u32[]{:S(2)}, u32[]{:S(2)}) collective-permute-start(f32[296,256]{1,0:T(8,128)} %get-tuple-element.41.near), channel_id=1, source_target_pairs={{0,1},{1,0},{2,3},{3,2},{4,5},{5,4},{6,7},{7,6},{8,9},{9,8},{10,11... | collective-permute-start | bytes 909320 | tf_op jit(solution)/shard_map/ppermute | solution.py:430
  5.7 3.4 %copy-start.4 = (f32[296,256]{1,0:T(8,128)S(1)}, f32[296,256]{1,0:T(8,128)}, u32[]{:S(2)}) copy-start(f32[296,256]{1,0:T(8,128)} %get-tuple-element.57) | copy-start | bytes 909316
  5.7 8.8 %copy-start = (f32[8,2,128,256]{3,2,1,0:T(8,128)S(1)}, f32[8,2,128,256]{3,2,1,0:T(8,128)}, u32[]{:S(2)}) copy-start(f32[8,2,128,256]{3,2,1,0:T(8,128)} %param.7) | copy-start | bytes 6291460
  5.7 8.8 %copy-start.1 = (f32[40,256]{1,0:T(8,128)S(1)}, f32[40,256]{1,0:T(8,128)}, u32[]{:S(2)}) copy-start(f32[40,256]{1,0:T(8,128)} %get-tuple-element.40.mine) | copy-start | bytes 122884
  5.7 8.8 %copy-start.2 = (bf16[2,2,2,256,256]{4,3,2,1,0:T(8,128)(2,1)S(1)}, bf16[2,2,2,256,256]{4,3,2,1,0:T(8,128)(2,1)}, u32[]{:S(2)}) copy-start(bf16[2,2,2,256,256]{4,3,2,1,0:T(8,128)(2,1)} %constant.2.clone.table) | copy-start | bytes 3145732
  5.7 26.8 %collective-permute-start.2 = (f32[296,256]{1,0:T(8,128)}, f32[296,256]{1,0:T(8,128)S(1)}, u32[]{:S(2)}, u32[]{:S(2)}) collective-permute-start(f32[296,256]{1,0:T(8,128)} %get-tuple-element.57), channel_id=1, source_target_pairs={{62,65},{126,1}} | collective-permute-start | bytes 909320 | tf_op jit(solution)/shard_map/ppermute | solution.py:431
  9.2 37.4 %collective-permute-start.6 = (f32[296,256]{1,0:T(8,128)S(1)}, f32[296,256]{1,0:T(8,128)S(1)}, u32[]{:S(2)}, u32[]{:S(2)}) collective-permute-start(f32[296,256]{1,0:T(8,128)S(1)} %copy-done.4), channel_id=1, source_target_pairs={{0,2},{1,1},{2,4},{3,3},{4,6},{5,5},{6,8},{7,7},{8,10},{9,9},{10,1... | collective-permute-start | bytes 909320 | tf_op jit(solution)/shard_map/ppermute | solution.py:439
  12.0 12.1 %collective-permute-start.1 = (f32[376,256]{1,0:T(8,128)}, f32[376,256]{1,0:T(8,128)S(1)}, u32[]{:S(2)}, u32[]{:S(2)}) collective-permute-start(f32[376,256]{1,0:T(8,128)} %get-tuple-element.44), channel_id=1, source_target_pairs={{0,1},{1,0},{2,3},{3,2},{4,5},{5,4},{6,7},{7,6},{8,9},{9,8},{10,11... | collective-permute-start | bytes 1155080 | tf_op jit(solution)/shard_map/ppermute | solution.py:437
  14.5 4.7 %copy-start.6 = (f32[256,256]{1,0:T(8,128)S(1)}, f32[256,256]{1,0:T(8,128)}, u32[]{:S(2)}) copy-start(f32[256,256]{1,0:T(8,128)} %get-tuple-element.53) | copy-start | bytes 786436
  14.6 9.6 %copy-start.5 = (f32[296,256]{1,0:T(8,128)S(1)}, f32[296,256]{1,0:T(8,128)}, u32[]{:S(2)}) copy-start(f32[296,256]{1,0:T(8,128)} %get-tuple-element.56) | copy-start | bytes 909316
  14.6 9.6 %copy-start.3 = (f32[8,40,256]{2,1,0:T(8,128)S(1)}, f32[8,40,256]{2,1,0:T(8,128)}, u32[]{:S(2)}) copy-start(f32[8,40,256]{2,1,0:T(8,128)} %get-tuple-element.43.parts) | copy-start | bytes 983044
  19.3 16.2 %collective-permute-start.3 = (f32[256,256]{1,0:T(8,128)S(1)}, f32[256,256]{1,0:T(8,128)S(1)}, u32[]{:S(2)}, u32[]{:S(2)}) collective-permute-start(f32[256,256]{1,0:T(8,128)S(1)} %copy-done.6), channel_id=1, source_target_pairs={{0,1},{1,2},{2,3},{3,4},{4,5},{5,6},{6,7},{7,8},{8,9},{9,10},{10,1... | collective-permute-start | bytes 786440 | tf_op jit(solution)/shard_map/ppermute | solution.py:445
  24.1 22.5 %collective-permute-start.5 = (f32[296,256]{1,0:T(8,128)S(1)}, f32[296,256]{1,0:T(8,128)S(1)}, u32[]{:S(2)}, u32[]{:S(2)}) collective-permute-start(f32[296,256]{1,0:T(8,128)S(1)} %copy-done.5), channel_id=1, source_target_pairs={{0,1},{1,2},{2,3},{3,4},{4,5},{5,6},{6,7},{7,8},{8,9},{9,10},{10,1... | collective-permute-start | bytes 909320 | tf_op jit(solution)/shard_map/ppermute | solution.py:446
  32.6 24.4 %collective-permute-start.9 = (f32[272,256]{1,0:T(8,128)S(1)}, f32[272,256]{1,0:T(8,128)S(1)}, u32[]{:S(2)}, u32[]{:S(2)}) collective-permute-start(f32[272,256]{1,0:T(8,128)S(1)} %get-tuple-element.63), channel_id=1, source_target_pairs={{0,1},{1,0},{2,3},{3,2},{4,5},{5,4},{6,7},{7,6},{8,9},{9,8},{10,11... | collective-permute-start | bytes 835592 | tf_op jit(solution)/shard_map/ppermute | solution.py:453
  34.2 12.5 %collective-permute-start.7 = (f32[296,256]{1,0:T(8,128)S(1)}, f32[296,256]{1,0:T(8,128)S(1)}, u32[]{:S(2)}, u32[]{:S(2)}) collective-permute-start(f32[296,256]{1,0:T(8,128)S(1)} %collective-permute-done.2), channel_id=1, source_target_pairs={{65,64},{1,0}} | collective-permute-start | bytes 909320 | tf_op jit(solution)/shard_map/ppermute | solution.py:452
  43.9 23.6 %collective-permute-start.11 = (f32[272,256]{1,0:T(8,128)S(1)}, f32[272,256]{1,0:T(8,128)S(1)}, u32[]{:S(2)}, u32[]{:S(2)}) collective-permute-start(f32[272,256]{1,0:T(8,128)S(1)} %get-tuple-element.68), channel_id=1, source_target_pairs={{0,1},{1,0},{2,3},{3,2},{4,5},{5,4},{6,7},{7,6},{8,9},{9,8},{10,11... | collective-permute-start | bytes 835592 | tf_op jit(solution)/shard_map/ppermute | solution.py:458
  51.8 9.6 %collective-permute-start.8 = (f32[2,16,256]{2,1,0:T(8,128)S(1)}, f32[2,16,256]{2,1,0:T(8,128)S(1)}, u32[]{:S(2)}, u32[]{:S(2)}) collective-permute-start(f32[2,16,256]{2,1,0:T(8,128)S(1)} %get-tuple-element.59), channel_id=1, source_target_pairs={{1,0},{2,1},{3,2},{4,3},{5,4},{6,5},{7,6},{8,7},{9,8},{10,9},{11,1... | collective-permute-start | bytes 98312 | tf_op jit(solution)/shard_map/ppermute | solution.py:462
  61.3 7.4 %collective-permute-start.12 = (f32[272,256]{1,0:T(8,128)S(1)}, f32[272,256]{1,0:T(8,128)S(1)}, u32[]{:S(2)}, u32[]{:S(2)}) collective-permute-start(f32[272,256]{1,0:T(8,128)S(1)} %get-tuple-element.69), channel_id=1, source_target_pairs={{0,1},{1,0},{2,3},{3,2},{4,5},{5,4},{6,7},{7,6},{8,9},{9,8},{10,11... | collective-permute-start | bytes 835592 | tf_op jit(solution)/shard_map/ppermute | solution.py:467
  65.4 6.6 %collective-permute-start.10 = (f32[272,256]{1,0:T(8,128)S(1)}, f32[272,256]{1,0:T(8,128)S(1)}, u32[]{:S(2)}, u32[]{:S(2)}) collective-permute-start(f32[272,256]{1,0:T(8,128)S(1)} %get-tuple-element.66), channel_id=1, source_target_pairs={{0,1},{1,0},{2,3},{3,2},{4,5},{5,4},{6,7},{7,6},{8,9},{9,8},{10,11... | collective-permute-start | bytes 835592 | tf_op jit(solution)/shard_map/ppermute | solution.py:472

commit v10 on v9

--- a/solution.py
+++ b/solution.py
@@ -18,6 +18,7 @@
 PART = 2048
 ROWS = PART // N
 WIN = 144
+NEAR = 136
 FIELDS = 5 * ROWS
 PUSHED = 2 * ROWS
 PIECE = 2 * HALF + PUSHED
@@ -75,56 +76,62 @@
     one = jnp.ones((16, N), BF)
     zero = jnp.zeros((16, N), BF)
     down = jnp.full((16, N), DOWN, BF)
-    iota_r = lax.broadcasted_iota(jnp.int32, (WIN, N), 0).astype(F32)
+    iota_r = lax.broadcasted_iota(jnp.int32, (NEAR, N), 0).astype(F32)
+    phase = jnp.concatenate([p_ref[0, :ROWS], p_ref[1, :ROWS]], 0)
+    sine, cosine = sincos(phase)
     for h in range(2):
         off = p_ref[h, 2 * ROWS:3 * ROWS]
         lower = 0.5 - off
         upper = 0.5 + off
-        w_ref[0] = 0.5 * lower * lower
-        w_ref[1] = 0.75 - off * off
-        w_ref[2] = 0.5 * upper * upper
+        w_ref[h, 0] = 0.5 * lower * lower
+        w_ref[h, 1] = 0.75 - off * off
+        w_ref[h, 2] = 0.5 * upper * upper
         win0 = 0 if h == 0 else N - WIN
+        skip = h * (WIN - NEAR)
         field = f_ref[:, win0:win0 + WIN, :].reshape(2 * WIN, N)
-        hi = field.astype(BF)
-        lo = ((field - hi.astype(F32)) * UP).astype(F8)
+        both = jnp.concatenate(hilo(field), 0)
         for k in range(ROWS):
             col = jnp.broadcast_to(p_ref[h, 4 * ROWS + k:4 * ROWS + k + 1, :], (16, N)).astype(BF)
             hot = jnp.where(iota_c == col[None], one[None], zero[None]).reshape(N, N)
             c_ref[h, :, N * k:N * k + N] = hot
             hot8 = jnp.where(iota_c == col[None], down[None], zero[None]).reshape(N, N).astype(F8)
             c8_ref[h, :, N * k:N * k + N] = hot8
-            g = mm(hi, hot) + mm(lo, hot8)
-            at = p_ref[h, 3 * ROWS + k:3 * ROWS + k + 1, :] - float(win0)
-            w = jnp.where(iota_r == at, w_ref[1, k:k + 1, :],
-                          jnp.where(iota_r == at - 1.0, w_ref[0, k:k + 1, :],
-                                    jnp.where(iota_r == at + 1.0, w_ref[2, k:k + 1, :], 0.0)))
-            samp_ref[0, k:k + 1, :] = jnp.sum(w * g[:WIN], 0, keepdims=True)
-            samp_ref[1, k:k + 1, :] = jnp.sum(w * g[WIN:], 0, keepdims=True)
-        phase = p_ref[h, :ROWS]
-        sine, cosine = sincos(phase)
-        energy = p_ref[h, ROWS:2 * ROWS] - 0.5 * (samp_ref[0] * cosine - samp_ref[1] * sine)
-        phase = phase + energy
-        q_ref[h, :ROWS] = phase
-        q_ref[h, ROWS:2 * ROWS] = energy
-        sine, cosine = sincos(phase)
-        for z, v in ((0, cosine), (1, -sine)):
-            vh = v.astype(BF).astype(F32)
-            s_ref[2 * z] = vh
-            s_ref[2 * z + 1] = v - vh
+            g = mm(both, hot)
+            g = g[:2 * WIN] + g[2 * WIN:]
+            at = p_ref[h, 3 * ROWS + k:3 * ROWS + k + 1, :] - float(win0 + skip)
+            w = jnp.where(iota_r == at, w_ref[h, 1, k:k + 1, :],
+                          jnp.where(iota_r == at - 1.0, w_ref[h, 0, k:k + 1, :],
+                                    jnp.where(iota_r == at + 1.0, w_ref[h, 2, k:k + 1, :], 0.0)))
+            samp_ref[0, h * ROWS + k:h * ROWS + k + 1, :] = jnp.sum(w * g[skip:skip + NEAR], 0, keepdims=True)
+            samp_ref[1, h * ROWS + k:h * ROWS + k + 1, :] = jnp.sum(
+                w * g[WIN + skip:WIN + skip + NEAR], 0, keepdims=True)
+    energy = jnp.concatenate([p_ref[0, ROWS:2 * ROWS], p_ref[1, ROWS:2 * ROWS]], 0)
+    energy = energy - 0.5 * (samp_ref[0] * cosine - samp_ref[1] * sine)
+    phase = phase + energy
+    for h in range(2):
+        q_ref[h, :ROWS] = phase[h * ROWS:h * ROWS + ROWS]
+        q_ref[h, ROWS:2 * ROWS] = energy[h * ROWS:h * ROWS + ROWS]
+    sine, cosine = sincos(phase)
+    for z, v in ((0, cosine), (1, -sine)):
+        vh = v.astype(BF).astype(F32)
+        s_ref[2 * z] = vh
+        s_ref[2 * z + 1] = (v - vh) * UP
+    for h in range(2):
         for k in range(ROWS):
             at = jnp.broadcast_to(p_ref[h, 3 * ROWS + k:3 * ROWS + k + 1, :] - float(HALF * h), (16, N)).astype(BF)
             here = iota_c[:8] == at[None]
+            row = h * ROWS + k
             for z in range(2):
-                value = jnp.broadcast_to(s_ref[2 * z, k:k + 1, :], (16, N)).astype(BF)
-                sr_ref[HALF * z:HALF * z + HALF, N * k:N * k + N] = jnp.where(here, value[None], zero[None]).reshape(HALF, N)
-                value = jnp.broadcast_to(s_ref[2 * z + 1, k:k + 1, :] * UP, (16, N)).astype(BF)
-                sr8_ref[HALF * z:HALF * z + HALF, N * k:N * k + N] = jnp.where(here, value[None], zero[None]).reshape(HALF, N).astype(F8)
-        d = lax.dot_general(sr_ref[...], c_ref[h], (((1,), (1,)), ((), ())), preferred_element_type=F32)
-        d = d + lax.dot_general(sr8_ref[...], c8_ref[h], (((1,), (1,)), ((), ())), preferred_element_type=F32)
+                value = jnp.broadcast_to(s_ref[2 * z, row:row + 1, :], (16, N)).astype(BF)
+                sr_ref[h, HALF * z:HALF * z + HALF, N * k:N * k + N] = jnp.where(here, value[None], zero[None]).reshape(HALF, N)
+                value = jnp.broadcast_to(s_ref[2 * z + 1, row:row + 1, :], (16, N)).astype(BF)
+                sr8_ref[h, HALF * z:HALF * z + HALF, N * k:N * k + N] = jnp.where(
+                    here, value[None], zero[None]).reshape(HALF, N).astype(F8)
+        d = lax.dot_general(sr8_ref[h], c8_ref[h], (((1,), (1,)), ((), ())), preferred_element_type=F32)
+        d = d + lax.dot_general(sr_ref[h], c_ref[h], (((1,), (1,)), ((), ())), preferred_element_type=F32)
         for z in range(2):
             x_ref[HALF * h:HALF * h + HALF, N * z:N * z + N] = (
-                f_ref[z, HALF * h:HALF * h + HALF, :]
-                + d[HALF * z:HALF * z + HALF])
+                f_ref[z, HALF * h:HALF * h + HALF, :] + d[HALF * z:HALF * z + HALF])
     if ready is not None:
         ready.wait()
     quads = [[], []]
@@ -154,9 +161,9 @@
         out_ref[1, HALF * e:HALF * e + HALF] = out[HALF:]
 
 
-WORK = [pltpu.VMEM((2, N, PART), BF), pltpu.VMEM((3, ROWS, N), F32), pltpu.VMEM((4, ROWS, N), F32),
-        pltpu.VMEM((N, PART), BF), pltpu.VMEM((N, 2 * N), F32), pltpu.VMEM((2, ROWS, N), F32),
-        pltpu.VMEM((2, N, PART), F8), pltpu.VMEM((N, PART), F8)]
+WORK = [pltpu.VMEM((2, N, PART), BF), pltpu.VMEM((2, 3, ROWS, N), F32), pltpu.VMEM((4, 2 * ROWS, N), F32),
+        pltpu.VMEM((2, N, PART), BF), pltpu.VMEM((N, 2 * N), F32), pltpu.VMEM((2, 2 * ROWS, N), F32),
+        pltpu.VMEM((2, N, PART), F8), pltpu.VMEM((2, N, PART), F8)]
 FIELD = pltpu.VMEM((2, N, N), F32)
 PARTS = pltpu.VMEM((2, FIELDS, N), F32)
 TABLE = pltpu.VMEM((2, 2, 2, N, N), BF)
@@ -206,14 +213,13 @@
 
 
 def early_pack_kernel(wave, *refs):
-    sources, (near_ref, ahead_ref, next_ref, mine_ref), (floats, ints, sems) = refs[:5], refs[5:9], refs[9:]
+    sources, (near_ref, ahead_ref, mine_ref), (floats, ints, sems) = refs[:5], refs[5:8], refs[8:]
     r = lax.axis_index("row")
     loads, copies = Copies(sems), Copies(sems)
     copies.used = 5
     load_all(loads, sources, floats, ints)
     copies.start(wave.at[pl.ds(N * (5 - 4 * r), N)], near_ref.at[pl.ds(0, N)])
     copies.start(wave.at[pl.ds(N * (6 - 4 * r), N)], ahead_ref.at[pl.ds(0, N)])
-    copies.start(wave.at[pl.ds(N * (7 - 4 * r), N)], next_ref)
     loads.wait()
     pack_slice(floats, ints, 6 - 4 * r, near_ref, N)
     pack_slice(floats, ints, 2 + 4 * r, mine_ref, 0)
@@ -222,7 +228,7 @@
 
 
 def pack_kernel(near, wave, *refs):
-    sources, (all_ref, swap_ref, chain_ref, link_ref), (floats, ints, sems) = refs[:5], refs[5:9], refs[9:]
+    sources, (all_ref, swap_ref, chain_ref, link_ref, next_ref), (floats, ints, sems) = refs[:5], refs[5:10], refs[10:]
     r = lax.axis_index("row")
     loads, copies = Copies(sems), Copies(sems)
     copies.used = 5
@@ -230,6 +236,7 @@
     copies.start(wave.at[pl.ds(N * (4 - 4 * r), N)], swap_ref.at[pl.ds(0, N)])
     copies.start(wave.at[pl.ds(N * (2 + 4 * r), N)], chain_ref.at[pl.ds(0, N)])
     copies.start(wave.at[pl.ds(N * (3 + 4 * r), N)], link_ref)
+    copies.start(wave.at[pl.ds(N * (7 - 4 * r), N)], next_ref)
     loads.wait()
     for s in range(8):
         pack_slice(floats, ints, s, all_ref.at[s], 0)
@@ -423,27 +430,26 @@
     pieces = [(PIECE, N), (PIECE, N)]
     raw = (wave, particle_phase, particle_energy, row_offset, row_cell, col_cell)
     stage = [pltpu.VMEM((3, 8, PART), F32), pltpu.VMEM((2, 8, PART), jnp.int32)]
-    to_near, to_ahead, to_next, mine = call(
-        early_pack_kernel, [(N + FIELDS, N), (N + FIELDS, N), (N, N), (FIELDS, N)], [VM] * 4, stage, 8, [HB] * 6, 1 << 20,
+    to_near, to_ahead, mine = call(
+        early_pack_kernel, [(N + FIELDS, N), (N + FIELDS, N), (FIELDS, N)], [VM] * 3, stage, 8, [HB] * 6, 1 << 20,
         vmem=61000 << 10,
     )(*raw)
     f_near = lax.ppermute(to_near, both, swap)
     f_around = lax.ppermute(to_ahead, both, around)
-    f_next = lax.ppermute(to_next, both, ahead + direct)
-    parts, to_swap, to_chain, to_link = call(
-        pack_kernel, [(8, FIELDS, N), (N + 3 * FIELDS, N), (N + FIELDS, N), (N, N)],
-        [VM] * 4, stage, 8, [ANY] + [HB] * 6, 4 * unit, vmem=61000 << 10,
+    parts, to_swap, to_chain, to_link, to_next = call(
+        pack_kernel, [(8, FIELDS, N), (N + 3 * FIELDS, N), (N + FIELDS, N), (N, N), (N, N)],
+        [VM] * 5, stage, 12, [ANY] + [HB] * 6, 4 * unit, vmem=61000 << 10,
     )(to_near, *raw)
     f_swap = lax.ppermute(to_swap, both, swap)
-    to_ahead, to_chain = lax.optimization_barrier((to_ahead, to_chain))
-    f_ahead = lax.ppermute(to_ahead, both, ahead)
+    f_next = lax.ppermute(to_next, both, ahead + direct)
 
     d3, q2 = call(
         near_kernel, [field, full], [VM, VM], [FIELD, PARTS, TABLE] + WORK, 8, [ANY] * 4, unit, vmem=50000 << 10,
     )(wave, mine, f_near, table)
-    q2, to_chain, to_link = lax.optimization_barrier((q2, to_chain, to_link))
+    q2, to_chain, to_link, to_ahead = lax.optimization_barrier((q2, to_chain, to_link, to_ahead))
     f_link = lax.ppermute(to_link, both, chain)
     f_chain = lax.ppermute(to_chain, both, chain)
+    f_ahead = lax.ppermute(to_ahead, both, ahead)
     q1, own_a, away_a = call(
         first_kernel, [full] + pieces, [VM] * 3, [FIELD, PARTS, PUSH, FIELD, TABLE] + WORK, 8,
         [VM] + [ANY] * 4, 2 * unit,

time: 74.6 us -> 71.2 us (0.954)
  Pallas kernels: 42.4 us -> 38 us
  starting transfers between devices: 20.9 us -> 21.7 us
    ppermute x1, starting transfers between devices: 1.56 us -> 0.09 us  [body(): back_a = lax.ppermute(away_a, both, swap)]
    ppermute x1, waiting for transfers between devices: 0.01 us -> 1.31 us  [body(): f_relay = lax.ppermute(f_around, both, onward)]
    ppermute x1, waiting for transfers between devices: 2.43 us -> 1.34 us  [body(): f_near = lax.ppermute(to_near, both, swap)]
    pallas_call x1, Pallas kernels: 8.39 us -> 7.31 us  [body(): call(first_kernel, [full] + pieces, [VM] * 3, [FIELD, PARTS, PUSH, FIELD,...]
    ppermute x1, starting transfers between devices: 0.08 us -> 1.13 us  [body(): f_swap = lax.ppermute(to_swap, both, swap)]
    pallas_call x1, Pallas kernels: 8.43 us -> 7.49 us  [body(): call(second_kernel, [full] + pieces, [VM] * 3, [FIELD, PARTS, PUSH, FIELD...]
  transfers between devices with their start and end apart: 13 -> 13, of which waited for: 4 -> 5; matrix products, arithmetic and copies ran while one was open for 0% -> 0% of each run, Pallas kernels for 52% -> 49%
where the time goes in v10:
time: 71.2 us; the launch traced here: 70.2 us
  Pallas kernels  38 us (53%)
  starting transfers between devices  21.7 us (30%)
  waiting for transfers between devices  9.44 us (13%)
  between operations  1.02 us (1%)
    pallas_call x1, Pallas kernels, body(): call(second_kernel, [full] + pieces, [VM] * 3, [FIELD, PARTS, PUSH, FIELD...  7.49 us
    pallas_call x1, Pallas kernels, body(): call(first_kernel, [full] + pieces, [VM] * 3, [FIELD, PARTS, PUSH, FIELD,...  7.31 us
    ppermute x1, starting transfers between devices, body(): from_back = lax.ppermute(to_back, both, back)  5.37 us
    pallas_call x1, Pallas kernels, body(): call(edge_kernel, [field, (2, PUSHED, N)], [VM, VM], [FIELD, PARTS, TABLE...  4.57 us
    pallas_call x1, Pallas kernels, body(): call(near_kernel, [field, full], [VM, VM], [FIELD, PARTS, TABLE] + WORK,...  4.14 us
    pallas_call x1, Pallas kernels, body(): call(fourth_kernel, pieces + [(8 * N, N)], [VM, VM, ANY], [PARTS, PUSH, F...  3.6 us
    pallas_call x1, Pallas kernels, body(): call(third_kernel, pieces + [(8 * N, N)], [VM, VM, ANY], [FIELD, PUSH, FI...  3.47 us
    ppermute x1, waiting for transfers between devices, body(): f_swap = lax.ppermute(to_swap, both, swap)  3.38 us
  transfers between devices with their start and end apart: 13, of which 5 were waited for; matrix products, arithmetic and copies ran while one was open for 0% of the time, Pallas kernels for 49%

profile of v10, /device:TPU:4, one launch (start us, length us, event | category | flops | bytes accessed | tf_op | source)
XLA Modules:
  0.0 70.2 jit_solution(5451338380824067640)
XLA Ops:
  0.6 2.1 %shard_map.94 = (f32[296,256]{1,0:T(8,128)}, f32[296,256]{1,0:T(8,128)}, f32[40,256]{1,0:T(8,128)}) custom-call(f32[2048,256]{1,0:T(8,128)} %bitcast.2, f32[8,2048]{1,0:T(8,128)} %refs_0_.3, f32[8,2048]{1,0:T(8,128)} %refs_1_.3, f32[8,2048]{1,0:T(8,128)} %refs_2_.3, s32[8,2048]{1,0:T(8,128)} %refs_3_.3, s32[8,2048]{1,0:T(8,128)} %refs_4_.3), custom_call_target="tpu_custom_call" | custom-call | flops 1048576 | bytes 4194304 | tf_op jit(solution)/shard_map/pallas_call | solution.py:433
  2.7 1.3 %collective-permute-start = (f32[296,256]{1,0:T(8,128)}, f32[296,256]{1,0:T(8,128)S(1)}, u32[]{:S(2)}, u32[]{:S(2)}) collective-permute-start(f32[296,256]{1,0:T(8,128)} %get-tuple-element.40.near), channel_id=1, source_target_pairs={{0,1},{1,0},{2,3},{3,2},{4,5},{5,4},{6,7},{7,6},{8,9},{9,8},{10,11... | collective-permute-start | bytes 909320 | tf_op jit(solution)/shard_map/ppermute | solution.py:437
  4.0 0.0 copy-start
  4.0 0.8 %collective-permute-start.2 = (f32[296,256]{1,0:T(8,128)}, f32[296,256]{1,0:T(8,128)S(1)}, u32[]{:S(2)}, u32[]{:S(2)}) collective-permute-start(f32[296,256]{1,0:T(8,128)} %get-tuple-element.55), channel_id=1, source_target_pairs={{62,65},{126,1}} | collective-permute-start | bytes 909320 | tf_op jit(solution)/shard_map/ppermute | solution.py:438
  4.8 2.7 %shard_map.96 = (f32[8,40,256]{2,1,0:T(8,128)}, f32[376,256]{1,0:T(8,128)}, f32[296,256]{1,0:T(8,128)}, f32[256,256]{1,0:T(8,128)}, f32[256,256]{1,0:T(8,128)}) custom-call(f32[296,256]{1,0:T(8,128)} %get-tuple-element.40.near, f32[2048,256]{1,0:T(8,128)} %bitcast.3, f32[8,2048]{1,0:T(8,128)} %refs_0_.3, f32[8,2048]{1,0:T(8,128)} %refs_1_.3, ...), custom_call_target="tpu_custom_call" | custom-call | flops 34359738368 | bytes 4194304 | tf_op jit(solution)/shard_map/pallas_call | solution.py:439
  7.6 1.9 %collective-permute-start.4 = (f32[256,256]{1,0:T(8,128)}, f32[256,256]{1,0:T(8,128)S(1)}, u32[]{:S(2)}, u32[]{:S(2)}) collective-permute-start(f32[256,256]{1,0:T(8,128)} %get-tuple-element.52), channel_id=1, source_target_pairs={{0,2},{1,1},{2,4},{3,3},{4,6},{5,5},{6,8},{7,7},{8,10},{9,9},{10,1... | collective-permute-start | bytes 786440 | tf_op jit(solution)/shard_map/ppermute | solution.py:444
  9.5 1.1 %collective-permute-start.1 = (f32[376,256]{1,0:T(8,128)}, f32[376,256]{1,0:T(8,128)S(1)}, u32[]{:S(2)}, u32[]{:S(2)}) collective-permute-start(f32[376,256]{1,0:T(8,128)} %get-tuple-element.43), channel_id=1, source_target_pairs={{0,1},{1,0},{2,3},{3,2},{4,5},{5,4},{6,7},{7,6},{8,9},{9,8},{10,11... | collective-permute-start | bytes 1155080 | tf_op jit(solution)/shard_map/ppermute | solution.py:443
  10.6 1.3 %collective-permute-done.near = f32[296,256]{1,0:T(8,128)S(1)} collective-permute-done((f32[296,256]{1,0:T(8,128)}, f32[296,256]{1,0:T(8,128)S(1)}, u32[]{:S(2)}, u32[]{:S(2)}) %collective-permute-start) | collective-permute-done | bytes 303136 | tf_op jit(solution)/shard_map/ppermute | solution.py:437
  12.0 0.0 copy-done
  12.0 0.0 copy-done.1
  12.0 0.0 copy-done.2
  12.0 0.0 copy-start.6
  12.0 0.0 copy-start.5
  12.0 0.0 copy-start.4
  12.0 0.0 copy-start.3
  12.0 4.1 %shard_map.95 = (f32[2,256,256]{2,1,0:T(8,128)S(1)}, f32[2,40,256]{2,1,0:T(8,128)S(1)}) custom-call(f32[2048,256]{1,0:T(8,128)S(1)} %bitcast.4, f32[40,256]{1,0:T(8,128)S(1)} %copy-done.1, f32[296,256]{1,0:T(8,128)S(1)} %collective-permute-done.near, bf16[2,2,2,256,256]{4,3,2,1,0:T(8,128)(2,1)S(1)} %copy-done.2), custom_call_target="tpu_custom_call" | custom-call | flops 8589934592 | bytes 4194304 | tf_op jit(solution)/shard_map/pallas_call | solution.py:446
  16.2 0.0 copy-done.6
  16.2 1.3 %collective-permute-start.3 = (f32[256,256]{1,0:T(8,128)S(1)}, f32[256,256]{1,0:T(8,128)S(1)}, u32[]{:S(2)}, u32[]{:S(2)}) collective-permute-start(f32[256,256]{1,0:T(8,128)S(1)} %copy-done.6), channel_id=1, source_target_pairs={{0,1},{1,2},{2,3},{3,4},{4,5},{5,6},{6,7},{7,8},{8,9},{9,10},{10,1... | collective-permute-start | bytes 786440 | tf_op jit(solution)/shard_map/ppermute | solution.py:450
  17.4 0.0 copy-done.5
  17.5 0.1 collective-permute-start.5
  17.5 3.4 %collective-permute-done.1.swap = f32[376,256]{1,0:T(8,128)S(1)} collective-permute-done((f32[376,256]{1,0:T(8,128)}, f32[376,256]{1,0:T(8,128)S(1)}, u32[]{:S(2)}, u32[]{:S(2)}) %collective-permute-start.1) | collective-permute-done | bytes 385056 | tf_op jit(solution)/shard_map/ppermute | solution.py:443
  20.9 0.0 copy-done.4
  20.9 3.4 %collective-permute-start.6 = (f32[296,256]{1,0:T(8,128)S(1)}, f32[296,256]{1,0:T(8,128)S(1)}, u32[]{:S(2)}, u32[]{:S(2)}) collective-permute-start(f32[296,256]{1,0:T(8,128)S(1)} %copy-done.4), channel_id=1, source_target_pairs={{0,2},{1,1},{2,4},{3,3},{4,6},{5,5},{6,8},{7,7},{8,10},{9,9},{10,1... | collective-permute-start | bytes 909320 | tf_op jit(solution)/shard_map/ppermute | solution.py:452
  24.3 0.0 copy-done.3
  24.3 7.3 %shard_map.97 = (f32[2,40,256]{2,1,0:T(8,128)S(1)}, f32[272,256]{1,0:T(8,128)S(1)}, f32[272,256]{1,0:T(8,128)S(1)}) custom-call(f32[2,40,256]{2,1,0:T(8,128)S(1)} %get-tuple-element.48.q2, f32[2048,256]{1,0:T(8,128)S(1)} %bitcast.5, f32[8,40,256]{2,1,0:T(8,128)S(1)} %copy-done.3, f32[376,256]{1,0:T(8,128)S(1)} %collective-permute-done.1.swap, ...), custom_call_target="tpu_custom_call" | custom-call | flops 17179869184 | bytes 4194304 | tf_op jit(solution)/shard_map/pallas_call | solution.py:453
  31.6 0.0 collective-permute-done.2
  31.6 0.1 collective-permute-start.9
  31.7 0.0 collective-permute-done.4.following
  31.7 1.3 %collective-permute-start.7 = (f32[296,256]{1,0:T(8,128)S(1)}, f32[296,256]{1,0:T(8,128)S(1)}, u32[]{:S(2)}, u32[]{:S(2)}) collective-permute-start(f32[296,256]{1,0:T(8,128)S(1)} %collective-permute-done.2), channel_id=1, source_target_pairs={{65,64},{1,0}} | collective-permute-start | bytes 909320 | tf_op jit(solution)/shard_map/ppermute | solution.py:458
  33.0 0.0 collective-permute-done.3.link
  33.1 7.5 %shard_map.98 = (f32[2,40,256]{2,1,0:T(8,128)S(1)}, f32[272,256]{1,0:T(8,128)S(1)}, f32[272,256]{1,0:T(8,128)S(1)}) custom-call(f32[2,40,256]{2,1,0:T(8,128)S(1)} %get-tuple-element.50.q1, f32[8,40,256]{2,1,0:T(8,128)S(1)} %copy-done.3, f32[376,256]{1,0:T(8,128)S(1)} %collective-permute-done.1.swap, f32[256,256]{1,0:T(8,128)S(1)} %collective-permute-done.3.link, ...), custom_call_target="tpu_custom_call" | custom-call | flops 17179869184 | bytes 4194304 | tf_op jit(solution)/shard_map/pallas_call | solution.py:460
  40.6 2.7 %collective-permute-start.11 = (f32[272,256]{1,0:T(8,128)S(1)}, f32[272,256]{1,0:T(8,128)S(1)}, u32[]{:S(2)}, u32[]{:S(2)}) collective-permute-start(f32[272,256]{1,0:T(8,128)S(1)} %get-tuple-element.66), channel_id=1, source_target_pairs={{0,1},{1,0},{2,3},{3,2},{4,5},{5,4},{6,7},{7,6},{8,9},{9,8},{10,11... | collective-permute-start | bytes 835592 | tf_op jit(solution)/shard_map/ppermute | solution.py:464
  43.3 0.0 collective-permute-done.5.chain
  43.3 0.0 collective-permute-done.6.ahead
  43.3 1.3 %collective-permute-done.7.relay = f32[296,256]{1,0:T(8,128)S(1)} collective-permute-done((f32[296,256]{1,0:T(8,128)S(1)}, f32[296,256]{1,0:T(8,128)S(1)}, u32[]{:S(2)}, u32[]{:S(2)}) %collective-permute-start.7) | collective-permute-done | bytes 303136 | tf_op jit(solution)/shard_map/ppermute | solution.py:458
  44.6 4.6 %shard_map.99 = (f32[2,256,256]{2,1,0:T(8,128)S(1)}, f32[2,16,256]{2,1,0:T(8,128)S(1)}) custom-call(f32[2,40,256]{2,1,0:T(8,128)S(1)} %get-tuple-element.53.after.q0, f32[296,256]{1,0:T(8,128)S(1)} %collective-permute-done.5.chain, f32[296,256]{1,0:T(8,128)S(1)} %collective-permute-done.6.ahead, f32[296,256]{1,0:T(8,128)S(1)} %collective-permute-done.7.relay, ...), custom_call_target="tpu_custom_call" | custom-call | flops 8589934592 | bytes 4194304 | tf_op jit(solution)/shard_map/pallas_call | solution.py:465
  49.2 5.4 %collective-permute-start.8 = (f32[2,16,256]{2,1,0:T(8,128)S(1)}, f32[2,16,256]{2,1,0:T(8,128)S(1)}, u32[]{:S(2)}, u32[]{:S(2)}) collective-permute-start(f32[2,16,256]{2,1,0:T(8,128)S(1)} %get-tuple-element.57), channel_id=1, source_target_pairs={{1,0},{2,1},{3,2},{4,3},{5,4},{6,5},{7,6},{8,7},{9,8},{10,9},{11,1... | collective-permute-start | bytes 98312 | tf_op jit(solution)/shard_map/ppermute | solution.py:468
  54.6 0.0 collective-permute-done.9.back_a
  54.6 3.5 %shard_map.100 = (f32[272,256]{1,0:T(8,128)S(1)}, f32[272,256]{1,0:T(8,128)S(1)}, f32[2048,256]{1,0:T(8,128)}) custom-call(f32[2,256,256]{2,1,0:T(8,128)S(1)} %get-tuple-element.58.d_ref, f32[2,40,256]{2,1,0:T(8,128)S(1)} %get-tuple-element.53.after.q0, f32[272,256]{1,0:T(8,128)S(1)} %get-tuple-element.59.own_a, f32[272,256]{1,0:T(8,128)S(1)} %get-tuple-element.60.own_b, ...), custom_call_target="tpu_custom_call" | custom-call | flops 8589934592 | bytes 4194304 | tf_op jit(solution)/shard_map/pallas_call | solution.py:469
  58.1 0.3 collective-permute-start.12
  58.4 0.0 collective-permute-done.8.from_back
  58.4 3.6 %shard_map.101 = (f32[272,256]{1,0:T(8,128)S(1)}, f32[272,256]{1,0:T(8,128)S(1)}, f32[2048,256]{1,0:T(8,128)}) custom-call(f32[2,256,256]{2,1,0:T(8,128)S(1)} %get-tuple-element.41.d_ref, f32[8,40,256]{2,1,0:T(8,128)S(1)} %copy-done.3, f32[376,256]{1,0:T(8,128)S(1)} %collective-permute-done.1.swap, ...), custom_call_target="tpu_custom_call", output_to_operand_aliasing={{2}: (6, {})} | custom-call | flops 17179869184 | bytes 4194304 | tf_op jit(solution)/shard_map/pallas_call | solution.py:474
  62.0 2.1 %collective-permute-start.10 = (f32[272,256]{1,0:T(8,128)S(1)}, f32[272,256]{1,0:T(8,128)S(1)}, u32[]{:S(2)}, u32[]{:S(2)}) collective-permute-start(f32[272,256]{1,0:T(8,128)S(1)} %get-tuple-element.64), channel_id=1, source_target_pairs={{0,1},{1,0},{2,3},{3,2},{4,5},{5,4},{6,7},{7,6},{8,9},{9,8},{10,11... | collective-permute-start | bytes 835592 | tf_op jit(solution)/shard_map/ppermute | solution.py:478
  64.0 0.0 collective-permute-done.11.back_b
  64.0 0.9 %collective-permute-done.12.back_c = f32[272,256]{1,0:T(8,128)S(1)} collective-permute-done((f32[272,256]{1,0:T(8,128)S(1)}, f32[272,256]{1,0:T(8,128)S(1)}, u32[]{:S(2)}, u32[]{:S(2)}) %collective-permute-start.12) | collective-permute-done | bytes 278560 | tf_op jit(solution)/shard_map/ppermute | solution.py:473
  64.9 1.2 %shard_map.102 = (f32[2048,256]{1,0:T(8,128)}, f32[8,2048]{1,0:T(8,128)S(1)}, f32[8,2048]{1,0:T(8,128)S(1)}) custom-call(f32[272,256]{1,0:T(8,128)S(1)} %get-tuple-element.59.own_a, f32[272,256]{1,0:T(8,128)S(1)} %get-tuple-element.60.own_b, f32[272,256]{1,0:T(8,128)S(1)} %get-tuple-element.62.own_c, ...), custom_call_target="tpu_custom_call", output_to_operand_aliasing={{0}: (7, {})} | custom-call | flops 1048576 | bytes 4194304 | tf_op jit(solution)/shard_map/pallas_call | solution.py:480
  66.1 2.5 %collective-permute-done.10.back_d = f32[272,256]{1,0:T(8,128)S(1)} collective-permute-done((f32[272,256]{1,0:T(8,128)S(1)}, f32[272,256]{1,0:T(8,128)S(1)}, u32[]{:S(2)}, u32[]{:S(2)}) %collective-permute-start.10) | collective-permute-done | bytes 278560 | tf_op jit(solution)/shard_map/ppermute | solution.py:478
  68.6 1.4 %shard_map.103 = (f32[2048,256]{1,0:T(8,128)}, f32[8,2048]{1,0:T(8,128)}, f32[8,2048]{1,0:T(8,128)}) custom-call(f32[272,256]{1,0:T(8,128)S(1)} %collective-permute-done.10.back_d, f32[2048,256]{1,0:T(8,128)} %get-tuple-element.69.wave_in, f32[8,2048]{1,0:T(8,128)S(1)} %get-tuple-element.70.phase_in, ...), custom_call_target="tpu_custom_call", output_to_operand_aliasing={{0}: (1, {})} | custom-call | flops 1048576 | bytes 4194304 | tf_op jit(solution)/shard_map/pallas_call | solution.py:484
  (2 shorter events, 0.0 us)
Async XLA Ops:
  2.7 9.2 %collective-permute-start = (f32[296,256]{1,0:T(8,128)}, f32[296,256]{1,0:T(8,128)S(1)}, u32[]{:S(2)}, u32[]{:S(2)}) collective-permute-start(f32[296,256]{1,0:T(8,128)} %get-tuple-element.40.near), channel_id=1, source_target_pairs={{0,1},{1,0},{2,3},{3,2},{4,5},{5,4},{6,7},{7,6},{8,9},{9,8},{10,11... | collective-permute-start | bytes 909320 | tf_op jit(solution)/shard_map/ppermute | solution.py:437
  4.0 7.9 %copy-start = (f32[8,2,128,256]{3,2,1,0:T(8,128)S(1)}, f32[8,2,128,256]{3,2,1,0:T(8,128)}, u32[]{:S(2)}) copy-start(f32[8,2,128,256]{3,2,1,0:T(8,128)} %param.7) | copy-start | bytes 6291460
  4.0 7.9 %copy-start.1 = (f32[40,256]{1,0:T(8,128)S(1)}, f32[40,256]{1,0:T(8,128)}, u32[]{:S(2)}) copy-start(f32[40,256]{1,0:T(8,128)} %get-tuple-element.39.mine) | copy-start | bytes 122884
  4.0 7.9 %copy-start.2 = (bf16[2,2,2,256,256]{4,3,2,1,0:T(8,128)(2,1)S(1)}, bf16[2,2,2,256,256]{4,3,2,1,0:T(8,128)(2,1)}, u32[]{:S(2)}) copy-start(bf16[2,2,2,256,256]{4,3,2,1,0:T(8,128)(2,1)} %constant.2.clone.table) | copy-start | bytes 3145732
  4.0 27.6 %collective-permute-start.2 = (f32[296,256]{1,0:T(8,128)}, f32[296,256]{1,0:T(8,128)S(1)}, u32[]{:S(2)}, u32[]{:S(2)}) collective-permute-start(f32[296,256]{1,0:T(8,128)} %get-tuple-element.55), channel_id=1, source_target_pairs={{62,65},{126,1}} | collective-permute-start | bytes 909320 | tf_op jit(solution)/shard_map/ppermute | solution.py:438
  7.6 24.2 %collective-permute-start.4 = (f32[256,256]{1,0:T(8,128)}, f32[256,256]{1,0:T(8,128)S(1)}, u32[]{:S(2)}, u32[]{:S(2)}) collective-permute-start(f32[256,256]{1,0:T(8,128)} %get-tuple-element.52), channel_id=1, source_target_pairs={{0,2},{1,1},{2,4},{3,3},{4,6},{5,5},{6,8},{7,7},{8,10},{9,9},{10,1... | collective-permute-start | bytes 786440 | tf_op jit(solution)/shard_map/ppermute | solution.py:444
  9.5 11.4 %collective-permute-start.1 = (f32[376,256]{1,0:T(8,128)}, f32[376,256]{1,0:T(8,128)S(1)}, u32[]{:S(2)}, u32[]{:S(2)}) collective-permute-start(f32[376,256]{1,0:T(8,128)} %get-tuple-element.43), channel_id=1, source_target_pairs={{0,1},{1,0},{2,3},{3,2},{4,5},{5,4},{6,7},{7,6},{8,9},{9,8},{10,11... | collective-permute-start | bytes 1155080 | tf_op jit(solution)/shard_map/ppermute | solution.py:443
  12.0 4.2 %copy-start.6 = (f32[256,256]{1,0:T(8,128)S(1)}, f32[256,256]{1,0:T(8,128)}, u32[]{:S(2)}) copy-start(f32[256,256]{1,0:T(8,128)} %get-tuple-element.51) | copy-start | bytes 786436
  12.0 5.5 %copy-start.5 = (f32[296,256]{1,0:T(8,128)S(1)}, f32[296,256]{1,0:T(8,128)}, u32[]{:S(2)}) copy-start(f32[296,256]{1,0:T(8,128)} %get-tuple-element.54) | copy-start | bytes 909316
  12.0 8.9 %copy-start.4 = (f32[296,256]{1,0:T(8,128)S(1)}, f32[296,256]{1,0:T(8,128)}, u32[]{:S(2)}) copy-start(f32[296,256]{1,0:T(8,128)} %get-tuple-element.55) | copy-start | bytes 909316
  12.0 12.3 %copy-start.3 = (f32[8,40,256]{2,1,0:T(8,128)S(1)}, f32[8,40,256]{2,1,0:T(8,128)}, u32[]{:S(2)}) copy-start(f32[8,40,256]{2,1,0:T(8,128)} %get-tuple-element.42.parts) | copy-start | bytes 983044
  16.2 16.9 %collective-permute-start.3 = (f32[256,256]{1,0:T(8,128)S(1)}, f32[256,256]{1,0:T(8,128)S(1)}, u32[]{:S(2)}, u32[]{:S(2)}) collective-permute-start(f32[256,256]{1,0:T(8,128)S(1)} %copy-done.6), channel_id=1, source_target_pairs={{0,1},{1,2},{2,3},{3,4},{4,5},{5,6},{6,7},{7,8},{8,9},{9,10},{10,1... | collective-permute-start | bytes 786440 | tf_op jit(solution)/shard_map/ppermute | solution.py:450
  17.5 25.8 %collective-permute-start.5 = (f32[296,256]{1,0:T(8,128)S(1)}, f32[296,256]{1,0:T(8,128)S(1)}, u32[]{:S(2)}, u32[]{:S(2)}) collective-permute-start(f32[296,256]{1,0:T(8,128)S(1)} %copy-done.5), channel_id=1, source_target_pairs={{0,1},{1,2},{2,3},{3,4},{4,5},{5,6},{6,7},{7,8},{8,9},{9,10},{10,1... | collective-permute-start | bytes 909320 | tf_op jit(solution)/shard_map/ppermute | solution.py:451
  20.9 22.4 %collective-permute-start.6 = (f32[296,256]{1,0:T(8,128)S(1)}, f32[296,256]{1,0:T(8,128)S(1)}, u32[]{:S(2)}, u32[]{:S(2)}) collective-permute-start(f32[296,256]{1,0:T(8,128)S(1)} %copy-done.4), channel_id=1, source_target_pairs={{0,2},{1,1},{2,4},{3,3},{4,6},{5,5},{6,8},{7,7},{8,10},{9,9},{10,1... | collective-permute-start | bytes 909320 | tf_op jit(solution)/shard_map/ppermute | solution.py:452
  31.6 22.9 %collective-permute-start.9 = (f32[272,256]{1,0:T(8,128)S(1)}, f32[272,256]{1,0:T(8,128)S(1)}, u32[]{:S(2)}, u32[]{:S(2)}) collective-permute-start(f32[272,256]{1,0:T(8,128)S(1)} %get-tuple-element.61), channel_id=1, source_target_pairs={{0,1},{1,0},{2,3},{3,2},{4,5},{5,4},{6,7},{7,6},{8,9},{9,8},{10,11... | collective-permute-start | bytes 835592 | tf_op jit(solution)/shard_map/ppermute | solution.py:459
  31.7 12.9 %collective-permute-start.7 = (f32[296,256]{1,0:T(8,128)S(1)}, f32[296,256]{1,0:T(8,128)S(1)}, u32[]{:S(2)}, u32[]{:S(2)}) collective-permute-start(f32[296,256]{1,0:T(8,128)S(1)} %collective-permute-done.2), channel_id=1, source_target_pairs={{65,64},{1,0}} | collective-permute-start | bytes 909320 | tf_op jit(solution)/shard_map/ppermute | solution.py:458
  40.6 23.5 %collective-permute-start.11 = (f32[272,256]{1,0:T(8,128)S(1)}, f32[272,256]{1,0:T(8,128)S(1)}, u32[]{:S(2)}, u32[]{:S(2)}) collective-permute-start(f32[272,256]{1,0:T(8,128)S(1)} %get-tuple-element.66), channel_id=1, source_target_pairs={{0,1},{1,0},{2,3},{3,2},{4,5},{5,4},{6,7},{7,6},{8,9},{9,8},{10,11... | collective-permute-start | bytes 835592 | tf_op jit(solution)/shard_map/ppermute | solution.py:464
  49.2 9.2 %collective-permute-start.8 = (f32[2,16,256]{2,1,0:T(8,128)S(1)}, f32[2,16,256]{2,1,0:T(8,128)S(1)}, u32[]{:S(2)}, u32[]{:S(2)}) collective-permute-start(f32[2,16,256]{2,1,0:T(8,128)S(1)} %get-tuple-element.57), channel_id=1, source_target_pairs={{1,0},{2,1},{3,2},{4,3},{5,4},{6,5},{7,6},{8,7},{9,8},{10,9},{11,1... | collective-permute-start | bytes 98312 | tf_op jit(solution)/shard_map/ppermute | solution.py:468
  58.1 6.8 %collective-permute-start.12 = (f32[272,256]{1,0:T(8,128)S(1)}, f32[272,256]{1,0:T(8,128)S(1)}, u32[]{:S(2)}, u32[]{:S(2)}) collective-permute-start(f32[272,256]{1,0:T(8,128)S(1)} %get-tuple-element.67), channel_id=1, source_target_pairs={{0,1},{1,0},{2,3},{3,2},{4,5},{5,4},{6,7},{7,6},{8,9},{9,8},{10,11... | collective-permute-start | bytes 835592 | tf_op jit(solution)/shard_map/ppermute | solution.py:473
  62.0 6.6 %collective-permute-start.10 = (f32[272,256]{1,0:T(8,128)S(1)}, f32[272,256]{1,0:T(8,128)S(1)}, u32[]{:S(2)}, u32[]{:S(2)}) collective-permute-start(f32[272,256]{1,0:T(8,128)S(1)} %get-tuple-element.64), channel_id=1, source_target_pairs={{0,1},{1,0},{2,3},{3,2},{4,5},{5,4},{6,7},{7,6},{8,9},{9,8},{10,11... | collective-permute-start | bytes 835592 | tf_op jit(solution)/shard_map/ppermute | solution.py:478

commit v11 on v10

--- a/solution.py
+++ b/solution.py
@@ -441,20 +441,20 @@
         [VM] * 5, stage, 12, [ANY] + [HB] * 6, 4 * unit, vmem=61000 << 10,
     )(to_near, *raw)
     f_swap = lax.ppermute(to_swap, both, swap)
-    f_next = lax.ppermute(to_next, both, ahead + direct)
 
     d3, q2 = call(
         near_kernel, [field, full], [VM, VM], [FIELD, PARTS, TABLE] + WORK, 8, [ANY] * 4, unit, vmem=50000 << 10,
     )(wave, mine, f_near, table)
-    q2, to_chain, to_link, to_ahead = lax.optimization_barrier((q2, to_chain, to_link, to_ahead))
+    q2, to_chain, to_link, to_next = lax.optimization_barrier((q2, to_chain, to_link, to_next))
+    f_next = lax.ppermute(to_next, both, ahead + direct)
     f_link = lax.ppermute(to_link, both, chain)
     f_chain = lax.ppermute(to_chain, both, chain)
-    f_ahead = lax.ppermute(to_ahead, both, ahead)
     q1, own_a, away_a = call(
         first_kernel, [full] + pieces, [VM] * 3, [FIELD, PARTS, PUSH, FIELD, TABLE] + WORK, 8,
         [VM] + [ANY] * 4, 2 * unit,
     )(q2, wave, parts, f_swap, table)
-    q1, f_around = lax.optimization_barrier((q1, f_around))
+    q1, f_around, to_ahead = lax.optimization_barrier((q1, f_around, to_ahead))
+    f_ahead = lax.ppermute(to_ahead, both, ahead)
     f_relay = lax.ppermute(f_around, both, onward)
     back_a = lax.ppermute(away_a, both, swap)
     q0, own_b, away_b = call(

time: 71.2 us -> 71 us (level)
  waiting for transfers between devices: 9.44 us -> 15.2 us
  starting transfers between devices: 21.7 us -> 16.3 us
    ppermute x1, starting transfers between devices: 5.37 us -> 0.72 us  [body(): from_back = lax.ppermute(to_back, both, back)]
    ppermute x1, waiting for transfers between devices: 3.38 us -> 0.01 us  [body(): f_swap = lax.ppermute(to_swap, both, swap)]
    ppermute x1, starting transfers between devices: 0.09 us -> 3.35 us  [body(): back_a = lax.ppermute(away_a, both, swap)]
    ppermute x1, waiting for transfers between devices: 0.86 us -> 3.8 us  [body(): back_c = lax.ppermute(away_c, both, swap)]
    ppermute x1, waiting for transfers between devices: 1.34 us -> 4 us  [body(): f_near = lax.ppermute(to_near, both, swap)]
    ppermute x1, waiting for transfers between devices: 0.01 us -> 2.62 us  [body(): f_next = lax.ppermute(to_next, both, ahead + direct)]
    ppermute x1, starting transfers between devices: 2.75 us -> 0.16 us  [body(): back_b = lax.ppermute(away_b, both, swap)]
    ppermute x1, waiting for transfers between devices: 2.54 us -> 4.8 us  [body(): back_d = lax.ppermute(away_d, both, swap)]
  transfers between devices with their start and end apart: 13 -> 13, of which waited for: 5 -> 4; matrix products, arithmetic and copies ran while one was open for 0% -> 0% of each run, Pallas kernels for 49% -> 49%
where the time goes in v11:
time: 71 us; the launch traced here: 70.6 us
  Pallas kernels  38 us (54%)
  starting transfers between devices  16.3 us (23%)
  waiting for transfers between devices  15.2 us (21%)
  between operations  1.03 us (1%)
    pallas_call x1, Pallas kernels, body(): call(second_kernel, [full] + pieces, [VM] * 3, [FIELD, PARTS, PUSH, FIELD...  7.45 us
    pallas_call x1, Pallas kernels, body(): call(first_kernel, [full] + pieces, [VM] * 3, [FIELD, PARTS, PUSH, FIELD,...  7.31 us
    ppermute x1, waiting for transfers between devices, body(): back_d = lax.ppermute(away_d, both, swap)  4.8 us
    pallas_call x1, Pallas kernels, body(): call(edge_kernel, [field, (2, PUSHED, N)], [VM, VM], [FIELD, PARTS, TABLE...  4.62 us
    pallas_call x1, Pallas kernels, body(): call(near_kernel, [field, full], [VM, VM], [FIELD, PARTS, TABLE] + WORK,...  4.14 us
    ppermute x1, waiting for transfers between devices, body(): f_near = lax.ppermute(to_near, both, swap)  4 us
    ppermute x1, waiting for transfers between devices, body(): back_c = lax.ppermute(away_c, both, swap)  3.8 us
    pallas_call x1, Pallas kernels, body(): call(fourth_kernel, pieces + [(8 * N, N)], [VM, VM, ANY], [PARTS, PUSH, F...  3.56 us
  transfers between devices with their start and end apart: 13, of which 4 were waited for; matrix products, arithmetic and copies ran while one was open for 0% of the time, Pallas kernels for 49%

profile of v11, /device:TPU:4, one launch (start us, length us, event | category | flops | bytes accessed | tf_op | source)
XLA Modules:
  0.0 70.6 jit_solution(14763724773098376472)
XLA Ops:
  0.6 2.1 %shard_map.94 = (f32[296,256]{1,0:T(8,128)}, f32[296,256]{1,0:T(8,128)}, f32[40,256]{1,0:T(8,128)}) custom-call(f32[2048,256]{1,0:T(8,128)} %bitcast.2, f32[8,2048]{1,0:T(8,128)} %refs_0_.3, f32[8,2048]{1,0:T(8,128)} %refs_1_.3, f32[8,2048]{1,0:T(8,128)} %refs_2_.3, s32[8,2048]{1,0:T(8,128)} %refs_3_.3, s32[8,2048]{1,0:T(8,128)} %refs_4_.3), custom_call_target="tpu_custom_call" | custom-call | flops 1048576 | bytes 4194304 | tf_op jit(solution)/shard_map/pallas_call | solution.py:433
  2.7 1.3 %collective-permute-start = (f32[296,256]{1,0:T(8,128)}, f32[296,256]{1,0:T(8,128)S(1)}, u32[]{:S(2)}, u32[]{:S(2)}) collective-permute-start(f32[296,256]{1,0:T(8,128)} %get-tuple-element.41.near), channel_id=1, source_target_pairs={{0,1},{1,0},{2,3},{3,2},{4,5},{5,4},{6,7},{7,6},{8,9},{9,8},{10,11... | collective-permute-start | bytes 909320 | tf_op jit(solution)/shard_map/ppermute | solution.py:437
  4.0 0.8 %collective-permute-start.2 = (f32[296,256]{1,0:T(8,128)}, f32[296,256]{1,0:T(8,128)S(1)}, u32[]{:S(2)}, u32[]{:S(2)}) collective-permute-start(f32[296,256]{1,0:T(8,128)} %get-tuple-element.57), channel_id=1, source_target_pairs={{62,65},{126,1}} | collective-permute-start | bytes 909320 | tf_op jit(solution)/shard_map/ppermute | solution.py:438
  4.8 2.7 %shard_map.96 = (f32[8,40,256]{2,1,0:T(8,128)}, f32[376,256]{1,0:T(8,128)}, f32[296,256]{1,0:T(8,128)}, f32[256,256]{1,0:T(8,128)}, f32[256,256]{1,0:T(8,128)}) custom-call(f32[296,256]{1,0:T(8,128)} %get-tuple-element.41.near, f32[2048,256]{1,0:T(8,128)} %bitcast.3, f32[8,2048]{1,0:T(8,128)} %refs_0_.3, f32[8,2048]{1,0:T(8,128)} %refs_1_.3, ...), custom_call_target="tpu_custom_call" | custom-call | flops 34359738368 | bytes 4194304 | tf_op jit(solution)/shard_map/pallas_call | solution.py:439
  7.6 1.5 %collective-permute-start.1 = (f32[376,256]{1,0:T(8,128)}, f32[376,256]{1,0:T(8,128)S(1)}, u32[]{:S(2)}, u32[]{:S(2)}) collective-permute-start(f32[376,256]{1,0:T(8,128)} %get-tuple-element.44), channel_id=1, source_target_pairs={{0,1},{1,0},{2,3},{3,2},{4,5},{5,4},{6,7},{7,6},{8,9},{9,8},{10,11... | collective-permute-start | bytes 1155080 | tf_op jit(solution)/shard_map/ppermute | solution.py:443
  9.1 4.0 %collective-permute-done.near = f32[296,256]{1,0:T(8,128)S(1)} collective-permute-done((f32[296,256]{1,0:T(8,128)}, f32[296,256]{1,0:T(8,128)S(1)}, u32[]{:S(2)}, u32[]{:S(2)}) %collective-permute-start) | collective-permute-done | bytes 303136 | tf_op jit(solution)/shard_map/ppermute | solution.py:437
  13.1 0.0 copy-done
  13.1 0.0 copy-done.1
  13.1 0.0 copy-done.2
  13.1 0.0 copy-start.7
  13.1 0.0 copy-start.6
  13.1 0.0 copy-start.5
  13.1 0.0 copy-start.3
  13.2 4.1 %shard_map.95 = (f32[2,256,256]{2,1,0:T(8,128)S(1)}, f32[2,40,256]{2,1,0:T(8,128)S(1)}) custom-call(f32[2048,256]{1,0:T(8,128)S(1)} %bitcast.4, f32[40,256]{1,0:T(8,128)S(1)} %copy-done.1, f32[296,256]{1,0:T(8,128)S(1)} %collective-permute-done.near, bf16[2,2,2,256,256]{4,3,2,1,0:T(8,128)(2,1)S(1)} %copy-done.2), custom_call_target="tpu_custom_call" | custom-call | flops 8589934592 | bytes 4194304 | tf_op jit(solution)/shard_map/pallas_call | solution.py:445
  17.3 0.0 copy-done.7
  17.3 1.3 %collective-permute-start.3 = (f32[256,256]{1,0:T(8,128)S(1)}, f32[256,256]{1,0:T(8,128)S(1)}, u32[]{:S(2)}, u32[]{:S(2)}) collective-permute-start(f32[256,256]{1,0:T(8,128)S(1)} %copy-done.7), channel_id=1, source_target_pairs={{0,1},{1,2},{2,3},{3,4},{4,5},{5,6},{6,7},{7,8},{8,9},{9,10},{10,1... | collective-permute-start | bytes 786440 | tf_op jit(solution)/shard_map/ppermute | solution.py:450
  18.6 0.0 copy-done.6
  18.6 1.9 %collective-permute-start.4 = (f32[256,256]{1,0:T(8,128)S(1)}, f32[256,256]{1,0:T(8,128)S(1)}, u32[]{:S(2)}, u32[]{:S(2)}) collective-permute-start(f32[256,256]{1,0:T(8,128)S(1)} %copy-done.6), channel_id=1, source_target_pairs={{0,2},{1,1},{2,4},{3,3},{4,6},{5,5},{6,8},{7,7},{8,10},{9,9},{10,1... | collective-permute-start | bytes 786440 | tf_op jit(solution)/shard_map/ppermute | solution.py:449
  20.5 0.0 copy-done.5
  20.5 0.1 collective-permute-start.5
  20.6 0.0 collective-permute-done.1.swap
  20.6 0.0 copy-done.3
  20.6 0.0 copy-start.4
  20.6 7.3 %shard_map.97 = (f32[2,40,256]{2,1,0:T(8,128)S(1)}, f32[272,256]{1,0:T(8,128)S(1)}, f32[272,256]{1,0:T(8,128)S(1)}) custom-call(f32[2,40,256]{2,1,0:T(8,128)S(1)} %get-tuple-element.49.q2, f32[2048,256]{1,0:T(8,128)S(1)} %bitcast.5, f32[8,40,256]{2,1,0:T(8,128)S(1)} %copy-done.3, f32[376,256]{1,0:T(8,128)S(1)} %collective-permute-done.1.swap, ...), custom_call_target="tpu_custom_call" | custom-call | flops 17179869184 | bytes 4194304 | tf_op jit(solution)/shard_map/pallas_call | solution.py:452
  28.0 0.0 collective-permute-done.2
  28.0 3.3 %collective-permute-start.9 = (f32[272,256]{1,0:T(8,128)S(1)}, f32[272,256]{1,0:T(8,128)S(1)}, u32[]{:S(2)}, u32[]{:S(2)}) collective-permute-start(f32[272,256]{1,0:T(8,128)S(1)} %get-tuple-element.63), channel_id=1, source_target_pairs={{0,1},{1,0},{2,3},{3,2},{4,5},{5,4},{6,7},{7,6},{8,9},{9,8},{10,11... | collective-permute-start | bytes 835592 | tf_op jit(solution)/shard_map/ppermute | solution.py:459
  31.3 1.5 %collective-permute-start.6 = (f32[296,256]{1,0:T(8,128)S(1)}, f32[296,256]{1,0:T(8,128)S(1)}, u32[]{:S(2)}, u32[]{:S(2)}) collective-permute-start(f32[296,256]{1,0:T(8,128)S(1)} %copy-done.4), channel_id=1, source_target_pairs={{0,2},{1,1},{2,4},{3,3},{4,6},{5,5},{6,8},{7,7},{8,10},{9,9},{10,1... | collective-permute-start | bytes 909320 | tf_op jit(solution)/shard_map/ppermute | solution.py:457
  32.8 0.0 collective-permute-done.3.link
  32.8 1.3 %collective-permute-start.7 = (f32[296,256]{1,0:T(8,128)S(1)}, f32[296,256]{1,0:T(8,128)S(1)}, u32[]{:S(2)}, u32[]{:S(2)}) collective-permute-start(f32[296,256]{1,0:T(8,128)S(1)} %collective-permute-done.2), channel_id=1, source_target_pairs={{65,64},{1,0}} | collective-permute-start | bytes 909320 | tf_op jit(solution)/shard_map/ppermute | solution.py:458
  34.1 2.6 %collective-permute-done.4.following = f32[256,256]{1,0:T(8,128)S(1)} collective-permute-done((f32[256,256]{1,0:T(8,128)S(1)}, f32[256,256]{1,0:T(8,128)S(1)}, u32[]{:S(2)}, u32[]{:S(2)}) %collective-permute-start.4) | collective-permute-done | bytes 262176 | tf_op jit(solution)/shard_map/ppermute | solution.py:449
  36.7 7.5 %shard_map.98 = (f32[2,40,256]{2,1,0:T(8,128)S(1)}, f32[272,256]{1,0:T(8,128)S(1)}, f32[272,256]{1,0:T(8,128)S(1)}) custom-call(f32[2,40,256]{2,1,0:T(8,128)S(1)} %get-tuple-element.52.q1, f32[8,40,256]{2,1,0:T(8,128)S(1)} %copy-done.3, f32[376,256]{1,0:T(8,128)S(1)} %collective-permute-done.1.swap, f32[256,256]{1,0:T(8,128)S(1)} %collective-permute-done.3.link, ...), custom_call_target="tpu_custom_call" | custom-call | flops 17179869184 | bytes 4194304 | tf_op jit(solution)/shard_map/pallas_call | solution.py:460
  44.2 0.2 collective-permute-start.11
  44.4 0.0 collective-permute-done.5.chain
  44.4 0.0 collective-permute-done.6.ahead
  44.4 0.0 collective-permute-done.7.relay
  44.4 4.6 %shard_map.99 = (f32[2,256,256]{2,1,0:T(8,128)S(1)}, f32[2,16,256]{2,1,0:T(8,128)S(1)}) custom-call(f32[2,40,256]{2,1,0:T(8,128)S(1)} %get-tuple-element.55.after.q0, f32[296,256]{1,0:T(8,128)S(1)} %collective-permute-done.5.chain, f32[296,256]{1,0:T(8,128)S(1)} %collective-permute-done.6.ahead, f32[296,256]{1,0:T(8,128)S(1)} %collective-permute-done.7.relay, ...), custom_call_target="tpu_custom_call" | custom-call | flops 8589934592 | bytes 4194304 | tf_op jit(solution)/shard_map/pallas_call | solution.py:465
  49.0 0.7 %collective-permute-start.8 = (f32[2,16,256]{2,1,0:T(8,128)S(1)}, f32[2,16,256]{2,1,0:T(8,128)S(1)}, u32[]{:S(2)}, u32[]{:S(2)}) collective-permute-start(f32[2,16,256]{2,1,0:T(8,128)S(1)} %get-tuple-element.59), channel_id=1, source_target_pairs={{1,0},{2,1},{3,2},{4,3},{5,4},{6,5},{7,6},{8,7},{9,8},{10,9},{11,1... | collective-permute-start | bytes 98312 | tf_op jit(solution)/shard_map/ppermute | solution.py:468
  49.7 0.0 collective-permute-done.9.back_a
  49.7 3.5 %shard_map.100 = (f32[272,256]{1,0:T(8,128)S(1)}, f32[272,256]{1,0:T(8,128)S(1)}, f32[2048,256]{1,0:T(8,128)}) custom-call(f32[2,256,256]{2,1,0:T(8,128)S(1)} %get-tuple-element.60.d_ref, f32[2,40,256]{2,1,0:T(8,128)S(1)} %get-tuple-element.55.after.q0, f32[272,256]{1,0:T(8,128)S(1)} %get-tuple-element.61.own_a, f32[272,256]{1,0:T(8,128)S(1)} %get-tuple-element.62.own_b, ...), custom_call_target="tpu_custom_call" | custom-call | flops 8589934592 | bytes 4194304 | tf_op jit(solution)/shard_map/pallas_call | solution.py:469
  53.2 1.7 %collective-permute-start.12 = (f32[272,256]{1,0:T(8,128)S(1)}, f32[272,256]{1,0:T(8,128)S(1)}, u32[]{:S(2)}, u32[]{:S(2)}) collective-permute-start(f32[272,256]{1,0:T(8,128)S(1)} %get-tuple-element.69), channel_id=1, source_target_pairs={{0,1},{1,0},{2,3},{3,2},{4,5},{5,4},{6,7},{7,6},{8,9},{9,8},{10,11... | collective-permute-start | bytes 835592 | tf_op jit(solution)/shard_map/ppermute | solution.py:473
  54.9 0.0 collective-permute-done.8.from_back
  54.9 3.6 %shard_map.101 = (f32[272,256]{1,0:T(8,128)S(1)}, f32[272,256]{1,0:T(8,128)S(1)}, f32[2048,256]{1,0:T(8,128)}) custom-call(f32[2,256,256]{2,1,0:T(8,128)S(1)} %get-tuple-element.42.d_ref, f32[8,40,256]{2,1,0:T(8,128)S(1)} %copy-done.3, f32[376,256]{1,0:T(8,128)S(1)} %collective-permute-done.1.swap, ...), custom_call_target="tpu_custom_call", output_to_operand_aliasing={{2}: (6, {})} | custom-call | flops 17179869184 | bytes 4194304 | tf_op jit(solution)/shard_map/pallas_call | solution.py:474
  58.5 0.7 %collective-permute-start.10 = (f32[272,256]{1,0:T(8,128)S(1)}, f32[272,256]{1,0:T(8,128)S(1)}, u32[]{:S(2)}, u32[]{:S(2)}) collective-permute-start(f32[272,256]{1,0:T(8,128)S(1)} %get-tuple-element.66), channel_id=1, source_target_pairs={{0,1},{1,0},{2,3},{3,2},{4,5},{5,4},{6,7},{7,6},{8,9},{9,8},{10,11... | collective-permute-start | bytes 835592 | tf_op jit(solution)/shard_map/ppermute | solution.py:478
  59.2 0.0 collective-permute-done.11.back_b
  59.2 3.8 %collective-permute-done.12.back_c = f32[272,256]{1,0:T(8,128)S(1)} collective-permute-done((f32[272,256]{1,0:T(8,128)S(1)}, f32[272,256]{1,0:T(8,128)S(1)}, u32[]{:S(2)}, u32[]{:S(2)}) %collective-permute-start.12) | collective-permute-done | bytes 278560 | tf_op jit(solution)/shard_map/ppermute | solution.py:473
  63.0 1.2 %shard_map.102 = (f32[2048,256]{1,0:T(8,128)}, f32[8,2048]{1,0:T(8,128)S(1)}, f32[8,2048]{1,0:T(8,128)S(1)}) custom-call(f32[272,256]{1,0:T(8,128)S(1)} %get-tuple-element.61.own_a, f32[272,256]{1,0:T(8,128)S(1)} %get-tuple-element.62.own_b, f32[272,256]{1,0:T(8,128)S(1)} %get-tuple-element.64.own_c, ...), custom_call_target="tpu_custom_call", output_to_operand_aliasing={{0}: (7, {})} | custom-call | flops 1048576 | bytes 4194304 | tf_op jit(solution)/shard_map/pallas_call | solution.py:480
  64.2 4.8 %collective-permute-done.10.back_d = f32[272,256]{1,0:T(8,128)S(1)} collective-permute-done((f32[272,256]{1,0:T(8,128)S(1)}, f32[272,256]{1,0:T(8,128)S(1)}, u32[]{:S(2)}, u32[]{:S(2)}) %collective-permute-start.10) | collective-permute-done | bytes 278560 | tf_op jit(solution)/shard_map/ppermute | solution.py:478
  69.0 1.4 %shard_map.103 = (f32[2048,256]{1,0:T(8,128)}, f32[8,2048]{1,0:T(8,128)}, f32[8,2048]{1,0:T(8,128)}) custom-call(f32[272,256]{1,0:T(8,128)S(1)} %collective-permute-done.10.back_d, f32[2048,256]{1,0:T(8,128)} %get-tuple-element.71.wave_in, f32[8,2048]{1,0:T(8,128)S(1)} %get-tuple-element.72.phase_in, ...), custom_call_target="tpu_custom_call", output_to_operand_aliasing={{0}: (1, {})} | custom-call | flops 1048576 | bytes 4194304 | tf_op jit(solution)/shard_map/pallas_call | solution.py:484
  (4 shorter events, 0.0 us)
Async XLA Ops:
  2.7 10.4 %collective-permute-start = (f32[296,256]{1,0:T(8,128)}, f32[296,256]{1,0:T(8,128)S(1)}, u32[]{:S(2)}, u32[]{:S(2)}) collective-permute-start(f32[296,256]{1,0:T(8,128)} %get-tuple-element.41.near), channel_id=1, source_target_pairs={{0,1},{1,0},{2,3},{3,2},{4,5},{5,4},{6,7},{7,6},{8,9},{9,8},{10,11... | collective-permute-start | bytes 909320 | tf_op jit(solution)/shard_map/ppermute | solution.py:437
  4.0 9.1 %copy-start = (f32[8,2,128,256]{3,2,1,0:T(8,128)S(1)}, f32[8,2,128,256]{3,2,1,0:T(8,128)}, u32[]{:S(2)}) copy-start(f32[8,2,128,256]{3,2,1,0:T(8,128)} %param.7) | copy-start | bytes 6291460
  4.0 9.1 %copy-start.1 = (f32[40,256]{1,0:T(8,128)S(1)}, f32[40,256]{1,0:T(8,128)}, u32[]{:S(2)}) copy-start(f32[40,256]{1,0:T(8,128)} %get-tuple-element.40.mine) | copy-start | bytes 122884
  4.0 9.1 %copy-start.2 = (bf16[2,2,2,256,256]{4,3,2,1,0:T(8,128)(2,1)S(1)}, bf16[2,2,2,256,256]{4,3,2,1,0:T(8,128)(2,1)}, u32[]{:S(2)}) copy-start(bf16[2,2,2,256,256]{4,3,2,1,0:T(8,128)(2,1)} %constant.2.clone.table) | copy-start | bytes 3145732
  4.0 23.9 %collective-permute-start.2 = (f32[296,256]{1,0:T(8,128)}, f32[296,256]{1,0:T(8,128)S(1)}, u32[]{:S(2)}, u32[]{:S(2)}) collective-permute-start(f32[296,256]{1,0:T(8,128)} %get-tuple-element.57), channel_id=1, source_target_pairs={{62,65},{126,1}} | collective-permute-start | bytes 909320 | tf_op jit(solution)/shard_map/ppermute | solution.py:438
  7.6 13.0 %collective-permute-start.1 = (f32[376,256]{1,0:T(8,128)}, f32[376,256]{1,0:T(8,128)S(1)}, u32[]{:S(2)}, u32[]{:S(2)}) collective-permute-start(f32[376,256]{1,0:T(8,128)} %get-tuple-element.44), channel_id=1, source_target_pairs={{0,1},{1,0},{2,3},{3,2},{4,5},{5,4},{6,7},{7,6},{8,9},{9,8},{10,11... | collective-permute-start | bytes 1155080 | tf_op jit(solution)/shard_map/ppermute | solution.py:443
  13.1 4.2 %copy-start.7 = (f32[256,256]{1,0:T(8,128)S(1)}, f32[256,256]{1,0:T(8,128)}, u32[]{:S(2)}) copy-start(f32[256,256]{1,0:T(8,128)} %get-tuple-element.53) | copy-start | bytes 786436
  13.1 5.5 %copy-start.6 = (f32[256,256]{1,0:T(8,128)S(1)}, f32[256,256]{1,0:T(8,128)}, u32[]{:S(2)}) copy-start(f32[256,256]{1,0:T(8,128)} %get-tuple-element.54) | copy-start | bytes 786436
  13.1 7.4 %copy-start.5 = (f32[296,256]{1,0:T(8,128)S(1)}, f32[296,256]{1,0:T(8,128)}, u32[]{:S(2)}) copy-start(f32[296,256]{1,0:T(8,128)} %get-tuple-element.56) | copy-start | bytes 909316
  13.1 7.5 %copy-start.3 = (f32[8,40,256]{2,1,0:T(8,128)S(1)}, f32[8,40,256]{2,1,0:T(8,128)}, u32[]{:S(2)}) copy-start(f32[8,40,256]{2,1,0:T(8,128)} %get-tuple-element.43.parts) | copy-start | bytes 983044
  17.3 15.5 %collective-permute-start.3 = (f32[256,256]{1,0:T(8,128)S(1)}, f32[256,256]{1,0:T(8,128)S(1)}, u32[]{:S(2)}, u32[]{:S(2)}) collective-permute-start(f32[256,256]{1,0:T(8,128)S(1)} %copy-done.7), channel_id=1, source_target_pairs={{0,1},{1,2},{2,3},{3,4},{4,5},{5,6},{6,7},{7,8},{8,9},{9,10},{10,1... | collective-permute-start | bytes 786440 | tf_op jit(solution)/shard_map/ppermute | solution.py:450
  18.6 18.2 %collective-permute-start.4 = (f32[256,256]{1,0:T(8,128)S(1)}, f32[256,256]{1,0:T(8,128)S(1)}, u32[]{:S(2)}, u32[]{:S(2)}) collective-permute-start(f32[256,256]{1,0:T(8,128)S(1)} %copy-done.6), channel_id=1, source_target_pairs={{0,2},{1,1},{2,4},{3,3},{4,6},{5,5},{6,8},{7,7},{8,10},{9,9},{10,1... | collective-permute-start | bytes 786440 | tf_op jit(solution)/shard_map/ppermute | solution.py:449
  20.5 23.9 %collective-permute-start.5 = (f32[296,256]{1,0:T(8,128)S(1)}, f32[296,256]{1,0:T(8,128)S(1)}, u32[]{:S(2)}, u32[]{:S(2)}) collective-permute-start(f32[296,256]{1,0:T(8,128)S(1)} %copy-done.5), channel_id=1, source_target_pairs={{0,1},{1,2},{2,3},{3,4},{4,5},{5,6},{6,7},{7,8},{8,9},{9,10},{10,1... | collective-permute-start | bytes 909320 | tf_op jit(solution)/shard_map/ppermute | solution.py:451
  20.6 10.7 %copy-start.4 = (f32[296,256]{1,0:T(8,128)S(1)}, f32[296,256]{1,0:T(8,128)}, u32[]{:S(2)}) copy-start(f32[296,256]{1,0:T(8,128)} %get-tuple-element.57) | copy-start | bytes 909316
  28.0 21.8 %collective-permute-start.9 = (f32[272,256]{1,0:T(8,128)S(1)}, f32[272,256]{1,0:T(8,128)S(1)}, u32[]{:S(2)}, u32[]{:S(2)}) collective-permute-start(f32[272,256]{1,0:T(8,128)S(1)} %get-tuple-element.63), channel_id=1, source_target_pairs={{0,1},{1,0},{2,3},{3,2},{4,5},{5,4},{6,7},{7,6},{8,9},{9,8},{10,11... | collective-permute-start | bytes 835592 | tf_op jit(solution)/shard_map/ppermute | solution.py:459
  31.3 13.0 %collective-permute-start.6 = (f32[296,256]{1,0:T(8,128)S(1)}, f32[296,256]{1,0:T(8,128)S(1)}, u32[]{:S(2)}, u32[]{:S(2)}) collective-permute-start(f32[296,256]{1,0:T(8,128)S(1)} %copy-done.4), channel_id=1, source_target_pairs={{0,2},{1,1},{2,4},{3,3},{4,6},{5,5},{6,8},{7,7},{8,10},{9,9},{10,1... | collective-permute-start | bytes 909320 | tf_op jit(solution)/shard_map/ppermute | solution.py:457
  32.8 11.6 %collective-permute-start.7 = (f32[296,256]{1,0:T(8,128)S(1)}, f32[296,256]{1,0:T(8,128)S(1)}, u32[]{:S(2)}, u32[]{:S(2)}) collective-permute-start(f32[296,256]{1,0:T(8,128)S(1)} %collective-permute-done.2), channel_id=1, source_target_pairs={{65,64},{1,0}} | collective-permute-start | bytes 909320 | tf_op jit(solution)/shard_map/ppermute | solution.py:458
  44.2 15.0 %collective-permute-start.11 = (f32[272,256]{1,0:T(8,128)S(1)}, f32[272,256]{1,0:T(8,128)S(1)}, u32[]{:S(2)}, u32[]{:S(2)}) collective-permute-start(f32[272,256]{1,0:T(8,128)S(1)} %get-tuple-element.68), channel_id=1, source_target_pairs={{0,1},{1,0},{2,3},{3,2},{4,5},{5,4},{6,7},{7,6},{8,9},{9,8},{10,11... | collective-permute-start | bytes 835592 | tf_op jit(solution)/shard_map/ppermute | solution.py:464
  49.0 5.9 %collective-permute-start.8 = (f32[2,16,256]{2,1,0:T(8,128)S(1)}, f32[2,16,256]{2,1,0:T(8,128)S(1)}, u32[]{:S(2)}, u32[]{:S(2)}) collective-permute-start(f32[2,16,256]{2,1,0:T(8,128)S(1)} %get-tuple-element.59), channel_id=1, source_target_pairs={{1,0},{2,1},{3,2},{4,3},{5,4},{6,5},{7,6},{8,7},{9,8},{10,9},{11,1... | collective-permute-start | bytes 98312 | tf_op jit(solution)/shard_map/ppermute | solution.py:468
  53.2 9.8 %collective-permute-start.12 = (f32[272,256]{1,0:T(8,128)S(1)}, f32[272,256]{1,0:T(8,128)S(1)}, u32[]{:S(2)}, u32[]{:S(2)}) collective-permute-start(f32[272,256]{1,0:T(8,128)S(1)} %get-tuple-element.69), channel_id=1, source_target_pairs={{0,1},{1,0},{2,3},{3,2},{4,5},{5,4},{6,7},{7,6},{8,9},{9,8},{10,11... | collective-permute-start | bytes 835592 | tf_op jit(solution)/shard_map/ppermute | solution.py:473
  58.5 10.5 %collective-permute-start.10 = (f32[272,256]{1,0:T(8,128)S(1)}, f32[272,256]{1,0:T(8,128)S(1)}, u32[]{:S(2)}, u32[]{:S(2)}) collective-permute-start(f32[272,256]{1,0:T(8,128)S(1)} %get-tuple-element.66), channel_id=1, source_target_pairs={{0,1},{1,0},{2,3},{3,2},{4,5},{5,4},{6,7},{7,6},{8,9},{9,8},{10,11... | collective-permute-start | bytes 835592 | tf_op jit(solution)/shard_map/ppermute | solution.py:478

commit v12 on v10

--- a/solution.py
+++ b/solution.py
@@ -300,7 +300,7 @@
     piece_out(r, f2, pushed, own, away)
 
 
-def second_kernel(q1, parts, swap, link, following, table, q_ref, own, away, f1, p0, pushed, z, tab, *rest):
+def second_kernel(q1, parts, swap, link, following, straight, table, q_ref, own, away, f1, p0, pushed, z, tab, *rest):
     work, sems = rest[:-1], rest[-1]
     r = lax.axis_index("row")
     copies, later = Copies(sems), Copies(sems)
@@ -309,6 +309,14 @@
     parts_in(copies, r, p0, parts, 0, swap, N)
     later.start(table, tab)
     copies.wait()
+
+    @pl.when((r == 0) & (lax.axis_index("tm") == lax.axis_size("tm") // 2))
+    def _():
+        again = Copies(sems)
+        again.used = 8
+        for zz in range(2):
+            again.start(straight.at[pl.ds(HALF * zz, HALF)], f1.at[zz, pl.ds(pl.multiple_of(HALF * r, HALF), HALF)])
+        again.wait()
 
     @pl.when((r == 0) & (lax.axis_index("tm") == 0))
     def _():
@@ -441,12 +449,13 @@
         [VM] * 5, stage, 12, [ANY] + [HB] * 6, 4 * unit, vmem=61000 << 10,
     )(to_near, *raw)
     f_swap = lax.ppermute(to_swap, both, swap)
-    f_next = lax.ppermute(to_next, both, ahead + direct)
+    f_next = lax.ppermute(to_next, both, ahead)
 
     d3, q2 = call(
         near_kernel, [field, full], [VM, VM], [FIELD, PARTS, TABLE] + WORK, 8, [ANY] * 4, unit, vmem=50000 << 10,
     )(wave, mine, f_near, table)
-    q2, to_chain, to_link, to_ahead = lax.optimization_barrier((q2, to_chain, to_link, to_ahead))
+    q2, to_chain, to_link, to_ahead, to_next = lax.optimization_barrier((q2, to_chain, to_link, to_ahead, to_next))
+    f_direct = lax.ppermute(to_next, both, direct)
     f_link = lax.ppermute(to_link, both, chain)
     f_chain = lax.ppermute(to_chain, both, chain)
     f_ahead = lax.ppermute(to_ahead, both, ahead)
@@ -458,9 +467,9 @@
     f_relay = lax.ppermute(f_around, both, onward)
     back_a = lax.ppermute(away_a, both, swap)
     q0, own_b, away_b = call(
-        second_kernel, [full] + pieces, [VM] * 3, [FIELD, PARTS, PUSH, FIELD, TABLE] + WORK, 8,
-        [VM] + [ANY] * 5, 2 * unit,
-    )(q1, parts, f_swap, f_link, f_next, table)
+        second_kernel, [full] + pieces, [VM] * 3, [FIELD, PARTS, PUSH, FIELD, TABLE] + WORK, 12,
+        [VM] + [ANY] * 6, 2 * unit,
+    )(q1, parts, f_swap, f_link, f_next, f_direct, table)
     back_b = lax.ppermute(away_b, both, swap)
     d0, to_back = call(
         edge_kernel, [field, (2, PUSHED, N)], [VM, VM], [FIELD, PARTS, TABLE] + WORK, 16, [ANY] * 5, unit,

time: 71.2 us -> 71 us (level)
  waiting for transfers between devices: 9.44 us -> 15.4 us
  starting transfers between devices: 21.7 us -> 15.8 us
    ppermute x1, starting transfers between devices: 5.37 us -> 0.08 us  [body(): from_back = lax.ppermute(to_back, both, back)]
    ppermute x1 -> x2, waiting for transfers between devices: 0.01 us -> 3.45 us  [the longest x1 3.45 us: body(): f_direct = lax.ppermute(to_next, both, direct)]
    ppermute x1, waiting for transfers between devices: 0.86 us -> 3.64 us  [body(): back_c = lax.ppermute(away_c, both, swap)]
    ppermute x1, starting transfers between devices: 2.75 us -> 0.09 us  [body(): back_b = lax.ppermute(away_b, both, swap)]
    ppermute x1, starting transfers between devices: 0.1 us -> 2.38 us  [body(): f_chain = lax.ppermute(to_chain, both, chain)]
    ppermute x1, waiting for transfers between devices: 2.54 us -> 4.8 us  [body(): back_d = lax.ppermute(away_d, both, swap)]
    ppermute x1, starting transfers between devices: 0.31 us -> 2.29 us  [body(): back_c = lax.ppermute(away_c, both, swap)]
    ppermute x1, starting transfers between devices: 2.05 us -> 0.14 us  [body(): back_d = lax.ppermute(away_d, both, swap)]
  transfers between devices with their start and end apart: 13 -> 14, of which waited for: 5 -> 6; matrix products, arithmetic and copies ran while one was open for 0% -> 0% of each run, Pallas kernels for 49% -> 49%
where the time goes in v12:
time: 71 us; the launch traced here: 70.5 us
  Pallas kernels  38.3 us (54%)
  starting transfers between devices  15.8 us (22%)
  waiting for transfers between devices  15.4 us (22%)
  between operations  1.04 us (1%)
    pallas_call x1, Pallas kernels, body(): call(second_kernel, [full] + pieces, [VM] * 3, [FIELD, PARTS, PUSH, FIELD...  7.83 us
    pallas_call x1, Pallas kernels, body(): call(first_kernel, [full] + pieces, [VM] * 3, [FIELD, PARTS, PUSH, FIELD,...  7.29 us
    ppermute x1, waiting for transfers between devices, body(): back_d = lax.ppermute(away_d, both, swap)  4.8 us
    pallas_call x1, Pallas kernels, body(): call(edge_kernel, [field, (2, PUSHED, N)], [VM, VM], [FIELD, PARTS, TABLE...  4.58 us
    pallas_call x1, Pallas kernels, body(): call(near_kernel, [field, full], [VM, VM], [FIELD, PARTS, TABLE] + WORK,...  4.15 us
    ppermute x1, waiting for transfers between devices, body(): back_c = lax.ppermute(away_c, both, swap)  3.64 us
    pallas_call x1, Pallas kernels, body(): call(fourth_kernel, pieces + [(8 * N, N)], [VM, VM, ANY], [PARTS, PUSH, F...  3.56 us
    pallas_call x1, Pallas kernels, body(): call(third_kernel, pieces + [(8 * N, N)], [VM, VM, ANY], [FIELD, PUSH, FI...  3.49 us
  transfers between devices with their start and end apart: 14, of which 6 were waited for; matrix products, arithmetic and copies ran while one was open for 0% of the time, Pallas kernels for 49%

profile of v12, /device:TPU:4, one launch (start us, length us, event | category | flops | bytes accessed | tf_op | source)
XLA Modules:
  0.0 70.5 jit_solution(6612034135706067907)
XLA Ops:
  0.6 2.1 %shard_map.94 = (f32[296,256]{1,0:T(8,128)}, f32[296,256]{1,0:T(8,128)}, f32[40,256]{1,0:T(8,128)}) custom-call(f32[2048,256]{1,0:T(8,128)} %bitcast.2, f32[8,2048]{1,0:T(8,128)} %refs_0_.3, f32[8,2048]{1,0:T(8,128)} %refs_1_.3, f32[8,2048]{1,0:T(8,128)} %refs_2_.3, s32[8,2048]{1,0:T(8,128)} %refs_3_.3, s32[8,2048]{1,0:T(8,128)} %refs_4_.3), custom_call_target="tpu_custom_call" | custom-call | flops 1048576 | bytes 4194304 | tf_op jit(solution)/shard_map/pallas_call | solution.py:441
  2.7 1.3 %collective-permute-start = (f32[296,256]{1,0:T(8,128)}, f32[296,256]{1,0:T(8,128)S(1)}, u32[]{:S(2)}, u32[]{:S(2)}) collective-permute-start(f32[296,256]{1,0:T(8,128)} %get-tuple-element.41.near), channel_id=1, source_target_pairs={{0,1},{1,0},{2,3},{3,2},{4,5},{5,4},{6,7},{7,6},{8,9},{9,8},{10,11... | collective-permute-start | bytes 909320 | tf_op jit(solution)/shard_map/ppermute | solution.py:445
  4.0 0.8 %collective-permute-start.2 = (f32[296,256]{1,0:T(8,128)}, f32[296,256]{1,0:T(8,128)S(1)}, u32[]{:S(2)}, u32[]{:S(2)}) collective-permute-start(f32[296,256]{1,0:T(8,128)} %get-tuple-element.57), channel_id=1, source_target_pairs={{62,65},{126,1}} | collective-permute-start | bytes 909320 | tf_op jit(solution)/shard_map/ppermute | solution.py:446
  4.8 2.7 %shard_map.96 = (f32[8,40,256]{2,1,0:T(8,128)}, f32[376,256]{1,0:T(8,128)}, f32[296,256]{1,0:T(8,128)}, f32[256,256]{1,0:T(8,128)}, f32[256,256]{1,0:T(8,128)}) custom-call(f32[296,256]{1,0:T(8,128)} %get-tuple-element.41.near, f32[2048,256]{1,0:T(8,128)} %bitcast.3, f32[8,2048]{1,0:T(8,128)} %refs_0_.3, f32[8,2048]{1,0:T(8,128)} %refs_1_.3, ...), custom_call_target="tpu_custom_call" | custom-call | flops 34359738368 | bytes 4194304 | tf_op jit(solution)/shard_map/pallas_call | solution.py:447
  7.6 1.5 %collective-permute-start.4 = (f32[256,256]{1,0:T(8,128)}, f32[256,256]{1,0:T(8,128)S(1)}, u32[]{:S(2)}, u32[]{:S(2)}) collective-permute-start(f32[256,256]{1,0:T(8,128)} %get-tuple-element.54), channel_id=1, source_target_pairs={{0,2},{1,1},{2,4},{3,3},{4,6},{5,5},{6,8},{7,7},{8,10},{9,9},{10,1... | collective-permute-start | bytes 786440 | tf_op jit(solution)/shard_map/ppermute | solution.py:452
  9.1 1.6 %collective-permute-start.1 = (f32[376,256]{1,0:T(8,128)}, f32[376,256]{1,0:T(8,128)S(1)}, u32[]{:S(2)}, u32[]{:S(2)}) collective-permute-start(f32[376,256]{1,0:T(8,128)} %get-tuple-element.44), channel_id=1, source_target_pairs={{0,1},{1,0},{2,3},{3,2},{4,5},{5,4},{6,7},{7,6},{8,9},{9,8},{10,11... | collective-permute-start | bytes 1155080 | tf_op jit(solution)/shard_map/ppermute | solution.py:451
  10.6 1.3 %collective-permute-done.near = f32[296,256]{1,0:T(8,128)S(1)} collective-permute-done((f32[296,256]{1,0:T(8,128)}, f32[296,256]{1,0:T(8,128)S(1)}, u32[]{:S(2)}, u32[]{:S(2)}) %collective-permute-start) | collective-permute-done | bytes 303136 | tf_op jit(solution)/shard_map/ppermute | solution.py:445
  12.0 0.0 copy-done
  12.0 0.0 copy-done.1
  12.0 0.0 copy-done.2
  12.0 0.0 copy-start.7
  12.0 0.0 copy-start.6
  12.0 0.0 copy-start.5
  12.0 0.0 copy-start.3
  12.0 4.1 %shard_map.95 = (f32[2,256,256]{2,1,0:T(8,128)S(1)}, f32[2,40,256]{2,1,0:T(8,128)S(1)}) custom-call(f32[2048,256]{1,0:T(8,128)S(1)} %bitcast.4, f32[40,256]{1,0:T(8,128)S(1)} %copy-done.1, f32[296,256]{1,0:T(8,128)S(1)} %collective-permute-done.near, bf16[2,2,2,256,256]{4,3,2,1,0:T(8,128)(2,1)S(1)} %copy-done.2), custom_call_target="tpu_custom_call" | custom-call | flops 8589934592 | bytes 4194304 | tf_op jit(solution)/shard_map/pallas_call | solution.py:454
  16.2 0.0 copy-done.7
  16.2 1.3 %collective-permute-start.3 = (f32[256,256]{1,0:T(8,128)S(1)}, f32[256,256]{1,0:T(8,128)S(1)}, u32[]{:S(2)}, u32[]{:S(2)}) collective-permute-start(f32[256,256]{1,0:T(8,128)S(1)} %copy-done.7), channel_id=1, source_target_pairs={{0,1},{1,2},{2,3},{3,4},{4,5},{5,6},{6,7},{7,8},{8,9},{9,10},{10,1... | collective-permute-start | bytes 786440 | tf_op jit(solution)/shard_map/ppermute | solution.py:459
  17.4 0.0 copy-done.6
  17.5 1.3 %collective-permute-start.5 = (f32[256,256]{1,0:T(8,128)S(1)}, f32[256,256]{1,0:T(8,128)S(1)}, u32[]{:S(2)}, u32[]{:S(2)}) collective-permute-start(f32[256,256]{1,0:T(8,128)S(1)} %copy-done.6), channel_id=1, source_target_pairs={{62,64}} | collective-permute-start | bytes 786440 | tf_op jit(solution)/shard_map/ppermute | solution.py:458
  18.7 1.5 %collective-permute-done.1.swap = f32[376,256]{1,0:T(8,128)S(1)} collective-permute-done((f32[376,256]{1,0:T(8,128)}, f32[376,256]{1,0:T(8,128)S(1)}, u32[]{:S(2)}, u32[]{:S(2)}) %collective-permute-start.1) | collective-permute-done | bytes 385056 | tf_op jit(solution)/shard_map/ppermute | solution.py:451
  20.3 2.4 %collective-permute-start.6 = (f32[296,256]{1,0:T(8,128)S(1)}, f32[296,256]{1,0:T(8,128)S(1)}, u32[]{:S(2)}, u32[]{:S(2)}) collective-permute-start(f32[296,256]{1,0:T(8,128)S(1)} %copy-done.5), channel_id=1, source_target_pairs={{0,1},{1,2},{2,3},{3,4},{4,5},{5,6},{6,7},{7,8},{8,9},{9,10},{10,1... | collective-permute-start | bytes 909320 | tf_op jit(solution)/shard_map/ppermute | solution.py:460
  22.7 7.3 %shard_map.97 = (f32[2,40,256]{2,1,0:T(8,128)S(1)}, f32[272,256]{1,0:T(8,128)S(1)}, f32[272,256]{1,0:T(8,128)S(1)}) custom-call(f32[2,40,256]{2,1,0:T(8,128)S(1)} %get-tuple-element.50.q2, f32[2048,256]{1,0:T(8,128)S(1)} %bitcast.5, f32[8,40,256]{2,1,0:T(8,128)S(1)} %copy-done.3, f32[376,256]{1,0:T(8,128)S(1)} %collective-permute-done.1.swap, ...), custom_call_target="tpu_custom_call" | custom-call | flops 17179869184 | bytes 4194304 | tf_op jit(solution)/shard_map/pallas_call | solution.py:462
  30.0 0.0 collective-permute-done.2
  30.0 0.0 copy-done.4
  30.0 1.6 %collective-permute-start.7 = (f32[296,256]{1,0:T(8,128)S(1)}, f32[296,256]{1,0:T(8,128)S(1)}, u32[]{:S(2)}, u32[]{:S(2)}) collective-permute-start(f32[296,256]{1,0:T(8,128)S(1)} %copy-done.4), channel_id=1, source_target_pairs={{0,2},{1,1},{2,4},{3,3},{4,6},{5,5},{6,8},{7,7},{8,10},{9,9},{10,1... | collective-permute-start | bytes 909320 | tf_op jit(solution)/shard_map/ppermute | solution.py:461
  31.6 0.0 collective-permute-done.4.following
  31.6 0.3 collective-permute-start.10
  31.9 0.0 collective-permute-done.3.link
  31.9 1.3 %collective-permute-start.8 = (f32[296,256]{1,0:T(8,128)S(1)}, f32[296,256]{1,0:T(8,128)S(1)}, u32[]{:S(2)}, u32[]{:S(2)}) collective-permute-start(f32[296,256]{1,0:T(8,128)S(1)} %collective-permute-done.2), channel_id=1, source_target_pairs={{65,64},{1,0}} | collective-permute-start | bytes 909320 | tf_op jit(solution)/shard_map/ppermute | solution.py:467
  33.2 3.4 %collective-permute-done.5.straight = f32[256,256]{1,0:T(8,128)S(1)} collective-permute-done((f32[256,256]{1,0:T(8,128)S(1)}, f32[256,256]{1,0:T(8,128)S(1)}, u32[]{:S(2)}, u32[]{:S(2)}) %collective-permute-start.5) | collective-permute-done | bytes 262176 | tf_op jit(solution)/shard_map/ppermute | solution.py:458
  36.6 7.8 %shard_map.98 = (f32[2,40,256]{2,1,0:T(8,128)S(1)}, f32[272,256]{1,0:T(8,128)S(1)}, f32[272,256]{1,0:T(8,128)S(1)}) custom-call(f32[2,40,256]{2,1,0:T(8,128)S(1)} %get-tuple-element.52.q1, f32[8,40,256]{2,1,0:T(8,128)S(1)} %copy-done.3, f32[376,256]{1,0:T(8,128)S(1)} %collective-permute-done.1.swap, f32[256,256]{1,0:T(8,128)S(1)} %collective-permute-done.3.link, ...), custom_call_target="tpu_custom_call" | custom-call | flops 17179869184 | bytes 4194304 | tf_op jit(solution)/shard_map/pallas_call | solution.py:469
  44.5 0.1 collective-permute-start.12
  44.6 0.0 collective-permute-done.6.chain
  44.6 0.0 collective-permute-done.7.ahead
  44.6 0.6 collective-permute-done.8.relay
  45.2 4.6 %shard_map.99 = (f32[2,256,256]{2,1,0:T(8,128)S(1)}, f32[2,16,256]{2,1,0:T(8,128)S(1)}) custom-call(f32[2,40,256]{2,1,0:T(8,128)S(1)} %get-tuple-element.55.after.q0, f32[296,256]{1,0:T(8,128)S(1)} %collective-permute-done.6.chain, f32[296,256]{1,0:T(8,128)S(1)} %collective-permute-done.7.ahead, f32[296,256]{1,0:T(8,128)S(1)} %collective-permute-done.8.relay, ...), custom_call_target="tpu_custom_call" | custom-call | flops 8589934592 | bytes 4194304 | tf_op jit(solution)/shard_map/pallas_call | solution.py:474
  49.8 0.1 collective-permute-start.9
  49.8 0.0 collective-permute-done.10.back_a
  49.9 3.5 %shard_map.100 = (f32[272,256]{1,0:T(8,128)S(1)}, f32[272,256]{1,0:T(8,128)S(1)}, f32[2048,256]{1,0:T(8,128)}) custom-call(f32[2,256,256]{2,1,0:T(8,128)S(1)} %get-tuple-element.60.d_ref, f32[2,40,256]{2,1,0:T(8,128)S(1)} %get-tuple-element.55.after.q0, f32[272,256]{1,0:T(8,128)S(1)} %get-tuple-element.61.own_a, f32[272,256]{1,0:T(8,128)S(1)} %get-tuple-element.62.own_b, ...), custom_call_target="tpu_custom_call" | custom-call | flops 8589934592 | bytes 4194304 | tf_op jit(solution)/shard_map/pallas_call | solution.py:478
  53.3 2.3 %collective-permute-start.13 = (f32[272,256]{1,0:T(8,128)S(1)}, f32[272,256]{1,0:T(8,128)S(1)}, u32[]{:S(2)}, u32[]{:S(2)}) collective-permute-start(f32[272,256]{1,0:T(8,128)S(1)} %get-tuple-element.69), channel_id=1, source_target_pairs={{0,1},{1,0},{2,3},{3,2},{4,5},{5,4},{6,7},{7,6},{8,9},{9,8},{10,11... | collective-permute-start | bytes 835592 | tf_op jit(solution)/shard_map/ppermute | solution.py:482
  55.6 0.0 collective-permute-done.9.from_back
  55.6 3.6 %shard_map.101 = (f32[272,256]{1,0:T(8,128)S(1)}, f32[272,256]{1,0:T(8,128)S(1)}, f32[2048,256]{1,0:T(8,128)}) custom-call(f32[2,256,256]{2,1,0:T(8,128)S(1)} %get-tuple-element.42.d_ref, f32[8,40,256]{2,1,0:T(8,128)S(1)} %copy-done.3, f32[376,256]{1,0:T(8,128)S(1)} %collective-permute-done.1.swap, ...), custom_call_target="tpu_custom_call", output_to_operand_aliasing={{2}: (6, {})} | custom-call | flops 17179869184 | bytes 4194304 | tf_op jit(solution)/shard_map/pallas_call | solution.py:483
  59.2 0.1 collective-permute-start.11
  59.3 0.0 collective-permute-done.12.back_b
  59.4 3.6 %collective-permute-done.13.back_c = f32[272,256]{1,0:T(8,128)S(1)} collective-permute-done((f32[272,256]{1,0:T(8,128)S(1)}, f32[272,256]{1,0:T(8,128)S(1)}, u32[]{:S(2)}, u32[]{:S(2)}) %collective-permute-start.13) | collective-permute-done | bytes 278560 | tf_op jit(solution)/shard_map/ppermute | solution.py:482
  63.0 1.2 %shard_map.102 = (f32[2048,256]{1,0:T(8,128)}, f32[8,2048]{1,0:T(8,128)S(1)}, f32[8,2048]{1,0:T(8,128)S(1)}) custom-call(f32[272,256]{1,0:T(8,128)S(1)} %get-tuple-element.61.own_a, f32[272,256]{1,0:T(8,128)S(1)} %get-tuple-element.62.own_b, f32[272,256]{1,0:T(8,128)S(1)} %get-tuple-element.64.own_c, ...), custom_call_target="tpu_custom_call", output_to_operand_aliasing={{0}: (7, {})} | custom-call | flops 1048576 | bytes 4194304 | tf_op jit(solution)/shard_map/pallas_call | solution.py:489
  64.2 4.8 %collective-permute-done.11.back_d = f32[272,256]{1,0:T(8,128)S(1)} collective-permute-done((f32[272,256]{1,0:T(8,128)S(1)}, f32[272,256]{1,0:T(8,128)S(1)}, u32[]{:S(2)}, u32[]{:S(2)}) %collective-permute-start.11) | collective-permute-done | bytes 278560 | tf_op jit(solution)/shard_map/ppermute | solution.py:487
  69.0 1.4 %shard_map.103 = (f32[2048,256]{1,0:T(8,128)}, f32[8,2048]{1,0:T(8,128)}, f32[8,2048]{1,0:T(8,128)}) custom-call(f32[272,256]{1,0:T(8,128)S(1)} %collective-permute-done.11.back_d, f32[2048,256]{1,0:T(8,128)} %get-tuple-element.71.wave_in, f32[8,2048]{1,0:T(8,128)S(1)} %get-tuple-element.72.phase_in, ...), custom_call_target="tpu_custom_call", output_to_operand_aliasing={{0}: (1, {})} | custom-call | flops 1048576 | bytes 4194304 | tf_op jit(solution)/shard_map/pallas_call | solution.py:493
  (6 shorter events, 0.0 us)
Async XLA Ops:
  2.7 9.2 %collective-permute-start = (f32[296,256]{1,0:T(8,128)}, f32[296,256]{1,0:T(8,128)S(1)}, u32[]{:S(2)}, u32[]{:S(2)}) collective-permute-start(f32[296,256]{1,0:T(8,128)} %get-tuple-element.41.near), channel_id=1, source_target_pairs={{0,1},{1,0},{2,3},{3,2},{4,5},{5,4},{6,7},{7,6},{8,9},{9,8},{10,11... | collective-permute-start | bytes 909320 | tf_op jit(solution)/shard_map/ppermute | solution.py:445
  4.0 7.9 %copy-start = (f32[8,2,128,256]{3,2,1,0:T(8,128)S(1)}, f32[8,2,128,256]{3,2,1,0:T(8,128)}, u32[]{:S(2)}) copy-start(f32[8,2,128,256]{3,2,1,0:T(8,128)} %param.7) | copy-start | bytes 6291460
  4.0 7.9 %copy-start.1 = (f32[40,256]{1,0:T(8,128)S(1)}, f32[40,256]{1,0:T(8,128)}, u32[]{:S(2)}) copy-start(f32[40,256]{1,0:T(8,128)} %get-tuple-element.40.mine) | copy-start | bytes 122884
  4.0 7.9 %copy-start.2 = (bf16[2,2,2,256,256]{4,3,2,1,0:T(8,128)(2,1)S(1)}, bf16[2,2,2,256,256]{4,3,2,1,0:T(8,128)(2,1)}, u32[]{:S(2)}) copy-start(bf16[2,2,2,256,256]{4,3,2,1,0:T(8,128)(2,1)} %constant.2.clone.table) | copy-start | bytes 3145732
  4.0 25.9 %collective-permute-start.2 = (f32[296,256]{1,0:T(8,128)}, f32[296,256]{1,0:T(8,128)S(1)}, u32[]{:S(2)}, u32[]{:S(2)}) collective-permute-start(f32[296,256]{1,0:T(8,128)} %get-tuple-element.57), channel_id=1, source_target_pairs={{62,65},{126,1}} | collective-permute-start | bytes 909320 | tf_op jit(solution)/shard_map/ppermute | solution.py:446
  7.6 24.1 %collective-permute-start.4 = (f32[256,256]{1,0:T(8,128)}, f32[256,256]{1,0:T(8,128)S(1)}, u32[]{:S(2)}, u32[]{:S(2)}) collective-permute-start(f32[256,256]{1,0:T(8,128)} %get-tuple-element.54), channel_id=1, source_target_pairs={{0,2},{1,1},{2,4},{3,3},{4,6},{5,5},{6,8},{7,7},{8,10},{9,9},{10,1... | collective-permute-start | bytes 786440 | tf_op jit(solution)/shard_map/ppermute | solution.py:452
  9.1 11.2 %collective-permute-start.1 = (f32[376,256]{1,0:T(8,128)}, f32[376,256]{1,0:T(8,128)S(1)}, u32[]{:S(2)}, u32[]{:S(2)}) collective-permute-start(f32[376,256]{1,0:T(8,128)} %get-tuple-element.44), channel_id=1, source_target_pairs={{0,1},{1,0},{2,3},{3,2},{4,5},{5,4},{6,7},{7,6},{8,9},{9,8},{10,11... | collective-permute-start | bytes 1155080 | tf_op jit(solution)/shard_map/ppermute | solution.py:451
  12.0 4.2 %copy-start.7 = (f32[256,256]{1,0:T(8,128)S(1)}, f32[256,256]{1,0:T(8,128)}, u32[]{:S(2)}) copy-start(f32[256,256]{1,0:T(8,128)} %get-tuple-element.53) | copy-start | bytes 786436
  12.0 5.5 %copy-start.6 = (f32[256,256]{1,0:T(8,128)S(1)}, f32[256,256]{1,0:T(8,128)}, u32[]{:S(2)}) copy-start(f32[256,256]{1,0:T(8,128)} %get-tuple-element.54) | copy-start | bytes 786436
  12.0 8.3 %copy-start.5 = (f32[296,256]{1,0:T(8,128)S(1)}, f32[296,256]{1,0:T(8,128)}, u32[]{:S(2)}) copy-start(f32[296,256]{1,0:T(8,128)} %get-tuple-element.56) | copy-start | bytes 909316
  12.0 10.7 %copy-start.3 = (f32[8,40,256]{2,1,0:T(8,128)S(1)}, f32[8,40,256]{2,1,0:T(8,128)}, u32[]{:S(2)}) copy-start(f32[8,40,256]{2,1,0:T(8,128)} %get-tuple-element.43.parts) | copy-start | bytes 983044
  16.2 15.7 %collective-permute-start.3 = (f32[256,256]{1,0:T(8,128)S(1)}, f32[256,256]{1,0:T(8,128)S(1)}, u32[]{:S(2)}, u32[]{:S(2)}) collective-permute-start(f32[256,256]{1,0:T(8,128)S(1)} %copy-done.7), channel_id=1, source_target_pairs={{0,1},{1,2},{2,3},{3,4},{4,5},{5,6},{6,7},{7,8},{8,9},{9,10},{10,1... | collective-permute-start | bytes 786440 | tf_op jit(solution)/shard_map/ppermute | solution.py:459
  17.5 19.2 %collective-permute-start.5 = (f32[256,256]{1,0:T(8,128)S(1)}, f32[256,256]{1,0:T(8,128)S(1)}, u32[]{:S(2)}, u32[]{:S(2)}) collective-permute-start(f32[256,256]{1,0:T(8,128)S(1)} %copy-done.6), channel_id=1, source_target_pairs={{62,64}} | collective-permute-start | bytes 786440 | tf_op jit(solution)/shard_map/ppermute | solution.py:458
  20.3 24.3 %collective-permute-start.6 = (f32[296,256]{1,0:T(8,128)S(1)}, f32[296,256]{1,0:T(8,128)S(1)}, u32[]{:S(2)}, u32[]{:S(2)}) collective-permute-start(f32[296,256]{1,0:T(8,128)S(1)} %copy-done.5), channel_id=1, source_target_pairs={{0,1},{1,2},{2,3},{3,4},{4,5},{5,6},{6,7},{7,8},{8,9},{9,10},{10,1... | collective-permute-start | bytes 909320 | tf_op jit(solution)/shard_map/ppermute | solution.py:460
  22.7 7.3 %copy-start.4 = (f32[296,256]{1,0:T(8,128)S(1)}, f32[296,256]{1,0:T(8,128)}, u32[]{:S(2)}) copy-start(f32[296,256]{1,0:T(8,128)} %get-tuple-element.57) | copy-start | bytes 909316
  30.0 14.6 %collective-permute-start.7 = (f32[296,256]{1,0:T(8,128)S(1)}, f32[296,256]{1,0:T(8,128)S(1)}, u32[]{:S(2)}, u32[]{:S(2)}) collective-permute-start(f32[296,256]{1,0:T(8,128)S(1)} %copy-done.4), channel_id=1, source_target_pairs={{0,2},{1,1},{2,4},{3,3},{4,6},{5,5},{6,8},{7,7},{8,10},{9,9},{10,1... | collective-permute-start | bytes 909320 | tf_op jit(solution)/shard_map/ppermute | solution.py:461
  31.6 18.2 %collective-permute-start.10 = (f32[272,256]{1,0:T(8,128)S(1)}, f32[272,256]{1,0:T(8,128)S(1)}, u32[]{:S(2)}, u32[]{:S(2)}) collective-permute-start(f32[272,256]{1,0:T(8,128)S(1)} %get-tuple-element.63), channel_id=1, source_target_pairs={{0,1},{1,0},{2,3},{3,2},{4,5},{5,4},{6,7},{7,6},{8,9},{9,8},{10,11... | collective-permute-start | bytes 835592 | tf_op jit(solution)/shard_map/ppermute | solution.py:468
  31.9 13.3 %collective-permute-start.8 = (f32[296,256]{1,0:T(8,128)S(1)}, f32[296,256]{1,0:T(8,128)S(1)}, u32[]{:S(2)}, u32[]{:S(2)}) collective-permute-start(f32[296,256]{1,0:T(8,128)S(1)} %collective-permute-done.2), channel_id=1, source_target_pairs={{65,64},{1,0}} | collective-permute-start | bytes 909320 | tf_op jit(solution)/shard_map/ppermute | solution.py:467
  44.5 14.9 %collective-permute-start.12 = (f32[272,256]{1,0:T(8,128)S(1)}, f32[272,256]{1,0:T(8,128)S(1)}, u32[]{:S(2)}, u32[]{:S(2)}) collective-permute-start(f32[272,256]{1,0:T(8,128)S(1)} %get-tuple-element.68), channel_id=1, source_target_pairs={{0,1},{1,0},{2,3},{3,2},{4,5},{5,4},{6,7},{7,6},{8,9},{9,8},{10,11... | collective-permute-start | bytes 835592 | tf_op jit(solution)/shard_map/ppermute | solution.py:473
  49.8 5.9 %collective-permute-start.9 = (f32[2,16,256]{2,1,0:T(8,128)S(1)}, f32[2,16,256]{2,1,0:T(8,128)S(1)}, u32[]{:S(2)}, u32[]{:S(2)}) collective-permute-start(f32[2,16,256]{2,1,0:T(8,128)S(1)} %get-tuple-element.59), channel_id=1, source_target_pairs={{1,0},{2,1},{3,2},{4,3},{5,4},{6,5},{7,6},{8,7},{9,8},{10,9},{11,1... | collective-permute-start | bytes 98312 | tf_op jit(solution)/shard_map/ppermute | solution.py:477
  53.3 9.6 %collective-permute-start.13 = (f32[272,256]{1,0:T(8,128)S(1)}, f32[272,256]{1,0:T(8,128)S(1)}, u32[]{:S(2)}, u32[]{:S(2)}) collective-permute-start(f32[272,256]{1,0:T(8,128)S(1)} %get-tuple-element.69), channel_id=1, source_target_pairs={{0,1},{1,0},{2,3},{3,2},{4,5},{5,4},{6,7},{7,6},{8,9},{9,8},{10,11... | collective-permute-start | bytes 835592 | tf_op jit(solution)/shard_map/ppermute | solution.py:482
  59.2 9.8 %collective-permute-start.11 = (f32[272,256]{1,0:T(8,128)S(1)}, f32[272,256]{1,0:T(8,128)S(1)}, u32[]{:S(2)}, u32[]{:S(2)}) collective-permute-start(f32[272,256]{1,0:T(8,128)S(1)} %get-tuple-element.66), channel_id=1, source_target_pairs={{0,1},{1,0},{2,3},{3,2},{4,5},{5,4},{6,7},{7,6},{8,9},{9,8},{10,11... | collective-permute-start | bytes 835592 | tf_op jit(solution)/shard_map/ppermute | solution.py:487
